TPU v7x, 256 devices: a whole 4x4x8 slice. The times are simulated.
256 devices in a mesh: site: 64 (over z_lo, y, x), cons: 4 (over z_hi, core).
Axes of the slice: x: 4, y: 4, z: 8 (z_hi: 2, z_lo: 4; z = z_hi * 4 + z_lo), core: 2. Of those that a mesh axis runs over, the one named last changes fastest.
Arguments:
- tile_values: bfloat16 [5120, 128, 128], P(('site', 'cons')), may hold values from 0 to 64, as said below
- patient_block: int32 [5120], P(('site', 'cons')), may hold values from 0 to 7
- code_block: int32 [5120], P(('site', 'cons')), may hold values from 0 to 19
- month_index: int32 [5120], P(('site', 'cons')), may hold values from 0 to 119
- live_count: int32 [256], P(('site', 'cons')), may hold values from 4 to 20, as said below
- patient_factor: bfloat16 [65536, 256], P('site'), may hold values from 0.0009 to 0.5, as said below
- month_factor: float32 [120, 256], replicated, may hold values from 0.001 to 0.01
- consensus: float32 [2560, 1024], P('site', 'cons'), may hold values from 0.05 to 1
- scaled_duals: float32 [163840, 1024], P('site', 'cons'), may hold values from -1.2 to 1.2
Outputs:
- new_consensus: float32 [2560, 1024], P('site', 'cons')
- new_duals: float32 [163840, 1024], P('site', 'cons')
- new_months: float32 [120, 256], replicated
Inputs may be any that keep to these rules, and one draw needn't show every extreme that they name: `tile_values`: entries are whole counts. `live_count`: no device has more than 20 live slots, and some device has exactly 20. `patient_factor`: entries are positive.
All inputs are finite; a program needn't handle non-finite values.
Results may differ from a plain program's by a relative error of at most 0.0003.
Values may be sent and summed in bfloat16 or wider, within the bound.
No kernel may reach another device: no remote copies, remote signals or barrier semaphores. Data moves between devices by JAX's collectives and lax.ppermute only.
A program may use at most 64 MiB of HBM per device.

v0:
```python
import jax
import jax.numpy as jnp
from jax import lax
from jax.sharding import PartitionSpec as P

ITERS = 2


highest = lax.Precision.HIGHEST


def invert(matrix):
    factor = jnp.linalg.cholesky(matrix)
    identity = jnp.eye(matrix.shape[0], dtype=matrix.dtype)
    lower_inv = lax.linalg.triangular_solve(factor, identity, left_side=True, lower=True)
    return jnp.dot(lower_inv.T, lower_inv, precision=highest, preferred_element_type=jnp.float32)


def block_window(first, stop, turn, width, total):
    start = first + turn * width
    base = jnp.minimum(start, total - width)
    slot_ids = base + jnp.arange(width, dtype=jnp.int32)
    keep = (slot_ids >= start) & (slot_ids < stop)
    return (base, keep)


def turn_count(first, stop, width):
    return jnp.maximum(stop - first + width - 1, 0) // width


def tile_pass(
    first, stop, width, values, patient_at, code_at, month_at, factor, month_factor, code_rows
):
    total = values.shape[0]
    tile_size = values.shape[1]
    rank_size = factor.shape[1]
    month_count = month_factor.shape[0]
    factor_blocks = factor.reshape(factor.shape[0] // tile_size, tile_size, rank_size)
    block_count = code_rows // tile_size
    block_ids = jnp.arange(block_count, dtype=jnp.int32)
    month_ids = jnp.arange(month_count, dtype=jnp.int32)

    def tile_visit(turn, carry):
        grad_blocks, stored = carry
        base, keep = block_window(first, stop, turn, width, total)
        tiles_now = lax.dynamic_slice_in_dim(values, base, width, 0)
        patients_now = lax.dynamic_slice_in_dim(patient_at, base, width, 0)
        codes_now = lax.dynamic_slice_in_dim(code_at, base, width, 0)
        months_now = lax.dynamic_slice_in_dim(month_at, base, width, 0)
        patient_rows = jnp.take(factor_blocks, patients_now, axis=0)
        product = jnp.einsum(
            "kij,kir->kjr", tiles_now, patient_rows, preferred_element_type=jnp.float32
        )
        month_hot = (months_now[:, None] == month_ids[None, :]).astype(jnp.float32)
        scale = jnp.dot(
            month_hot, month_factor, precision=highest, preferred_element_type=jnp.float32
        )
        code_hot = ((block_ids[:, None] == codes_now[None, :]) & keep[None, :]).astype(jnp.float32)
        grad_blocks = grad_blocks + jnp.einsum(
            "bk,kjr->bjr", code_hot, product * scale[:, None, :], precision=highest
        )
        stored = lax.dynamic_update_slice_in_dim(stored, product, base, 0)
        return (grad_blocks, stored)

    start_grad = jnp.zeros((block_count, tile_size, rank_size), jnp.float32)
    start_store = jnp.zeros((total, tile_size, rank_size), jnp.float32)
    grad_blocks, stored = lax.fori_loop(
        0, turn_count(first, stop, width), tile_visit, (start_grad, start_store)
    )
    return (grad_blocks.reshape(code_rows, rank_size), stored)


def month_pass(first, stop, width, stored, code_at, month_at, anchor_blocks, totals):
    total = stored.shape[0]
    month_ids = jnp.arange(totals.shape[0], dtype=jnp.int32)

    def month_visit(turn, running):
        base, keep = block_window(first, stop, turn, width, total)
        product = lax.dynamic_slice_in_dim(stored, base, width, 0)
        codes_now = lax.dynamic_slice_in_dim(code_at, base, width, 0)
        months_now = lax.dynamic_slice_in_dim(month_at, base, width, 0)
        anchor = jnp.take(anchor_blocks, codes_now, axis=0)
        column = jnp.sum(product * anchor, axis=1)
        month_hot = ((month_ids[:, None] == months_now[None, :]) & keep[None, :]).astype(
            jnp.float32
        )
        return running + jnp.dot(
            month_hot, column, precision=highest, preferred_element_type=jnp.float32
        )

    return lax.fori_loop(0, turn_count(first, stop, width), month_visit, totals)


def on_device(
    tile_values,
    patient_block,
    code_block,
    month_index,
    live_count,
    patient_factor,
    month_factor,
    consensus,
    scaled_duals,
):
    tile_size = tile_values.shape[1]
    capacity = tile_values.shape[0]
    width = capacity // 10
    rank_size = patient_factor.shape[1]
    code_rows = scaled_duals.shape[0]
    share_rows = consensus.shape[0]
    live = live_count[0]
    identity = jnp.eye(rank_size, dtype=jnp.float32)
    month_gram = jnp.dot(
        month_factor.T, month_factor, precision=highest, preferred_element_type=jnp.float32
    )
    patient_gram = jnp.dot(patient_factor.T, patient_factor, preferred_element_type=jnp.float32)
    local_hess = patient_gram * month_gram
    local_rho = jnp.trace(local_hess) / rank_size
    inverse = invert(local_hess + local_rho * identity)
    rho_total, global_gram = lax.psum((local_rho, patient_gram), "site")
    gradient, stored = tile_pass(
        0,
        live,
        width,
        tile_values,
        patient_block,
        code_block,
        month_index,
        patient_factor,
        month_factor,
        code_rows,
    )
    share_start = lax.axis_index("site") * share_rows
    full_block = lax.all_gather(consensus, "site", axis=0, tiled=True)
    duals = scaled_duals
    for sweep in range(ITERS):
        local_copy = jnp.dot(
            gradient + local_rho * (full_block - duals),
            inverse,
            precision=highest,
            preferred_element_type=jnp.float32,
        )
        summed = lax.psum(local_rho * (local_copy + duals), "site")
        full_block = jnp.maximum(summed / rho_total, 0.0)
        owned_rows = lax.dynamic_slice_in_dim(full_block, share_start, share_rows, 0)
        duals = duals + local_copy - full_block
    anchor_blocks = full_block.reshape(code_rows // tile_size, tile_size, rank_size)
    month_zero = jnp.zeros(month_factor.shape, jnp.float32)
    month_sum = month_pass(
        0, live, width, stored, code_block, month_index, anchor_blocks, month_zero
    )
    code_gram = jnp.dot(
        owned_rows.T, owned_rows, precision=highest, preferred_element_type=jnp.float32
    )
    month_grad, code_gram_all = lax.psum((month_sum, code_gram), ("site", "cons"))
    month_hess = global_gram * code_gram_all
    month_rho = jnp.trace(month_hess) / rank_size
    solved = jnp.dot(
        month_grad + month_rho * month_factor,
        invert(month_hess + month_rho * identity),
        precision=highest,
        preferred_element_type=jnp.float32,
    )
    solved = jnp.maximum(solved, 0.0)
    new_months = solved / (jnp.mean(solved, axis=0, keepdims=True) + 1e-06)
    return (owned_rows, duals, new_months)


def solution(mesh):
    placed = (
        P(("site", "cons"), None, None),
        P(("site", "cons")),
        P(("site", "cons")),
        P(("site", "cons")),
        P(("site", "cons")),
        P("site", None),
        P(),
        P("site", "cons"),
        P("site", "cons"),
    )
    return jax.shard_map(
        on_device,
        mesh=mesh,
        in_specs=placed,
        out_specs=(P("site", "cons"), P("site", "cons"), P()),
        check_vma=False,
    )
```

profile of v0, /device:TPU:1, one launch (start us, length us, event | category | flops | bytes accessed | tf_op | source)
XLA Modules:
  0.0 2175.9 jit_solution(10285461429307609168)
XLA Ops:
  7.2 0.7 all-gather.2.cloned.1.call-update
  8.6 1.5 fusion.62
  10.2 0.7 copy-done.6
  10.9 2.0 select_reduce_fusion.1
  13.7 11.7 cholesky.130
  25.5 9.8 custom-call.13
  35.8 11.7 cholesky.147
  47.6 0.7 compare_reduce_fusion.2
  49.7 4.1 while.30
  49.9 0.6 fusion.101
  50.4 1.4 bitcast_dynamic-update-slice_fusion.4
  51.8 0.6 fusion.101
  52.4 1.4 bitcast_dynamic-update-slice_fusion.4
  53.8 19.7 custom-call.14
  73.8 1.8 broadcast.146.clone
  75.6 13.7 while.28
  75.7 0.7 compare_and_fusion.6
  76.4 1.6 gather_fusion
  78.3 1.8 constant_dynamic-update-slice_fusion.6
  80.2 2.3 convolution_add_fusion.6
  82.5 0.7 compare_and_fusion.6
  83.2 1.6 gather_fusion
  85.1 1.9 constant_dynamic-update-slice_fusion.6
  87.0 2.3 convolution_add_fusion.6
  89.4 2.3 copy.17
  91.7 0.3 fusion.41
  92.0 1.2 convolution_subtract_fusion.1
  93.3 0.3 fusion.50
  93.6 0.6 fusion.28
  94.2 223.0 %all-gather.2.cloned.1.call-done = f32[2560,256]{1,0:T(8,128)} async-done(((f32[40,256]{1,0:T(8,128)}), f32[2560,256]{1,0:T(8,128)}) %all-gather.2.cloned.1.call-update) | async-done | bytes 2621456 | tf_op jit(solution)/shard_map/all_gather | solution.py:134
  317.2 3.8 bitcast_add_fusion.1
  321.0 4.5 broadcast_multiply_fusion.2
  325.6 161.7 %psum.43 = f32[]{:T(128)} all-reduce(f32[]{:T(128)S(6)} %div.41), channel_id=1, replica_groups=mesh['site'=64,'cons'=4] {'site'}, use_global_device_ids=true, to_apply=%region_8.11 | all-reduce | flops 1 | bytes 8 | tf_op jit(solution)/shard_map/psum | solution.py:120
  487.3 559.5 %all-reduce.7.cloned.1.call-done = f32[2560,256]{1,0:T(8,128)} async-done(((f32[2560,256]{1,0:T(8,128)}), f32[2560,256]{1,0:T(8,128)}) %all-reduce.7.cloned.1.call-update) | async-done | bytes 2621456 | tf_op jit(solution)/shard_map/psum | solution.py:143
  1046.8 4.6 bitcast_add_fusion
  1051.4 4.6 broadcast_multiply_fusion.1
  1056.1 715.8 %all-reduce.11.cloned.1.call-done = (f32[2560,256]{1,0:T(8,128)}, f32[256,256]{0,1:T(8,128)}) async-done(((f32[2560,256]{1,0:T(8,128)}, f32[256,256]{0,1:T(8,128)}), (f32[2560,256]{1,0:T(8,128)}, f32[256,256]{0,1:T(8,128)})) %all-reduce.11.cloned.1.call-update) | async-done | bytes 2883600 | tf_op jit(solution)/shard_map/psum | solution.py:143
  1771.8 5.2 fusion.58
  1777.1 9.1 while.29
  1777.1 0.8 compare_and_fusion.7
  1777.9 2.3 gather_fusion.1
  1780.2 1.1 multiply_reduce_fusion.2
  1781.6 0.7 compare_and_fusion.7
  1782.3 2.3 gather_fusion.1
  1784.6 1.1 multiply_reduce_fusion.2
  1786.2 0.8 constant_dynamic-slice_fusion.2
  1787.1 1.1 fusion.63
  1788.2 315.0 %all-reduce.9.cloned.1.call-done = (f32[256,256]{0,1:T(8,128)}, f32[120,256]{1,0:T(8,128)}) async-done(((f32[256,256]{0,1:T(8,128)}, f32[120,256]{1,0:T(8,128)}), (f32[256,256]{0,1:T(8,128)}, f32[120,256]{1,0:T(8,128)})) %all-reduce.9.cloned.1.call-update) | async-done | bytes 385040 | tf_op jit(solution)/shard_map/psum | solution.py:155
  2103.2 1.6 select_reduce_fusion
  2105.7 11.7 cholesky.164
  2117.5 9.8 custom-call.15
  2127.8 11.7 cholesky.181
  2139.5 0.7 compare_reduce_fusion
  2140.2 0.6 compare_reduce_fusion.1
  2142.3 4.4 while.31
  2142.6 0.6 fusion.102
  2143.2 1.4 bitcast_dynamic-update-slice_fusion.5
  2144.6 0.6 fusion.102
  2145.2 1.4 bitcast_dynamic-update-slice_fusion.5
  2146.7 19.7 custom-call.16
  2166.7 0.4 convolution_subtract_fusion
  2167.0 0.3 fusion.46
  2167.4 0.6 fusion.32
  2168.3 0.7 broadcast_divide_fusion
  (86 shorter events, 4.1 us)
Async XLA Ops:
  7.2 310.0 %all-gather.2.cloned.1.call-start = ((), (), s32[]{:S(2)}) async-start(), calls=%async_computation | async-start | bytes 2662400 | tf_op jit(solution)/shard_map/all_gather | solution.py:134
  7.9 1038.9 %all-reduce.7.cloned.1.call-start = ((), (), s32[]{:S(2)}) async-start(), calls=%async_computation.1 | async-start | bytes 5242880 | tf_op jit(solution)/shard_map/psum | solution.py:143
  10.2 0.7 copy-start.6
  53.8 19.7 copy-start.7
  53.8 19.7 copy-start.14
  73.5 2.1 copy-start.4
  73.5 2.1 copy-start.11
  73.5 2.1 copy-start.12
  73.6 2.1 copy-start.13
  94.2 226.8 %copy-start.2 = (f32[2560,256]{1,0:T(8,128)S(1)}, f32[2560,256]{1,0:T(8,128)}, u32[]{:S(2)}) copy-start(f32[2560,256]{1,0:T(8,128)} %param.24) | copy-start | bytes 7864324
  325.5 721.2 %copy-start = (f32[20,128,256]{2,1,0:T(8,128)S(1)}, f32[20,128,256]{2,1,0:T(8,128)}, u32[]{:S(2)}) copy-start(f32[20,128,256]{2,1,0:T(8,128)} %copy.17) | copy-start | bytes 7864324
  325.6 1446.3 %all-reduce.11.cloned.1.call-start = ((), (), s32[]{:S(2)}) async-start(), calls=%async_computation.3 | async-start | bytes 5767168 | tf_op jit(solution)/shard_map/psum | solution.py:143
  1046.8 4.6 copy-start.1
  1046.8 4.6 copy-start.3
  1056.0 1047.2 %all-reduce.9.cloned.1.call-start = ((), (), s32[]{:S(2)}) async-start(), calls=%async_computation.2 | async-start | bytes 770048 | tf_op jit(solution)/shard_map/psum | solution.py:155
  1777.0 326.2 %copy-start.9 = (f32[256,256]{0,1:T(8,128)S(1)}, f32[256,256]{0,1:T(8,128)}, u32[]{:S(2)}) copy-start(f32[256,256]{0,1:T(8,128)} %get-tuple-element.254) | copy-start | bytes 786436
  1786.2 2.0 copy-start.5
  1787.1 355.2 %copy-start.8 = (f32[40,256]{1,0:T(8,128)}, f32[40,256]{1,0:T(8,128)S(1)}, u32[]{:S(2)}) copy-start(f32[40,256]{1,0:T(8,128)S(1)} %constant_dynamic-slice_fusion.2) | copy-start | bytes 122884
  1787.1 355.2 %copy-start.15 = (s32[2,2]{1,0:T(2,128)S(1)}, s32[2,2]{1,0:T(2,128)}, u32[]{:S(2)}) copy-start(s32[2,2]{1,0:T(2,128)} %copy-done.14) | copy-start | bytes 52
  2105.6 62.4 %copy-start.10 = (f32[120,256]{1,0:T(8,128)S(1)}, f32[120,256]{1,0:T(8,128)}, u32[]{:S(2)}) copy-start(f32[120,256]{1,0:T(8,128)} %get-tuple-element.252) | copy-start | bytes 368644
Sparse Core Ops, SparseCore 0:
  9.8 307.3 all-gather.1
  325.7 721.0 all-reduce.6
  1056.2 715.6 all-reduce.10
  1788.3 314.8 all-reduce.8
where the time goes:
time: 2190 us; the launch traced here: 2180 us
  waiting for transfers between devices  1810 us (83%)
  blocking collectives  162 us (7%)
  other arithmetic  129 us (6%)
  matrix products  28.2 us (1%)
  local copies, waits for them, and re-layouts  22.6 us (1%)
    psum x2, waiting for transfers between devices, on_device(): summed = lax.psum(local_rho * (local_copy + duals), 'site')  1280 us
    psum x1, waiting for transfers between devices, on_device(): lax.psum((month_sum, code_gram), ('site', 'cons'))  315 us
    all_gather x1, waiting for transfers between devices, on_device(): full_block = lax.all_gather(consensus, 'site', axis=0, tiled=True)  223 us
    psum x1, blocking collectives, on_device(): rho_total, global_gram = lax.psum((local_rho, patient_gram), 'site')  162 us
    another operation x13, other arithmetic, invert(): factor = jnp.linalg.cholesky(matrix)  68.7 us
  transfers between devices with their start and end apart: 4, of which 4 were waited for; matrix products, arithmetic and copies ran while one was open for 4% of the time, Pallas kernels for 0%

commit v1 on v0

v1 whole, which is shorter than its diff:
```python
import functools

import jax
import jax.numpy as jnp
from jax import lax
from jax.experimental import pallas as pl
from jax.experimental.pallas import tpu as pltpu
from jax.sharding import PartitionSpec as P

R = 256
MONTHS = 120
BLOCK = 128
SHARE = 40
CHUNK = 640
ROWS = 2560
F32 = jnp.float32
BF16 = jnp.bfloat16
AXES = ("site", "cons")


def number(z, y, x, h, c):
    return ((z * 4 + y) * 4 + x) * 4 + h * 2 + c


def pairs_of(move):
    out = []
    for z in range(4):
        for y in range(4):
            for x in range(4):
                for h in range(2):
                    for c in range(2):
                        out.append((number(z, y, x, h, c), number(*move(z, y, x, h, c))))
    return out


def first_move(k):
    def move(z, y, x, h, c):
        return (z, y, (x + k) % 4, h, c) if c == 0 else (z, (y + k) % 4, x, h, c)

    return pairs_of(move)


def second_move(k):
    def move(z, y, x, h, c):
        return (z, (y + k) % 4, x, h, c) if c == 0 else (z, y, (x + k) % 4, h, c)

    return pairs_of(move)


def depth_move(k):
    return pairs_of(lambda z, y, x, h, c: ((z + k) % 4, y, x, h, c))


HALF_MOVE = pairs_of(lambda z, y, x, h, c: (z, y, x, 1 - h, c))
CORE_MOVE = pairs_of(lambda z, y, x, h, c: (z, y, x, h, 1 - c))


def send(value, pairs):
    return lax.ppermute(value, AXES, pairs)


def scatter_sum(parts, moves):
    return [parts[0]] + [send(parts[k], moves(k)) for k in (1, 2, 3)]


def gather(value, moves):
    return [value] + [send(value, moves((4 - k) % 4)) for k in (1, 2, 3)]


def full_sum(value, moves):
    got = [send(value, moves(k)) for k in (1, 2, 3)]
    return (value + got[0]) + (got[1] + got[2])


def gather_rows(own):
    rows = jnp.concatenate(gather(own, depth_move), 0)
    rows = jnp.concatenate(gather(rows, second_move), 0)
    return gather(rows, first_move)


def split(a):
    hi = a.astype(BF16)
    return hi, (a - hi.astype(F32)).astype(BF16)


def dot3(a, b):
    ah, al = a
    bh, bl = b
    dot = functools.partial(jnp.dot, preferred_element_type=F32)
    return dot(ah, bh) + (dot(ah, bl) + dot(al, bh))


def dot6(a, b):
    return jnp.dot(a, b, precision=lax.Precision.HIGHEST, preferred_element_type=F32)


def eye(n):
    return (
        lax.broadcasted_iota(jnp.int32, (n, n), 0) == lax.broadcasted_iota(jnp.int32, (n, n), 1)
    ).astype(F32)


def total(a):
    return jnp.sum(jnp.sum(a, axis=1, keepdims=True), axis=0, keepdims=True)


def shifted_inverse(hess):
    n = hess.shape[0]
    ident = eye(n)
    rho = total(hess * ident) * (1.0 / n)
    mat = hess * (1.0 / rho) + ident
    low, high = 0.999, n + 1.5
    c0 = 2.0 / (low + high)
    a = low * c0
    mat_parts = split(mat)

    def grow(a):
        up = a * (2.0 - a)
        s = 2.0 / (1.0 + up)
        return s, s * up

    s, a = grow(a)
    x = (s * c0) * (2.0 * ident - c0 * mat)
    for step in range(5):
        s, a = grow(a)
        x_parts = split(x)
        y = 2.0 * ident - dot3(mat_parts, x_parts)
        x = s * dot3(x_parts, split(y))
    for step in range(2):
        y = 2.0 * ident - dot6(mat, x)
        x = dot6(x, y)
    return rho, x


def inverse_kernel(place, patient, month, gram_ref, near_ref, rho_ref, m0, m1, m2, m3, mat):
    rows = patient[...]
    gram = lax.dot_general(rows, rows, (((0,), (0,)), ((), ())), preferred_element_type=F32)
    gram_ref[...] = gram
    mf = month[...]
    month_gram = lax.dot_general(
        mf, mf, (((0,), (0,)), ((), ())), precision=lax.Precision.HIGHEST, preferred_element_type=F32
    )
    rho, near = shifted_inverse(gram * month_gram)
    near_ref[...] = near
    rho_ref[...] = jnp.broadcast_to(rho, rho_ref.shape)
    core = place[4]
    square = dot6(near, near)
    mat[...] = rho * jnp.where(core == 0, near, square)
    for k, ref in enumerate((m0, m1, m2, m3)):
        at = lax.rem(place[0] + k, 4)
        ref[0:64, :] = mat[pl.ds(pl.multiple_of(at * 64, 64), 64), :]
        ref[64:72, :] = jnp.broadcast_to(rho, (8, R))


def block_row(place, k, b):
    j, i = b // 4, b % 4
    first = lax.rem(place[0] + k, 4)
    second = lax.rem(place[1] + j, 4)
    depth = lax.rem(place[2] + i, 4)
    block = depth * 16 + first * place[5] + second * place[6]
    return pl.multiple_of(block * SHARE, 8)


def local_kernel(
    place, live, patient_at, code_at, month_at,
    tiles, patient, month, duals, near, rho_ref,
    prod, a0, a1, a2, a3, grad, u_part, g_part,
):
    grad[...] = jnp.zeros_like(grad)

    def visit(k, _):
        pat = patient[pl.ds(pl.multiple_of(patient_at[k] * BLOCK, BLOCK), BLOCK), :]
        product = lax.dot_general(
            tiles[k], pat, (((0,), (0,)), ((), ())), preferred_element_type=F32
        )
        prod[k] = product
        at = pl.ds(pl.multiple_of(code_at[k] * BLOCK, BLOCK), BLOCK)
        grad[at, :] += product * month[pl.ds(month_at[k], 1), :]
        return 0

    lax.fori_loop(0, live[0], visit, 0)
    rho = rho_ref[0:1, 0:1]
    near_parts = split(near[...])
    for k, out in enumerate((a0, a1, a2, a3)):
        for b in range(16):
            at = pl.ds(block_row(place, k, b), SHARE)
            u_part[b * SHARE : (b + 1) * SHARE, :] = duals[at, :]
            g_part[b * SHARE : (b + 1) * SHARE, :] = grad[at, :]
        u = u_part[...]
        g = g_part[...] * (1.0 / rho)
        once = u + dot3(split(g - u), near_parts)
        twice = once + dot3(split(g - once), near_parts)
        once = rho * once
        twice = rho * twice
        for b in range(16):
            out[b * 80 : b * 80 + SHARE, :] = once[b * SHARE : (b + 1) * SHARE]
            out[b * 80 + SHARE : b * 80 + 80, :] = twice[b * SHARE : (b + 1) * SHARE]


def owner_kernel(place, s0, s1, s2, s3, z0_ref, mine, other, z1_ref, z2_ref, code_ref, own, oth):
    summed = (s0[...] + s1[...]) + (s2[...] + s3[...])
    for k in range(4):
        at = pl.ds(pl.multiple_of(lax.rem(place[0] + k, 4) * 64, 64), 64)
        own[at, :] = mine[k * 72 : k * 72 + 64, :]
        at = pl.ds(pl.multiple_of(lax.rem(place[1] + k, 4) * 64, 64), 64)
        oth[at, :] = other[k * 72 : k * 72 + 64, :]
    rho_total = mine[64:65, :]
    core = place[4]
    a = own[...]
    b = oth[...]
    plain = jnp.where(core == 0, a, b)
    square = jnp.where(core == 0, b, a)
    z0 = z0_ref[...]
    first = summed[0:SHARE] + dot6(z0, plain)
    z1 = jnp.maximum(first / rho_total, 0.0)
    second = summed[SHARE:] + dot6(z0, plain - square) + 2.0 * dot6(z1, plain) - rho_total * z1
    z2 = jnp.maximum(second / rho_total, 0.0)
    z1_ref[...] = z1
    z2_ref[...] = z2
    code_ref[...] = lax.dot_general(
        z2, z2, (((0,), (0,)), ((), ())), precision=lax.Precision.HIGHEST, preferred_element_type=F32
    )


def month_kernel(place, live, code_at, month_at, w0, w1, w2, w3, prod, out, natural):
    for k, w in enumerate((w0, w1, w2, w3)):
        for b in range(16):
            natural[pl.ds(block_row(place, k, b), SHARE), :] = w[b * SHARE : (b + 1) * SHARE, :]
    out[...] = jnp.zeros_like(out)

    def visit(k, _):
        at = pl.ds(pl.multiple_of(code_at[k] * BLOCK, BLOCK), BLOCK)
        column = jnp.sum(prod[k] * natural[at, :], axis=0, keepdims=True)
        out[pl.ds(month_at[k], 1), :] += column
        return 0

    lax.fori_loop(0, live[0], visit, 0)


def duals_kernel(place, *refs):
    a = refs[0:4]
    zero = refs[4:8]
    one = refs[8:12]
    two = refs[12:16]
    near, rho_ref, out, v_part = refs[16:]
    scale = 1.0 / rho_ref[0:1, 0:1]
    near_parts = split(near[...])
    for k in range(4):
        for b in range(16):
            v_part[b * SHARE : (b + 1) * SHARE, :] = a[k][b * 80 + SHARE : b * 80 + 80, :]
        z0 = zero[k][...]
        z1 = one[k][...]
        inner = z0 - dot3(split(z0), near_parts) + 2.0 * z1
        value = scale * v_part[...] + dot3(split(inner), near_parts) - z1 - two[k][...]
        for b in range(16):
            out[pl.ds(block_row(place, k, b), SHARE), :] = value[b * SHARE : (b + 1) * SHARE]


def month_inverse_kernel(place, mine, other, near_ref, rho_ref, own, oth):
    for k in range(4):
        at = pl.ds(pl.multiple_of(lax.rem(place[0] + k, 4) * 64, 64), 64)
        own[at, :] = mine[k * 64 : k * 64 + 64, :]
        at = pl.ds(pl.multiple_of(lax.rem(place[1] + k, 4) * 64, 64), 64)
        oth[at, :] = other[k * 64 : k * 64 + 64, :]
    rho, near = shifted_inverse(own[...] * (0.5 * oth[...]))
    near_ref[...] = near
    rho_ref[...] = jnp.broadcast_to(rho, rho_ref.shape)


def solve_kernel(place, top, bottom, month, near, rho_ref, out, grad):
    for k in range(4):
        at = pl.ds(pl.multiple_of(lax.rem(place[0] + k, 4) * 16, 16), 16)
        upper = jnp.where(place[4] == 0, 0, 64)
        grad[pl.ds(pl.multiple_of(upper + lax.rem(place[0] + k, 4) * 16, 16), 16), :] = top[
            k * 16 : k * 16 + 16, :
        ]
        grad[pl.ds(pl.multiple_of(64 - upper + lax.rem(place[1] + k, 4) * 16, 16), 16), :] = bottom[
            k * 16 : k * 16 + 16, :
        ]
    scaled = grad[0:MONTHS, :] * (1.0 / rho_ref[0:1, 0:1]) + month[...]
    solved = jnp.maximum(dot6(scaled, near[...]), 0.0)
    mean = jnp.sum(solved, axis=0, keepdims=True) * (1.0 / MONTHS)
    out[...] = solved / (mean + 1e-06)


def call(body, outs, scalars, scratch, *args):
    specs = [pl.BlockSpec(memory_space=pltpu.SMEM)] * scalars
    specs += [pl.BlockSpec(memory_space=pltpu.VMEM)] * (len(args) - scalars)
    shapes = [jax.ShapeDtypeStruct(s, F32) for s in outs]
    return pl.pallas_call(
        body,
        out_shape=shapes,
        in_specs=specs,
        out_specs=[pl.BlockSpec(memory_space=pltpu.VMEM)] * len(outs),
        scratch_shapes=[pltpu.VMEM(s, F32) for s in scratch],
        compiler_params=pltpu.CompilerParams(vmem_limit_bytes=48 << 20),
    )(*args)


def on_device(
    tile_values, patient_block, code_block, month_index, live_count,
    patient_factor, month_factor, consensus, scaled_duals,
):
    site = lax.axis_index("site")
    cons = lax.axis_index("cons")
    z, y, x = site // 16, (site // 4) % 4, site % 4
    h, core = cons // 2, cons % 2
    flat = core == 0
    place = jnp.stack(
        [jnp.where(flat, x, y), jnp.where(flat, y, x), z, h, core,
         jnp.where(flat, 1, 4), jnp.where(flat, 4, 1), cons]
    ).astype(jnp.int32)

    gram, near, rho, *mats = call(
        inverse_kernel, [(R, R), (R, R), (8, 128)] + [(72, R)] * 4, 1, [(R, R)],
        place, patient_factor, month_factor,
    )
    m = scatter_sum(mats, first_move)
    m = (m[0] + m[1]) + (m[2] + m[3])
    m = full_sum(m, second_move)
    m = full_sum(m, depth_move)
    mine = jnp.concatenate(gather(m, first_move), 0)
    other = send(mine, CORE_MOVE)

    prod, *parts = call(
        local_kernel, [(tile_values.shape[0], BLOCK, R)] + [(2 * CHUNK, R)] * 4, 5,
        [(ROWS, R), (CHUNK, R), (CHUNK, R)],
        place, live_count, patient_block, code_block, month_index,
        tile_values, patient_factor, month_factor, scaled_duals, near, rho,
    )
    zero = gather_rows(consensus)
    s = scatter_sum(parts, first_move)
    s = [
        (s[0][j : j + 320] + s[1][j : j + 320]) + (s[2][j : j + 320] + s[3][j : j + 320])
        for j in (0, 320, 640, 960)
    ]
    s = scatter_sum(s, second_move)
    s = [
        (s[0][i : i + 80] + s[1][i : i + 80]) + (s[2][i : i + 80] + s[3][i : i + 80])
        for i in (0, 80, 160, 240)
    ]
    s = scatter_sum(s, depth_move)
    z1, z2, code_gram = call(
        owner_kernel, [(SHARE, R), (SHARE, R), (R, R)], 1, [(R, R), (R, R)],
        place, *s, consensus, mine, other,
    )

    two = gather_rows(z2)
    one = gather_rows(z1)

    code_gram = code_gram + send(code_gram, CORE_MOVE)
    pair = jnp.where(flat, code_gram, gram)
    pair = [
        lax.dynamic_slice_in_dim(pair, ((place[0] + k) % 4) * 64, 64, 0) for k in range(4)
    ]
    g = scatter_sum(pair, first_move)
    g = (g[0] + g[1]) + (g[2] + g[3])
    g = full_sum(g, second_move)
    g = full_sum(g, depth_move)
    g = g + send(g, HALF_MOVE)
    g = jnp.concatenate(gather(g, first_move), 0)
    g_other = send(g, CORE_MOVE)
    near_m, rho_m = call(
        month_inverse_kernel, [(R, R), (8, 128)], 1, [(R, R), (R, R)], place, g, g_other
    )

    (month_sum,) = call(
        month_kernel, [(BLOCK, R)], 4, [(ROWS, R)],
        place, live_count, code_block, month_index, *two, prod,
    )
    keep = lax.dynamic_slice_in_dim(month_sum, core * 64, 64, 0)
    give = lax.dynamic_slice_in_dim(month_sum, 64 - core * 64, 64, 0)
    t = keep + send(give, CORE_MOVE)
    t = [lax.dynamic_slice_in_dim(t, ((place[0] + k) % 4) * 16, 16, 0) for k in range(4)]
    t = scatter_sum(t, first_move)
    t = (t[0] + t[1]) + (t[2] + t[3])
    t = full_sum(t, second_move)
    t = full_sum(t, depth_move)
    t = t + send(t, HALF_MOVE)
    t = jnp.concatenate(gather(t, first_move), 0)
    t_other = send(t, CORE_MOVE)

    (duals,) = call(
        duals_kernel, [(ROWS, R)], 1, [(CHUNK, R)],
        place, *parts, *zero, *one, *two, near, rho,
    )
    (new_months,) = call(
        solve_kernel, [(MONTHS, R)], 1, [(BLOCK, R)],
        place, t, t_other, month_factor, near_m, rho_m,
    )
    return (z2, duals, new_months)


def solution(mesh):
    placed = (
        P(("site", "cons"), None, None),
        P(("site", "cons")),
        P(("site", "cons")),
        P(("site", "cons")),
        P(("site", "cons")),
        P("site", None),
        P(),
        P("site", "cons"),
        P("site", "cons"),
    )
    return jax.shard_map(
        on_device,
        mesh=mesh,
        in_specs=placed,
        out_specs=(P("site", "cons"), P("site", "cons"), P()),
        check_vma=False,
    )
```

time: 2190 us -> 290 us (0.13)
  waiting for transfers between devices: 1810 us -> 105 us
  blocking collectives: 162 us -> 0 us
  starting transfers between devices: 0.16 us -> 134 us
  other arithmetic: 129 us -> 1.68 us
  Pallas kernels: 0 us -> 33.7 us
  matrix products: 28.2 us -> 0 us
    psum x3 -> x0, waiting for transfers between devices: 1590 us -> none  [the longest x2 1280 us: on_device(): summed = lax.psum(local_rho * (local_copy + duals), 'site')]
    all_gather x1 -> x0, waiting for transfers between devices: 223 us -> none  [on_device(): full_block = lax.all_gather(consensus, 'site', axis=0, tiled=True)]
    psum x1 -> x0, blocking collectives: 162 us -> none  [on_device(): rho_total, global_gram = lax.psum((local_rho, patient_gram), 'site')]
    ppermute x0 -> x79, starting transfers between devices: none -> 134 us  [send(): return lax.ppermute(value, AXES, pairs)]
    another operation x18 -> x0, other arithmetic: 108 us -> none  [the longest x13 68.7 us: invert(): factor = jnp.linalg.cholesky(matrix)]
    ppermute x0 -> x79, waiting for transfers between devices: none -> 105 us  [send(): return lax.ppermute(value, AXES, pairs)]
    pallas_call x0 -> x7, Pallas kernels: none -> 33.7 us  [call(): pl.pallas_call(body, out_shape=shapes, in_specs=specs, out_specs=[pl.Bloc...]
    dot_general x16 -> x0, matrix products: 24.4 us -> none  [the longest x2 9.13 us: on_device(): jnp.dot(gradient + local_rho * (full_block - duals), inverse, precision=h...]
  transfers between devices with their start and end apart: 4 -> 79, of which waited for: 4 -> 30; matrix products, arithmetic and copies ran while one was open for 4% -> 2% of each run, Pallas kernels for 0% -> 6%
where the time goes in v1:
time: 290 us; the launch traced here: 286 us
  starting transfers between devices  134 us (46%)
  waiting for transfers between devices  105 us (36%)
  Pallas kernels  33.7 us (12%)
  local copies, waits for them, and re-layouts  9.66 us (3%)
    ppermute x79, starting transfers between devices, send(): return lax.ppermute(value, AXES, pairs)  134 us
    ppermute x79, waiting for transfers between devices, send(): return lax.ppermute(value, AXES, pairs)  105 us
    pallas_call x7, Pallas kernels, call(): pl.pallas_call(body, out_shape=shapes, in_specs=specs, out_specs=[pl.Bloc...  33.7 us
    unnamed x56, local copies, waits for them, and re-layouts  8.86 us
  transfers between devices with their start and end apart: 79, of which 30 were waited for; matrix products, arithmetic and copies ran while one was open for 2% of the time, Pallas kernels for 6%

profile of v1, /device:TPU:1, one launch (start us, length us, event | category | flops | bytes accessed | tf_op | source)
XLA Modules:
  0.0 286.3 jit_solution(9867207628582040551)
XLA Ops:
  3.4 7.3 %shard_map.112 = (f32[256,256]{1,0:T(8,128)S(1)}, f32[256,256]{1,0:T(8,128)S(1)}, f32[8,128]{1,0:T(8,128)S(1)}, f32[72,256]{1,0:T(8,128)S(1)}, f32[72,256]{1,0:T...) custom-call(s32[8]{0:T(128)S(1)} %stack.35.place, bf16[1024,256]{1,0:T(8,128)(2,1)S(1)} %copy-done.5, ...), custom_call_target="tpu_custom_call" | custom-call | tf_op jit(solution)/shard_map/pallas_call | solution.py:290
  13.8 8.0 %shard_map.113 = (f32[20,128,256]{2,1,0:T(8,128)}, f32[1280,256]{1,0:T(8,128)S(1)}, f32[1280,256]{1,0:T(8,128)S(1)}, f32[1280,256]{1,0:T(8,128)S(1)}, f32[1280,256]{1,0:T(8,128)}) custom-call(s32[8]{0:T(128)S(1)} %stack.35.place, s32[1]{0:T(128)S(6)} %copy.39.live, s32[20]{0:T(128)S(1)} %copy-done.19, s32[20]{0:T(128)S(1)} %copy-done.15, s32[20]{0:T(128)S(1)} %copy-done.17, ...), custom_call_target="tpu_custom_call" | custom-call | tf_op jit(solution)/shard_map/pallas_call | solution.py:290
  21.9 1.8 collective-permute-start
  23.7 3.0 %collective-permute-start.1 = (f32[1280,256]{1,0:T(8,128)S(1)}, f32[1280,256]{1,0:T(8,128)S(1)}, u32[]{:S(2)}, u32[]{:S(2)}) collective-permute-start(f32[1280,256]{1,0:T(8,128)S(1)} %get-tuple-element.24.refs_2_), channel_id=1, source_target_pairs={{0,8},{1,33},{2,10},{3,35},{4,12},{5,37},{6,14},{7,39},{8,0},{9,41... | collective-permute-start | bytes 3932168 | tf_op jit(solution)/shard_map/ppermute | solution.py:59
  26.7 1.3 collective-permute-start.2
  28.0 4.7 %collective-permute-start.22 = (f32[40,256]{1,0:T(8,128)S(1)}, f32[40,256]{1,0:T(8,128)S(1)}, u32[]{:S(2)}, u32[]{:S(2)}) collective-permute-start(f32[40,256]{1,0:T(8,128)S(1)} %copy-done.13), channel_id=1, source_target_pairs={{0,192},{1,193},{2,194},{3,195},{4,196},{5,197},{6,198},{7,199},{8... | collective-permute-start | bytes 122888 | tf_op jit(solution)/shard_map/ppermute | solution.py:59
  33.8 2.2 collective-permute-start.11
  36.0 20.8 %collective-permute-done.10 = f32[72,256]{1,0:T(8,128)S(1)} collective-permute-done((f32[72,256]{1,0:T(8,128)S(1)}, f32[72,256]{1,0:T(8,128)S(1)}, u32[]{:S(2)}, u32[]{:S(2)}) %collective-permute-start.10) | collective-permute-done | bytes 73760 | tf_op jit(solution)/shard_map/ppermute | solution.py:59
  56.8 1.9 collective-permute-start.9
  59.3 2.2 collective-permute-start.23
  61.6 2.8 collective-permute-start.24
  65.8 1.4 collective-permute-done.24
  67.2 4.5 %collective-permute-start.13 = (f32[72,256]{1,0:T(8,128)S(1)}, f32[72,256]{1,0:T(8,128)S(1)}, u32[]{:S(2)}, u32[]{:S(2)}) collective-permute-start(f32[72,256]{1,0:T(8,128)S(1)} %add_add_fusion.2), channel_id=1, source_target_pairs={{0,32},{1,9},{2,34},{3,11},{4,36},{5,13},{6,38},{7,15},{8,40},{9,1... | collective-permute-start | bytes 221192 | tf_op jit(solution)/shard_map/ppermute | solution.py:59
  73.5 1.4 collective-permute-done.14
  75.0 1.7 collective-permute-start.16
  76.7 1.6 collective-permute-start.17
  78.3 1.3 fusion.3
  80.2 2.6 collective-permute-start.4
  84.9 1.9 collective-permute-done.18
  87.8 1.8 collective-permute-done.19
  90.5 1.8 collective-permute-done.20
  93.1 17.9 %collective-permute-start.21 = (f32[288,256]{1,0:T(8,128)S(1)}, f32[288,256]{1,0:T(8,128)S(1)}, u32[]{:S(2)}, u32[]{:S(2)}) collective-permute-start(f32[288,256]{1,0:T(8,128)S(1)} %pad_maximum_fusion.mine), channel_id=1, source_target_pairs={{0,1},{1,0},{2,3},{3,2},{4,5},{5,4},{6,7},{7,6},{8,9},{9,8},{10,11... | collective-permute-start | bytes 884744 | tf_op jit(solution)/shard_map/ppermute | solution.py:59
  111.2 1.8 collective-permute-start.7
  113.0 1.4 collective-permute-start.8
  114.5 2.5 collective-permute-done.6.s1
  117.0 2.6 collective-permute-done.7.s2
  119.6 1.9 shard_map.114
  121.5 3.1 %collective-permute-start.40 = (f32[40,256]{1,0:T(8,128)}, f32[40,256]{1,0:T(8,128)S(1)}, u32[]{:S(2)}, u32[]{:S(2)}) collective-permute-start(f32[40,256]{1,0:T(8,128)} %get-tuple-element.17), channel_id=1, source_target_pairs={{0,192},{1,193},{2,194},{3,195},{4,196},{5,197},{6,198},{7,199},{8... | collective-permute-start | bytes 122888 | tf_op jit(solution)/shard_map/ppermute | solution.py:59
  125.9 3.1 %collective-permute-start.31 = (f32[40,256]{1,0:T(8,128)S(1)}, f32[40,256]{1,0:T(8,128)S(1)}, u32[]{:S(2)}, u32[]{:S(2)}) collective-permute-start(f32[40,256]{1,0:T(8,128)S(1)} %get-tuple-element.31), channel_id=1, source_target_pairs={{0,192},{1,193},{2,194},{3,195},{4,196},{5,197},{6,198},{7,199},{8... | collective-permute-start | bytes 122888 | tf_op jit(solution)/shard_map/ppermute | solution.py:59
  130.0 2.6 collective-permute-start.64
  132.6 1.8 collective-permute-start.43
  135.5 3.0 %collective-permute-done.43 = f32[160,256]{1,0:T(8,128)S(1)} collective-permute-done((f32[160,256]{1,0:T(8,128)S(1)}, f32[160,256]{1,0:T(8,128)S(1)}, u32[]{:S(2)}, u32[]{:S(2)}) %collective-permute-start.43) | collective-permute-done | bytes 163872 | tf_op jit(solution)/shard_map/ppermute | solution.py:59
  138.4 3.1 %collective-permute-start.34 = (f32[160,256]{1,0:T(8,128)S(1)}, f32[160,256]{1,0:T(8,128)S(1)}, u32[]{:S(2)}, u32[]{:S(2)}) collective-permute-start(f32[160,256]{1,0:T(8,128)S(1)} %get-tuple-element.59), channel_id=1, source_target_pairs={{0,48},{1,13},{2,50},{3,15},{4,52},{5,1},{6,54},{7,3},{8,56},{9,5}... | collective-permute-start | bytes 491528 | tf_op jit(solution)/shard_map/ppermute | solution.py:59
  142.1 1.9 collective-permute-start.46
  145.6 1.6 collective-permute-start.65
  147.2 2.4 collective-permute-start.66
  149.6 13.3 %collective-permute-done.65 = f32[64,256]{1,0:T(8,128)S(1)} collective-permute-done((f32[64,256]{1,0:T(8,128)S(1)}, f32[64,256]{1,0:T(8,128)S(1)}, u32[]{:S(2)}, u32[]{:S(2)}) %collective-permute-start.65) | collective-permute-done | bytes 65568 | tf_op jit(solution)/shard_map/ppermute | solution.py:59
  164.4 1.9 collective-permute-done.67
  167.6 1.5 collective-permute-start.69
  172.6 7.1 %collective-permute-start.49 = (f32[64,256]{1,0:T(8,128)S(1)}, f32[64,256]{1,0:T(8,128)S(1)}, u32[]{:S(2)}, u32[]{:S(2)}) collective-permute-start(f32[64,256]{1,0:T(8,128)S(1)} %constant_dynamic-slice_fusion.6), channel_id=1, source_target_pairs={{0,1},{1,0},{2,3},{3,2},{4,5},{5,4},{6,7},{7,6},{8,9},{9,8},{10,11... | collective-permute-start | bytes 196616 | tf_op jit(solution)/shard_map/ppermute | solution.py:59
  179.7 1.3 collective-permute-start.71
  181.1 1.9 collective-permute-start.72
  183.5 1.8 collective-permute-done.71
  185.3 3.2 %collective-permute-done.72 = f32[64,256]{1,0:T(8,128)S(1)} collective-permute-done((f32[64,256]{1,0:T(8,128)S(1)}, f32[64,256]{1,0:T(8,128)S(1)}, u32[]{:S(2)}, u32[]{:S(2)}) %collective-permute-start.72) | collective-permute-done | bytes 65568 | tf_op jit(solution)/shard_map/ppermute | solution.py:59
  189.2 3.3 %collective-permute-done.51 = f32[16,256]{1,0:T(8,128)S(1)} collective-permute-done((f32[16,256]{1,0:T(8,128)S(1)}, f32[16,256]{1,0:T(8,128)S(1)}, u32[]{:S(2)}, u32[]{:S(2)}) %collective-permute-start.51) | collective-permute-done | bytes 16416 | tf_op jit(solution)/shard_map/ppermute | solution.py:59
  192.6 3.5 %collective-permute-start.74 = (f32[64,256]{1,0:T(8,128)S(1)}, f32[64,256]{1,0:T(8,128)S(1)}, u32[]{:S(2)}, u32[]{:S(2)}) collective-permute-start(f32[64,256]{1,0:T(8,128)S(1)} %add_add_fusion.3), channel_id=1, source_target_pairs={{0,2},{1,3},{2,0},{3,1},{4,6},{5,7},{6,4},{7,5},{8,10},{9,11},{10,... | collective-permute-start | bytes 196616 | tf_op jit(solution)/shard_map/ppermute | solution.py:59
  196.4 1.4 collective-permute-start.54
  197.8 2.5 collective-permute-done.74
  200.4 1.5 collective-permute-start.36
  203.3 2.5 collective-permute-done.36
  206.7 1.5 collective-permute-start.30
  210.1 3.2 %collective-permute-start.76 = (f32[64,256]{1,0:T(8,128)S(1)}, f32[64,256]{1,0:T(8,128)S(1)}, u32[]{:S(2)}, u32[]{:S(2)}) collective-permute-start(f32[64,256]{1,0:T(8,128)S(1)} %add.311), channel_id=1, source_target_pairs={{0,8},{1,33},{2,10},{3,35},{4,12},{5,37},{6,14},{7,39},{8,0},{9,41... | collective-permute-start | bytes 196616 | tf_op jit(solution)/shard_map/ppermute | solution.py:59
  213.3 18.3 %collective-permute-done.76 = f32[64,256]{1,0:T(8,128)S(1)} collective-permute-done((f32[64,256]{1,0:T(8,128)S(1)}, f32[64,256]{1,0:T(8,128)S(1)}, u32[]{:S(2)}, u32[]{:S(2)}) %collective-permute-start.76) | collective-permute-done | bytes 65568 | tf_op jit(solution)/shard_map/ppermute | solution.py:59
  231.6 4.4 %collective-permute-start.59 = (f32[16,256]{1,0:T(8,128)S(1)}, f32[16,256]{1,0:T(8,128)S(1)}, u32[]{:S(2)}, u32[]{:S(2)}) collective-permute-start(f32[16,256]{1,0:T(8,128)S(1)} %add_add_fusion.6), channel_id=1, source_target_pairs={{0,2},{1,3},{2,0},{3,1},{4,6},{5,7},{6,4},{7,5},{8,10},{9,11},{10,... | collective-permute-start | bytes 49160 | tf_op jit(solution)/shard_map/ppermute | solution.py:59
  235.9 2.1 collective-permute-done.59
  238.1 4.3 %collective-permute-done.77 = f32[64,256]{1,0:T(8,128)S(1)} collective-permute-done((f32[64,256]{1,0:T(8,128)S(1)}, f32[64,256]{1,0:T(8,128)S(1)}, u32[]{:S(2)}, u32[]{:S(2)}) %collective-permute-start.77) | collective-permute-done | bytes 65568 | tf_op jit(solution)/shard_map/ppermute | solution.py:59
  242.7 2.3 collective-permute-done.60
  245.0 1.8 collective-permute-start.61
  246.8 2.4 collective-permute-done.61
  249.2 3.8 %collective-permute-done.62 = f32[16,256]{1,0:T(8,128)S(1)} collective-permute-done((f32[16,256]{1,0:T(8,128)S(1)}, f32[16,256]{1,0:T(8,128)S(1)}, u32[]{:S(2)}, u32[]{:S(2)}) %collective-permute-start.62) | collective-permute-done | bytes 16416 | tf_op jit(solution)/shard_map/ppermute | solution.py:59
  253.0 16.2 %collective-permute-start.78 = (f32[256,256]{1,0:T(8,128)S(1)}, f32[256,256]{1,0:T(8,128)S(1)}, u32[]{:S(2)}, u32[]{:S(2)}) collective-permute-start(f32[256,256]{1,0:T(8,128)S(1)} %pad_maximum_fusion.1.mine), channel_id=1, source_target_pairs={{0,1},{1,0},{2,3},{3,2},{4,5},{5,4},{6,7},{7,6},{8,9},{9,8},{10,11... | collective-permute-start | bytes 786440 | tf_op jit(solution)/shard_map/ppermute | solution.py:59
  270.7 6.1 %shard_map.117 = (f32[256,256]{1,0:T(8,128)S(1)}, f32[8,128]{1,0:T(8,128)S(1)}) custom-call(s32[8]{0:T(128)S(1)} %stack.35.place, f32[256,256]{1,0:T(8,128)S(1)} %pad_maximum_fusion.1.mine, f32[256,256]{1,0:T(8,128)S(1)} %collective-permute-done.78.other), custom_call_target="tpu_custom_call" | custom-call | tf_op jit(solution)/shard_map/pallas_call | solution.py:290
  276.9 7.7 %shard_map.115 = f32[2560,256]{1,0:T(8,128)} custom-call(s32[8]{0:T(128)S(1)} %stack.35.place, f32[1280,256]{1,0:T(8,128)} %copy-done, f32[1280,256]{1,0:T(8,128)} %copy-done.6, f32[1280,256]{1,0:T(8,128)} %copy-done.7, f32[1280,256]{1,0:T(8,128)} %get-tuple-element.25.refs_3_, f32[640,256]{1,0:T(8,128)S(1)} %constant_dynamic-update-slice_fusion.4.refs_4_, ...), custom_call_target="tpu_custom_call" | custom-call | tf_op jit(solution)/shard_map/pallas_call | solution.py:290
  284.6 1.5 shard_map.118
  (185 shorter events, 35.0 us)
Async XLA Ops:
  21.9 53.1 %collective-permute-start = (f32[1280,256]{1,0:T(8,128)S(1)}, f32[1280,256]{1,0:T(8,128)S(1)}, u32[]{:S(2)}, u32[]{:S(2)}) collective-permute-start(f32[1280,256]{1,0:T(8,128)S(1)} %get-tuple-element.23.refs_1_), channel_id=1, source_target_pairs={{0,4},{1,17},{2,6},{3,19},{4,8},{5,21},{6,10},{7,23},{8,12},{9,25}... | collective-permute-start | bytes 3932168 | tf_op jit(solution)/shard_map/ppermute | solution.py:59
  23.7 53.0 %collective-permute-start.1 = (f32[1280,256]{1,0:T(8,128)S(1)}, f32[1280,256]{1,0:T(8,128)S(1)}, u32[]{:S(2)}, u32[]{:S(2)}) collective-permute-start(f32[1280,256]{1,0:T(8,128)S(1)} %get-tuple-element.24.refs_2_), channel_id=1, source_target_pairs={{0,8},{1,33},{2,10},{3,35},{4,12},{5,37},{6,14},{7,39},{8,0},{9,41... | collective-permute-start | bytes 3932168 | tf_op jit(solution)/shard_map/ppermute | solution.py:59
  26.7 51.6 %collective-permute-start.2 = (f32[1280,256]{1,0:T(8,128)}, f32[1280,256]{1,0:T(8,128)S(1)}, u32[]{:S(2)}, u32[]{:S(2)}) collective-permute-start(f32[1280,256]{1,0:T(8,128)} %get-tuple-element.25.refs_3_), channel_id=1, source_target_pairs={{0,12},{1,49},{2,14},{3,51},{4,0},{5,53},{6,2},{7,55},{8,4},{9,57}... | collective-permute-start | bytes 3932168 | tf_op jit(solution)/shard_map/ppermute | solution.py:59
  28.0 28.9 %collective-permute-start.10 = (f32[72,256]{1,0:T(8,128)S(1)}, f32[72,256]{1,0:T(8,128)S(1)}, u32[]{:S(2)}, u32[]{:S(2)}) collective-permute-start(f32[72,256]{1,0:T(8,128)S(1)} %get-tuple-element.28), channel_id=1, source_target_pairs={{0,8},{1,33},{2,10},{3,35},{4,12},{5,37},{6,14},{7,39},{8,0},{9,41... | collective-permute-start | bytes 221192 | tf_op jit(solution)/shard_map/ppermute | solution.py:59
  28.0 5.8 %collective-permute-start.22 = (f32[40,256]{1,0:T(8,128)S(1)}, f32[40,256]{1,0:T(8,128)S(1)}, u32[]{:S(2)}, u32[]{:S(2)}) collective-permute-start(f32[40,256]{1,0:T(8,128)S(1)} %copy-done.13), channel_id=1, source_target_pairs={{0,192},{1,193},{2,194},{3,195},{4,196},{5,197},{6,198},{7,199},{8... | collective-permute-start | bytes 122888 | tf_op jit(solution)/shard_map/ppermute | solution.py:59
  33.8 25.5 %collective-permute-start.11 = (f32[72,256]{1,0:T(8,128)S(1)}, f32[72,256]{1,0:T(8,128)S(1)}, u32[]{:S(2)}, u32[]{:S(2)}) collective-permute-start(f32[72,256]{1,0:T(8,128)S(1)} %get-tuple-element.29), channel_id=1, source_target_pairs={{0,12},{1,49},{2,14},{3,51},{4,0},{5,53},{6,2},{7,55},{8,4},{9,57}... | collective-permute-start | bytes 221192 | tf_op jit(solution)/shard_map/ppermute | solution.py:59
  61.6 5.6 %collective-permute-start.24 = (f32[40,256]{1,0:T(8,128)S(1)}, f32[40,256]{1,0:T(8,128)S(1)}, u32[]{:S(2)}, u32[]{:S(2)}) collective-permute-start(f32[40,256]{1,0:T(8,128)S(1)} %copy-done.13), channel_id=1, source_target_pairs={{0,64},{1,65},{2,66},{3,67},{4,68},{5,69},{6,70},{7,71},{8,72},{9,... | collective-permute-start | bytes 122888 | tf_op jit(solution)/shard_map/ppermute | solution.py:59
  64.3 7.3 %collective-permute-start.12 = (f32[72,256]{1,0:T(8,128)S(1)}, f32[72,256]{1,0:T(8,128)S(1)}, u32[]{:S(2)}, u32[]{:S(2)}) collective-permute-start(f32[72,256]{1,0:T(8,128)S(1)} %add_add_fusion.2), channel_id=1, source_target_pairs={{0,16},{1,5},{2,18},{3,7},{4,20},{5,9},{6,22},{7,11},{8,24},{9,13}... | collective-permute-start | bytes 221192 | tf_op jit(solution)/shard_map/ppermute | solution.py:59
  67.2 6.2 %collective-permute-start.13 = (f32[72,256]{1,0:T(8,128)S(1)}, f32[72,256]{1,0:T(8,128)S(1)}, u32[]{:S(2)}, u32[]{:S(2)}) collective-permute-start(f32[72,256]{1,0:T(8,128)S(1)} %add_add_fusion.2), channel_id=1, source_target_pairs={{0,32},{1,9},{2,34},{3,11},{4,36},{5,13},{6,38},{7,15},{8,40},{9,1... | collective-permute-start | bytes 221192 | tf_op jit(solution)/shard_map/ppermute | solution.py:59
  73.4 11.1 %collective-permute-start.25 = (f32[160,256]{1,0:T(8,128)}, f32[160,256]{1,0:T(8,128)}, u32[]{:S(2)}, u32[]{:S(2)}) collective-permute-start(f32[160,256]{1,0:T(8,128)} %get-tuple-element.67), channel_id=1, source_target_pairs={{0,48},{1,13},{2,50},{3,15},{4,52},{5,1},{6,54},{7,3},{8,56},{9,5}... | collective-permute-start | bytes 491528 | tf_op jit(solution)/shard_map/ppermute | solution.py:59
  74.9 5.3 %collective-permute-start.15 = (f32[72,256]{1,0:T(8,128)S(1)}, f32[72,256]{1,0:T(8,128)S(1)}, u32[]{:S(2)}, u32[]{:S(2)}) collective-permute-start(f32[72,256]{1,0:T(8,128)S(1)} %add_add_fusion.1), channel_id=1, source_target_pairs={{0,64},{1,65},{2,66},{3,67},{4,68},{5,69},{6,70},{7,71},{8,72},{9,... | collective-permute-start | bytes 221192 | tf_op jit(solution)/shard_map/ppermute | solution.py:59
  75.0 7.8 %collective-permute-start.16 = (f32[72,256]{1,0:T(8,128)S(1)}, f32[72,256]{1,0:T(8,128)S(1)}, u32[]{:S(2)}, u32[]{:S(2)}) collective-permute-start(f32[72,256]{1,0:T(8,128)S(1)} %add_add_fusion.1), channel_id=1, source_target_pairs={{0,128},{1,129},{2,130},{3,131},{4,132},{5,133},{6,134},{7,135},{8... | collective-permute-start | bytes 221192 | tf_op jit(solution)/shard_map/ppermute | solution.py:59
  76.7 6.8 %collective-permute-start.17 = (f32[72,256]{1,0:T(8,128)S(1)}, f32[72,256]{1,0:T(8,128)S(1)}, u32[]{:S(2)}, u32[]{:S(2)}) collective-permute-start(f32[72,256]{1,0:T(8,128)S(1)} %add_add_fusion.1), channel_id=1, source_target_pairs={{0,192},{1,193},{2,194},{3,195},{4,196},{5,197},{6,198},{7,199},{8... | collective-permute-start | bytes 221192 | tf_op jit(solution)/shard_map/ppermute | solution.py:59
  79.7 13.5 %collective-permute-start.3 = (f32[320,256]{1,0:T(8,128)}, f32[320,256]{1,0:T(8,128)S(1)}, u32[]{:S(2)}, u32[]{:S(2)}) collective-permute-start(f32[320,256]{1,0:T(8,128)} %get-tuple-element.40), channel_id=1, source_target_pairs={{0,16},{1,5},{2,18},{3,7},{4,20},{5,9},{6,22},{7,11},{8,24},{9,13}... | collective-permute-start | bytes 983048 | tf_op jit(solution)/shard_map/ppermute | solution.py:59
  80.2 30.8 %collective-permute-start.4 = (f32[320,256]{1,0:T(8,128)}, f32[320,256]{1,0:T(8,128)S(1)}, u32[]{:S(2)}, u32[]{:S(2)}) collective-permute-start(f32[320,256]{1,0:T(8,128)} %get-tuple-element.39), channel_id=1, source_target_pairs={{0,32},{1,9},{2,34},{3,11},{4,36},{5,13},{6,38},{7,15},{8,40},{9,1... | collective-permute-start | bytes 983048 | tf_op jit(solution)/shard_map/ppermute | solution.py:59
  82.8 28.2 %collective-permute-start.5 = (f32[320,256]{1,0:T(8,128)}, f32[320,256]{1,0:T(8,128)S(1)}, u32[]{:S(2)}, u32[]{:S(2)}) collective-permute-start(f32[320,256]{1,0:T(8,128)} %get-tuple-element.38), channel_id=1, source_target_pairs={{0,48},{1,13},{2,50},{3,15},{4,52},{5,1},{6,54},{7,3},{8,56},{9,5}... | collective-permute-start | bytes 983048 | tf_op jit(solution)/shard_map/ppermute | solution.py:59
  84.5 5.0 %collective-permute-start.19 = (f32[72,256]{1,0:T(8,128)S(1)}, f32[72,256]{1,0:T(8,128)S(1)}, u32[]{:S(2)}, u32[]{:S(2)}) collective-permute-start(f32[72,256]{1,0:T(8,128)S(1)} %add_add_fusion), channel_id=1, source_target_pairs={{0,8},{1,33},{2,10},{3,35},{4,12},{5,37},{6,14},{7,39},{8,0},{9,41... | collective-permute-start | bytes 221192 | tf_op jit(solution)/shard_map/ppermute | solution.py:59
  86.8 5.5 %collective-permute-start.20 = (f32[72,256]{1,0:T(8,128)S(1)}, f32[72,256]{1,0:T(8,128)S(1)}, u32[]{:S(2)}, u32[]{:S(2)}) collective-permute-start(f32[72,256]{1,0:T(8,128)S(1)} %add_add_fusion), channel_id=1, source_target_pairs={{0,4},{1,17},{2,6},{3,19},{4,8},{5,21},{6,10},{7,23},{8,12},{9,25}... | collective-permute-start | bytes 221192 | tf_op jit(solution)/shard_map/ppermute | solution.py:59
  89.5 23.5 %collective-permute-start.26 = (f32[160,256]{1,0:T(8,128)}, f32[160,256]{1,0:T(8,128)S(1)}, u32[]{:S(2)}, u32[]{:S(2)}) collective-permute-start(f32[160,256]{1,0:T(8,128)} %get-tuple-element.67), channel_id=1, source_target_pairs={{0,32},{1,9},{2,34},{3,11},{4,36},{5,13},{6,38},{7,15},{8,40},{9,1... | collective-permute-start | bytes 491528 | tf_op jit(solution)/shard_map/ppermute | solution.py:59
  92.3 53.2 %collective-permute-start.27 = (f32[160,256]{1,0:T(8,128)}, f32[160,256]{1,0:T(8,128)S(1)}, u32[]{:S(2)}, u32[]{:S(2)}) collective-permute-start(f32[160,256]{1,0:T(8,128)} %get-tuple-element.67), channel_id=1, source_target_pairs={{0,16},{1,5},{2,18},{3,7},{4,20},{5,9},{6,22},{7,11},{8,24},{9,13}... | collective-permute-start | bytes 491528 | tf_op jit(solution)/shard_map/ppermute | solution.py:59
  93.1 21.3 %collective-permute-start.21 = (f32[288,256]{1,0:T(8,128)S(1)}, f32[288,256]{1,0:T(8,128)S(1)}, u32[]{:S(2)}, u32[]{:S(2)}) collective-permute-start(f32[288,256]{1,0:T(8,128)S(1)} %pad_maximum_fusion.mine), channel_id=1, source_target_pairs={{0,1},{1,0},{2,3},{3,2},{4,5},{5,4},{6,7},{7,6},{8,9},{9,8},{10,11... | collective-permute-start | bytes 884744 | tf_op jit(solution)/shard_map/ppermute | solution.py:59
  111.1 5.9 %collective-permute-start.6 = (f32[80,256]{1,0:T(8,128)S(1)}, f32[80,256]{1,0:T(8,128)S(1)}, u32[]{:S(2)}, u32[]{:S(2)}) collective-permute-start(f32[80,256]{1,0:T(8,128)S(1)} %get-tuple-element.43), channel_id=1, source_target_pairs={{0,64},{1,65},{2,66},{3,67},{4,68},{5,69},{6,70},{7,71},{8,72},{9,... | collective-permute-start | bytes 245768 | tf_op jit(solution)/shard_map/ppermute | solution.py:59
  111.2 8.4 %collective-permute-start.7 = (f32[80,256]{1,0:T(8,128)S(1)}, f32[80,256]{1,0:T(8,128)S(1)}, u32[]{:S(2)}, u32[]{:S(2)}) collective-permute-start(f32[80,256]{1,0:T(8,128)S(1)} %get-tuple-element.42), channel_id=1, source_target_pairs={{0,128},{1,129},{2,130},{3,131},{4,132},{5,133},{6,134},{7,135},{8... | collective-permute-start | bytes 245768 | tf_op jit(solution)/shard_map/ppermute | solution.py:59
  113.0 6.6 %collective-permute-start.8 = (f32[80,256]{1,0:T(8,128)S(1)}, f32[80,256]{1,0:T(8,128)S(1)}, u32[]{:S(2)}, u32[]{:S(2)}) collective-permute-start(f32[80,256]{1,0:T(8,128)S(1)} %get-tuple-element.41), channel_id=1, source_target_pairs={{0,192},{1,193},{2,194},{3,195},{4,196},{5,197},{6,198},{7,199},{8... | collective-permute-start | bytes 245768 | tf_op jit(solution)/shard_map/ppermute | solution.py:59
  121.5 7.5 %collective-permute-start.40 = (f32[40,256]{1,0:T(8,128)}, f32[40,256]{1,0:T(8,128)S(1)}, u32[]{:S(2)}, u32[]{:S(2)}) collective-permute-start(f32[40,256]{1,0:T(8,128)} %get-tuple-element.17), channel_id=1, source_target_pairs={{0,192},{1,193},{2,194},{3,195},{4,196},{5,197},{6,198},{7,199},{8... | collective-permute-start | bytes 122888 | tf_op jit(solution)/shard_map/ppermute | solution.py:59
  124.8 5.1 %collective-permute-start.42 = (f32[40,256]{1,0:T(8,128)}, f32[40,256]{1,0:T(8,128)S(1)}, u32[]{:S(2)}, u32[]{:S(2)}) collective-permute-start(f32[40,256]{1,0:T(8,128)} %get-tuple-element.17), channel_id=1, source_target_pairs={{0,64},{1,65},{2,66},{3,67},{4,68},{5,69},{6,70},{7,71},{8,72},{9,... | collective-permute-start | bytes 122888 | tf_op jit(solution)/shard_map/ppermute | solution.py:59
  125.9 6.7 %collective-permute-start.31 = (f32[40,256]{1,0:T(8,128)S(1)}, f32[40,256]{1,0:T(8,128)S(1)}, u32[]{:S(2)}, u32[]{:S(2)}) collective-permute-start(f32[40,256]{1,0:T(8,128)S(1)} %get-tuple-element.31), channel_id=1, source_target_pairs={{0,192},{1,193},{2,194},{3,195},{4,196},{5,197},{6,198},{7,199},{8... | collective-permute-start | bytes 122888 | tf_op jit(solution)/shard_map/ppermute | solution.py:59
  129.0 5.4 %collective-permute-start.32 = (f32[40,256]{1,0:T(8,128)S(1)}, f32[40,256]{1,0:T(8,128)S(1)}, u32[]{:S(2)}, u32[]{:S(2)}) collective-permute-start(f32[40,256]{1,0:T(8,128)S(1)} %get-tuple-element.31), channel_id=1, source_target_pairs={{0,128},{1,129},{2,130},{3,131},{4,132},{5,133},{6,134},{7,135},{8... | collective-permute-start | bytes 122888 | tf_op jit(solution)/shard_map/ppermute | solution.py:59
  129.4 5.1 %collective-permute-start.33 = (f32[40,256]{1,0:T(8,128)S(1)}, f32[40,256]{1,0:T(8,128)S(1)}, u32[]{:S(2)}, u32[]{:S(2)}) collective-permute-start(f32[40,256]{1,0:T(8,128)S(1)} %get-tuple-element.31), channel_id=1, source_target_pairs={{0,64},{1,65},{2,66},{3,67},{4,68},{5,69},{6,70},{7,71},{8,72},{9,... | collective-permute-start | bytes 122888 | tf_op jit(solution)/shard_map/ppermute | solution.py:59
  130.0 15.1 %collective-permute-start.64 = (f32[256,256]{1,0:T(8,128)S(1)}, f32[256,256]{1,0:T(8,128)S(1)}, u32[]{:S(2)}, u32[]{:S(2)}) collective-permute-start(f32[256,256]{1,0:T(8,128)S(1)} %get-tuple-element.33), channel_id=1, source_target_pairs={{0,1},{1,0},{2,3},{3,2},{4,5},{5,4},{6,7},{7,6},{8,9},{9,8},{10,11... | collective-permute-start | bytes 786440 | tf_op jit(solution)/shard_map/ppermute | solution.py:59
  132.6 5.8 %collective-permute-start.43 = (f32[160,256]{1,0:T(8,128)S(1)}, f32[160,256]{1,0:T(8,128)S(1)}, u32[]{:S(2)}, u32[]{:S(2)}) collective-permute-start(f32[160,256]{1,0:T(8,128)S(1)} %get-tuple-element.51), channel_id=1, source_target_pairs={{0,48},{1,13},{2,50},{3,15},{4,52},{5,1},{6,54},{7,3},{8,56},{9,5}... | collective-permute-start | bytes 491528 | tf_op jit(solution)/shard_map/ppermute | solution.py:59
  134.4 7.1 %collective-permute-start.44 = (f32[160,256]{1,0:T(8,128)S(1)}, f32[160,256]{1,0:T(8,128)S(1)}, u32[]{:S(2)}, u32[]{:S(2)}) collective-permute-start(f32[160,256]{1,0:T(8,128)S(1)} %get-tuple-element.51), channel_id=1, source_target_pairs={{0,32},{1,9},{2,34},{3,11},{4,36},{5,13},{6,38},{7,15},{8,40},{9,1... | collective-permute-start | bytes 491528 | tf_op jit(solution)/shard_map/ppermute | solution.py:59
  134.5 7.5 %collective-permute-start.45 = (f32[160,256]{1,0:T(8,128)S(1)}, f32[160,256]{1,0:T(8,128)S(1)}, u32[]{:S(2)}, u32[]{:S(2)}) collective-permute-start(f32[160,256]{1,0:T(8,128)S(1)} %get-tuple-element.51), channel_id=1, source_target_pairs={{0,16},{1,5},{2,18},{3,7},{4,20},{5,9},{6,22},{7,11},{8,24},{9,13}... | collective-permute-start | bytes 491528 | tf_op jit(solution)/shard_map/ppermute | solution.py:59
  138.4 8.7 %collective-permute-start.34 = (f32[160,256]{1,0:T(8,128)S(1)}, f32[160,256]{1,0:T(8,128)S(1)}, u32[]{:S(2)}, u32[]{:S(2)}) collective-permute-start(f32[160,256]{1,0:T(8,128)S(1)} %get-tuple-element.59), channel_id=1, source_target_pairs={{0,48},{1,13},{2,50},{3,15},{4,52},{5,1},{6,54},{7,3},{8,56},{9,5}... | collective-permute-start | bytes 491528 | tf_op jit(solution)/shard_map/ppermute | solution.py:59
  142.1 25.4 %collective-permute-start.46 = (f32[640,256]{1,0:T(8,128)S(1)}, f32[640,256]{1,0:T(8,128)S(1)}, u32[]{:S(2)}, u32[]{:S(2)}) collective-permute-start(f32[640,256]{1,0:T(8,128)S(1)} %constant_dynamic-update-slice_fusion.26.refs_12_.w0), channel_id=1, source_target_pairs={{0,12},{1,49},{2,14},{3,51},{4,0},{5,53},{6,2},{7,55},{8,4},{9,57}... | collective-permute-start | bytes 1966088 | tf_op jit(solution)/shard_map/ppermute | solution.py:59
  143.9 23.6 %collective-permute-start.47 = (f32[640,256]{1,0:T(8,128)S(1)}, f32[640,256]{1,0:T(8,128)S(1)}, u32[]{:S(2)}, u32[]{:S(2)}) collective-permute-start(f32[640,256]{1,0:T(8,128)S(1)} %constant_dynamic-update-slice_fusion.26.refs_12_.w0), channel_id=1, source_target_pairs={{0,8},{1,33},{2,10},{3,35},{4,12},{5,37},{6,14},{7,39},{8,0},{9,41... | collective-permute-start | bytes 1966088 | tf_op jit(solution)/shard_map/ppermute | solution.py:59
  145.1 24.0 %collective-permute-start.48 = (f32[640,256]{1,0:T(8,128)S(1)}, f32[640,256]{1,0:T(8,128)S(1)}, u32[]{:S(2)}, u32[]{:S(2)}) collective-permute-start(f32[640,256]{1,0:T(8,128)S(1)} %constant_dynamic-update-slice_fusion.26.refs_12_.w0), channel_id=1, source_target_pairs={{0,4},{1,17},{2,6},{3,19},{4,8},{5,21},{6,10},{7,23},{8,12},{9,25}... | collective-permute-start | bytes 1966088 | tf_op jit(solution)/shard_map/ppermute | solution.py:59
  145.6 17.3 %collective-permute-start.65 = (f32[64,256]{1,0:T(8,128)S(1)}, f32[64,256]{1,0:T(8,128)S(1)}, u32[]{:S(2)}, u32[]{:S(2)}) collective-permute-start(f32[64,256]{1,0:T(8,128)S(1)} %get-tuple-element.45), channel_id=1, source_target_pairs={{0,4},{1,17},{2,6},{3,19},{4,8},{5,21},{6,10},{7,23},{8,12},{9,25}... | collective-permute-start | bytes 196616 | tf_op jit(solution)/shard_map/ppermute | solution.py:59
  147.2 16.2 %collective-permute-start.66 = (f32[64,256]{1,0:T(8,128)S(1)}, f32[64,256]{1,0:T(8,128)S(1)}, u32[]{:S(2)}, u32[]{:S(2)}) collective-permute-start(f32[64,256]{1,0:T(8,128)S(1)} %get-tuple-element.47), channel_id=1, source_target_pairs={{0,8},{1,33},{2,10},{3,35},{4,12},{5,37},{6,14},{7,39},{8,0},{9,41... | collective-permute-start | bytes 196616 | tf_op jit(solution)/shard_map/ppermute | solution.py:59
  163.3 39.8 %collective-permute-start.28 = (f32[640,256]{1,0:T(8,128)S(1)}, f32[640,256]{1,0:T(8,128)S(1)}, u32[]{:S(2)}, u32[]{:S(2)}) collective-permute-start(f32[640,256]{1,0:T(8,128)S(1)} %constant_dynamic-update-slice_fusion.4.refs_4_), channel_id=1, source_target_pairs={{0,12},{1,49},{2,14},{3,51},{4,0},{5,53},{6,2},{7,55},{8,4},{9,57}... | collective-permute-start | bytes 1966088 | tf_op jit(solution)/shard_map/ppermute | solution.py:59
  166.3 40.4 %collective-permute-start.29 = (f32[640,256]{1,0:T(8,128)S(1)}, f32[640,256]{1,0:T(8,128)S(1)}, u32[]{:S(2)}, u32[]{:S(2)}) collective-permute-start(f32[640,256]{1,0:T(8,128)S(1)} %constant_dynamic-update-slice_fusion.4.refs_4_), channel_id=1, source_target_pairs={{0,8},{1,33},{2,10},{3,35},{4,12},{5,37},{6,14},{7,39},{8,0},{9,41... | collective-permute-start | bytes 1966088 | tf_op jit(solution)/shard_map/ppermute | solution.py:59
  167.5 5.1 %collective-permute-start.68 = (f32[64,256]{1,0:T(8,128)S(1)}, f32[64,256]{1,0:T(8,128)S(1)}, u32[]{:S(2)}, u32[]{:S(2)}) collective-permute-start(f32[64,256]{1,0:T(8,128)S(1)} %add_add_fusion.5), channel_id=1, source_target_pairs={{0,16},{1,5},{2,18},{3,7},{4,20},{5,9},{6,22},{7,11},{8,24},{9,13}... | collective-permute-start | bytes 196616 | tf_op jit(solution)/shard_map/ppermute | solution.py:59
  167.6 12.1 %collective-permute-start.69 = (f32[64,256]{1,0:T(8,128)S(1)}, f32[64,256]{1,0:T(8,128)S(1)}, u32[]{:S(2)}, u32[]{:S(2)}) collective-permute-start(f32[64,256]{1,0:T(8,128)S(1)} %add_add_fusion.5), channel_id=1, source_target_pairs={{0,32},{1,9},{2,34},{3,11},{4,36},{5,13},{6,38},{7,15},{8,40},{9,1... | collective-permute-start | bytes 196616 | tf_op jit(solution)/shard_map/ppermute | solution.py:59
  169.1 10.6 %collective-permute-start.70 = (f32[64,256]{1,0:T(8,128)S(1)}, f32[64,256]{1,0:T(8,128)S(1)}, u32[]{:S(2)}, u32[]{:S(2)}) collective-permute-start(f32[64,256]{1,0:T(8,128)S(1)} %add_add_fusion.5), channel_id=1, source_target_pairs={{0,48},{1,13},{2,50},{3,15},{4,52},{5,1},{6,54},{7,3},{8,56},{9,5}... | collective-permute-start | bytes 196616 | tf_op jit(solution)/shard_map/ppermute | solution.py:59
  172.6 10.3 %collective-permute-start.49 = (f32[64,256]{1,0:T(8,128)S(1)}, f32[64,256]{1,0:T(8,128)S(1)}, u32[]{:S(2)}, u32[]{:S(2)}) collective-permute-start(f32[64,256]{1,0:T(8,128)S(1)} %constant_dynamic-slice_fusion.6), channel_id=1, source_target_pairs={{0,1},{1,0},{2,3},{3,2},{4,5},{5,4},{6,7},{7,6},{8,9},{9,8},{10,11... | collective-permute-start | bytes 196616 | tf_op jit(solution)/shard_map/ppermute | solution.py:59
  179.7 5.5 %collective-permute-start.71 = (f32[64,256]{1,0:T(8,128)S(1)}, f32[64,256]{1,0:T(8,128)S(1)}, u32[]{:S(2)}, u32[]{:S(2)}) collective-permute-start(f32[64,256]{1,0:T(8,128)S(1)} %add_add_fusion.4), channel_id=1, source_target_pairs={{0,64},{1,65},{2,66},{3,67},{4,68},{5,69},{6,70},{7,71},{8,72},{9,... | collective-permute-start | bytes 196616 | tf_op jit(solution)/shard_map/ppermute | solution.py:59
  181.1 7.4 %collective-permute-start.72 = (f32[64,256]{1,0:T(8,128)S(1)}, f32[64,256]{1,0:T(8,128)S(1)}, u32[]{:S(2)}, u32[]{:S(2)}) collective-permute-start(f32[64,256]{1,0:T(8,128)S(1)} %add_add_fusion.4), channel_id=1, source_target_pairs={{0,128},{1,129},{2,130},{3,131},{4,132},{5,133},{6,134},{7,135},{8... | collective-permute-start | bytes 196616 | tf_op jit(solution)/shard_map/ppermute | solution.py:59
  182.9 5.6 %collective-permute-start.73 = (f32[64,256]{1,0:T(8,128)S(1)}, f32[64,256]{1,0:T(8,128)S(1)}, u32[]{:S(2)}, u32[]{:S(2)}) collective-permute-start(f32[64,256]{1,0:T(8,128)S(1)} %add_add_fusion.4), channel_id=1, source_target_pairs={{0,192},{1,193},{2,194},{3,195},{4,196},{5,197},{6,198},{7,199},{8... | collective-permute-start | bytes 196616 | tf_op jit(solution)/shard_map/ppermute | solution.py:59
  188.5 7.6 %collective-permute-start.52 = (f32[16,256]{1,0:T(8,128)S(1)}, f32[16,256]{1,0:T(8,128)S(1)}, u32[]{:S(2)}, u32[]{:S(2)}) collective-permute-start(f32[16,256]{1,0:T(8,128)S(1)} %get-tuple-element.49), channel_id=1, source_target_pairs={{0,12},{1,49},{2,14},{3,51},{4,0},{5,53},{6,2},{7,55},{8,4},{9,57}... | collective-permute-start | bytes 49160 | tf_op jit(solution)/shard_map/ppermute | solution.py:59
  189.1 7.3 %collective-permute-start.35 = (f32[160,256]{1,0:T(8,128)S(1)}, f32[160,256]{1,0:T(8,128)S(1)}, u32[]{:S(2)}, u32[]{:S(2)}) collective-permute-start(f32[160,256]{1,0:T(8,128)S(1)} %get-tuple-element.59), channel_id=1, source_target_pairs={{0,32},{1,9},{2,34},{3,11},{4,36},{5,13},{6,38},{7,15},{8,40},{9,1... | collective-permute-start | bytes 491528 | tf_op jit(solution)/shard_map/ppermute | solution.py:59
  192.6 7.7 %collective-permute-start.74 = (f32[64,256]{1,0:T(8,128)S(1)}, f32[64,256]{1,0:T(8,128)S(1)}, u32[]{:S(2)}, u32[]{:S(2)}) collective-permute-start(f32[64,256]{1,0:T(8,128)S(1)} %add_add_fusion.3), channel_id=1, source_target_pairs={{0,2},{1,3},{2,0},{3,1},{4,6},{5,7},{6,4},{7,5},{8,10},{9,11},{10,... | collective-permute-start | bytes 196616 | tf_op jit(solution)/shard_map/ppermute | solution.py:59
  196.4 5.5 %collective-permute-start.54 = (f32[16,256]{1,0:T(8,128)S(1)}, f32[16,256]{1,0:T(8,128)S(1)}, u32[]{:S(2)}, u32[]{:S(2)}) collective-permute-start(f32[16,256]{1,0:T(8,128)S(1)} %add_add_fusion.8), channel_id=1, source_target_pairs={{0,32},{1,9},{2,34},{3,11},{4,36},{5,13},{6,38},{7,15},{8,40},{9,1... | collective-permute-start | bytes 49160 | tf_op jit(solution)/shard_map/ppermute | solution.py:59
  200.4 5.5 %collective-permute-start.36 = (f32[160,256]{1,0:T(8,128)S(1)}, f32[160,256]{1,0:T(8,128)S(1)}, u32[]{:S(2)}, u32[]{:S(2)}) collective-permute-start(f32[160,256]{1,0:T(8,128)S(1)} %get-tuple-element.59), channel_id=1, source_target_pairs={{0,16},{1,5},{2,18},{3,7},{4,20},{5,9},{6,22},{7,11},{8,24},{9,13}... | collective-permute-start | bytes 491528 | tf_op jit(solution)/shard_map/ppermute | solution.py:59
  201.9 6.3 %collective-permute-start.75 = (f32[64,256]{1,0:T(8,128)S(1)}, f32[64,256]{1,0:T(8,128)S(1)}, u32[]{:S(2)}, u32[]{:S(2)}) collective-permute-start(f32[64,256]{1,0:T(8,128)S(1)} %add.311), channel_id=1, source_target_pairs={{0,12},{1,49},{2,14},{3,51},{4,0},{5,53},{6,2},{7,55},{8,4},{9,57}... | collective-permute-start | bytes 196616 | tf_op jit(solution)/shard_map/ppermute | solution.py:59
  203.1 6.4 %collective-permute-start.56 = (f32[16,256]{1,0:T(8,128)S(1)}, f32[16,256]{1,0:T(8,128)S(1)}, u32[]{:S(2)}, u32[]{:S(2)}) collective-permute-start(f32[16,256]{1,0:T(8,128)S(1)} %add_add_fusion.7), channel_id=1, source_target_pairs={{0,64},{1,65},{2,66},{3,67},{4,68},{5,69},{6,70},{7,71},{8,72},{9,... | collective-permute-start | bytes 49160 | tf_op jit(solution)/shard_map/ppermute | solution.py:59
  203.2 7.0 %collective-permute-start.57 = (f32[16,256]{1,0:T(8,128)S(1)}, f32[16,256]{1,0:T(8,128)S(1)}, u32[]{:S(2)}, u32[]{:S(2)}) collective-permute-start(f32[16,256]{1,0:T(8,128)S(1)} %add_add_fusion.7), channel_id=1, source_target_pairs={{0,128},{1,129},{2,130},{3,131},{4,132},{5,133},{6,134},{7,135},{8... | collective-permute-start | bytes 49160 | tf_op jit(solution)/shard_map/ppermute | solution.py:59
  206.7 70.1 %collective-permute-start.30 = (f32[640,256]{1,0:T(8,128)S(1)}, f32[640,256]{1,0:T(8,128)S(1)}, u32[]{:S(2)}, u32[]{:S(2)}) collective-permute-start(f32[640,256]{1,0:T(8,128)S(1)} %constant_dynamic-update-slice_fusion.4.refs_4_), channel_id=1, source_target_pairs={{0,4},{1,17},{2,6},{3,19},{4,8},{5,21},{6,10},{7,23},{8,12},{9,25}... | collective-permute-start | bytes 1966088 | tf_op jit(solution)/shard_map/ppermute | solution.py:59
  208.2 68.6 %collective-permute-start.37 = (f32[640,256]{1,0:T(8,128)S(1)}, f32[640,256]{1,0:T(8,128)S(1)}, u32[]{:S(2)}, u32[]{:S(2)}) collective-permute-start(f32[640,256]{1,0:T(8,128)S(1)} %constant_dynamic-update-slice_fusion.15.refs_8_), channel_id=1, source_target_pairs={{0,12},{1,49},{2,14},{3,51},{4,0},{5,53},{6,2},{7,55},{8,4},{9,57}... | collective-permute-start | bytes 1966088 | tf_op jit(solution)/shard_map/ppermute | solution.py:59
  209.5 67.4 %collective-permute-start.38 = (f32[640,256]{1,0:T(8,128)S(1)}, f32[640,256]{1,0:T(8,128)S(1)}, u32[]{:S(2)}, u32[]{:S(2)}) collective-permute-start(f32[640,256]{1,0:T(8,128)S(1)} %constant_dynamic-update-slice_fusion.15.refs_8_), channel_id=1, source_target_pairs={{0,8},{1,33},{2,10},{3,35},{4,12},{5,37},{6,14},{7,39},{8,0},{9,41... | collective-permute-start | bytes 1966088 | tf_op jit(solution)/shard_map/ppermute | solution.py:59
  210.1 66.7 %collective-permute-start.39 = (f32[640,256]{1,0:T(8,128)S(1)}, f32[640,256]{1,0:T(8,128)S(1)}, u32[]{:S(2)}, u32[]{:S(2)}) collective-permute-start(f32[640,256]{1,0:T(8,128)S(1)} %constant_dynamic-update-slice_fusion.15.refs_8_), channel_id=1, source_target_pairs={{0,4},{1,17},{2,6},{3,19},{4,8},{5,21},{6,10},{7,23},{8,12},{9,25}... | collective-permute-start | bytes 1966088 | tf_op jit(solution)/shard_map/ppermute | solution.py:59
  210.1 21.4 %collective-permute-start.76 = (f32[64,256]{1,0:T(8,128)S(1)}, f32[64,256]{1,0:T(8,128)S(1)}, u32[]{:S(2)}, u32[]{:S(2)}) collective-permute-start(f32[64,256]{1,0:T(8,128)S(1)} %add.311), channel_id=1, source_target_pairs={{0,8},{1,33},{2,10},{3,35},{4,12},{5,37},{6,14},{7,39},{8,0},{9,41... | collective-permute-start | bytes 196616 | tf_op jit(solution)/shard_map/ppermute | solution.py:59
  231.6 6.5 %collective-permute-start.59 = (f32[16,256]{1,0:T(8,128)S(1)}, f32[16,256]{1,0:T(8,128)S(1)}, u32[]{:S(2)}, u32[]{:S(2)}) collective-permute-start(f32[16,256]{1,0:T(8,128)S(1)} %add_add_fusion.6), channel_id=1, source_target_pairs={{0,2},{1,3},{2,0},{3,1},{4,6},{5,7},{6,4},{7,5},{8,10},{9,11},{10,... | collective-permute-start | bytes 49160 | tf_op jit(solution)/shard_map/ppermute | solution.py:59
  253.0 17.4 %collective-permute-start.78 = (f32[256,256]{1,0:T(8,128)S(1)}, f32[256,256]{1,0:T(8,128)S(1)}, u32[]{:S(2)}, u32[]{:S(2)}) collective-permute-start(f32[256,256]{1,0:T(8,128)S(1)} %pad_maximum_fusion.1.mine), channel_id=1, source_target_pairs={{0,1},{1,0},{2,3},{3,2},{4,5},{5,4},{6,7},{7,6},{8,9},{9,8},{10,11... | collective-permute-start | bytes 786440 | tf_op jit(solution)/shard_map/ppermute | solution.py:59
  270.3 14.3 %collective-permute-start.63 = (f32[64,256]{1,0:T(8,128)S(1)}, f32[64,256]{1,0:T(8,128)S(1)}, u32[]{:S(2)}, u32[]{:S(2)}) collective-permute-start(f32[64,256]{1,0:T(8,128)S(1)} %pad_maximum_fusion.2.top), channel_id=1, source_target_pairs={{0,1},{1,0},{2,3},{3,2},{4,5},{5,4},{6,7},{7,6},{8,9},{9,8},{10,11... | collective-permute-start | bytes 196616 | tf_op jit(solution)/shard_map/ppermute | solution.py:59
  (36 other events, 455.7 us)

commit v2 on v1

v2 whole, which is shorter than its diff:
```python
import functools

import jax
import jax.numpy as jnp
from jax import lax
from jax.experimental import pallas as pl
from jax.experimental.pallas import tpu as pltpu
from jax.sharding import Mesh
from jax.sharding import PartitionSpec as P

R = 256
MONTHS = 120
BLOCK = 128
SHARE = 40
CHUNK = 640
ROWS = 2560
CAP = 20
F32 = jnp.float32
BF16 = jnp.bfloat16
AXES = ("z", "y", "x", "h", "c")
PLANE = ("y", "x")
COLUMN = ("z", "h", "c")


def number(z, y, x, h, c):
    return ((z * 4 + y) * 4 + x) * 4 + h * 2 + c


def pairs_of(move):
    out = []
    for z in range(4):
        for y in range(4):
            for x in range(4):
                for h in range(2):
                    for c in range(2):
                        out.append((number(z, y, x, h, c), number(*move(z, y, x, h, c))))
    return out


def first_move(k):
    def move(z, y, x, h, c):
        return (z, y, (x + k) % 4, h, c) if c == 0 else (z, (y + k) % 4, x, h, c)

    return pairs_of(move)


def second_move(k):
    def move(z, y, x, h, c):
        return (z, (y + k) % 4, x, h, c) if c == 0 else (z, y, (x + k) % 4, h, c)

    return pairs_of(move)


def depth_move(k):
    return pairs_of(lambda z, y, x, h, c: ((z + k) % 4, y, x, h, c))


CORE_MOVE = pairs_of(lambda z, y, x, h, c: (z, y, x, h, 1 - c))


def send(value, pairs):
    return lax.ppermute(value, AXES, pairs)


def scatter_sum(parts, moves):
    return [parts[0]] + [send(parts[k], moves(k)) for k in (1, 2, 3)]


def gather(value, moves):
    return [value] + [send(value, moves((4 - k) % 4)) for k in (1, 2, 3)]


def gather_rows(own, name):
    with jax.named_scope(name + "_depth"):
        rows = jnp.concatenate(gather(own, depth_move), 0)
    with jax.named_scope(name + "_second"):
        rows = jnp.concatenate(gather(rows, second_move), 0)
    with jax.named_scope(name + "_first"):
        return gather(rows, first_move)


def exchange(value, axes):
    return lax.all_to_all(value, axes, 0, 0, tiled=True)


def sum_to_all(value, count, axes):
    return jnp.sum(exchange(jnp.broadcast_to(value, (count, *value.shape)), axes), axis=0)


def sum_slices(value, axes):
    return jnp.sum(exchange(value.reshape(16, -1, R), axes), axis=0)


def spread_slices(value, axes):
    return exchange(jnp.broadcast_to(value, (16, *value.shape)), axes).reshape(-1, R)


def split(a):
    hi = a.astype(BF16)
    return hi, (a - hi.astype(F32)).astype(BF16)


def dot3(a, b):
    ah, al = a
    bh, bl = b
    dot = functools.partial(jnp.dot, preferred_element_type=F32)
    return dot(ah, bh) + (dot(ah, bl) + dot(al, bh))


def dot6(a, b):
    return jnp.dot(a, b, precision=lax.Precision.HIGHEST, preferred_element_type=F32)


def gram_of(a, precision=None):
    return lax.dot_general(
        a, a, (((0,), (0,)), ((), ())), precision=precision, preferred_element_type=F32
    )


def eye(n):
    return (
        lax.broadcasted_iota(jnp.int32, (n, n), 0) == lax.broadcasted_iota(jnp.int32, (n, n), 1)
    ).astype(F32)


def total(a):
    return jnp.sum(jnp.sum(a, axis=1, keepdims=True), axis=0, keepdims=True)


def shifted_inverse(hess, mat_ref, x_ref):
    n = hess.shape[0]
    ident = eye(n)
    rho = total(hess * ident) * (1.0 / n)
    mat = hess * (1.0 / rho) + ident
    mat_ref[...] = mat
    mat_parts = split(mat)
    low, high = 0.999, n + 1.5
    c0 = 2.0 / (low + high)

    def grow(a):
        up = a * (2.0 - a)
        s = 2.0 / (1.0 + up)
        return s, s * up

    s, a = grow(low * c0)
    x_ref[...] = (s * c0) * (2.0 * ident - c0 * mat)

    def coarse(_, a):
        s, a = grow(a)
        x_parts = split(x_ref[...])
        y = 2.0 * ident - dot3(mat_parts, x_parts)
        x_ref[...] = s * dot3(x_parts, split(y))
        return a

    lax.fori_loop(0, 5, coarse, jnp.float32(a))

    def fine(_, carry):
        x = x_ref[...]
        x_ref[...] = dot6(x, 2.0 * ident - dot6(mat_ref[...], x))
        return carry

    lax.fori_loop(0, 2, fine, 0)
    return rho


def block_row(place, k, b):
    j, i = b // 4, b % 4
    first = lax.rem(place[0] + k, 4)
    second = lax.rem(place[1] + j, 4)
    depth = lax.rem(place[2] + i, 4)
    block = depth * 16 + first * place[5] + second * place[6]
    return pl.multiple_of(block * SHARE, 8)


def head_kernel(
    place, patient_hbm, month_hbm, tiles_hbm, duals_hbm,
    near, rho_ref, weights, prod_hbm, a0, a1, a2, a3,
    patient, month, tiles, duals, prod, mat, square, grad, u_part, g_part, held, sems, outs,
):
    copies = [
        pltpu.make_async_copy(src, dst, sems.at[n])
        for n, (src, dst) in enumerate(
            [
                (month_hbm, month), (patient_hbm, patient), (tiles_hbm, tiles), (duals_hbm, duals),
            ]
        )
    ]
    for copy in copies:
        copy.start()
    copies[0].wait()
    mf = month[...]
    month_gram = gram_of(mf, lax.Precision.HIGHEST)
    copies[1].wait()
    gram = gram_of(patient[...])
    rho = shifted_inverse(gram * month_gram, mat, near)
    rho_ref[...] = jnp.broadcast_to(rho, rho_ref.shape)
    core = place[4]
    mat[...] = near[...]

    @pl.when(core == 1)
    def _():
        mat[...] = dot6(near[...], near[...])

    square[...] = gram
    half = pl.multiple_of(core * 128, 128)
    for p in range(16):
        weights[p * 24 : p * 24 + 16, :] = rho * mat[p * 16 : p * 16 + 16, :]
        weights[p * 24 + 16 : p * 24 + 24, :] = square[pl.ds(half + p * 8, 8), :]

    grad[...] = jnp.zeros_like(grad)
    copies[2].wait()

    def visit(k, _):
        pat = patient[pl.ds(pl.multiple_of(place[8 + k] * BLOCK, BLOCK), BLOCK), :]
        product = lax.dot_general(
            tiles[k], pat, (((0,), (0,)), ((), ())), preferred_element_type=F32
        )
        prod[k] = product
        at = pl.ds(pl.multiple_of(place[8 + CAP + k] * BLOCK, BLOCK), BLOCK)
        grad[at, :] += product * month[pl.ds(place[8 + 2 * CAP + k], 1), :]
        return 0

    lax.fori_loop(0, place[7], visit, 0)
    prod_out = pltpu.make_async_copy(prod, prod_hbm, outs.at[4])
    prod_out.start()
    near_parts = split(near[...])
    copies[3].wait()

    def chunk(k, _):
        for b in range(16):
            at = pl.ds(block_row(place, k, b), SHARE)
            u_part[b * SHARE : (b + 1) * SHARE, :] = duals[at, :]
            g_part[b * SHARE : (b + 1) * SHARE, :] = grad[at, :]
        u = u_part[...]
        g = g_part[...] * (1.0 / rho)
        once = u + dot3(split(g - u), near_parts)
        twice = once + dot3(split(g - once), near_parts)
        once = rho * once
        twice = rho * twice
        for b in range(16):
            held[k, b * 80 : b * 80 + SHARE, :] = once[b * SHARE : (b + 1) * SHARE]
            held[k, b * 80 + SHARE : b * 80 + 80, :] = twice[b * SHARE : (b + 1) * SHARE]
        for n, out in enumerate((a0, a1, a2, a3)):

            @pl.when(k == n)
            def _(n=n, out=out):
                pltpu.make_async_copy(held.at[n], out, outs.at[n]).start()

        return 0

    lax.fori_loop(0, 4, chunk, 0)
    for n, out in enumerate((a0, a1, a2, a3)):
        pltpu.make_async_copy(held.at[n], out, outs.at[n]).wait()
    prod_out.wait()


def owner_kernel(
    place, s0, s1, s2, s3, z0_ref, mine, other, month,
    both_ref, z2_ref, code_ref, gram_ref, own, oth,
):
    summed = (s0[...] + s1[...]) + (s2[...] + s3[...])
    core = place[4]
    half = pl.multiple_of(core * 128, 128)
    rest = pl.multiple_of(128 - core * 128, 128)
    for p in range(16):
        own[p * 16 : p * 16 + 16, :] = mine[p * 24 : p * 24 + 16, :]
        oth[p * 16 : p * 16 + 16, :] = other[p * 24 : p * 24 + 16, :]
        gram_ref[pl.ds(half + p * 8, 8), :] = mine[p * 24 + 16 : p * 24 + 24, :]
        gram_ref[pl.ds(rest + p * 8, 8), :] = other[p * 24 + 16 : p * 24 + 24, :]
    mf = month[...]
    diagonal = jnp.sum(gram_ref[...] * eye(R), axis=0, keepdims=True)
    rho_total = total(jnp.sum(mf * mf, axis=0, keepdims=True) * diagonal) * (1.0 / R)
    a = own[...]
    b = oth[...]
    plain = jnp.where(core == 0, a, b)
    square = jnp.where(core == 0, b, a)
    z0 = z0_ref[...]
    first = summed[0:SHARE] + dot6(z0, plain)
    z1 = jnp.maximum(first / rho_total, 0.0)
    second = summed[SHARE:] + dot6(z0, plain - square) + 2.0 * dot6(z1, plain) - rho_total * z1
    z2 = jnp.maximum(second / rho_total, 0.0)
    both_ref[0:SHARE, :] = z0
    both_ref[SHARE:, :] = z1
    z2_ref[...] = z2
    code_ref[...] = gram_of(z2, lax.Precision.HIGHEST)


def month_kernel(place, w0, w1, w2, w3, prod, code, out, natural):
    for k, w in enumerate((w0, w1, w2, w3)):
        for b in range(16):
            natural[pl.ds(block_row(place, k, b), SHARE), :] = w[b * SHARE : (b + 1) * SHARE, :]
    for p in range(16):
        out[p * 24 : p * 24 + 8, :] = jnp.zeros((8, R), F32)
        out[p * 24 + 8 : p * 24 + 24, :] = code[p * 16 : p * 16 + 16, :]

    def visit(k, _):
        at = pl.ds(pl.multiple_of(place[8 + CAP + k] * BLOCK, BLOCK), BLOCK)
        column = jnp.sum(prod[k] * natural[at, :], axis=0, keepdims=True)
        m = place[8 + 2 * CAP + k]
        out[pl.ds((m // 8) * 24 + m % 8, 1), :] += column
        return 0

    lax.fori_loop(0, place[7], visit, 0)


def duals_kernel(place, *refs):
    parts, both, two = refs[0:4], refs[4:8], refs[8:12]
    near, rho_ref, out, v_part, z0_part, z1_part = refs[12:]
    scale = 1.0 / rho_ref[0:1, 0:1]
    near_parts = split(near[...])

    def chunk(k, _):
        for n in range(4):

            @pl.when(k == n)
            def _(n=n):
                for b in range(16):
                    rows = pl.ds(b * SHARE, SHARE)
                    v_part[rows, :] = scale * parts[n][b * 80 + SHARE : b * 80 + 80, :] - two[n][rows, :]
                    z0_part[rows, :] = both[n][b * 80 : b * 80 + SHARE, :]
                    z1_part[rows, :] = both[n][b * 80 + SHARE : b * 80 + 80, :]

        z0 = z0_part[...]
        z1 = z1_part[...]
        inner = z0 - dot3(split(z0), near_parts) + 2.0 * z1
        v_part[...] = v_part[...] + dot3(split(inner), near_parts) - z1
        for b in range(16):
            out[pl.ds(block_row(place, k, b), SHARE), :] = v_part[b * SHARE : (b + 1) * SHARE, :]
        return 0

    lax.fori_loop(0, 4, chunk, 0)


def tail_kernel(sums, gram, month, out, mat, near, grad):
    for p in range(16):
        grad[p * 8 : p * 8 + 8, :] = sums[p * 24 : p * 24 + 8, :]
        mat[p * 16 : p * 16 + 16, :] = sums[p * 24 + 8 : p * 24 + 24, :]
    rho = shifted_inverse(gram[...] * mat[...], mat, near)
    scaled = grad[0:MONTHS, :] * (1.0 / rho) + month[...]
    solved = jnp.maximum(dot6(scaled, near[...]), 0.0)
    mean = jnp.sum(solved, axis=0, keepdims=True) * (1.0 / MONTHS)
    out[...] = solved / (mean + 1e-06)


def call(body, outs, spaces, scratch, *args, limit=48 << 20):
    n = len(args)
    space = {"s": pltpu.SMEM, "h": pltpu.HBM, "v": pltpu.VMEM}
    return pl.pallas_call(
        body,
        out_shape=[jax.ShapeDtypeStruct(s, F32) for s in outs],
        in_specs=[pl.BlockSpec(memory_space=space[c]) for c in spaces[:n]],
        out_specs=[pl.BlockSpec(memory_space=space[c]) for c in spaces[n:]],
        scratch_shapes=[pltpu.VMEM(s, F32) if isinstance(s, tuple) else s for s in scratch],
        compiler_params=pltpu.CompilerParams(vmem_limit_bytes=limit),
    )(*args)


def on_device(
    tile_values, patient_block, code_block, month_index, live_count,
    patient_factor, month_factor, consensus, scaled_duals,
):
    z, y, x, h, core = [lax.axis_index(a) for a in AXES]
    flat = core == 0
    place = jnp.stack(
        [jnp.where(flat, x, y), jnp.where(flat, y, x), z, h, core,
         jnp.where(flat, 1, 4), jnp.where(flat, 4, 1), live_count[0]]
    ).astype(jnp.int32)
    place = jnp.concatenate([place, patient_block, code_block, month_index])

    near, rho, weights, prod, *parts = call(
        head_kernel,
        [(R, R), (8, 128), (384, R), (CAP, BLOCK, R)] + [(2 * CHUNK, R)] * 4,
        "shhhh" + "vvvhhhhh",
        [
            pltpu.VMEM((1024, R), BF16), (MONTHS, R), pltpu.VMEM((CAP, BLOCK, BLOCK), BF16),
            (ROWS, R), (CAP, BLOCK, R), (R, R), (R, R), (ROWS, R), (CHUNK, R), (CHUNK, R),
            (4, 2 * CHUNK, R), pltpu.SemaphoreType.DMA((4,)), pltpu.SemaphoreType.DMA((5,)),
        ],
        place, patient_factor, month_factor, tile_values, scaled_duals, limit=None,
    )
    with jax.named_scope("rs_first"):
        s = scatter_sum(parts, first_move)
    with jax.named_scope("weights_plane"):
        m = sum_slices(weights, PLANE)
    m = sum_to_all(m, 4, "z")
    mine = spread_slices(m, PLANE)
    other = send(mine, CORE_MOVE)
    s = [
        (s[0][j : j + 320] + s[1][j : j + 320]) + (s[2][j : j + 320] + s[3][j : j + 320])
        for j in (0, 320, 640, 960)
    ]
    s = scatter_sum(s, second_move)
    s = [
        (s[0][i : i + 80] + s[1][i : i + 80]) + (s[2][i : i + 80] + s[3][i : i + 80])
        for i in (0, 80, 160, 240)
    ]
    s = scatter_sum(s, depth_move)
    both, z2, code_gram, gram = call(
        owner_kernel, [(2 * SHARE, R), (SHARE, R), (R, R), (R, R)], "svvvvvvvv" + "vvvv", [(R, R), (R, R)],
        place, *s, consensus, mine, other, month_factor,
    )
    two = gather_rows(z2, "two")
    both = gather_rows(both, "both")
    (sums,) = call(
        month_kernel, [(384, R)], "svvvvvv" + "v", [(ROWS, R)],
        place, *two, prod, code_gram,
    )
    t = sum_slices(sums, PLANE)
    t = sum_to_all(t, 16, COLUMN)
    t = spread_slices(t, PLANE)
    (duals,) = call(
        duals_kernel, [(ROWS, R)], "s" + "v" * 15, [(CHUNK, R)] * 3,
        place, *parts, *both, *two, near, rho,
    )
    (new_months,) = call(
        tail_kernel, [(MONTHS, R)], "vvvv", [(R, R), (R, R), (BLOCK, R)], t, gram, month_factor
    )
    return (z2, duals, new_months)


def solution(mesh):
    mesh = Mesh(mesh.devices.reshape(4, 4, 4, 2, 2), AXES)
    site, cons = ("z", "y", "x"), ("h", "c")
    every = site + cons
    placed = (
        P(every, None, None), P(every), P(every), P(every), P(every),
        P(site, None), P(), P(site, cons), P(site, cons),
    )
    return jax.shard_map(
        on_device,
        mesh=mesh,
        in_specs=placed,
        out_specs=(P(site, cons), P(site, cons), P()),
        check_vma=False,
    )
```

time: 290 us -> 227 us (0.78)
  blocking collectives: 0 us -> 81.2 us
  starting transfers between devices: 134 us -> 53.2 us
  waiting for transfers between devices: 105 us -> 30.4 us
  local copies, waits for them, and re-layouts: 9.66 us -> 14.9 us
  Pallas kernels: 33.7 us -> 38.5 us
  other arithmetic: 1.68 us -> 5.09 us
    ppermute x79 -> x28, starting transfers between devices: 134 us -> 36.9 us  [send(): return lax.ppermute(value, AXES, pairs)]
    all_to_all x0 -> x3, blocking collectives: none -> 81.2 us  [exchange(): return lax.all_to_all(value, axes, 0, 0, tiled=True)]
    ppermute x79 -> x28, waiting for transfers between devices: 105 us -> 28.8 us  [send(): return lax.ppermute(value, AXES, pairs)]
    all_to_all x0 -> x3, starting transfers between devices: none -> 16.3 us  [exchange(): return lax.all_to_all(value, axes, 0, 0, tiled=True)]
    pallas_call x7 -> x5, Pallas kernels: 33.7 us -> 38.5 us  [call(): pl.pallas_call(body, out_shape=[jax.ShapeDtypeStruct(s, F32) for s in out...]
    unnamed x56 -> x38, local copies, waits for them, and re-layouts: 8.86 us -> 9.61 us
  transfers between devices with their start and end apart: 79 -> 31, of which waited for: 30 -> 11; matrix products, arithmetic and copies ran while one was open for 2% -> 6% of each run, Pallas kernels for 6% -> 5%
where the time goes in v2:
time: 227 us; the launch traced here: 225 us
  blocking collectives  81.2 us (36%)
  starting transfers between devices  53.2 us (23%)
  Pallas kernels  38.5 us (17%)
  waiting for transfers between devices  30.4 us (13%)
  local copies, waits for them, and re-layouts  14.9 us (7%)
  other arithmetic  5.09 us (2%)
    all_to_all x3, blocking collectives, exchange(): return lax.all_to_all(value, axes, 0, 0, tiled=True)  81.2 us
    pallas_call x5, Pallas kernels, call(): pl.pallas_call(body, out_shape=[jax.ShapeDtypeStruct(s, F32) for s in out...  38.5 us
    ppermute x28, starting transfers between devices, send(): return lax.ppermute(value, AXES, pairs)  36.9 us
    ppermute x28, waiting for transfers between devices, send(): return lax.ppermute(value, AXES, pairs)  28.8 us
    all_to_all x3, starting transfers between devices, exchange(): return lax.all_to_all(value, axes, 0, 0, tiled=True)  16.3 us
    unnamed x38, local copies, waits for them, and re-layouts  9.61 us
  transfers between devices with their start and end apart: 31, of which 11 were waited for; matrix products, arithmetic and copies ran while one was open for 6% of the time, Pallas kernels for 5%

profile of v2, /device:TPU:1, one launch (start us, length us, event | category | flops | bytes accessed | tf_op | source)
XLA Modules:
  0.0 224.8 jit_solution(4224666241427070738)
XLA Ops:
  1.3 1.3 concatenate.17.place
  2.6 17.8 %shard_map.112 = (f32[256,256]{1,0:T(8,128)}, f32[8,128]{1,0:T(8,128)}, f32[384,256]{1,0:T(8,128)}, f32[20,128,256]{2,1,0:T(8,128)}, f32[1280,256]{1,0:T(8,128)}...) custom-call(s32[68]{0:T(128)} %concatenate.17.place, bf16[1024,256]{1,0:T(8,128)(2,1)} %patient_hbm.1, ...), custom_call_target="tpu_custom_call" | custom-call | tf_op jit(solution)/shard_map/pallas_call | solution.py:348
  20.3 2.4 %collective-permute-start = (f32[1280,256]{1,0:T(8,128)}, f32[1280,256]{1,0:T(8,128)S(1)}, u32[]{:S(2)}, u32[]{:S(2)}) collective-permute-start(f32[1280,256]{1,0:T(8,128)} %get-tuple-element.16.refs_1_), channel_id=1, source_target_pairs={{0,4},{1,17},{2,6},{3,19},{4,8},{5,21},{6,10},{7,23},{8,12},{9,25}... | collective-permute-start | bytes 3932168 | tf_op jit(solution)/shard_map/rs_first/ppermute | solution.py:62
  22.7 1.8 collective-permute-start.1
  24.5 0.7 collective-permute-start.2
  25.2 31.9 %all_to_all.30 = f32[16,24,256]{2,1,0:T(8,128)S(1)} all-to-all(f32[16,24,256]{2,1,0:T(8,128)} %bitcast.14), channel_id=1, replica_groups=mesh['z'=4,'y'=4,'x'=4,'h'=2,'c'=2] {'y','x'}, dimensions={0} | all-to-all | bytes 786432 | tf_op jit(solution)/shard_map/weights_plane/all_to_all | solution.py:83
  57.2 11.4 %all_to_all.31 = f32[4,24,256]{2,1,0:T(8,128)S(1)} all-to-all(f32[4,24,256]{2,1,0:T(8,128)S(1)} %broadcast_in_dim.12), channel_id=1, replica_groups=mesh['z'=4,'y'=4,'x'=4,'h'=2,'c'=2] {'z'}, dimensions={0} | all-to-all | bytes 196608 | tf_op jit(solution)/shard_map/all_to_all | solution.py:83
  68.6 0.8 broadcast_in_dim.13
  69.4 5.8 %all-to-all-start.2 = ((f32[16,24,256]{2,1,0:T(8,128)}), f32[16,24,256]{2,1,0:T(8,128)S(1)}, u32[]{:S(2)}, u32[]{:S(2)}) async-start(f32[16,24,256]{2,1,0:T(8,128)} %broadcast_in_dim.13), calls=%async_computation.2 | async-start | bytes 786432 | tf_op jit(solution)/shard_map/all_to_all | solution.py:83
  75.2 2.9 %fusion.3 = (f32[320,256]{1,0:T(8,128)S(1)}, f32[320,256]{1,0:T(8,128)}, f32[320,256]{1,0:T(8,128)}, f32[320,256]{1,0:T(8,128)}) fusion(f32[1280,256]{1,0:T(8,128)} %collective-permute-done.2, f32[1280,256]{1,0:T(8,128)} %collective-permute-done.1, f32[1280,256]{1,0:T(8,128)S(1)} %collective-permute-done, f32[1280,256]{1,0:T(8,128)S(1)} %copy-done), kind=kLoop, calls=%fused_computation.10 | loop fusion | flops 983040 | bytes 6553600 | tf_op jit(solution)/shard_map/add | solution.py:389
  78.1 2.6 %collective-permute-start.5 = (f32[320,256]{1,0:T(8,128)}, f32[320,256]{1,0:T(8,128)S(1)}, u32[]{:S(2)}, u32[]{:S(2)}) collective-permute-start(f32[320,256]{1,0:T(8,128)} %get-tuple-element.28), channel_id=1, source_target_pairs={{0,48},{1,13},{2,50},{3,15},{4,52},{5,1},{6,54},{7,3},{8,56},{9,5}... | collective-permute-start | bytes 983048 | tf_op jit(solution)/shard_map/ppermute | solution.py:62
  80.8 0.6 collective-permute-start.4
  81.4 0.6 collective-permute-start.3
  81.9 1.6 all-to-all-done.2
  83.5 5.3 %collective-permute-start.9 = (f32[384,256]{1,0:T(8,128)S(1)}, f32[384,256]{1,0:T(8,128)S(1)}, u32[]{:S(2)}, u32[]{:S(2)}) collective-permute-start(f32[384,256]{1,0:T(8,128)S(1)} %bitcast.12), channel_id=1, source_target_pairs={{0,1},{1,0},{2,3},{3,2},{4,5},{5,4},{6,7},{7,6},{8,9},{9,8},{10,11... | collective-permute-start | bytes 1179656 | tf_op jit(solution)/shard_map/ppermute | solution.py:62
  88.9 3.7 %collective-permute-done.3 = f32[320,256]{1,0:T(8,128)S(1)} collective-permute-done((f32[320,256]{1,0:T(8,128)}, f32[320,256]{1,0:T(8,128)S(1)}, u32[]{:S(2)}, u32[]{:S(2)}) %collective-permute-start.3) | collective-permute-done | bytes 327712 | tf_op jit(solution)/shard_map/ppermute | solution.py:62
  92.7 1.0 collective-permute-start.8
  93.7 1.1 collective-permute-start.7
  94.8 1.6 collective-permute-done.8.s3
  96.4 2.4 %collective-permute-done.7.s2 = f32[80,256]{1,0:T(8,128)S(1)} collective-permute-done((f32[80,256]{1,0:T(8,128)S(1)}, f32[80,256]{1,0:T(8,128)S(1)}, u32[]{:S(2)}, u32[]{:S(2)}) %collective-permute-start.7) | collective-permute-done | bytes 81952 | tf_op jit(solution)/shard_map/ppermute | solution.py:62
  98.8 1.1 collective-permute-done.6.s1
  99.9 1.9 shard_map.113
  101.8 0.9 collective-permute-start.20
  102.7 2.4 %collective-permute-start.19 = (f32[40,256]{1,0:T(8,128)}, f32[40,256]{1,0:T(8,128)S(1)}, u32[]{:S(2)}, u32[]{:S(2)}) collective-permute-start(f32[40,256]{1,0:T(8,128)} %get-tuple-element.12), channel_id=1, source_target_pairs={{0,192},{1,193},{2,194},{3,195},{4,196},{5,197},{6,198},{7,199},{8... | collective-permute-start | bytes 122888 | tf_op jit(solution)/shard_map/two_depth/ppermute | solution.py:62
  105.0 0.3 collective-permute-start.12
  105.3 1.2 collective-permute-start.11
  106.5 0.8 constant_dynamic-update-slice_fusion.14
  107.3 2.6 %collective-permute-start.10 = (f32[80,256]{1,0:T(8,128)S(1)}, f32[80,256]{1,0:T(8,128)S(1)}, u32[]{:S(2)}, u32[]{:S(2)}) collective-permute-start(f32[80,256]{1,0:T(8,128)S(1)} %get-tuple-element.21), channel_id=1, source_target_pairs={{0,192},{1,193},{2,194},{3,195},{4,196},{5,197},{6,198},{7,199},{8... | collective-permute-start | bytes 245768 | tf_op jit(solution)/shard_map/both_depth/ppermute | solution.py:62
  110.0 0.6 collective-permute-start.22
  110.6 0.6 constant_dynamic-update-slice_fusion.3
  111.2 1.0 collective-permute-start.24
  112.2 0.3 collective-permute-start.23
  112.5 0.6 constant_dynamic-update-slice_fusion.2
  113.1 1.3 collective-permute-done.22
  114.4 3.5 %collective-permute-done.23 = f32[160,256]{1,0:T(8,128)S(1)} collective-permute-done((f32[160,256]{1,0:T(8,128)S(1)}, f32[160,256]{1,0:T(8,128)S(1)}, u32[]{:S(2)}, u32[]{:S(2)}) %collective-permute-start.23) | collective-permute-done | bytes 163872 | tf_op jit(solution)/shard_map/two_second/ppermute | solution.py:62
  118.0 0.5 collective-permute-done.24
  118.5 1.9 collective-permute-start.27
  120.4 3.1 %collective-permute-start.26 = (f32[640,256]{1,0:T(8,128)S(1)}, f32[640,256]{1,0:T(8,128)S(1)}, u32[]{:S(2)}, u32[]{:S(2)}) collective-permute-start(f32[640,256]{1,0:T(8,128)S(1)} %constant_dynamic-update-slice_fusion.15.refs_8_.w0), channel_id=1, source_target_pairs={{0,8},{1,33},{2,10},{3,35},{4,12},{5,37},{6,14},{7,39},{8,0},{9,41... | collective-permute-start | bytes 1966088 | tf_op jit(solution)/shard_map/two_first/ppermute | solution.py:62
  123.5 0.5 collective-permute-start.25
  124.0 0.7 constant_dynamic-update-slice_fusion.1
  124.7 0.6 constant_dynamic-update-slice_fusion
  125.3 0.7 collective-permute-start.13
  126.1 0.6 collective-permute-start.14
  126.6 4.8 %collective-permute-done.13 = f32[320,256]{1,0:T(8,128)S(1)} collective-permute-done((f32[320,256]{1,0:T(8,128)}, f32[320,256]{1,0:T(8,128)S(1)}, u32[]{:S(2)}, u32[]{:S(2)}) %collective-permute-start.13) | collective-permute-done | bytes 327712 | tf_op jit(solution)/shard_map/both_second/ppermute | solution.py:62
  131.5 9.6 %collective-permute-done.27.refs_11_.w3 = f32[640,256]{1,0:T(8,128)S(1)} collective-permute-done((f32[640,256]{1,0:T(8,128)S(1)}, f32[640,256]{1,0:T(8,128)S(1)}, u32[]{:S(2)}, u32[]{:S(2)}) %collective-permute-start.27) | collective-permute-done | bytes 655392 | tf_op jit(solution)/shard_map/two_first/ppermute | solution.py:62
  141.2 1.1 shard_map.115
  142.3 0.7 copy-done.4
  143.1 5.7 %all-to-all-start.3 = ((f32[16,24,256]{2,1,0:T(8,128)}), f32[16,24,256]{2,1,0:T(8,128)}, u32[]{:S(2)}, u32[]{:S(2)}) async-start(f32[16,24,256]{2,1,0:T(8,128)} %bitcast.11), calls=%async_computation.3 | async-start | bytes 786432 | tf_op jit(solution)/shard_map/all_to_all | solution.py:83
  148.8 1.7 constant_dynamic-update-slice_fusion.5
  150.5 1.7 constant_dynamic-update-slice_fusion.4.refs_4_
  152.3 1.3 collective-permute-start.18
  153.6 2.4 %collective-permute-start.17 = (f32[1280,256]{1,0:T(8,128)}, f32[1280,256]{1,0:T(8,128)}, u32[]{:S(2)}, u32[]{:S(2)}) collective-permute-start(f32[1280,256]{1,0:T(8,128)} %constant_dynamic-update-slice_fusion.4.refs_4_), channel_id=1, source_target_pairs={{0,8},{1,33},{2,10},{3,35},{4,12},{5,37},{6,14},{7,39},{8,0},{9,41... | collective-permute-start | bytes 3932168 | tf_op jit(solution)/shard_map/both_first/ppermute | solution.py:62
  156.0 1.2 collective-permute-start.16
  157.2 1.0 reduce_sum.38
  158.2 37.8 %all_to_all.32 = f32[16,24,256]{2,1,0:T(8,128)} all-to-all(f32[16,24,256]{2,1,0:T(8,128)S(1)} %broadcast_in_dim.14), channel_id=1, replica_groups=mesh['z'=4,'y'=4,'x'=4,'h'=2,'c'=2] {'z','h','c'}, dimensions={0} | all-to-all | bytes 786432 | tf_op jit(solution)/shard_map/all_to_all | solution.py:83
  196.1 1.0 reduce_sum.39
  197.1 0.8 broadcast_in_dim.15
  197.9 4.8 %all-to-all-start.5 = ((f32[16,24,256]{2,1,0:T(8,128)}), f32[16,24,256]{2,1,0:T(8,128)}, u32[]{:S(2)}, u32[]{:S(2)}) async-start(f32[16,24,256]{2,1,0:T(8,128)} %broadcast_in_dim.15), calls=%async_computation.5 | async-start | bytes 786432 | tf_op jit(solution)/shard_map/all_to_all | solution.py:83
  202.7 1.1 copy-done.3
  203.8 1.3 copy-done.5
  205.1 0.9 copy-done.7
  206.1 10.0 %shard_map.114 = f32[2560,256]{1,0:T(8,128)} custom-call(s32[68]{0:T(128)S(1)} %copy-done.11, f32[1280,256]{1,0:T(8,128)S(1)} %copy-done, f32[1280,256]{1,0:T(8,128)S(1)} %copy-done.5, f32[1280,256]{1,0:T(8,128)} %get-tuple-element.17.refs_2_, f32[1280,256]{1,0:T(8,128)} %get-tuple-element.18.refs_3_, ...), custom_call_target="tpu_custom_call" | custom-call | tf_op jit(solution)/shard_map/pallas_call | solution.py:348
  216.1 0.9 copy-done.9
  217.1 7.8 %shard_map.116 = f32[120,256]{1,0:T(8,128)} custom-call(f32[384,256]{1,0:T(8,128)} %bitcast.10.sums, f32[256,256]{1,0:T(8,128)S(1)} %copy-done.9, f32[120,256]{1,0:T(8,128)S(1)} %copy-done.6), custom_call_target="tpu_custom_call" | custom-call | tf_op jit(solution)/shard_map/pallas_call | solution.py:348
  (59 shorter events, 0.6 us)
Async XLA Ops:
  20.3 54.8 %collective-permute-start = (f32[1280,256]{1,0:T(8,128)}, f32[1280,256]{1,0:T(8,128)S(1)}, u32[]{:S(2)}, u32[]{:S(2)}) collective-permute-start(f32[1280,256]{1,0:T(8,128)} %get-tuple-element.16.refs_1_), channel_id=1, source_target_pairs={{0,4},{1,17},{2,6},{3,19},{4,8},{5,21},{6,10},{7,23},{8,12},{9,25}... | collective-permute-start | bytes 3932168 | tf_op jit(solution)/shard_map/rs_first/ppermute | solution.py:62
  22.7 52.4 %collective-permute-start.1 = (f32[1280,256]{1,0:T(8,128)}, f32[1280,256]{1,0:T(8,128)}, u32[]{:S(2)}, u32[]{:S(2)}) collective-permute-start(f32[1280,256]{1,0:T(8,128)} %get-tuple-element.17.refs_2_), channel_id=1, source_target_pairs={{0,8},{1,33},{2,10},{3,35},{4,12},{5,37},{6,14},{7,39},{8,0},{9,41... | collective-permute-start | bytes 3932168 | tf_op jit(solution)/shard_map/rs_first/ppermute | solution.py:62
  24.5 50.6 %collective-permute-start.2 = (f32[1280,256]{1,0:T(8,128)}, f32[1280,256]{1,0:T(8,128)}, u32[]{:S(2)}, u32[]{:S(2)}) collective-permute-start(f32[1280,256]{1,0:T(8,128)} %get-tuple-element.18.refs_3_), channel_id=1, source_target_pairs={{0,12},{1,49},{2,14},{3,51},{4,0},{5,53},{6,2},{7,55},{8,4},{9,57}... | collective-permute-start | bytes 3932168 | tf_op jit(solution)/shard_map/rs_first/ppermute | solution.py:62
  25.2 50.0 %copy-start = (f32[1280,256]{1,0:T(8,128)S(1)}, f32[1280,256]{1,0:T(8,128)}, u32[]{:S(2)}) copy-start(f32[1280,256]{1,0:T(8,128)} %get-tuple-element.15.refs_0_) | copy-start | bytes 3932164
  69.4 14.1 %all-to-all-start.2 = ((f32[16,24,256]{2,1,0:T(8,128)}), f32[16,24,256]{2,1,0:T(8,128)S(1)}, u32[]{:S(2)}, u32[]{:S(2)}) async-start(f32[16,24,256]{2,1,0:T(8,128)} %broadcast_in_dim.13), calls=%async_computation.2 | async-start | bytes 786432 | tf_op jit(solution)/shard_map/all_to_all | solution.py:83
  78.1 21.8 %copy-start.6 = (f32[120,256]{1,0:T(8,128)S(1)}, f32[120,256]{1,0:T(8,128)}, u32[]{:S(2)}) copy-start(f32[120,256]{1,0:T(8,128)} %month.3) | copy-start | bytes 368644
  78.1 21.8 %copy-start.10 = (f32[40,256]{1,0:T(8,128)S(1)}, f32[40,256]{1,0:T(8,128)}, u32[]{:S(2)}) copy-start(f32[40,256]{1,0:T(8,128)} %z0_ref.1) | copy-start | bytes 122884
  78.1 21.8 %copy-start.11 = (s32[68]{0:T(128)S(1)}, s32[68]{0:T(128)}, u32[]{:S(2)}) copy-start(s32[68]{0:T(128)} %concatenate.17.place) | copy-start | bytes 820
  78.1 10.6 %collective-permute-start.5 = (f32[320,256]{1,0:T(8,128)}, f32[320,256]{1,0:T(8,128)S(1)}, u32[]{:S(2)}, u32[]{:S(2)}) collective-permute-start(f32[320,256]{1,0:T(8,128)} %get-tuple-element.28), channel_id=1, source_target_pairs={{0,48},{1,13},{2,50},{3,15},{4,52},{5,1},{6,54},{7,3},{8,56},{9,5}... | collective-permute-start | bytes 983048 | tf_op jit(solution)/shard_map/ppermute | solution.py:62
  80.8 8.2 %collective-permute-start.4 = (f32[320,256]{1,0:T(8,128)}, f32[320,256]{1,0:T(8,128)S(1)}, u32[]{:S(2)}, u32[]{:S(2)}) collective-permute-start(f32[320,256]{1,0:T(8,128)} %get-tuple-element.29), channel_id=1, source_target_pairs={{0,32},{1,9},{2,34},{3,11},{4,36},{5,13},{6,38},{7,15},{8,40},{9,1... | collective-permute-start | bytes 983048 | tf_op jit(solution)/shard_map/ppermute | solution.py:62
  81.4 11.3 %collective-permute-start.3 = (f32[320,256]{1,0:T(8,128)}, f32[320,256]{1,0:T(8,128)S(1)}, u32[]{:S(2)}, u32[]{:S(2)}) collective-permute-start(f32[320,256]{1,0:T(8,128)} %get-tuple-element.30), channel_id=1, source_target_pairs={{0,16},{1,5},{2,18},{3,7},{4,20},{5,9},{6,22},{7,11},{8,24},{9,13}... | collective-permute-start | bytes 983048 | tf_op jit(solution)/shard_map/ppermute | solution.py:62
  83.5 11.3 %collective-permute-start.9 = (f32[384,256]{1,0:T(8,128)S(1)}, f32[384,256]{1,0:T(8,128)S(1)}, u32[]{:S(2)}, u32[]{:S(2)}) collective-permute-start(f32[384,256]{1,0:T(8,128)S(1)} %bitcast.12), channel_id=1, source_target_pairs={{0,1},{1,0},{2,3},{3,2},{4,5},{5,4},{6,7},{7,6},{8,9},{9,8},{10,11... | collective-permute-start | bytes 1179656 | tf_op jit(solution)/shard_map/ppermute | solution.py:62
  92.7 3.7 %collective-permute-start.8 = (f32[80,256]{1,0:T(8,128)S(1)}, f32[80,256]{1,0:T(8,128)S(1)}, u32[]{:S(2)}, u32[]{:S(2)}) collective-permute-start(f32[80,256]{1,0:T(8,128)S(1)} %get-tuple-element.31), channel_id=1, source_target_pairs={{0,192},{1,193},{2,194},{3,195},{4,196},{5,197},{6,198},{7,199},{8... | collective-permute-start | bytes 245768 | tf_op jit(solution)/shard_map/ppermute | solution.py:62
  93.7 5.1 %collective-permute-start.7 = (f32[80,256]{1,0:T(8,128)S(1)}, f32[80,256]{1,0:T(8,128)S(1)}, u32[]{:S(2)}, u32[]{:S(2)}) collective-permute-start(f32[80,256]{1,0:T(8,128)S(1)} %get-tuple-element.32), channel_id=1, source_target_pairs={{0,128},{1,129},{2,130},{3,131},{4,132},{5,133},{6,134},{7,135},{8... | collective-permute-start | bytes 245768 | tf_op jit(solution)/shard_map/ppermute | solution.py:62
  94.8 5.1 %collective-permute-start.6 = (f32[80,256]{1,0:T(8,128)S(1)}, f32[80,256]{1,0:T(8,128)S(1)}, u32[]{:S(2)}, u32[]{:S(2)}) collective-permute-start(f32[80,256]{1,0:T(8,128)S(1)} %get-tuple-element.33), channel_id=1, source_target_pairs={{0,64},{1,65},{2,66},{3,67},{4,68},{5,69},{6,70},{7,71},{8,72},{9,... | collective-permute-start | bytes 245768 | tf_op jit(solution)/shard_map/ppermute | solution.py:62
  101.8 8.2 %copy-start.8 = (f32[256,256]{1,0:T(8,128)}, f32[256,256]{1,0:T(8,128)S(1)}, u32[]{:S(2)}) copy-start(f32[256,256]{1,0:T(8,128)S(1)} %get-tuple-element.26.gram) | copy-start | bytes 786436
  101.8 8.2 %collective-permute-start.21 = (f32[40,256]{1,0:T(8,128)}, f32[40,256]{1,0:T(8,128)S(1)}, u32[]{:S(2)}, u32[]{:S(2)}) collective-permute-start(f32[40,256]{1,0:T(8,128)} %get-tuple-element.12), channel_id=1, source_target_pairs={{0,64},{1,65},{2,66},{3,67},{4,68},{5,69},{6,70},{7,71},{8,72},{9,... | collective-permute-start | bytes 122888 | tf_op jit(solution)/shard_map/two_depth/ppermute | solution.py:62
  101.8 8.1 %collective-permute-start.20 = (f32[40,256]{1,0:T(8,128)}, f32[40,256]{1,0:T(8,128)S(1)}, u32[]{:S(2)}, u32[]{:S(2)}) collective-permute-start(f32[40,256]{1,0:T(8,128)} %get-tuple-element.12), channel_id=1, source_target_pairs={{0,128},{1,129},{2,130},{3,131},{4,132},{5,133},{6,134},{7,135},{8... | collective-permute-start | bytes 122888 | tf_op jit(solution)/shard_map/two_depth/ppermute | solution.py:62
  102.7 4.6 %collective-permute-start.19 = (f32[40,256]{1,0:T(8,128)}, f32[40,256]{1,0:T(8,128)S(1)}, u32[]{:S(2)}, u32[]{:S(2)}) collective-permute-start(f32[40,256]{1,0:T(8,128)} %get-tuple-element.12), channel_id=1, source_target_pairs={{0,192},{1,193},{2,194},{3,195},{4,196},{5,197},{6,198},{7,199},{8... | collective-permute-start | bytes 122888 | tf_op jit(solution)/shard_map/two_depth/ppermute | solution.py:62
  105.0 19.6 %collective-permute-start.12 = (f32[80,256]{1,0:T(8,128)S(1)}, f32[80,256]{1,0:T(8,128)S(1)}, u32[]{:S(2)}, u32[]{:S(2)}) collective-permute-start(f32[80,256]{1,0:T(8,128)S(1)} %get-tuple-element.21), channel_id=1, source_target_pairs={{0,64},{1,65},{2,66},{3,67},{4,68},{5,69},{6,70},{7,71},{8,72},{9,... | collective-permute-start | bytes 245768 | tf_op jit(solution)/shard_map/both_depth/ppermute | solution.py:62
  105.3 18.7 %collective-permute-start.11 = (f32[80,256]{1,0:T(8,128)S(1)}, f32[80,256]{1,0:T(8,128)S(1)}, u32[]{:S(2)}, u32[]{:S(2)}) collective-permute-start(f32[80,256]{1,0:T(8,128)S(1)} %get-tuple-element.21), channel_id=1, source_target_pairs={{0,128},{1,129},{2,130},{3,131},{4,132},{5,133},{6,134},{7,135},{8... | collective-permute-start | bytes 245768 | tf_op jit(solution)/shard_map/both_depth/ppermute | solution.py:62
  107.3 4.9 %collective-permute-start.10 = (f32[80,256]{1,0:T(8,128)S(1)}, f32[80,256]{1,0:T(8,128)S(1)}, u32[]{:S(2)}, u32[]{:S(2)}) collective-permute-start(f32[80,256]{1,0:T(8,128)S(1)} %get-tuple-element.21), channel_id=1, source_target_pairs={{0,192},{1,193},{2,194},{3,195},{4,196},{5,197},{6,198},{7,199},{8... | collective-permute-start | bytes 245768 | tf_op jit(solution)/shard_map/both_depth/ppermute | solution.py:62
  110.0 31.2 %copy-start.1 = (f32[20,128,256]{2,1,0:T(8,128)S(1)}, f32[20,128,256]{2,1,0:T(8,128)}, u32[]{:S(2)}) copy-start(f32[20,128,256]{2,1,0:T(8,128)} %get-tuple-element.24.prod) | copy-start | bytes 7864324
  110.0 4.4 %collective-permute-start.22 = (f32[160,256]{1,0:T(8,128)S(1)}, f32[160,256]{1,0:T(8,128)S(1)}, u32[]{:S(2)}, u32[]{:S(2)}) collective-permute-start(f32[160,256]{1,0:T(8,128)S(1)} %get-tuple-element.43), channel_id=1, source_target_pairs={{0,48},{1,13},{2,50},{3,15},{4,52},{5,1},{6,54},{7,3},{8,56},{9,5}... | collective-permute-start | bytes 491528 | tf_op jit(solution)/shard_map/two_second/ppermute | solution.py:62
  111.2 7.3 %collective-permute-start.24 = (f32[160,256]{1,0:T(8,128)S(1)}, f32[160,256]{1,0:T(8,128)S(1)}, u32[]{:S(2)}, u32[]{:S(2)}) collective-permute-start(f32[160,256]{1,0:T(8,128)S(1)} %get-tuple-element.43), channel_id=1, source_target_pairs={{0,16},{1,5},{2,18},{3,7},{4,20},{5,9},{6,22},{7,11},{8,24},{9,13}... | collective-permute-start | bytes 491528 | tf_op jit(solution)/shard_map/two_second/ppermute | solution.py:62
  112.2 5.8 %collective-permute-start.23 = (f32[160,256]{1,0:T(8,128)S(1)}, f32[160,256]{1,0:T(8,128)S(1)}, u32[]{:S(2)}, u32[]{:S(2)}) collective-permute-start(f32[160,256]{1,0:T(8,128)S(1)} %get-tuple-element.43), channel_id=1, source_target_pairs={{0,32},{1,9},{2,34},{3,11},{4,36},{5,13},{6,38},{7,15},{8,40},{9,1... | collective-permute-start | bytes 491528 | tf_op jit(solution)/shard_map/two_second/ppermute | solution.py:62
  118.5 22.6 %collective-permute-start.27 = (f32[640,256]{1,0:T(8,128)S(1)}, f32[640,256]{1,0:T(8,128)S(1)}, u32[]{:S(2)}, u32[]{:S(2)}) collective-permute-start(f32[640,256]{1,0:T(8,128)S(1)} %constant_dynamic-update-slice_fusion.15.refs_8_.w0), channel_id=1, source_target_pairs={{0,4},{1,17},{2,6},{3,19},{4,8},{5,21},{6,10},{7,23},{8,12},{9,25}... | collective-permute-start | bytes 1966088 | tf_op jit(solution)/shard_map/two_first/ppermute | solution.py:62
  120.4 20.7 %collective-permute-start.26 = (f32[640,256]{1,0:T(8,128)S(1)}, f32[640,256]{1,0:T(8,128)S(1)}, u32[]{:S(2)}, u32[]{:S(2)}) collective-permute-start(f32[640,256]{1,0:T(8,128)S(1)} %constant_dynamic-update-slice_fusion.15.refs_8_.w0), channel_id=1, source_target_pairs={{0,8},{1,33},{2,10},{3,35},{4,12},{5,37},{6,14},{7,39},{8,0},{9,41... | collective-permute-start | bytes 1966088 | tf_op jit(solution)/shard_map/two_first/ppermute | solution.py:62
  123.5 17.6 %collective-permute-start.25 = (f32[640,256]{1,0:T(8,128)S(1)}, f32[640,256]{1,0:T(8,128)S(1)}, u32[]{:S(2)}, u32[]{:S(2)}) collective-permute-start(f32[640,256]{1,0:T(8,128)S(1)} %constant_dynamic-update-slice_fusion.15.refs_8_.w0), channel_id=1, source_target_pairs={{0,12},{1,49},{2,14},{3,51},{4,0},{5,53},{6,2},{7,55},{8,4},{9,57}... | collective-permute-start | bytes 1966088 | tf_op jit(solution)/shard_map/two_first/ppermute | solution.py:62
  125.3 6.1 %collective-permute-start.13 = (f32[320,256]{1,0:T(8,128)}, f32[320,256]{1,0:T(8,128)S(1)}, u32[]{:S(2)}, u32[]{:S(2)}) collective-permute-start(f32[320,256]{1,0:T(8,128)} %get-tuple-element.35), channel_id=1, source_target_pairs={{0,48},{1,13},{2,50},{3,15},{4,52},{5,1},{6,54},{7,3},{8,56},{9,5}... | collective-permute-start | bytes 983048 | tf_op jit(solution)/shard_map/both_second/ppermute | solution.py:62
  126.1 22.7 %collective-permute-start.14 = (f32[320,256]{1,0:T(8,128)}, f32[320,256]{1,0:T(8,128)}, u32[]{:S(2)}, u32[]{:S(2)}) collective-permute-start(f32[320,256]{1,0:T(8,128)} %get-tuple-element.35), channel_id=1, source_target_pairs={{0,32},{1,9},{2,34},{3,11},{4,36},{5,13},{6,38},{7,15},{8,40},{9,1... | collective-permute-start | bytes 983048 | tf_op jit(solution)/shard_map/both_second/ppermute | solution.py:62
  131.5 19.1 %collective-permute-start.15 = (f32[320,256]{1,0:T(8,128)}, f32[320,256]{1,0:T(8,128)}, u32[]{:S(2)}, u32[]{:S(2)}) collective-permute-start(f32[320,256]{1,0:T(8,128)} %get-tuple-element.35), channel_id=1, source_target_pairs={{0,16},{1,5},{2,18},{3,7},{4,20},{5,9},{6,22},{7,11},{8,24},{9,13}... | collective-permute-start | bytes 983048 | tf_op jit(solution)/shard_map/both_second/ppermute | solution.py:62
  131.5 9.7 %copy-start.13 = (f32[1280,256]{1,0:T(8,128)}, f32[1280,256]{1,0:T(8,128)S(1)}, u32[]{:S(2)}) copy-start(f32[1280,256]{1,0:T(8,128)S(1)} %constant_dynamic-update-slice_fusion.6) | copy-start | bytes 3932164
  141.2 1.1 copy-start.2
  142.3 0.7 copy-start.4
  143.1 14.1 %all-to-all-start.3 = ((f32[16,24,256]{2,1,0:T(8,128)}), f32[16,24,256]{2,1,0:T(8,128)}, u32[]{:S(2)}, u32[]{:S(2)}) async-start(f32[16,24,256]{2,1,0:T(8,128)} %bitcast.11), calls=%async_computation.3 | async-start | bytes 786432 | tf_op jit(solution)/shard_map/all_to_all | solution.py:83
  152.3 50.4 %collective-permute-start.18 = (f32[1280,256]{1,0:T(8,128)}, f32[1280,256]{1,0:T(8,128)}, u32[]{:S(2)}, u32[]{:S(2)}) collective-permute-start(f32[1280,256]{1,0:T(8,128)} %constant_dynamic-update-slice_fusion.4.refs_4_), channel_id=1, source_target_pairs={{0,4},{1,17},{2,6},{3,19},{4,8},{5,21},{6,10},{7,23},{8,12},{9,25}... | collective-permute-start | bytes 3932168 | tf_op jit(solution)/shard_map/both_first/ppermute | solution.py:62
  153.6 49.1 %collective-permute-start.17 = (f32[1280,256]{1,0:T(8,128)}, f32[1280,256]{1,0:T(8,128)}, u32[]{:S(2)}, u32[]{:S(2)}) collective-permute-start(f32[1280,256]{1,0:T(8,128)} %constant_dynamic-update-slice_fusion.4.refs_4_), channel_id=1, source_target_pairs={{0,8},{1,33},{2,10},{3,35},{4,12},{5,37},{6,14},{7,39},{8,0},{9,41... | collective-permute-start | bytes 3932168 | tf_op jit(solution)/shard_map/both_first/ppermute | solution.py:62
  156.0 46.7 %collective-permute-start.16 = (f32[1280,256]{1,0:T(8,128)}, f32[1280,256]{1,0:T(8,128)}, u32[]{:S(2)}, u32[]{:S(2)}) collective-permute-start(f32[1280,256]{1,0:T(8,128)} %constant_dynamic-update-slice_fusion.4.refs_4_), channel_id=1, source_target_pairs={{0,12},{1,49},{2,14},{3,51},{4,0},{5,53},{6,2},{7,55},{8,4},{9,57}... | collective-permute-start | bytes 3932168 | tf_op jit(solution)/shard_map/both_first/ppermute | solution.py:62
  158.2 44.5 %copy-start.12 = (f32[8,128]{1,0:T(8,128)S(1)}, f32[8,128]{1,0:T(8,128)}, u32[]{:S(2)}) copy-start(f32[8,128]{1,0:T(8,128)} %get-tuple-element.23.refs_13_) | copy-start | bytes 12292
  197.9 18.2 %all-to-all-start.5 = ((f32[16,24,256]{2,1,0:T(8,128)}), f32[16,24,256]{2,1,0:T(8,128)}, u32[]{:S(2)}, u32[]{:S(2)}) async-start(f32[16,24,256]{2,1,0:T(8,128)} %broadcast_in_dim.15), calls=%async_computation.5 | async-start | bytes 786432 | tf_op jit(solution)/shard_map/all_to_all | solution.py:83
  202.7 1.1 copy-start.3
  203.8 1.3 copy-start.5
  205.1 0.9 copy-start.7
  216.1 1.0 copy-start.9

commit v3 on v2

--- a/solution.py
+++ b/solution.py
@@ -7,6 +7,7 @@
 from jax.experimental.pallas import tpu as pltpu
 from jax.sharding import Mesh
 from jax.sharding import PartitionSpec as P
+
 
 R = 256
 MONTHS = 120
@@ -70,13 +71,10 @@
     return [value] + [send(value, moves((4 - k) % 4)) for k in (1, 2, 3)]
 
 
-def gather_rows(own, name):
-    with jax.named_scope(name + "_depth"):
-        rows = jnp.concatenate(gather(own, depth_move), 0)
-    with jax.named_scope(name + "_second"):
-        rows = jnp.concatenate(gather(rows, second_move), 0)
-    with jax.named_scope(name + "_first"):
-        return gather(rows, first_move)
+def gather_rows(own):
+    rows = jnp.concatenate(gather(own, depth_move), 0)
+    rows = jnp.concatenate(gather(rows, second_move), 0)
+    return gather(rows, first_move)
 
 
 def exchange(value, axes):
@@ -163,6 +161,28 @@
     return rho
 
 
+STEP = 1.0 / 128.0
+ROOM = 14.98
+
+
+def encode(block):
+    top = jnp.max(jnp.abs(block), axis=0, keepdims=True)
+    code = jnp.ceil(jnp.log2(jnp.maximum(top, 1e-30)) * 128.0)
+    return jnp.round(block * jnp.exp2(ROOM - code * STEP)), code
+
+
+def decode(whole, code):
+    return whole * jnp.exp2(code * STEP - ROOM)
+
+
+def to_codes(a):
+    return a.astype(jnp.int32).astype(jnp.int16)
+
+
+def from_codes(a):
+    return a.astype(jnp.int32).astype(F32)
+
+
 def block_row(place, k, b):
     j, i = b // 4, b % 4
     first = lax.rem(place[0] + k, 4)
@@ -172,10 +192,29 @@
     return pl.multiple_of(block * SHARE, 8)
 
 
-def head_kernel(
-    place, patient_hbm, month_hbm, tiles_hbm, duals_hbm,
-    near, rho_ref, weights, prod_hbm, a0, a1, a2, a3,
-    patient, month, tiles, duals, prod, mat, square, grad, u_part, g_part, held, sems, outs,
+def inverse_kernel(place, patient, month, near, rho_ref, weights, mat, square):
+    month_gram = gram_of(month[...], lax.Precision.HIGHEST)
+    gram = gram_of(patient[...])
+    rho = shifted_inverse(gram * month_gram, mat, near)
+    rho_ref[...] = jnp.broadcast_to(rho, rho_ref.shape)
+    core = place[4]
+    mat[...] = near[...]
+
+    @pl.when(core == 1)
+    def _():
+        mat[...] = dot6(near[...], near[...])
+
+    square[...] = gram
+    half = pl.multiple_of(core * 128, 128)
+    for p in range(16):
+        weights[p * 24 : p * 24 + 16, :] = rho * mat[p * 16 : p * 16 + 16, :]
+        weights[p * 24 + 16 : p * 24 + 24, :] = square[pl.ds(half + p * 8, 8), :]
+
+
+def local_kernel(
+    place, near, rho_ref, patient_hbm, month_hbm, tiles_hbm, duals_hbm,
+    prod_hbm, v_hbm, a0, q1, q2, q3,
+    patient, month, tiles, duals, prod, grad, u_part, g_part, v, own, coded, held, sems, outs,
 ):
     copies = [
         pltpu.make_async_copy(src, dst, sems.at[n])
@@ -187,28 +226,10 @@
     ]
     for copy in copies:
         copy.start()
-    copies[0].wait()
-    mf = month[...]
-    month_gram = gram_of(mf, lax.Precision.HIGHEST)
-    copies[1].wait()
-    gram = gram_of(patient[...])
-    rho = shifted_inverse(gram * month_gram, mat, near)
-    rho_ref[...] = jnp.broadcast_to(rho, rho_ref.shape)
-    core = place[4]
-    mat[...] = near[...]
-
-    @pl.when(core == 1)
-    def _():
-        mat[...] = dot6(near[...], near[...])
-
-    square[...] = gram
-    half = pl.multiple_of(core * 128, 128)
-    for p in range(16):
-        weights[p * 24 : p * 24 + 16, :] = rho * mat[p * 16 : p * 16 + 16, :]
-        weights[p * 24 + 16 : p * 24 + 24, :] = square[pl.ds(half + p * 8, 8), :]
-
+    rho = rho_ref[0:1, 0:1]
     grad[...] = jnp.zeros_like(grad)
-    copies[2].wait()
+    for copy in copies[:3]:
+        copy.wait()
 
     def visit(k, _):
         pat = patient[pl.ds(pl.multiple_of(place[8 + k] * BLOCK, BLOCK), BLOCK), :]
@@ -226,7 +247,8 @@
     near_parts = split(near[...])
     copies[3].wait()
 
-    def chunk(k, _):
+    def chunk(step, _):
+        k = lax.rem(step + 1, 4)
         for b in range(16):
             at = pl.ds(block_row(place, k, b), SHARE)
             u_part[b * SHARE : (b + 1) * SHARE, :] = duals[at, :]
@@ -235,28 +257,58 @@
         g = g_part[...] * (1.0 / rho)
         once = u + dot3(split(g - u), near_parts)
         twice = once + dot3(split(g - once), near_parts)
-        once = rho * once
-        twice = rho * twice
-        for b in range(16):
-            held[k, b * 80 : b * 80 + SHARE, :] = once[b * SHARE : (b + 1) * SHARE]
-            held[k, b * 80 + SHARE : b * 80 + 80, :] = twice[b * SHARE : (b + 1) * SHARE]
-        for n, out in enumerate((a0, a1, a2, a3)):
-
-            @pl.when(k == n)
+        v[k] = twice
+        u_part[...] = rho * once
+        g_part[...] = rho * twice
+
+        @pl.when(k > 0)
+        def _():
+            for b in range(16):
+                for q, part in enumerate((u_part, g_part)):
+                    whole, code = encode(part[b * SHARE : (b + 1) * SHARE, :])
+                    row = b * 80 + q * SHARE
+                    coded[row : row + SHARE, :] = whole
+                    coded[1280 + 2 * b + q : 1281 + 2 * b + q, :] = code
+            held[k - 1] = to_codes(coded[...])
+
+        for n, out in enumerate((q1, q2, q3)):
+
+            @pl.when(k == n + 1)
             def _(n=n, out=out):
                 pltpu.make_async_copy(held.at[n], out, outs.at[n]).start()
 
         return 0
 
     lax.fori_loop(0, 4, chunk, 0)
-    for n, out in enumerate((a0, a1, a2, a3)):
+    for b in range(16):
+        own[b * 80 : b * 80 + SHARE, :] = u_part[b * SHARE : (b + 1) * SHARE, :]
+        own[b * 80 + SHARE : b * 80 + 80, :] = g_part[b * SHARE : (b + 1) * SHARE, :]
+    own_out = pltpu.make_async_copy(own, a0, outs.at[3])
+    own_out.start()
+    v_out = pltpu.make_async_copy(v, v_hbm, outs.at[5])
+    v_out.start()
+    for n, out in enumerate((q1, q2, q3)):
         pltpu.make_async_copy(held.at[n], out, outs.at[n]).wait()
     prod_out.wait()
+    own_out.wait()
+    v_out.wait()
+
+
+def sum_kernel(a0, r1, r2, r3, s0, s1, s2, s3, acc, part):
+    acc[...] = a0[...]
+    for r in (r1, r2, r3):
+        part[...] = from_codes(r[...])
+        for b in range(32):
+            acc[b * SHARE : (b + 1) * SHARE, :] += decode(
+                part[b * SHARE : (b + 1) * SHARE, :], part[1280 + b : 1281 + b, :]
+            )
+    for j, out in enumerate((s0, s1, s2, s3)):
+        out[...] = acc[j * 320 : j * 320 + 320, :]
 
 
 def owner_kernel(
     place, s0, s1, s2, s3, z0_ref, mine, other, month,
-    both_ref, z2_ref, code_ref, gram_ref, own, oth,
+    both_ref, two_ref, z2_ref, code_ref, gram_ref, own, oth, both, two,
 ):
     summed = (s0[...] + s1[...]) + (s2[...] + s3[...])
     core = place[4]
@@ -279,16 +331,24 @@
     z1 = jnp.maximum(first / rho_total, 0.0)
     second = summed[SHARE:] + dot6(z0, plain - square) + 2.0 * dot6(z1, plain) - rho_total * z1
     z2 = jnp.maximum(second / rho_total, 0.0)
-    both_ref[0:SHARE, :] = z0
-    both_ref[SHARE:, :] = z1
+    both[...] = jnp.zeros_like(both)
+    two[...] = jnp.zeros_like(two)
+    both[0:SHARE, :], both[80:81, :] = encode(z0)
+    both[SHARE:80, :], both[81:82, :] = encode(z1)
+    two[0:SHARE, :], two[SHARE : SHARE + 1, :] = encode(z2)
+    both_ref[...] = to_codes(both[...])
+    two_ref[...] = to_codes(two[...])
     z2_ref[...] = z2
     code_ref[...] = gram_of(z2, lax.Precision.HIGHEST)
 
 
-def month_kernel(place, w0, w1, w2, w3, prod, code, out, natural):
+def month_kernel(place, w0, w1, w2, w3, prod, code, out, natural, part):
     for k, w in enumerate((w0, w1, w2, w3)):
+        part[...] = from_codes(w[...])
         for b in range(16):
-            natural[pl.ds(block_row(place, k, b), SHARE), :] = w[b * SHARE : (b + 1) * SHARE, :]
+            natural[pl.ds(block_row(place, k, b), SHARE), :] = decode(
+                part[b * 48 : b * 48 + SHARE, :], part[b * 48 + SHARE : b * 48 + SHARE + 1, :]
+            )
     for p in range(16):
         out[p * 24 : p * 24 + 8, :] = jnp.zeros((8, R), F32)
         out[p * 24 + 8 : p * 24 + 24, :] = code[p * 16 : p * 16 + 16, :]
@@ -304,9 +364,8 @@
 
 
 def duals_kernel(place, *refs):
-    parts, both, two = refs[0:4], refs[4:8], refs[8:12]
-    near, rho_ref, out, v_part, z0_part, z1_part = refs[12:]
-    scale = 1.0 / rho_ref[0:1, 0:1]
+    both, two = refs[0:4], refs[4:8]
+    v, near, _, out, part, z0_part, z1_part, z2_part = refs[8:]
     near_parts = split(near[...])
 
     def chunk(k, _):
@@ -314,18 +373,22 @@
 
             @pl.when(k == n)
             def _(n=n):
-                for b in range(16):
-                    rows = pl.ds(b * SHARE, SHARE)
-                    v_part[rows, :] = scale * parts[n][b * 80 + SHARE : b * 80 + 80, :] - two[n][rows, :]
-                    z0_part[rows, :] = both[n][b * 80 : b * 80 + SHARE, :]
-                    z1_part[rows, :] = both[n][b * 80 + SHARE : b * 80 + 80, :]
-
+                part[0:1536, :] = from_codes(both[n][...])
+                part[1536:, :] = from_codes(two[n][...])
+
+        for b in range(16):
+            rows = slice(b * SHARE, (b + 1) * SHARE)
+            at = b * 96
+            z0_part[rows, :] = decode(part[at : at + 40, :], part[at + 80 : at + 81, :])
+            z1_part[rows, :] = decode(part[at + 40 : at + 80, :], part[at + 81 : at + 82, :])
+            at = 1536 + b * 48
+            z2_part[rows, :] = decode(part[at : at + 40, :], part[at + 40 : at + 41, :])
         z0 = z0_part[...]
         z1 = z1_part[...]
         inner = z0 - dot3(split(z0), near_parts) + 2.0 * z1
-        v_part[...] = v_part[...] + dot3(split(inner), near_parts) - z1
+        z2_part[...] = v[k] + dot3(split(inner), near_parts) - z1 - z2_part[...]
         for b in range(16):
-            out[pl.ds(block_row(place, k, b), SHARE), :] = v_part[b * SHARE : (b + 1) * SHARE, :]
+            out[pl.ds(block_row(place, k, b), SHARE), :] = z2_part[b * SHARE : (b + 1) * SHARE, :]
         return 0
 
     lax.fori_loop(0, 4, chunk, 0)
@@ -347,7 +410,7 @@
     space = {"s": pltpu.SMEM, "h": pltpu.HBM, "v": pltpu.VMEM}
     return pl.pallas_call(
         body,
-        out_shape=[jax.ShapeDtypeStruct(s, F32) for s in outs],
+        out_shape=[s if isinstance(s, jax.ShapeDtypeStruct) else jax.ShapeDtypeStruct(s, F32) for s in outs],
         in_specs=[pl.BlockSpec(memory_space=space[c]) for c in spaces[:n]],
         out_specs=[pl.BlockSpec(memory_space=space[c]) for c in spaces[n:]],
         scratch_shapes=[pltpu.VMEM(s, F32) if isinstance(s, tuple) else s for s in scratch],
@@ -355,7 +418,7 @@
     )(*args)
 
 
-def on_device(
+def compute(
     tile_values, patient_block, code_block, month_index, live_count,
     patient_factor, month_factor, consensus, scaled_duals,
 ):
@@ -367,50 +430,54 @@
     ).astype(jnp.int32)
     place = jnp.concatenate([place, patient_block, code_block, month_index])
 
-    near, rho, weights, prod, *parts = call(
-        head_kernel,
-        [(R, R), (8, 128), (384, R), (CAP, BLOCK, R)] + [(2 * CHUNK, R)] * 4,
-        "shhhh" + "vvvhhhhh",
+    near, rho, weights = call(
+        inverse_kernel, [(R, R), (8, 128), (384, R)], "svv" + "vvv", [(R, R), (R, R)],
+        place, patient_factor, month_factor, limit=None,
+    )
+    m = sum_slices(weights, PLANE)
+    codes = [jax.ShapeDtypeStruct((1312, R), jnp.int16)] * 3
+    prod, v, *parts = call(
+        local_kernel,
+        [(CAP, BLOCK, R), (4, CHUNK, R), (2 * CHUNK, R)] + codes,
+        "svvhhhh" + "hhhhhh",
         [
             pltpu.VMEM((1024, R), BF16), (MONTHS, R), pltpu.VMEM((CAP, BLOCK, BLOCK), BF16),
-            (ROWS, R), (CAP, BLOCK, R), (R, R), (R, R), (ROWS, R), (CHUNK, R), (CHUNK, R),
-            (4, 2 * CHUNK, R), pltpu.SemaphoreType.DMA((4,)), pltpu.SemaphoreType.DMA((5,)),
+            (ROWS, R), (CAP, BLOCK, R), (ROWS, R), (CHUNK, R), (CHUNK, R), (4, CHUNK, R),
+            (2 * CHUNK, R), (1312, R), pltpu.VMEM((3, 1312, R), jnp.int16),
+            pltpu.SemaphoreType.DMA((4,)), pltpu.SemaphoreType.DMA((6,)),
         ],
-        place, patient_factor, month_factor, tile_values, scaled_duals, limit=None,
-    )
-    with jax.named_scope("rs_first"):
-        s = scatter_sum(parts, first_move)
-    with jax.named_scope("weights_plane"):
-        m = sum_slices(weights, PLANE)
+        place, near, rho, patient_factor, month_factor, tile_values, scaled_duals, limit=None,
+    )
+    s = scatter_sum(parts, first_move)
     m = sum_to_all(m, 4, "z")
     mine = spread_slices(m, PLANE)
     other = send(mine, CORE_MOVE)
-    s = [
-        (s[0][j : j + 320] + s[1][j : j + 320]) + (s[2][j : j + 320] + s[3][j : j + 320])
-        for j in (0, 320, 640, 960)
-    ]
+    s = call(sum_kernel, [(320, R)] * 4, "vvvv" + "vvvv", [(2 * CHUNK, R), (1312, R)], *s)
     s = scatter_sum(s, second_move)
     s = [
         (s[0][i : i + 80] + s[1][i : i + 80]) + (s[2][i : i + 80] + s[3][i : i + 80])
         for i in (0, 80, 160, 240)
     ]
     s = scatter_sum(s, depth_move)
-    both, z2, code_gram, gram = call(
-        owner_kernel, [(2 * SHARE, R), (SHARE, R), (R, R), (R, R)], "svvvvvvvv" + "vvvv", [(R, R), (R, R)],
+    both, two, z2, code_gram, gram = call(
+        owner_kernel,
+        [jax.ShapeDtypeStruct((96, R), jnp.int16), jax.ShapeDtypeStruct((48, R), jnp.int16),
+         (SHARE, R), (R, R), (R, R)],
+        "svvvvvvvv" + "vvvvv", [(R, R), (R, R), (96, R), (48, R)],
         place, *s, consensus, mine, other, month_factor,
     )
-    two = gather_rows(z2, "two")
-    both = gather_rows(both, "both")
+    two = gather_rows(two)
+    both = gather_rows(both)
     (sums,) = call(
-        month_kernel, [(384, R)], "svvvvvv" + "v", [(ROWS, R)],
+        month_kernel, [(384, R)], "svvvvvv" + "v", [(ROWS, R), (768, R)],
         place, *two, prod, code_gram,
     )
     t = sum_slices(sums, PLANE)
     t = sum_to_all(t, 16, COLUMN)
     t = spread_slices(t, PLANE)
     (duals,) = call(
-        duals_kernel, [(ROWS, R)], "s" + "v" * 15, [(CHUNK, R)] * 3,
-        place, *parts, *both, *two, near, rho,
+        duals_kernel, [(ROWS, R)], "s" + "v" * 12, [(2304, R)] + [(CHUNK, R)] * 3,
+        place, *both, *two, v, near, rho,
     )
     (new_months,) = call(
         tail_kernel, [(MONTHS, R)], "vvvv", [(R, R), (R, R), (BLOCK, R)], t, gram, month_factor
@@ -427,7 +494,7 @@
         P(site, None), P(), P(site, cons), P(site, cons),
     )
     return jax.shard_map(
-        on_device,
+        compute,
         mesh=mesh,
         in_specs=placed,
         out_specs=(P(site, cons), P(site, cons), P()),

time: 227 us -> 209 us (0.921)
  blocking collectives: 81.2 us -> 29.9 us
  starting transfers between devices: 53.2 us -> 70.9 us
  waiting for transfers between devices: 30.4 us -> 41.1 us
  Pallas kernels: 38.5 us -> 42.2 us
    all_to_all x3 -> x2, blocking collectives: 81.2 us -> 29.9 us  [exchange(): return lax.all_to_all(value, axes, 0, 0, tiled=True)]
    all_to_all x3 -> x4, starting transfers between devices: 16.3 us -> 33.6 us  [exchange(): return lax.all_to_all(value, axes, 0, 0, tiled=True)]
    all_to_all x3 -> x4, waiting for transfers between devices: 1.58 us -> 14.8 us  [exchange(): return lax.all_to_all(value, axes, 0, 0, tiled=True)]
    pallas_call x5 -> x7, Pallas kernels: 38.5 us -> 42.2 us  [call(): pl.pallas_call(body, out_shape=[s if isinstance(s, jax.ShapeDtypeStruct)...]
    ppermute x28, waiting for transfers between devices: 28.8 us -> 26.3 us  [send(): return lax.ppermute(value, AXES, pairs)]
    unnamed x38 -> x44, local copies, waits for them, and re-layouts: 9.61 us -> 8.53 us
  transfers between devices with their start and end apart: 31 -> 32, of which waited for: 11 -> 15; matrix products, arithmetic and copies ran while one was open for 6% -> 7% of each run, Pallas kernels for 5% -> 6%
where the time goes in v3:
time: 209 us; the launch traced here: 206 us
  starting transfers between devices  70.9 us (34%)
  Pallas kernels  42.2 us (20%)
  waiting for transfers between devices  41.1 us (20%)
  blocking collectives  29.9 us (14%)
  local copies, waits for them, and re-layouts  15.1 us (7%)
  other arithmetic  4.99 us (2%)
    pallas_call x7, Pallas kernels, call(): pl.pallas_call(body, out_shape=[s if isinstance(s, jax.ShapeDtypeStruct)...  42.2 us
    ppermute x28, starting transfers between devices, send(): return lax.ppermute(value, AXES, pairs)  37.3 us
    all_to_all x4, starting transfers between devices, exchange(): return lax.all_to_all(value, axes, 0, 0, tiled=True)  33.6 us
    all_to_all x2, blocking collectives, exchange(): return lax.all_to_all(value, axes, 0, 0, tiled=True)  29.9 us
    ppermute x28, waiting for transfers between devices, send(): return lax.ppermute(value, AXES, pairs)  26.3 us
    all_to_all x4, waiting for transfers between devices, exchange(): return lax.all_to_all(value, axes, 0, 0, tiled=True)  14.8 us
    unnamed x44, local copies, waits for them, and re-layouts  8.53 us
  transfers between devices with their start and end apart: 32, of which 15 were waited for; matrix products, arithmetic and copies ran while one was open for 7% of the time, Pallas kernels for 6%

profile of v3, /device:TPU:1, one launch (start us, length us, event | category | flops | bytes accessed | tf_op | source)
XLA Modules:
  0.0 205.8 jit_solution(11819487735307278629)
XLA Ops:
  1.3 1.4 concatenate.17.place
  2.6 8.7 %shard_map.112 = (f32[256,256]{1,0:T(8,128)}, f32[8,128]{1,0:T(8,128)}, f32[384,256]{1,0:T(8,128)}) custom-call(s32[68]{0:T(128)} %concatenate.17.place, bf16[1024,256]{1,0:T(8,128)(2,1)} %patient_hbm.1, f32[120,256]{1,0:T(8,128)} %month.5), custom_call_target="tpu_custom_call" | custom-call | tf_op jit(solution)/shard_map/pallas_call | solution.py:411
  11.3 11.3 %shard_map.113 = (f32[20,128,256]{2,1,0:T(8,128)}, f32[4,640,256]{2,1,0:T(8,128)}, f32[1280,256]{1,0:T(8,128)}, s16[1312,256]{1,0:T(8,128)(2,1)}, s16[1312,256]{1,0:T(8,128)(2,1)}, /*index=5*/s16[1312,256]{1,0:T(8,128)(2,1)}) custom-call(s32[68]{0:T(128)} %concatenate.17.place, f32[256,256]{1,0:T(8,128)} %get-tuple-element.21.near.refs_9_, ...), custom_call_target="tpu_custom_call" | custom-call | tf_op jit(solution)/shard_map/pallas_call | solution.py:411
  22.6 2.6 %collective-permute-start = (s16[1312,256]{1,0:T(8,128)(2,1)}, s16[1312,256]{1,0:T(8,128)(2,1)S(1)}, u32[]{:S(2)}, u32[]{:S(2)}) collective-permute-start(s16[1312,256]{1,0:T(8,128)(2,1)} %get-tuple-element.24), channel_id=1, source_target_pairs={{0,4},{1,17},{2,6},{3,19},{4,8},{5,21},{6,10},{7,23},{8,12},{9,25}... | collective-permute-start | bytes 2015240 | tf_op jit(solution)/shard_map/ppermute | solution.py:63
  25.2 2.2 %collective-permute-start.1 = (s16[1312,256]{1,0:T(8,128)(2,1)}, s16[1312,256]{1,0:T(8,128)(2,1)S(1)}, u32[]{:S(2)}, u32[]{:S(2)}) collective-permute-start(s16[1312,256]{1,0:T(8,128)(2,1)} %get-tuple-element.25), channel_id=1, source_target_pairs={{0,8},{1,33},{2,10},{3,35},{4,12},{5,37},{6,14},{7,39},{8,0},{9,41... | collective-permute-start | bytes 2015240 | tf_op jit(solution)/shard_map/ppermute | solution.py:63
  27.5 1.3 collective-permute-start.2
  28.7 20.0 %all_to_all.30 = f32[16,24,256]{2,1,0:T(8,128)} all-to-all(f32[16,24,256]{2,1,0:T(8,128)} %bitcast.12), channel_id=1, replica_groups=mesh['z'=4,'y'=4,'x'=4,'h'=2,'c'=2] {'y','x'}, dimensions={0} | all-to-all | bytes 786432 | tf_op jit(solution)/shard_map/all_to_all | solution.py:81
  48.8 1.0 reduce_sum.36
  49.8 9.9 %all_to_all.31 = f32[4,24,256]{2,1,0:T(8,128)} all-to-all(f32[4,24,256]{2,1,0:T(8,128)S(1)} %broadcast_in_dim.12), channel_id=1, replica_groups=mesh['z'=4,'y'=4,'x'=4,'h'=2,'c'=2] {'z'}, dimensions={0} | all-to-all | bytes 196608 | tf_op jit(solution)/shard_map/all_to_all | solution.py:81
  59.7 0.9 reduce_sum.37
  60.6 0.8 broadcast_in_dim.13
  61.3 5.0 %all-to-all-start.2 = ((f32[16,24,256]{2,1,0:T(8,128)}), f32[16,24,256]{2,1,0:T(8,128)}, u32[]{:S(2)}, u32[]{:S(2)}) async-start(f32[16,24,256]{2,1,0:T(8,128)} %broadcast_in_dim.13), calls=%async_computation.2 | async-start | bytes 786432 | tf_op jit(solution)/shard_map/all_to_all | solution.py:81
  66.4 1.7 shard_map.114
  68.1 0.7 copy-done.10
  68.8 1.3 collective-permute-start.3
  70.1 2.4 %collective-permute-start.4 = (f32[320,256]{1,0:T(8,128)}, f32[320,256]{1,0:T(8,128)}, u32[]{:S(2)}, u32[]{:S(2)}) collective-permute-start(f32[320,256]{1,0:T(8,128)} %get-tuple-element.29), channel_id=1, source_target_pairs={{0,32},{1,9},{2,34},{3,11},{4,36},{5,13},{6,38},{7,15},{8,40},{9,1... | collective-permute-start | bytes 983048 | tf_op jit(solution)/shard_map/ppermute | solution.py:63
  72.5 1.2 collective-permute-start.5
  73.7 0.9 all-to-all-done.2
  74.7 9.3 %collective-permute-start.9 = (f32[384,256]{1,0:T(8,128)}, f32[384,256]{1,0:T(8,128)S(1)}, u32[]{:S(2)}, u32[]{:S(2)}) collective-permute-start(f32[384,256]{1,0:T(8,128)} %bitcast.8.mine), channel_id=1, source_target_pairs={{0,1},{1,0},{2,3},{3,2},{4,5},{5,4},{6,7},{7,6},{8,9},{9,8},{10,11... | collective-permute-start | bytes 1179656 | tf_op jit(solution)/shard_map/ppermute | solution.py:63
  84.0 1.4 fusion
  85.4 0.9 collective-permute-start.6
  86.5 2.2 %collective-permute-start.8 = (f32[80,256]{1,0:T(8,128)S(1)}, f32[80,256]{1,0:T(8,128)S(1)}, u32[]{:S(2)}, u32[]{:S(2)}) collective-permute-start(f32[80,256]{1,0:T(8,128)S(1)} %get-tuple-element.39), channel_id=1, source_target_pairs={{0,192},{1,193},{2,194},{3,195},{4,196},{5,197},{6,198},{7,199},{8... | collective-permute-start | bytes 245768 | tf_op jit(solution)/shard_map/ppermute | solution.py:63
  88.7 2.0 collective-permute-done.6.s1
  90.7 1.5 collective-permute-done.7.s2
  92.2 2.8 %shard_map.115 = (s16[96,256]{1,0:T(8,128)(2,1)}, s16[48,256]{1,0:T(8,128)(2,1)S(1)}, f32[40,256]{1,0:T(8,128)}, f32[256,256]{1,0:T(8,128)S(1)}, f32[256,256]{1,0:T(8,128)S(1)}) custom-call(s32[68]{0:T(128)S(1)} %copy-done.14, f32[80,256]{1,0:T(8,128)S(1)} %get-tuple-element.42.s0, f32[80,256]{1,0:T(8,128)S(1)} %collective-permute-done.6.s1, ...), custom_call_target="tpu_custom_call" | custom-call | tf_op jit(solution)/shard_map/pallas_call | solution.py:411
  95.1 1.8 collective-permute-start.19
  97.8 2.6 %collective-permute-done.20 = s16[48,256]{1,0:T(8,128)(2,1)S(1)} collective-permute-done((s16[48,256]{1,0:T(8,128)(2,1)S(1)}, s16[48,256]{1,0:T(8,128)(2,1)S(1)}, u32[]{:S(2)}, u32[]{:S(2)}) %collective-permute-start.20) | collective-permute-done | bytes 24608 | tf_op jit(solution)/shard_map/ppermute | solution.py:63
  100.5 1.4 collective-permute-done.21
  101.9 1.1 collective-permute-start.22
  103.0 1.0 collective-permute-start.23
  104.3 1.1 collective-permute-done.22
  105.4 2.6 %collective-permute-done.23 = s16[192,256]{1,0:T(8,128)(2,1)S(1)} collective-permute-done((s16[192,256]{1,0:T(8,128)(2,1)S(1)}, s16[192,256]{1,0:T(8,128)(2,1)S(1)}, u32[]{:S(2)}, u32[]{:S(2)}) %collective-permute-start.23) | collective-permute-done | bytes 98336 | tf_op jit(solution)/shard_map/ppermute | solution.py:63
  108.0 1.0 collective-permute-done.24
  109.0 2.7 %collective-permute-start.25 = (s16[768,256]{1,0:T(8,128)(2,1)S(1)}, s16[768,256]{1,0:T(8,128)(2,1)S(1)}, u32[]{:S(2)}, u32[]{:S(2)}) collective-permute-start(s16[768,256]{1,0:T(8,128)(2,1)S(1)} %constant_dynamic-update-slice_fusion.15.refs_4_.w0), channel_id=1, source_target_pairs={{0,12},{1,49},{2,14},{3,51},{4,0},{5,53},{6,2},{7,55},{8,4},{9,57}... | collective-permute-start | bytes 1179656 | tf_op jit(solution)/shard_map/ppermute | solution.py:63
  112.7 1.4 constant_dynamic-update-slice_fusion.3
  114.2 2.0 collective-permute-done.10
  116.2 0.6 constant_dynamic-update-slice_fusion.2
  116.8 5.8 %collective-permute-done.25.refs_5_.w1 = s16[768,256]{1,0:T(8,128)(2,1)S(1)} collective-permute-done((s16[768,256]{1,0:T(8,128)(2,1)S(1)}, s16[768,256]{1,0:T(8,128)(2,1)S(1)}, u32[]{:S(2)}, u32[]{:S(2)}) %collective-permute-start.25) | collective-permute-done | bytes 393248 | tf_op jit(solution)/shard_map/ppermute | solution.py:63
  122.6 3.6 %collective-permute-done.27.refs_7_.w3 = s16[768,256]{1,0:T(8,128)(2,1)S(1)} collective-permute-done((s16[768,256]{1,0:T(8,128)(2,1)S(1)}, s16[768,256]{1,0:T(8,128)(2,1)S(1)}, u32[]{:S(2)}, u32[]{:S(2)}) %collective-permute-start.27) | collective-permute-done | bytes 393248 | tf_op jit(solution)/shard_map/ppermute | solution.py:63
  126.2 1.2 shard_map.117
  127.4 0.7 copy-done.6
  128.2 3.7 %all-to-all-start.3 = ((f32[16,24,256]{2,1,0:T(8,128)}), f32[16,24,256]{2,1,0:T(8,128)S(1)}, u32[]{:S(2)}, u32[]{:S(2)}) async-start(f32[16,24,256]{2,1,0:T(8,128)} %bitcast.11), calls=%async_computation.3 | async-start | bytes 786432 | tf_op jit(solution)/shard_map/all_to_all | solution.py:81
  131.9 1.5 constant_dynamic-update-slice_fusion.1
  133.4 1.4 constant_dynamic-update-slice_fusion
  134.8 2.5 %collective-permute-start.13 = (s16[384,256]{1,0:T(8,128)(2,1)}, s16[384,256]{1,0:T(8,128)(2,1)S(1)}, u32[]{:S(2)}, u32[]{:S(2)}) collective-permute-start(s16[384,256]{1,0:T(8,128)(2,1)} %get-tuple-element.43), channel_id=1, source_target_pairs={{0,48},{1,13},{2,50},{3,15},{4,52},{5,1},{6,54},{7,3},{8,56},{9,5}... | collective-permute-start | bytes 589832 | tf_op jit(solution)/shard_map/ppermute | solution.py:63
  137.3 0.6 collective-permute-start.14
  137.8 0.6 collective-permute-start.15
  138.4 3.2 %all-to-all-done.3 = f32[16,24,256]{2,1,0:T(8,128)S(1)} async-done(((f32[16,24,256]{2,1,0:T(8,128)}), f32[16,24,256]{2,1,0:T(8,128)S(1)}, u32[]{:S(2)}, u32[]{:S(2)}) %all-to-all-start.3) | async-done | bytes 393248 | tf_op jit(solution)/shard_map/all_to_all | solution.py:81
  141.7 0.8 broadcast_in_dim.14
  142.4 20.6 %all-to-all-start.4 = ((f32[16,24,256]{2,1,0:T(8,128)}), f32[16,24,256]{2,1,0:T(8,128)}, u32[]{:S(2)}, u32[]{:S(2)}) async-start(f32[16,24,256]{2,1,0:T(8,128)} %broadcast_in_dim.14), calls=%async_computation.4 | async-start | bytes 786432 | tf_op jit(solution)/shard_map/all_to_all | solution.py:81
  163.1 0.7 constant_dynamic-update-slice_fusion.6
  163.8 0.7 constant_dynamic-update-slice_fusion.5
  164.5 0.7 constant_dynamic-update-slice_fusion.4.refs_0_
  165.2 0.5 collective-permute-start.16
  165.7 1.1 collective-permute-start.17
  166.8 10.7 %all-to-all-done.4 = f32[16,24,256]{2,1,0:T(8,128)} async-done(((f32[16,24,256]{2,1,0:T(8,128)}), f32[16,24,256]{2,1,0:T(8,128)}, u32[]{:S(2)}, u32[]{:S(2)}) %all-to-all-start.4) | async-done | bytes 393248 | tf_op jit(solution)/shard_map/all_to_all | solution.py:81
  177.5 1.6 reduce_sum.39
  179.1 1.5 broadcast_in_dim.15
  180.6 4.2 %all-to-all-start.5 = ((f32[16,24,256]{2,1,0:T(8,128)}), f32[16,24,256]{2,1,0:T(8,128)}, u32[]{:S(2)}, u32[]{:S(2)}) async-start(f32[16,24,256]{2,1,0:T(8,128)} %broadcast_in_dim.15), calls=%async_computation.5 | async-start | bytes 786432 | tf_op jit(solution)/shard_map/all_to_all | solution.py:81
  184.9 2.2 %collective-permute-done.18.refs_3_ = s16[1536,256]{1,0:T(8,128)(2,1)} collective-permute-done((s16[1536,256]{1,0:T(8,128)(2,1)}, s16[1536,256]{1,0:T(8,128)(2,1)}, u32[]{:S(2)}, u32[]{:S(2)}) %collective-permute-start.18) | collective-permute-done | bytes 786464 | tf_op jit(solution)/shard_map/ppermute | solution.py:63
  187.1 1.1 copy-done.9
  188.3 8.8 %shard_map.116 = f32[2560,256]{1,0:T(8,128)} custom-call(s32[68]{0:T(128)S(1)} %copy-done.14, s16[1536,256]{1,0:T(8,128)(2,1)S(1)} %copy-done.9, s16[1536,256]{1,0:T(8,128)(2,1)S(1)} %collective-permute-done.16.refs_1_, s16[1536,256]{1,0:T(8,128)(2,1)S(1)} %collective-permute-done.17.refs_2_, s16[1536,256]{1,0:T(8,128)(2,1)} %collective-permute-done.18.refs_3_, ...), custom_call_target="tpu_custom_call" | custom-call | tf_op jit(solution)/shard_map/pallas_call | solution.py:411
  197.0 0.9 copy-done.12
  198.0 7.8 %shard_map.118 = f32[120,256]{1,0:T(8,128)} custom-call(f32[384,256]{1,0:T(8,128)} %bitcast.10.sums, f32[256,256]{1,0:T(8,128)S(1)} %copy-done.12, f32[120,256]{1,0:T(8,128)S(1)} %copy-done.1), custom_call_target="tpu_custom_call" | custom-call | tf_op jit(solution)/shard_map/pallas_call | solution.py:411
  (67 shorter events, 2.7 us)
Async XLA Ops:
  22.6 43.8 %copy-start.7 = (f32[1280,256]{1,0:T(8,128)S(1)}, f32[1280,256]{1,0:T(8,128)}, u32[]{:S(2)}) copy-start(f32[1280,256]{1,0:T(8,128)} %get-tuple-element.23.a0) | copy-start | bytes 3932164
  22.6 43.7 %collective-permute-start = (s16[1312,256]{1,0:T(8,128)(2,1)}, s16[1312,256]{1,0:T(8,128)(2,1)S(1)}, u32[]{:S(2)}, u32[]{:S(2)}) collective-permute-start(s16[1312,256]{1,0:T(8,128)(2,1)} %get-tuple-element.24), channel_id=1, source_target_pairs={{0,4},{1,17},{2,6},{3,19},{4,8},{5,21},{6,10},{7,23},{8,12},{9,25}... | collective-permute-start | bytes 2015240 | tf_op jit(solution)/shard_map/ppermute | solution.py:63
  25.2 41.2 %collective-permute-start.1 = (s16[1312,256]{1,0:T(8,128)(2,1)}, s16[1312,256]{1,0:T(8,128)(2,1)S(1)}, u32[]{:S(2)}, u32[]{:S(2)}) collective-permute-start(s16[1312,256]{1,0:T(8,128)(2,1)} %get-tuple-element.25), channel_id=1, source_target_pairs={{0,8},{1,33},{2,10},{3,35},{4,12},{5,37},{6,14},{7,39},{8,0},{9,41... | collective-permute-start | bytes 2015240 | tf_op jit(solution)/shard_map/ppermute | solution.py:63
  27.5 39.0 %collective-permute-start.2 = (s16[1312,256]{1,0:T(8,128)(2,1)}, s16[1312,256]{1,0:T(8,128)(2,1)S(1)}, u32[]{:S(2)}, u32[]{:S(2)}) collective-permute-start(s16[1312,256]{1,0:T(8,128)(2,1)} %get-tuple-element.26), channel_id=1, source_target_pairs={{0,12},{1,49},{2,14},{3,51},{4,0},{5,53},{6,2},{7,55},{8,4},{9,57}... | collective-permute-start | bytes 2015240 | tf_op jit(solution)/shard_map/ppermute | solution.py:63
  61.3 13.3 %all-to-all-start.2 = ((f32[16,24,256]{2,1,0:T(8,128)}), f32[16,24,256]{2,1,0:T(8,128)}, u32[]{:S(2)}, u32[]{:S(2)}) async-start(f32[16,24,256]{2,1,0:T(8,128)} %broadcast_in_dim.13), calls=%async_computation.2 | async-start | bytes 786432 | tf_op jit(solution)/shard_map/all_to_all | solution.py:81
  66.4 25.9 %copy-start.1 = (f32[120,256]{1,0:T(8,128)S(1)}, f32[120,256]{1,0:T(8,128)}, u32[]{:S(2)}) copy-start(f32[120,256]{1,0:T(8,128)} %month.5) | copy-start | bytes 368644
  66.4 25.9 %copy-start.13 = (f32[40,256]{1,0:T(8,128)S(1)}, f32[40,256]{1,0:T(8,128)}, u32[]{:S(2)}) copy-start(f32[40,256]{1,0:T(8,128)} %z0_ref.1) | copy-start | bytes 122884
  66.4 25.8 %copy-start.14 = (s32[68]{0:T(128)S(1)}, s32[68]{0:T(128)}, u32[]{:S(2)}) copy-start(s32[68]{0:T(128)} %concatenate.17.place) | copy-start | bytes 820
  68.1 0.7 copy-start.10
  68.8 57.4 %copy-start = (f32[20,128,256]{2,1,0:T(8,128)S(1)}, f32[20,128,256]{2,1,0:T(8,128)}, u32[]{:S(2)}) copy-start(f32[20,128,256]{2,1,0:T(8,128)} %get-tuple-element.36.prod) | copy-start | bytes 7864324
  68.8 15.1 %collective-permute-start.3 = (f32[320,256]{1,0:T(8,128)}, f32[320,256]{1,0:T(8,128)S(1)}, u32[]{:S(2)}, u32[]{:S(2)}) collective-permute-start(f32[320,256]{1,0:T(8,128)} %get-tuple-element.28), channel_id=1, source_target_pairs={{0,16},{1,5},{2,18},{3,7},{4,20},{5,9},{6,22},{7,11},{8,24},{9,13}... | collective-permute-start | bytes 983048 | tf_op jit(solution)/shard_map/ppermute | solution.py:63
  70.1 13.8 %collective-permute-start.4 = (f32[320,256]{1,0:T(8,128)}, f32[320,256]{1,0:T(8,128)}, u32[]{:S(2)}, u32[]{:S(2)}) collective-permute-start(f32[320,256]{1,0:T(8,128)} %get-tuple-element.29), channel_id=1, source_target_pairs={{0,32},{1,9},{2,34},{3,11},{4,36},{5,13},{6,38},{7,15},{8,40},{9,1... | collective-permute-start | bytes 983048 | tf_op jit(solution)/shard_map/ppermute | solution.py:63
  72.5 11.4 %collective-permute-start.5 = (f32[320,256]{1,0:T(8,128)}, f32[320,256]{1,0:T(8,128)}, u32[]{:S(2)}, u32[]{:S(2)}) collective-permute-start(f32[320,256]{1,0:T(8,128)} %get-tuple-element.30), channel_id=1, source_target_pairs={{0,48},{1,13},{2,50},{3,15},{4,52},{5,1},{6,54},{7,3},{8,56},{9,5}... | collective-permute-start | bytes 983048 | tf_op jit(solution)/shard_map/ppermute | solution.py:63
  74.7 17.5 %collective-permute-start.9 = (f32[384,256]{1,0:T(8,128)}, f32[384,256]{1,0:T(8,128)S(1)}, u32[]{:S(2)}, u32[]{:S(2)}) collective-permute-start(f32[384,256]{1,0:T(8,128)} %bitcast.8.mine), channel_id=1, source_target_pairs={{0,1},{1,0},{2,3},{3,2},{4,5},{5,4},{6,7},{7,6},{8,9},{9,8},{10,11... | collective-permute-start | bytes 1179656 | tf_op jit(solution)/shard_map/ppermute | solution.py:63
  85.4 5.3 %collective-permute-start.6 = (f32[80,256]{1,0:T(8,128)S(1)}, f32[80,256]{1,0:T(8,128)S(1)}, u32[]{:S(2)}, u32[]{:S(2)}) collective-permute-start(f32[80,256]{1,0:T(8,128)S(1)} %get-tuple-element.41), channel_id=1, source_target_pairs={{0,64},{1,65},{2,66},{3,67},{4,68},{5,69},{6,70},{7,71},{8,72},{9,... | collective-permute-start | bytes 245768 | tf_op jit(solution)/shard_map/ppermute | solution.py:63
  86.3 5.9 %collective-permute-start.7 = (f32[80,256]{1,0:T(8,128)S(1)}, f32[80,256]{1,0:T(8,128)S(1)}, u32[]{:S(2)}, u32[]{:S(2)}) collective-permute-start(f32[80,256]{1,0:T(8,128)S(1)} %get-tuple-element.40), channel_id=1, source_target_pairs={{0,128},{1,129},{2,130},{3,131},{4,132},{5,133},{6,134},{7,135},{8... | collective-permute-start | bytes 245768 | tf_op jit(solution)/shard_map/ppermute | solution.py:63
  86.5 5.7 %collective-permute-start.8 = (f32[80,256]{1,0:T(8,128)S(1)}, f32[80,256]{1,0:T(8,128)S(1)}, u32[]{:S(2)}, u32[]{:S(2)}) collective-permute-start(f32[80,256]{1,0:T(8,128)S(1)} %get-tuple-element.39), channel_id=1, source_target_pairs={{0,192},{1,193},{2,194},{3,195},{4,196},{5,197},{6,198},{7,199},{8... | collective-permute-start | bytes 245768 | tf_op jit(solution)/shard_map/ppermute | solution.py:63
  95.1 14.0 %copy-start.11 = (f32[256,256]{1,0:T(8,128)}, f32[256,256]{1,0:T(8,128)S(1)}, u32[]{:S(2)}) copy-start(f32[256,256]{1,0:T(8,128)S(1)} %get-tuple-element.38.gram) | copy-start | bytes 786436
  95.1 2.8 %collective-permute-start.19 = (s16[48,256]{1,0:T(8,128)(2,1)S(1)}, s16[48,256]{1,0:T(8,128)(2,1)S(1)}, u32[]{:S(2)}, u32[]{:S(2)}) collective-permute-start(s16[48,256]{1,0:T(8,128)(2,1)S(1)} %get-tuple-element.34), channel_id=1, source_target_pairs={{0,192},{1,193},{2,194},{3,195},{4,196},{5,197},{6,198},{7,199},{8... | collective-permute-start | bytes 73736 | tf_op jit(solution)/shard_map/ppermute | solution.py:63
  96.9 3.6 %collective-permute-start.20 = (s16[48,256]{1,0:T(8,128)(2,1)S(1)}, s16[48,256]{1,0:T(8,128)(2,1)S(1)}, u32[]{:S(2)}, u32[]{:S(2)}) collective-permute-start(s16[48,256]{1,0:T(8,128)(2,1)S(1)} %get-tuple-element.34), channel_id=1, source_target_pairs={{0,128},{1,129},{2,130},{3,131},{4,132},{5,133},{6,134},{7,135},{8... | collective-permute-start | bytes 73736 | tf_op jit(solution)/shard_map/ppermute | solution.py:63
  97.4 4.5 %collective-permute-start.21 = (s16[48,256]{1,0:T(8,128)(2,1)S(1)}, s16[48,256]{1,0:T(8,128)(2,1)S(1)}, u32[]{:S(2)}, u32[]{:S(2)}) collective-permute-start(s16[48,256]{1,0:T(8,128)(2,1)S(1)} %get-tuple-element.34), channel_id=1, source_target_pairs={{0,64},{1,65},{2,66},{3,67},{4,68},{5,69},{6,70},{7,71},{8,72},{9,... | collective-permute-start | bytes 73736 | tf_op jit(solution)/shard_map/ppermute | solution.py:63
  101.9 3.5 %collective-permute-start.22 = (s16[192,256]{1,0:T(8,128)(2,1)S(1)}, s16[192,256]{1,0:T(8,128)(2,1)S(1)}, u32[]{:S(2)}, u32[]{:S(2)}) collective-permute-start(s16[192,256]{1,0:T(8,128)(2,1)S(1)} %get-tuple-element.51), channel_id=1, source_target_pairs={{0,48},{1,13},{2,50},{3,15},{4,52},{5,1},{6,54},{7,3},{8,56},{9,5}... | collective-permute-start | bytes 294920 | tf_op jit(solution)/shard_map/ppermute | solution.py:63
  103.0 5.0 %collective-permute-start.23 = (s16[192,256]{1,0:T(8,128)(2,1)S(1)}, s16[192,256]{1,0:T(8,128)(2,1)S(1)}, u32[]{:S(2)}, u32[]{:S(2)}) collective-permute-start(s16[192,256]{1,0:T(8,128)(2,1)S(1)} %get-tuple-element.51), channel_id=1, source_target_pairs={{0,32},{1,9},{2,34},{3,11},{4,36},{5,13},{6,38},{7,15},{8,40},{9,1... | collective-permute-start | bytes 294920 | tf_op jit(solution)/shard_map/ppermute | solution.py:63
  104.0 5.0 %collective-permute-start.24 = (s16[192,256]{1,0:T(8,128)(2,1)S(1)}, s16[192,256]{1,0:T(8,128)(2,1)S(1)}, u32[]{:S(2)}, u32[]{:S(2)}) collective-permute-start(s16[192,256]{1,0:T(8,128)(2,1)S(1)} %get-tuple-element.51), channel_id=1, source_target_pairs={{0,16},{1,5},{2,18},{3,7},{4,20},{5,9},{6,22},{7,11},{8,24},{9,13}... | collective-permute-start | bytes 294920 | tf_op jit(solution)/shard_map/ppermute | solution.py:63
  109.0 13.5 %collective-permute-start.25 = (s16[768,256]{1,0:T(8,128)(2,1)S(1)}, s16[768,256]{1,0:T(8,128)(2,1)S(1)}, u32[]{:S(2)}, u32[]{:S(2)}) collective-permute-start(s16[768,256]{1,0:T(8,128)(2,1)S(1)} %constant_dynamic-update-slice_fusion.15.refs_4_.w0), channel_id=1, source_target_pairs={{0,12},{1,49},{2,14},{3,51},{4,0},{5,53},{6,2},{7,55},{8,4},{9,57}... | collective-permute-start | bytes 1179656 | tf_op jit(solution)/shard_map/ppermute | solution.py:63
  111.7 10.9 %collective-permute-start.26 = (s16[768,256]{1,0:T(8,128)(2,1)S(1)}, s16[768,256]{1,0:T(8,128)(2,1)S(1)}, u32[]{:S(2)}, u32[]{:S(2)}) collective-permute-start(s16[768,256]{1,0:T(8,128)(2,1)S(1)} %constant_dynamic-update-slice_fusion.15.refs_4_.w0), channel_id=1, source_target_pairs={{0,8},{1,33},{2,10},{3,35},{4,12},{5,37},{6,14},{7,39},{8,0},{9,41... | collective-permute-start | bytes 1179656 | tf_op jit(solution)/shard_map/ppermute | solution.py:63
  112.2 14.0 %collective-permute-start.27 = (s16[768,256]{1,0:T(8,128)(2,1)S(1)}, s16[768,256]{1,0:T(8,128)(2,1)S(1)}, u32[]{:S(2)}, u32[]{:S(2)}) collective-permute-start(s16[768,256]{1,0:T(8,128)(2,1)S(1)} %constant_dynamic-update-slice_fusion.15.refs_4_.w0), channel_id=1, source_target_pairs={{0,4},{1,17},{2,6},{3,19},{4,8},{5,21},{6,10},{7,23},{8,12},{9,25}... | collective-permute-start | bytes 1179656 | tf_op jit(solution)/shard_map/ppermute | solution.py:63
  112.7 3.4 %collective-permute-start.10 = (s16[96,256]{1,0:T(8,128)(2,1)}, s16[96,256]{1,0:T(8,128)(2,1)S(1)}, u32[]{:S(2)}, u32[]{:S(2)}) collective-permute-start(s16[96,256]{1,0:T(8,128)(2,1)} %get-tuple-element.33), channel_id=1, source_target_pairs={{0,192},{1,193},{2,194},{3,195},{4,196},{5,197},{6,198},{7,199},{8... | collective-permute-start | bytes 147464 | tf_op jit(solution)/shard_map/ppermute | solution.py:63
  114.2 17.7 %collective-permute-start.11 = (s16[96,256]{1,0:T(8,128)(2,1)}, s16[96,256]{1,0:T(8,128)(2,1)}, u32[]{:S(2)}, u32[]{:S(2)}) collective-permute-start(s16[96,256]{1,0:T(8,128)(2,1)} %get-tuple-element.33), channel_id=1, source_target_pairs={{0,128},{1,129},{2,130},{3,131},{4,132},{5,133},{6,134},{7,135},{8... | collective-permute-start | bytes 147464 | tf_op jit(solution)/shard_map/ppermute | solution.py:63
  116.2 17.2 %collective-permute-start.12 = (s16[96,256]{1,0:T(8,128)(2,1)}, s16[96,256]{1,0:T(8,128)(2,1)}, u32[]{:S(2)}, u32[]{:S(2)}) collective-permute-start(s16[96,256]{1,0:T(8,128)(2,1)} %get-tuple-element.33), channel_id=1, source_target_pairs={{0,64},{1,65},{2,66},{3,67},{4,68},{5,69},{6,70},{7,71},{8,72},{9,... | collective-permute-start | bytes 147464 | tf_op jit(solution)/shard_map/ppermute | solution.py:63
  116.8 9.4 %copy-start.16 = (s16[384,256]{1,0:T(8,128)(2,1)}, s16[384,256]{1,0:T(8,128)(2,1)S(1)}, u32[]{:S(2)}) copy-start(s16[384,256]{1,0:T(8,128)(2,1)S(1)} %get-tuple-element.47) | copy-start | bytes 589828
  122.6 4.8 %copy-start.2 = (s16[768,256]{1,0:T(8,128)(2,1)}, s16[768,256]{1,0:T(8,128)(2,1)S(1)}, u32[]{:S(2)}) copy-start(s16[768,256]{1,0:T(8,128)(2,1)S(1)} %collective-permute-done.26.refs_6_.w2) | copy-start | bytes 1179652
  126.2 1.2 copy-start.4
  127.4 0.7 copy-start.6
  128.2 58.9 %copy-start.3 = (s16[768,256]{1,0:T(8,128)(2,1)S(1)}, s16[768,256]{1,0:T(8,128)(2,1)}, u32[]{:S(2)}) copy-start(s16[768,256]{1,0:T(8,128)(2,1)} %copy-done.2) | copy-start | bytes 1179652
  128.2 58.9 %copy-start.5 = (s16[768,256]{1,0:T(8,128)(2,1)S(1)}, s16[768,256]{1,0:T(8,128)(2,1)}, u32[]{:S(2)}) copy-start(s16[768,256]{1,0:T(8,128)(2,1)} %copy-done.4) | copy-start | bytes 1179652
  128.2 58.9 %copy-start.8 = (f32[256,256]{1,0:T(8,128)S(1)}, f32[256,256]{1,0:T(8,128)}, u32[]{:S(2)}) copy-start(f32[256,256]{1,0:T(8,128)} %get-tuple-element.21.near.refs_9_) | copy-start | bytes 786436
  128.2 58.9 %copy-start.15 = (f32[8,128]{1,0:T(8,128)S(1)}, f32[8,128]{1,0:T(8,128)}, u32[]{:S(2)}) copy-start(f32[8,128]{1,0:T(8,128)} %get-tuple-element.22.rho_ref.refs_10_) | copy-start | bytes 12292
  128.2 13.4 %all-to-all-start.3 = ((f32[16,24,256]{2,1,0:T(8,128)}), f32[16,24,256]{2,1,0:T(8,128)S(1)}, u32[]{:S(2)}, u32[]{:S(2)}) async-start(f32[16,24,256]{2,1,0:T(8,128)} %bitcast.11), calls=%async_computation.3 | async-start | bytes 786432 | tf_op jit(solution)/shard_map/all_to_all | solution.py:81
  134.8 28.3 %collective-permute-start.13 = (s16[384,256]{1,0:T(8,128)(2,1)}, s16[384,256]{1,0:T(8,128)(2,1)S(1)}, u32[]{:S(2)}, u32[]{:S(2)}) collective-permute-start(s16[384,256]{1,0:T(8,128)(2,1)} %get-tuple-element.43), channel_id=1, source_target_pairs={{0,48},{1,13},{2,50},{3,15},{4,52},{5,1},{6,54},{7,3},{8,56},{9,5}... | collective-permute-start | bytes 589832 | tf_op jit(solution)/shard_map/ppermute | solution.py:63
  137.3 26.5 %collective-permute-start.14 = (s16[384,256]{1,0:T(8,128)(2,1)}, s16[384,256]{1,0:T(8,128)(2,1)S(1)}, u32[]{:S(2)}, u32[]{:S(2)}) collective-permute-start(s16[384,256]{1,0:T(8,128)(2,1)} %get-tuple-element.43), channel_id=1, source_target_pairs={{0,32},{1,9},{2,34},{3,11},{4,36},{5,13},{6,38},{7,15},{8,40},{9,1... | collective-permute-start | bytes 589832 | tf_op jit(solution)/shard_map/ppermute | solution.py:63
  137.8 26.6 %collective-permute-start.15 = (s16[384,256]{1,0:T(8,128)(2,1)}, s16[384,256]{1,0:T(8,128)(2,1)S(1)}, u32[]{:S(2)}, u32[]{:S(2)}) collective-permute-start(s16[384,256]{1,0:T(8,128)(2,1)} %get-tuple-element.43), channel_id=1, source_target_pairs={{0,16},{1,5},{2,18},{3,7},{4,20},{5,9},{6,22},{7,11},{8,24},{9,13}... | collective-permute-start | bytes 589832 | tf_op jit(solution)/shard_map/ppermute | solution.py:63
  142.4 35.1 %all-to-all-start.4 = ((f32[16,24,256]{2,1,0:T(8,128)}), f32[16,24,256]{2,1,0:T(8,128)}, u32[]{:S(2)}, u32[]{:S(2)}) async-start(f32[16,24,256]{2,1,0:T(8,128)} %broadcast_in_dim.14), calls=%async_computation.4 | async-start | bytes 786432 | tf_op jit(solution)/shard_map/all_to_all | solution.py:81
  165.2 19.7 %collective-permute-start.16 = (s16[1536,256]{1,0:T(8,128)(2,1)}, s16[1536,256]{1,0:T(8,128)(2,1)S(1)}, u32[]{:S(2)}, u32[]{:S(2)}) collective-permute-start(s16[1536,256]{1,0:T(8,128)(2,1)} %constant_dynamic-update-slice_fusion.4.refs_0_), channel_id=1, source_target_pairs={{0,12},{1,49},{2,14},{3,51},{4,0},{5,53},{6,2},{7,55},{8,4},{9,57}... | collective-permute-start | bytes 2359304 | tf_op jit(solution)/shard_map/ppermute | solution.py:63
  165.7 19.2 %collective-permute-start.17 = (s16[1536,256]{1,0:T(8,128)(2,1)}, s16[1536,256]{1,0:T(8,128)(2,1)S(1)}, u32[]{:S(2)}, u32[]{:S(2)}) collective-permute-start(s16[1536,256]{1,0:T(8,128)(2,1)} %constant_dynamic-update-slice_fusion.4.refs_0_), channel_id=1, source_target_pairs={{0,8},{1,33},{2,10},{3,35},{4,12},{5,37},{6,14},{7,39},{8,0},{9,41... | collective-permute-start | bytes 2359304 | tf_op jit(solution)/shard_map/ppermute | solution.py:63
  166.8 20.3 %collective-permute-start.18 = (s16[1536,256]{1,0:T(8,128)(2,1)}, s16[1536,256]{1,0:T(8,128)(2,1)}, u32[]{:S(2)}, u32[]{:S(2)}) collective-permute-start(s16[1536,256]{1,0:T(8,128)(2,1)} %constant_dynamic-update-slice_fusion.4.refs_0_), channel_id=1, source_target_pairs={{0,4},{1,17},{2,6},{3,19},{4,8},{5,21},{6,10},{7,23},{8,12},{9,25}... | collective-permute-start | bytes 2359304 | tf_op jit(solution)/shard_map/ppermute | solution.py:63
  180.6 16.4 %all-to-all-start.5 = ((f32[16,24,256]{2,1,0:T(8,128)}), f32[16,24,256]{2,1,0:T(8,128)}, u32[]{:S(2)}, u32[]{:S(2)}) async-start(f32[16,24,256]{2,1,0:T(8,128)} %broadcast_in_dim.15), calls=%async_computation.5 | async-start | bytes 786432 | tf_op jit(solution)/shard_map/all_to_all | solution.py:81
  187.1 1.1 copy-start.9
  197.0 1.0 copy-start.12

commit v4 on v3

--- a/solution.py
+++ b/solution.py
@@ -20,7 +20,6 @@
 BF16 = jnp.bfloat16
 AXES = ("z", "y", "x", "h", "c")
 PLANE = ("y", "x")
-COLUMN = ("z", "h", "c")
 
 
 def number(z, y, x, h, c):
@@ -71,12 +70,6 @@
     return [value] + [send(value, moves((4 - k) % 4)) for k in (1, 2, 3)]
 
 
-def gather_rows(own):
-    rows = jnp.concatenate(gather(own, depth_move), 0)
-    rows = jnp.concatenate(gather(rows, second_move), 0)
-    return gather(rows, first_move)
-
-
 def exchange(value, axes):
     return lax.all_to_all(value, axes, 0, 0, tiled=True)
 
@@ -151,13 +144,8 @@
         return a
 
     lax.fori_loop(0, 5, coarse, jnp.float32(a))
-
-    def fine(_, carry):
-        x = x_ref[...]
-        x_ref[...] = dot6(x, 2.0 * ident - dot6(mat_ref[...], x))
-        return carry
-
-    lax.fori_loop(0, 2, fine, 0)
+    x = x_ref[...]
+    x_ref[...] = dot6(x, 2.0 * ident - dot6(mat_ref[...], x))
     return rho
 
 
@@ -181,6 +169,15 @@
 
 def from_codes(a):
     return a.astype(jnp.int32).astype(F32)
+
+
+def placed():
+    z, y, x, _, core = [lax.axis_index(a) for a in AXES]
+    flat = core == 0
+    return (
+        jnp.where(flat, x, y), jnp.where(flat, y, x), z, core,
+        jnp.where(flat, 1, 4), jnp.where(flat, 4, 1),
+    )
 
 
 def block_row(place, k, b):
@@ -188,16 +185,38 @@
     first = lax.rem(place[0] + k, 4)
     second = lax.rem(place[1] + j, 4)
     depth = lax.rem(place[2] + i, 4)
-    block = depth * 16 + first * place[5] + second * place[6]
+    block = depth * 16 + first * place[4] + second * place[5]
     return pl.multiple_of(block * SHARE, 8)
 
 
-def inverse_kernel(place, patient, month, near, rho_ref, weights, mat, square):
+def coded_rows(blocks):
+    return -(-blocks * (SHARE + 1) // 16) * 16
+
+
+def encode_blocks(source, first, blocks, coded, out):
+    coded[blocks * SHARE :, :] = jnp.zeros((coded.shape[0] - blocks * SHARE, R), F32)
+    for b in range(blocks):
+        whole, code = encode(source[(first + b) * SHARE : (first + b + 1) * SHARE, :])
+        coded[b * SHARE : (b + 1) * SHARE, :] = whole
+        coded[blocks * SHARE + b : blocks * SHARE + b + 1, :] = code
+    out[...] = to_codes(coded[...])
+
+
+def add_blocks(acc, blocks, part, r):
+    part[...] = from_codes(r[...])
+    for b in range(blocks):
+        acc[b * SHARE : (b + 1) * SHARE, :] += decode(
+            part[b * SHARE : (b + 1) * SHARE, :],
+            part[blocks * SHARE + b : blocks * SHARE + b + 1, :],
+        )
+
+
+def inverse_kernel(patient, month, near, rho_ref, weights, mat, square):
     month_gram = gram_of(month[...], lax.Precision.HIGHEST)
     gram = gram_of(patient[...])
     rho = shifted_inverse(gram * month_gram, mat, near)
     rho_ref[...] = jnp.broadcast_to(rho, rho_ref.shape)
-    core = place[4]
+    core = placed()[3]
     mat[...] = near[...]
 
     @pl.when(core == 1)
@@ -212,7 +231,7 @@
 
 
 def local_kernel(
-    place, near, rho_ref, patient_hbm, month_hbm, tiles_hbm, duals_hbm,
+    live, patient_at, code_at, month_at, near, rho_ref, patient_hbm, month_hbm, tiles_hbm, duals_hbm,
     prod_hbm, v_hbm, a0, q1, q2, q3,
     patient, month, tiles, duals, prod, grad, u_part, g_part, v, own, coded, held, sems, outs,
 ):
@@ -227,21 +246,24 @@
     for copy in copies:
         copy.start()
     rho = rho_ref[0:1, 0:1]
+    place = placed()
     grad[...] = jnp.zeros_like(grad)
     for copy in copies[:3]:
         copy.wait()
 
-    def visit(k, _):
-        pat = patient[pl.ds(pl.multiple_of(place[8 + k] * BLOCK, BLOCK), BLOCK), :]
-        product = lax.dot_general(
-            tiles[k], pat, (((0,), (0,)), ((), ())), preferred_element_type=F32
-        )
-        prod[k] = product
-        at = pl.ds(pl.multiple_of(place[8 + CAP + k] * BLOCK, BLOCK), BLOCK)
-        grad[at, :] += product * month[pl.ds(place[8 + 2 * CAP + k], 1), :]
+    def visit(turn, _):
+        for k in [turn * 4 + n for n in range(4)]:
+            pat = patient[pl.ds(pl.multiple_of(patient_at[k] * BLOCK, BLOCK), BLOCK), :]
+            prod[k] = lax.dot_general(
+                tiles[k], pat, (((0,), (0,)), ((), ())), preferred_element_type=F32
+            )
+        for k in [turn * 4 + n for n in range(4)]:
+            scale = jnp.where(k < live[0], month[pl.ds(month_at[k], 1), :], 0.0)
+            at = pl.ds(pl.multiple_of(code_at[k] * BLOCK, BLOCK), BLOCK)
+            grad[at, :] += prod[k] * scale
         return 0
 
-    lax.fori_loop(0, place[7], visit, 0)
+    lax.fori_loop(0, (live[0] + 3) // 4, visit, 0)
     prod_out = pltpu.make_async_copy(prod, prod_hbm, outs.at[4])
     prod_out.start()
     near_parts = split(near[...])
@@ -294,24 +316,26 @@
     v_out.wait()
 
 
-def sum_kernel(a0, r1, r2, r3, s0, s1, s2, s3, acc, part):
-    acc[...] = a0[...]
+def sum_kernel(own, r1, r2, r3, s0, q1, q2, q3, acc, part, coded):
+    blocks = own.shape[0] // SHARE
+    few = blocks // 4
+    acc[...] = own[...]
     for r in (r1, r2, r3):
-        part[...] = from_codes(r[...])
-        for b in range(32):
-            acc[b * SHARE : (b + 1) * SHARE, :] += decode(
-                part[b * SHARE : (b + 1) * SHARE, :], part[1280 + b : 1281 + b, :]
-            )
-    for j, out in enumerate((s0, s1, s2, s3)):
-        out[...] = acc[j * 320 : j * 320 + 320, :]
+        add_blocks(acc, blocks, part, r)
+    s0[...] = acc[0 : few * SHARE, :]
+    for j, out in enumerate((q1, q2, q3)):
+        encode_blocks(acc, (j + 1) * few, few, coded, out)
 
 
 def owner_kernel(
-    place, s0, s1, s2, s3, z0_ref, mine, other, month,
-    both_ref, two_ref, z2_ref, code_ref, gram_ref, own, oth, both, two,
+    s0, s1, s2, s3, z0_ref, mine, other, month,
+    codes_ref, z2_ref, code_ref, gram_ref, own, oth, coded, acc, part,
 ):
-    summed = (s0[...] + s1[...]) + (s2[...] + s3[...])
-    core = place[4]
+    acc[...] = s0[...]
+    for r in (s1, s2, s3):
+        add_blocks(acc, 2, part, r)
+    summed = acc[...]
+    core = placed()[3]
     half = pl.multiple_of(core * 128, 128)
     rest = pl.multiple_of(128 - core * 128, 128)
     for p in range(16):
@@ -331,18 +355,17 @@
     z1 = jnp.maximum(first / rho_total, 0.0)
     second = summed[SHARE:] + dot6(z0, plain - square) + 2.0 * dot6(z1, plain) - rho_total * z1
     z2 = jnp.maximum(second / rho_total, 0.0)
-    both[...] = jnp.zeros_like(both)
-    two[...] = jnp.zeros_like(two)
-    both[0:SHARE, :], both[80:81, :] = encode(z0)
-    both[SHARE:80, :], both[81:82, :] = encode(z1)
-    two[0:SHARE, :], two[SHARE : SHARE + 1, :] = encode(z2)
-    both_ref[...] = to_codes(both[...])
-    two_ref[...] = to_codes(two[...])
+    coded[...] = jnp.zeros_like(coded)
+    coded[0:40, :], coded[40:41, :] = encode(z2)
+    coded[48:88, :], coded[41:42, :] = encode(z0)
+    coded[88:128, :], coded[42:43, :] = encode(z1)
+    codes_ref[...] = to_codes(coded[...])
     z2_ref[...] = z2
     code_ref[...] = gram_of(z2, lax.Precision.HIGHEST)
 
 
-def month_kernel(place, w0, w1, w2, w3, prod, code, out, natural, part):
+def month_kernel(live, code_at, month_at, w0, w1, w2, w3, prod, code, out, natural, part):
+    place = placed()
     for k, w in enumerate((w0, w1, w2, w3)):
         part[...] = from_codes(w[...])
         for b in range(16):
@@ -354,16 +377,17 @@
         out[p * 24 + 8 : p * 24 + 24, :] = code[p * 16 : p * 16 + 16, :]
 
     def visit(k, _):
-        at = pl.ds(pl.multiple_of(place[8 + CAP + k] * BLOCK, BLOCK), BLOCK)
+        at = pl.ds(pl.multiple_of(code_at[k] * BLOCK, BLOCK), BLOCK)
         column = jnp.sum(prod[k] * natural[at, :], axis=0, keepdims=True)
-        m = place[8 + 2 * CAP + k]
+        m = month_at[k]
         out[pl.ds((m // 8) * 24 + m % 8, 1), :] += column
         return 0
 
-    lax.fori_loop(0, place[7], visit, 0)
-
-
-def duals_kernel(place, *refs):
+    lax.fori_loop(0, live[0], visit, 0)
+
+
+def duals_kernel(*refs):
+    place = placed()
     both, two = refs[0:4], refs[4:8]
     v, near, _, out, part, z0_part, z1_part, z2_part = refs[8:]
     near_parts = split(near[...])
@@ -373,16 +397,16 @@
 
             @pl.when(k == n)
             def _(n=n):
-                part[0:1536, :] = from_codes(both[n][...])
-                part[1536:, :] = from_codes(two[n][...])
+                part[0:1280, :] = from_codes(both[n][...])
+                part[1280:, :] = from_codes(two[n][...])
 
         for b in range(16):
             rows = slice(b * SHARE, (b + 1) * SHARE)
-            at = b * 96
-            z0_part[rows, :] = decode(part[at : at + 40, :], part[at + 80 : at + 81, :])
-            z1_part[rows, :] = decode(part[at + 40 : at + 80, :], part[at + 81 : at + 82, :])
-            at = 1536 + b * 48
-            z2_part[rows, :] = decode(part[at : at + 40, :], part[at + 40 : at + 41, :])
+            at = b * 80
+            to = 1280 + b * 48
+            z0_part[rows, :] = decode(part[at : at + 40, :], part[to + 41 : to + 42, :])
+            z1_part[rows, :] = decode(part[at + 40 : at + 80, :], part[to + 42 : to + 43, :])
+            z2_part[rows, :] = decode(part[to : to + 40, :], part[to + 40 : to + 41, :])
         z0 = z0_part[...]
         z1 = z1_part[...]
         inner = z0 - dot3(split(z0), near_parts) + 2.0 * z1
@@ -422,62 +446,65 @@
     tile_values, patient_block, code_block, month_index, live_count,
     patient_factor, month_factor, consensus, scaled_duals,
 ):
-    z, y, x, h, core = [lax.axis_index(a) for a in AXES]
-    flat = core == 0
-    place = jnp.stack(
-        [jnp.where(flat, x, y), jnp.where(flat, y, x), z, h, core,
-         jnp.where(flat, 1, 4), jnp.where(flat, 4, 1), live_count[0]]
-    ).astype(jnp.int32)
-    place = jnp.concatenate([place, patient_block, code_block, month_index])
-
     near, rho, weights = call(
-        inverse_kernel, [(R, R), (8, 128), (384, R)], "svv" + "vvv", [(R, R), (R, R)],
-        place, patient_factor, month_factor, limit=None,
+        inverse_kernel, [(R, R), (8, 128), (384, R)], "vv" + "vvv", [(R, R), (R, R)],
+        patient_factor, month_factor, limit=None,
     )
     m = sum_slices(weights, PLANE)
-    codes = [jax.ShapeDtypeStruct((1312, R), jnp.int16)] * 3
-    prod, v, *parts = call(
+
+    def codes(rows):
+        return jax.ShapeDtypeStruct((rows, R), jnp.int16)
+
+    tops = [coded_rows(n) for n in (32, 8, 2)]
+    prod, v, *s = call(
         local_kernel,
-        [(CAP, BLOCK, R), (4, CHUNK, R), (2 * CHUNK, R)] + codes,
-        "svvhhhh" + "hhhhhh",
+        [(CAP, BLOCK, R), (4, CHUNK, R), (2 * CHUNK, R)] + [codes(tops[0])] * 3,
+        "ssssvvhhhh" + "hhhhhh",
         [
             pltpu.VMEM((1024, R), BF16), (MONTHS, R), pltpu.VMEM((CAP, BLOCK, BLOCK), BF16),
             (ROWS, R), (CAP, BLOCK, R), (ROWS, R), (CHUNK, R), (CHUNK, R), (4, CHUNK, R),
-            (2 * CHUNK, R), (1312, R), pltpu.VMEM((3, 1312, R), jnp.int16),
+            (2 * CHUNK, R), (tops[0], R), pltpu.VMEM((3, tops[0], R), jnp.int16),
             pltpu.SemaphoreType.DMA((4,)), pltpu.SemaphoreType.DMA((6,)),
         ],
-        place, near, rho, patient_factor, month_factor, tile_values, scaled_duals, limit=None,
-    )
-    s = scatter_sum(parts, first_move)
+        live_count, patient_block, code_block, month_index,
+        near, rho, patient_factor, month_factor, tile_values, scaled_duals, limit=None,
+    )
+    s = scatter_sum(s, first_move)
     m = sum_to_all(m, 4, "z")
     mine = spread_slices(m, PLANE)
     other = send(mine, CORE_MOVE)
-    s = call(sum_kernel, [(320, R)] * 4, "vvvv" + "vvvv", [(2 * CHUNK, R), (1312, R)], *s)
+    s = call(
+        sum_kernel, [(320, R)] + [codes(tops[1])] * 3, "vvvv" + "vvvv",
+        [(2 * CHUNK, R), (tops[0], R), (tops[1], R)], *s,
+    )
     s = scatter_sum(s, second_move)
-    s = [
-        (s[0][i : i + 80] + s[1][i : i + 80]) + (s[2][i : i + 80] + s[3][i : i + 80])
-        for i in (0, 80, 160, 240)
-    ]
+    s = call(
+        sum_kernel, [(80, R)] + [codes(tops[2])] * 3, "vvvv" + "vvvv",
+        [(320, R), (tops[1], R), (tops[2], R)], *s,
+    )
     s = scatter_sum(s, depth_move)
-    both, two, z2, code_gram, gram = call(
-        owner_kernel,
-        [jax.ShapeDtypeStruct((96, R), jnp.int16), jax.ShapeDtypeStruct((48, R), jnp.int16),
-         (SHARE, R), (R, R), (R, R)],
-        "svvvvvvvv" + "vvvvv", [(R, R), (R, R), (96, R), (48, R)],
-        place, *s, consensus, mine, other, month_factor,
-    )
-    two = gather_rows(two)
-    both = gather_rows(both)
+    rows, z2, code_gram, gram = call(
+        owner_kernel, [codes(128), (SHARE, R), (R, R), (R, R)], "vvvvvvvv" + "vvvv",
+        [(R, R), (R, R), (128, R), (80, R), (tops[2], R)],
+        *s, consensus, mine, other, month_factor,
+    )
+    rows = jnp.concatenate(gather(rows, depth_move), 0)
+    rows = [r.reshape(4, 128, R) for r in gather(rows, second_move)]
+    two = jnp.concatenate([r[:, :48].reshape(192, R) for r in rows], 0)
+    both = jnp.concatenate([r[:, 48:].reshape(320, R) for r in rows], 0)
+    two = gather(two, first_move)
+    both = gather(both, first_move)
     (sums,) = call(
-        month_kernel, [(384, R)], "svvvvvv" + "v", [(ROWS, R), (768, R)],
-        place, *two, prod, code_gram,
+        month_kernel, [(384, R)], "sssvvvvvv" + "v", [(ROWS, R), (768, R)],
+        live_count, code_block, month_index, *two, prod, code_gram,
     )
     t = sum_slices(sums, PLANE)
-    t = sum_to_all(t, 16, COLUMN)
+    t = t + send(t, CORE_MOVE)
+    t = sum_to_all(t, 8, ("z", "h"))
     t = spread_slices(t, PLANE)
     (duals,) = call(
-        duals_kernel, [(ROWS, R)], "s" + "v" * 12, [(2304, R)] + [(CHUNK, R)] * 3,
-        place, *both, *two, v, near, rho,
+        duals_kernel, [(ROWS, R)], "v" * 12, [(2048, R)] + [(CHUNK, R)] * 3,
+        *both, *two, v, near, rho,
     )
     (new_months,) = call(
         tail_kernel, [(MONTHS, R)], "vvvv", [(R, R), (R, R), (BLOCK, R)], t, gram, month_factor

time: 209 us -> 197 us (0.943); the launches traced: 206 us -> 196 us
  starting transfers between devices: 70.9 us -> 53 us
  blocking collectives: 29.9 us -> 47.6 us
  local copies, waits for them, and re-layouts: 15.1 us -> 7.44 us
  waiting for transfers between devices: 41.1 us -> 48.5 us
  Pallas kernels: 42.2 us -> 37.2 us
  other arithmetic: 4.99 us -> 1.15 us
    ppermute x28 -> x23, waiting for transfers between devices: 26.3 us -> 44.1 us  [send(): return lax.ppermute(value, AXES, pairs)]
    all_to_all x2 -> x3, blocking collectives: 29.9 us -> 47.6 us  [exchange(): return lax.all_to_all(value, axes, 0, 0, tiled=True)]
    all_to_all x4 -> x3, starting transfers between devices: 33.6 us -> 19.7 us  [exchange(): return lax.all_to_all(value, axes, 0, 0, tiled=True)]
    all_to_all x4 -> x3, waiting for transfers between devices: 14.8 us -> 4.36 us  [exchange(): return lax.all_to_all(value, axes, 0, 0, tiled=True)]
    unnamed x44 -> x23, local copies, waits for them, and re-layouts: 8.53 us -> 2.04 us
    pallas_call x7 -> x8, Pallas kernels: 42.2 us -> 37.2 us  [call(): pl.pallas_call(body, out_shape=[s if isinstance(s, jax.ShapeDtypeStruct)...]
    ppermute x28 -> x23, starting transfers between devices: 37.3 us -> 33.4 us  [send(): return lax.ppermute(value, AXES, pairs)]
    concatenate x5 -> x1, local copies, waits for them, and re-layouts: 3.52 us -> 0.01 us  [compute(): rows = jnp.concatenate(gather(rows, depth_move), 0)]
  transfers between devices with their start and end apart: 32 -> 26, of which waited for: 15 -> 15; matrix products, arithmetic and copies ran while one was open for 7% -> 3% of each run, Pallas kernels for 6% -> 11%
where the time goes in v4:
time: 197 us; the launch traced here: 196 us
  starting transfers between devices  53 us (27%)
  waiting for transfers between devices  48.5 us (25%)
  blocking collectives  47.6 us (24%)
  Pallas kernels  37.2 us (19%)
  local copies, waits for them, and re-layouts  7.44 us (4%)
    all_to_all x3, blocking collectives, exchange(): return lax.all_to_all(value, axes, 0, 0, tiled=True)  47.6 us
    ppermute x23, waiting for transfers between devices, send(): return lax.ppermute(value, AXES, pairs)  44.1 us
    pallas_call x8, Pallas kernels, call(): pl.pallas_call(body, out_shape=[s if isinstance(s, jax.ShapeDtypeStruct)...  37.2 us
    ppermute x23, starting transfers between devices, send(): return lax.ppermute(value, AXES, pairs)  33.4 us
    all_to_all x3, starting transfers between devices, exchange(): return lax.all_to_all(value, axes, 0, 0, tiled=True)  19.7 us
    all_to_all x3, waiting for transfers between devices, exchange(): return lax.all_to_all(value, axes, 0, 0, tiled=True)  4.36 us
  transfers between devices with their start and end apart: 26, of which 15 were waited for; matrix products, arithmetic and copies ran while one was open for 3% of the time, Pallas kernels for 11%

profile of v4, /device:TPU:1, one launch (start us, length us, event | category | flops | bytes accessed | tf_op | source)
XLA Modules:
  0.0 196.3 jit_solution(7402508873505340702)
XLA Ops:
  0.6 7.5 %shard_map.112 = (f32[256,256]{1,0:T(8,128)}, f32[8,128]{1,0:T(8,128)}, f32[384,256]{1,0:T(8,128)}) custom-call(bf16[1024,256]{1,0:T(8,128)(2,1)} %patient_hbm.1, f32[120,256]{1,0:T(8,128)} %month.5), custom_call_target="tpu_custom_call" | custom-call | tf_op jit(solution)/shard_map/pallas_call | solution.py:435
  8.2 17.1 %all_to_all.30 = f32[16,24,256]{2,1,0:T(8,128)S(1)} all-to-all(f32[16,24,256]{2,1,0:T(8,128)} %bitcast.26), channel_id=1, replica_groups=mesh['z'=4,'y'=4,'x'=4,'h'=2,'c'=2] {'y','x'}, dimensions={0} | all-to-all | bytes 786432 | tf_op jit(solution)/shard_map/all_to_all | solution.py:74
  25.3 0.6 broadcast_in_dim.12
  25.9 5.6 %all-to-all-start.1 = ((f32[4,24,256]{2,1,0:T(8,128)}), f32[4,24,256]{2,1,0:T(8,128)S(1)}, u32[]{:S(2)}, u32[]{:S(2)}) async-start(f32[4,24,256]{2,1,0:T(8,128)} %broadcast_in_dim.12), calls=%async_computation.1 | async-start | bytes 196608 | tf_op jit(solution)/shard_map/all_to_all | solution.py:74
  32.2 10.9 %shard_map.113 = (f32[20,128,256]{2,1,0:T(8,128)}, f32[4,640,256]{2,1,0:T(8,128)}, f32[1280,256]{1,0:T(8,128)}, s16[1312,256]{1,0:T(8,128)(2,1)}, s16[1312,256]{1,0:T(8,128)(2,1)}, /*index=5*/s16[1312,256]{1,0:T(8,128)(2,1)}) custom-call(s32[1]{0:T(128)S(6)} %copy.15.live, s32[20]{0:T(128)} %patient_at.1, s32[20]{0:T(128)} %code_at.3, s32[20]{0:T(128)} %month_at.3, ...), custom_call_target="tpu_custom_call" | custom-call | tf_op jit(solution)/shard_map/pallas_call | solution.py:435
  43.1 0.1 collective-permute-start
  43.2 1.8 collective-permute-start.1
  45.0 0.8 collective-permute-start.2
  45.8 0.0 all-to-all-done.1
  45.9 0.0 copy-start.1
  45.9 0.0 copy-start.4
  45.9 19.6 %all_to_all.31 = f32[16,24,256]{2,1,0:T(8,128)S(1)} all-to-all(f32[16,24,256]{2,1,0:T(8,128)S(1)} %broadcast_in_dim.13), channel_id=1, replica_groups=mesh['z'=4,'y'=4,'x'=4,'h'=2,'c'=2] {'y','x'}, dimensions={0} | all-to-all | bytes 786432 | tf_op jit(solution)/shard_map/all_to_all | solution.py:74
  65.5 3.7 %collective-permute-start.9 = (f32[384,256]{1,0:T(8,128)S(1)}, f32[384,256]{1,0:T(8,128)S(1)}, u32[]{:S(2)}, u32[]{:S(2)}) collective-permute-start(f32[384,256]{1,0:T(8,128)S(1)} %bitcast.18), channel_id=1, source_target_pairs={{0,1},{1,0},{2,3},{3,2},{4,5},{5,4},{6,7},{7,6},{8,9},{9,8},{10,11... | collective-permute-start | bytes 1179656 | tf_op jit(solution)/shard_map/ppermute | solution.py:62
  69.2 0.0 collective-permute-done.1.r2
  69.2 0.0 collective-permute-done.2.r3
  69.2 1.3 copy-done.2
  70.5 1.1 shard_map.114
  71.6 0.0 copy-start
  71.7 0.0 copy-start.6
  71.7 0.0 copy-start.7
  71.7 0.9 collective-permute-start.3
  72.6 3.0 %collective-permute-start.4 = (s16[336,256]{1,0:T(8,128)(2,1)S(1)}, s16[336,256]{1,0:T(8,128)(2,1)S(1)}, u32[]{:S(2)}, u32[]{:S(2)}) collective-permute-start(s16[336,256]{1,0:T(8,128)(2,1)S(1)} %get-tuple-element.32), channel_id=1, source_target_pairs={{0,32},{1,9},{2,34},{3,11},{4,36},{5,13},{6,38},{7,15},{8,40},{9,1... | collective-permute-start | bytes 516104 | tf_op jit(solution)/shard_map/ppermute | solution.py:62
  75.6 1.9 collective-permute-done.3.r1
  77.5 2.9 %collective-permute-done.4.r2 = s16[336,256]{1,0:T(8,128)(2,1)S(1)} collective-permute-done((s16[336,256]{1,0:T(8,128)(2,1)S(1)}, s16[336,256]{1,0:T(8,128)(2,1)S(1)}, u32[]{:S(2)}, u32[]{:S(2)}) %collective-permute-start.4) | collective-permute-done | bytes 172064 | tf_op jit(solution)/shard_map/ppermute | solution.py:62
  80.5 0.3 shard_map.115
  80.8 1.8 collective-permute-start.6
  82.6 2.1 %collective-permute-start.7 = (s16[96,256]{1,0:T(8,128)(2,1)S(1)}, s16[96,256]{1,0:T(8,128)(2,1)S(1)}, u32[]{:S(2)}, u32[]{:S(2)}) collective-permute-start(s16[96,256]{1,0:T(8,128)(2,1)S(1)} %get-tuple-element.36), channel_id=1, source_target_pairs={{0,128},{1,129},{2,130},{3,131},{4,132},{5,133},{6,134},{7,135},{8... | collective-permute-start | bytes 147464 | tf_op jit(solution)/shard_map/ppermute | solution.py:62
  84.7 1.2 collective-permute-start.8
  85.9 2.0 %collective-permute-done.7.s2 = s16[96,256]{1,0:T(8,128)(2,1)S(1)} collective-permute-done((s16[96,256]{1,0:T(8,128)(2,1)S(1)}, s16[96,256]{1,0:T(8,128)(2,1)S(1)}, u32[]{:S(2)}, u32[]{:S(2)}) %collective-permute-start.7) | collective-permute-done | bytes 49184 | tf_op jit(solution)/shard_map/ppermute | solution.py:62
  87.9 0.5 collective-permute-done.8.s3
  88.4 1.4 shard_map.116
  89.8 2.6 %collective-permute-start.10 = (s16[128,256]{1,0:T(8,128)(2,1)S(1)}, s16[128,256]{1,0:T(8,128)(2,1)S(1)}, u32[]{:S(2)}, u32[]{:S(2)}) collective-permute-start(s16[128,256]{1,0:T(8,128)(2,1)S(1)} %get-tuple-element.40), channel_id=1, source_target_pairs={{0,192},{1,193},{2,194},{3,195},{4,196},{5,197},{6,198},{7,199},{8... | collective-permute-start | bytes 196616 | tf_op jit(solution)/shard_map/ppermute | solution.py:62
  92.4 0.3 collective-permute-start.12
  92.7 1.0 collective-permute-done.10
  93.7 2.7 %collective-permute-done.11 = s16[128,256]{1,0:T(8,128)(2,1)S(1)} collective-permute-done((s16[128,256]{1,0:T(8,128)(2,1)S(1)}, s16[128,256]{1,0:T(8,128)(2,1)S(1)}, u32[]{:S(2)}, u32[]{:S(2)}) %collective-permute-start.11) | collective-permute-done | bytes 65568 | tf_op jit(solution)/shard_map/ppermute | solution.py:62
  96.5 1.5 collective-permute-done.12
  98.0 1.6 collective-permute-start.13
  99.6 0.7 collective-permute-start.15
  100.3 5.4 %collective-permute-done.13 = s16[512,256]{1,0:T(8,128)(2,1)S(1)} collective-permute-done((s16[512,256]{1,0:T(8,128)(2,1)S(1)}, s16[512,256]{1,0:T(8,128)(2,1)S(1)}, u32[]{:S(2)}, u32[]{:S(2)}) %collective-permute-start.13) | collective-permute-done | bytes 262176 | tf_op jit(solution)/shard_map/ppermute | solution.py:62
  105.7 0.7 collective-permute-done.14
  106.4 2.7 %collective-permute-done.15 = s16[512,256]{1,0:T(8,128)(2,1)S(1)} collective-permute-done((s16[512,256]{1,0:T(8,128)(2,1)S(1)}, s16[512,256]{1,0:T(8,128)(2,1)S(1)}, u32[]{:S(2)}, u32[]{:S(2)}) %collective-permute-start.15) | collective-permute-done | bytes 262176 | tf_op jit(solution)/shard_map/ppermute | solution.py:62
  109.2 0.7 copy-done.9
  109.9 2.0 collective-permute-start.19
  111.8 0.6 collective-permute-start.21
  112.4 8.3 %collective-permute-done.19.refs_5_.w1 = s16[768,256]{1,0:T(8,128)(2,1)S(1)} collective-permute-done((s16[768,256]{1,0:T(8,128)(2,1)S(1)}, s16[768,256]{1,0:T(8,128)(2,1)S(1)}, u32[]{:S(2)}, u32[]{:S(2)}) %collective-permute-start.19) | collective-permute-done | bytes 393248 | tf_op jit(solution)/shard_map/ppermute | solution.py:62
  120.7 3.4 %collective-permute-done.21.refs_7_.w3 = s16[768,256]{1,0:T(8,128)(2,1)S(1)} collective-permute-done((s16[768,256]{1,0:T(8,128)(2,1)S(1)}, s16[768,256]{1,0:T(8,128)(2,1)S(1)}, u32[]{:S(2)}, u32[]{:S(2)}) %collective-permute-start.21) | collective-permute-done | bytes 393248 | tf_op jit(solution)/shard_map/ppermute | solution.py:62
  124.2 1.2 shard_map.118
  125.4 10.8 %all_to_all.32 = f32[16,24,256]{2,1,0:T(8,128)S(1)} all-to-all(f32[16,24,256]{2,1,0:T(8,128)S(1)} %bitcast.17), channel_id=1, replica_groups=mesh['z'=4,'y'=4,'x'=4,'h'=2,'c'=2] {'y','x'}, dimensions={0} | all-to-all | bytes 786432 | tf_op jit(solution)/shard_map/all_to_all | solution.py:74
  136.3 8.7 %collective-permute-start.22 = (f32[24,256]{1,0:T(8,128)S(1)}, f32[24,256]{1,0:T(8,128)S(1)}, u32[]{:S(2)}, u32[]{:S(2)}) collective-permute-start(f32[24,256]{1,0:T(8,128)S(1)} %reduce_sum.38), channel_id=1, source_target_pairs={{0,1},{1,0},{2,3},{3,2},{4,5},{5,4},{6,7},{7,6},{8,9},{9,8},{10,11... | collective-permute-start | bytes 73736 | tf_op jit(solution)/shard_map/ppermute | solution.py:62
  145.0 1.6 slice.34
  146.6 1.6 slice.35
  148.2 0.7 broadcast_in_dim.14
  148.9 10.3 %all-to-all-start.4 = ((f32[8,24,256]{2,1,0:T(8,128)}), f32[8,24,256]{2,1,0:T(8,128)S(1)}, u32[]{:S(2)}, u32[]{:S(2)}) async-start(f32[8,24,256]{2,1,0:T(8,128)} %broadcast_in_dim.14), calls=%async_computation.4 | async-start | bytes 393216 | tf_op jit(solution)/shard_map/all_to_all | solution.py:74
  159.2 1.0 pad_add_fusion.refs_0_
  160.2 0.6 collective-permute-start.16
  160.8 0.7 collective-permute-start.17
  161.6 0.2 collective-permute-start.18
  161.8 4.4 %all-to-all-done.4 = f32[8,24,256]{2,1,0:T(8,128)S(1)} async-done(((f32[8,24,256]{2,1,0:T(8,128)}), f32[8,24,256]{2,1,0:T(8,128)S(1)}, u32[]{:S(2)}, u32[]{:S(2)}) %all-to-all-start.4) | async-done | bytes 196640 | tf_op jit(solution)/shard_map/all_to_all | solution.py:74
  166.1 0.8 broadcast_in_dim.15
  166.9 3.8 %all-to-all-start.5 = ((f32[16,24,256]{2,1,0:T(8,128)}), f32[16,24,256]{2,1,0:T(8,128)S(1)}, u32[]{:S(2)}, u32[]{:S(2)}) async-start(f32[16,24,256]{2,1,0:T(8,128)} %broadcast_in_dim.15), calls=%async_computation.5 | async-start | bytes 786432 | tf_op jit(solution)/shard_map/all_to_all | solution.py:74
  170.7 1.5 collective-permute-done.17.refs_2_
  172.2 9.3 %collective-permute-done.18.refs_3_ = s16[1280,256]{1,0:T(8,128)(2,1)} collective-permute-done((s16[1280,256]{1,0:T(8,128)(2,1)S(1)}, s16[1280,256]{1,0:T(8,128)(2,1)}, u32[]{:S(2)}, u32[]{:S(2)}) %collective-permute-start.18) | collective-permute-done | bytes 655392 | tf_op jit(solution)/shard_map/ppermute | solution.py:62
  181.6 9.1 %shard_map.117 = f32[2560,256]{1,0:T(8,128)} custom-call(s16[1280,256]{1,0:T(8,128)(2,1)S(1)} %pad_add_fusion.refs_0_, s16[1280,256]{1,0:T(8,128)(2,1)} %collective-permute-done.16.refs_1_, s16[1280,256]{1,0:T(8,128)(2,1)} %collective-permute-done.17.refs_2_, s16[1280,256]{1,0:T(8,128)(2,1)} %collective-permute-done.18.refs_3_, ...), custom_call_target="tpu_custom_call" | custom-call | tf_op jit(solution)/shard_map/pallas_call | solution.py:435
  190.6 5.7 %shard_map.119 = f32[120,256]{1,0:T(8,128)} custom-call(f32[384,256]{1,0:T(8,128)S(1)} %bitcast.16, f32[256,256]{1,0:T(8,128)S(1)} %get-tuple-element.44.gram, f32[120,256]{1,0:T(8,128)S(1)} %copy-done.1), custom_call_target="tpu_custom_call" | custom-call | tf_op jit(solution)/shard_map/pallas_call | solution.py:435
  (42 shorter events, 0.3 us)
Async XLA Ops:
  25.9 19.9 %all-to-all-start.1 = ((f32[4,24,256]{2,1,0:T(8,128)}), f32[4,24,256]{2,1,0:T(8,128)S(1)}, u32[]{:S(2)}, u32[]{:S(2)}) async-start(f32[4,24,256]{2,1,0:T(8,128)} %broadcast_in_dim.12), calls=%async_computation.1 | async-start | bytes 196608 | tf_op jit(solution)/shard_map/all_to_all | solution.py:74
  43.1 26.1 %collective-permute-start = (s16[1312,256]{1,0:T(8,128)(2,1)}, s16[1312,256]{1,0:T(8,128)(2,1)S(1)}, u32[]{:S(2)}, u32[]{:S(2)}) collective-permute-start(s16[1312,256]{1,0:T(8,128)(2,1)} %get-tuple-element.27), channel_id=1, source_target_pairs={{0,4},{1,17},{2,6},{3,19},{4,8},{5,21},{6,10},{7,23},{8,12},{9,25}... | collective-permute-start | bytes 2015240 | tf_op jit(solution)/shard_map/ppermute | solution.py:62
  43.2 26.0 %collective-permute-start.1 = (s16[1312,256]{1,0:T(8,128)(2,1)}, s16[1312,256]{1,0:T(8,128)(2,1)S(1)}, u32[]{:S(2)}, u32[]{:S(2)}) collective-permute-start(s16[1312,256]{1,0:T(8,128)(2,1)} %get-tuple-element.28), channel_id=1, source_target_pairs={{0,8},{1,33},{2,10},{3,35},{4,12},{5,37},{6,14},{7,39},{8,0},{9,41... | collective-permute-start | bytes 2015240 | tf_op jit(solution)/shard_map/ppermute | solution.py:62
  45.0 24.2 %collective-permute-start.2 = (s16[1312,256]{1,0:T(8,128)(2,1)}, s16[1312,256]{1,0:T(8,128)(2,1)S(1)}, u32[]{:S(2)}, u32[]{:S(2)}) collective-permute-start(s16[1312,256]{1,0:T(8,128)(2,1)} %get-tuple-element.29), channel_id=1, source_target_pairs={{0,12},{1,49},{2,14},{3,51},{4,0},{5,53},{6,2},{7,55},{8,4},{9,57}... | collective-permute-start | bytes 2015240 | tf_op jit(solution)/shard_map/ppermute | solution.py:62
  45.9 42.6 %copy-start.1 = (f32[120,256]{1,0:T(8,128)S(1)}, f32[120,256]{1,0:T(8,128)}, u32[]{:S(2)}) copy-start(f32[120,256]{1,0:T(8,128)} %month.5) | copy-start | bytes 368644
  45.9 42.6 %copy-start.4 = (f32[40,256]{1,0:T(8,128)S(1)}, f32[40,256]{1,0:T(8,128)}, u32[]{:S(2)}) copy-start(f32[40,256]{1,0:T(8,128)} %z0_ref.1) | copy-start | bytes 122884
  65.5 22.9 %collective-permute-start.9 = (f32[384,256]{1,0:T(8,128)S(1)}, f32[384,256]{1,0:T(8,128)S(1)}, u32[]{:S(2)}, u32[]{:S(2)}) collective-permute-start(f32[384,256]{1,0:T(8,128)S(1)} %bitcast.18), channel_id=1, source_target_pairs={{0,1},{1,0},{2,3},{3,2},{4,5},{5,4},{6,7},{7,6},{8,9},{9,8},{10,11... | collective-permute-start | bytes 1179656 | tf_op jit(solution)/shard_map/ppermute | solution.py:62
  69.2 1.3 copy-start.2
  71.6 52.5 %copy-start = (f32[20,128,256]{2,1,0:T(8,128)S(1)}, f32[20,128,256]{2,1,0:T(8,128)}, u32[]{:S(2)}) copy-start(f32[20,128,256]{2,1,0:T(8,128)} %get-tuple-element.42.prod) | copy-start | bytes 7864324
  71.7 52.5 %copy-start.6 = (s32[20]{0:T(128)S(1)}, s32[20]{0:T(128)}, u32[]{:S(2)}) copy-start(s32[20]{0:T(128)} %code_at.3) | copy-start | bytes 244
  71.7 52.5 %copy-start.7 = (s32[20]{0:T(128)S(1)}, s32[20]{0:T(128)}, u32[]{:S(2)}) copy-start(s32[20]{0:T(128)} %month_at.3) | copy-start | bytes 244
  71.7 5.8 %collective-permute-start.3 = (s16[336,256]{1,0:T(8,128)(2,1)S(1)}, s16[336,256]{1,0:T(8,128)(2,1)S(1)}, u32[]{:S(2)}, u32[]{:S(2)}) collective-permute-start(s16[336,256]{1,0:T(8,128)(2,1)S(1)} %get-tuple-element.31), channel_id=1, source_target_pairs={{0,16},{1,5},{2,18},{3,7},{4,20},{5,9},{6,22},{7,11},{8,24},{9,13}... | collective-permute-start | bytes 516104 | tf_op jit(solution)/shard_map/ppermute | solution.py:62
  72.6 7.9 %collective-permute-start.4 = (s16[336,256]{1,0:T(8,128)(2,1)S(1)}, s16[336,256]{1,0:T(8,128)(2,1)S(1)}, u32[]{:S(2)}, u32[]{:S(2)}) collective-permute-start(s16[336,256]{1,0:T(8,128)(2,1)S(1)} %get-tuple-element.32), channel_id=1, source_target_pairs={{0,32},{1,9},{2,34},{3,11},{4,36},{5,13},{6,38},{7,15},{8,40},{9,1... | collective-permute-start | bytes 516104 | tf_op jit(solution)/shard_map/ppermute | solution.py:62
  75.6 4.9 %collective-permute-start.5 = (s16[336,256]{1,0:T(8,128)(2,1)S(1)}, s16[336,256]{1,0:T(8,128)(2,1)S(1)}, u32[]{:S(2)}, u32[]{:S(2)}) collective-permute-start(s16[336,256]{1,0:T(8,128)(2,1)S(1)} %get-tuple-element.33), channel_id=1, source_target_pairs={{0,48},{1,13},{2,50},{3,15},{4,52},{5,1},{6,54},{7,3},{8,56},{9,5}... | collective-permute-start | bytes 516104 | tf_op jit(solution)/shard_map/ppermute | solution.py:62
  80.8 5.1 %collective-permute-start.6 = (s16[96,256]{1,0:T(8,128)(2,1)S(1)}, s16[96,256]{1,0:T(8,128)(2,1)S(1)}, u32[]{:S(2)}, u32[]{:S(2)}) collective-permute-start(s16[96,256]{1,0:T(8,128)(2,1)S(1)} %get-tuple-element.35), channel_id=1, source_target_pairs={{0,64},{1,65},{2,66},{3,67},{4,68},{5,69},{6,70},{7,71},{8,72},{9,... | collective-permute-start | bytes 147464 | tf_op jit(solution)/shard_map/ppermute | solution.py:62
  82.6 5.3 %collective-permute-start.7 = (s16[96,256]{1,0:T(8,128)(2,1)S(1)}, s16[96,256]{1,0:T(8,128)(2,1)S(1)}, u32[]{:S(2)}, u32[]{:S(2)}) collective-permute-start(s16[96,256]{1,0:T(8,128)(2,1)S(1)} %get-tuple-element.36), channel_id=1, source_target_pairs={{0,128},{1,129},{2,130},{3,131},{4,132},{5,133},{6,134},{7,135},{8... | collective-permute-start | bytes 147464 | tf_op jit(solution)/shard_map/ppermute | solution.py:62
  84.7 3.8 %collective-permute-start.8 = (s16[96,256]{1,0:T(8,128)(2,1)S(1)}, s16[96,256]{1,0:T(8,128)(2,1)S(1)}, u32[]{:S(2)}, u32[]{:S(2)}) collective-permute-start(s16[96,256]{1,0:T(8,128)(2,1)S(1)} %get-tuple-element.37), channel_id=1, source_target_pairs={{0,192},{1,193},{2,194},{3,195},{4,196},{5,197},{6,198},{7,199},{8... | collective-permute-start | bytes 147464 | tf_op jit(solution)/shard_map/ppermute | solution.py:62
  89.8 3.9 %collective-permute-start.10 = (s16[128,256]{1,0:T(8,128)(2,1)S(1)}, s16[128,256]{1,0:T(8,128)(2,1)S(1)}, u32[]{:S(2)}, u32[]{:S(2)}) collective-permute-start(s16[128,256]{1,0:T(8,128)(2,1)S(1)} %get-tuple-element.40), channel_id=1, source_target_pairs={{0,192},{1,193},{2,194},{3,195},{4,196},{5,197},{6,198},{7,199},{8... | collective-permute-start | bytes 196616 | tf_op jit(solution)/shard_map/ppermute | solution.py:62
  92.4 4.1 %collective-permute-start.11 = (s16[128,256]{1,0:T(8,128)(2,1)S(1)}, s16[128,256]{1,0:T(8,128)(2,1)S(1)}, u32[]{:S(2)}, u32[]{:S(2)}) collective-permute-start(s16[128,256]{1,0:T(8,128)(2,1)S(1)} %get-tuple-element.40), channel_id=1, source_target_pairs={{0,128},{1,129},{2,130},{3,131},{4,132},{5,133},{6,134},{7,135},{8... | collective-permute-start | bytes 196616 | tf_op jit(solution)/shard_map/ppermute | solution.py:62
  92.4 5.6 %collective-permute-start.12 = (s16[128,256]{1,0:T(8,128)(2,1)S(1)}, s16[128,256]{1,0:T(8,128)(2,1)S(1)}, u32[]{:S(2)}, u32[]{:S(2)}) collective-permute-start(s16[128,256]{1,0:T(8,128)(2,1)S(1)} %get-tuple-element.40), channel_id=1, source_target_pairs={{0,64},{1,65},{2,66},{3,67},{4,68},{5,69},{6,70},{7,71},{8,72},{9,... | collective-permute-start | bytes 196616 | tf_op jit(solution)/shard_map/ppermute | solution.py:62
  98.0 7.7 %collective-permute-start.13 = (s16[512,256]{1,0:T(8,128)(2,1)S(1)}, s16[512,256]{1,0:T(8,128)(2,1)S(1)}, u32[]{:S(2)}, u32[]{:S(2)}) collective-permute-start(s16[512,256]{1,0:T(8,128)(2,1)S(1)} %constant_dynamic-update-slice_fusion), channel_id=1, source_target_pairs={{0,48},{1,13},{2,50},{3,15},{4,52},{5,1},{6,54},{7,3},{8,56},{9,5}... | collective-permute-start | bytes 786440 | tf_op jit(solution)/shard_map/ppermute | solution.py:62
  99.6 6.8 %collective-permute-start.14 = (s16[512,256]{1,0:T(8,128)(2,1)S(1)}, s16[512,256]{1,0:T(8,128)(2,1)S(1)}, u32[]{:S(2)}, u32[]{:S(2)}) collective-permute-start(s16[512,256]{1,0:T(8,128)(2,1)S(1)} %constant_dynamic-update-slice_fusion), channel_id=1, source_target_pairs={{0,32},{1,9},{2,34},{3,11},{4,36},{5,13},{6,38},{7,15},{8,40},{9,1... | collective-permute-start | bytes 786440 | tf_op jit(solution)/shard_map/ppermute | solution.py:62
  99.6 9.5 %collective-permute-start.15 = (s16[512,256]{1,0:T(8,128)(2,1)S(1)}, s16[512,256]{1,0:T(8,128)(2,1)S(1)}, u32[]{:S(2)}, u32[]{:S(2)}) collective-permute-start(s16[512,256]{1,0:T(8,128)(2,1)S(1)} %constant_dynamic-update-slice_fusion), channel_id=1, source_target_pairs={{0,16},{1,5},{2,18},{3,7},{4,20},{5,9},{6,22},{7,11},{8,24},{9,13}... | collective-permute-start | bytes 786440 | tf_op jit(solution)/shard_map/ppermute | solution.py:62
  106.4 29.9 %copy-start.8 = (s16[512,256]{1,0:T(8,128)(2,1)}, s16[512,256]{1,0:T(8,128)(2,1)S(1)}, u32[]{:S(2)}) copy-start(s16[512,256]{1,0:T(8,128)(2,1)S(1)} %collective-permute-done.14) | copy-start | bytes 786436
  109.1 0.7 copy-start.9
  109.9 10.9 %collective-permute-start.19 = (s16[768,256]{1,0:T(8,128)(2,1)S(1)}, s16[768,256]{1,0:T(8,128)(2,1)S(1)}, u32[]{:S(2)}, u32[]{:S(2)}) collective-permute-start(s16[768,256]{1,0:T(8,128)(2,1)S(1)} %pad_add_fusion.1.refs_4_.w0), channel_id=1, source_target_pairs={{0,12},{1,49},{2,14},{3,51},{4,0},{5,53},{6,2},{7,55},{8,4},{9,57}... | collective-permute-start | bytes 1179656 | tf_op jit(solution)/shard_map/ppermute | solution.py:62
  111.8 8.9 %collective-permute-start.20 = (s16[768,256]{1,0:T(8,128)(2,1)S(1)}, s16[768,256]{1,0:T(8,128)(2,1)S(1)}, u32[]{:S(2)}, u32[]{:S(2)}) collective-permute-start(s16[768,256]{1,0:T(8,128)(2,1)S(1)} %pad_add_fusion.1.refs_4_.w0), channel_id=1, source_target_pairs={{0,8},{1,33},{2,10},{3,35},{4,12},{5,37},{6,14},{7,39},{8,0},{9,41... | collective-permute-start | bytes 1179656 | tf_op jit(solution)/shard_map/ppermute | solution.py:62
  111.8 12.3 %collective-permute-start.21 = (s16[768,256]{1,0:T(8,128)(2,1)S(1)}, s16[768,256]{1,0:T(8,128)(2,1)S(1)}, u32[]{:S(2)}, u32[]{:S(2)}) collective-permute-start(s16[768,256]{1,0:T(8,128)(2,1)S(1)} %pad_add_fusion.1.refs_4_.w0), channel_id=1, source_target_pairs={{0,4},{1,17},{2,6},{3,19},{4,8},{5,21},{6,10},{7,23},{8,12},{9,25}... | collective-permute-start | bytes 1179656 | tf_op jit(solution)/shard_map/ppermute | solution.py:62
  136.3 45.3 %copy-start.3 = (f32[256,256]{1,0:T(8,128)S(1)}, f32[256,256]{1,0:T(8,128)}, u32[]{:S(2)}) copy-start(f32[256,256]{1,0:T(8,128)} %get-tuple-element.24.near.refs_9_) | copy-start | bytes 786436
  136.3 45.3 %copy-start.5 = (f32[8,128]{1,0:T(8,128)S(1)}, f32[8,128]{1,0:T(8,128)}, u32[]{:S(2)}) copy-start(f32[8,128]{1,0:T(8,128)} %get-tuple-element.25.rho_ref.refs_10_) | copy-start | bytes 12292
  136.3 11.9 %collective-permute-start.22 = (f32[24,256]{1,0:T(8,128)S(1)}, f32[24,256]{1,0:T(8,128)S(1)}, u32[]{:S(2)}, u32[]{:S(2)}) collective-permute-start(f32[24,256]{1,0:T(8,128)S(1)} %reduce_sum.38), channel_id=1, source_target_pairs={{0,1},{1,0},{2,3},{3,2},{4,5},{5,4},{6,7},{7,6},{8,9},{9,8},{10,11... | collective-permute-start | bytes 73736 | tf_op jit(solution)/shard_map/ppermute | solution.py:62
  148.9 17.2 %all-to-all-start.4 = ((f32[8,24,256]{2,1,0:T(8,128)}), f32[8,24,256]{2,1,0:T(8,128)S(1)}, u32[]{:S(2)}, u32[]{:S(2)}) async-start(f32[8,24,256]{2,1,0:T(8,128)} %broadcast_in_dim.14), calls=%async_computation.4 | async-start | bytes 393216 | tf_op jit(solution)/shard_map/all_to_all | solution.py:74
  160.2 10.5 %collective-permute-start.16 = (s16[1280,256]{1,0:T(8,128)(2,1)S(1)}, s16[1280,256]{1,0:T(8,128)(2,1)}, u32[]{:S(2)}, u32[]{:S(2)}) collective-permute-start(s16[1280,256]{1,0:T(8,128)(2,1)S(1)} %pad_add_fusion.refs_0_), channel_id=1, source_target_pairs={{0,12},{1,49},{2,14},{3,51},{4,0},{5,53},{6,2},{7,55},{8,4},{9,57}... | collective-permute-start | bytes 1966088 | tf_op jit(solution)/shard_map/ppermute | solution.py:62
  160.8 11.4 %collective-permute-start.17 = (s16[1280,256]{1,0:T(8,128)(2,1)S(1)}, s16[1280,256]{1,0:T(8,128)(2,1)}, u32[]{:S(2)}, u32[]{:S(2)}) collective-permute-start(s16[1280,256]{1,0:T(8,128)(2,1)S(1)} %pad_add_fusion.refs_0_), channel_id=1, source_target_pairs={{0,8},{1,33},{2,10},{3,35},{4,12},{5,37},{6,14},{7,39},{8,0},{9,41... | collective-permute-start | bytes 1966088 | tf_op jit(solution)/shard_map/ppermute | solution.py:62
  161.6 20.0 %collective-permute-start.18 = (s16[1280,256]{1,0:T(8,128)(2,1)S(1)}, s16[1280,256]{1,0:T(8,128)(2,1)}, u32[]{:S(2)}, u32[]{:S(2)}) collective-permute-start(s16[1280,256]{1,0:T(8,128)(2,1)S(1)} %pad_add_fusion.refs_0_), channel_id=1, source_target_pairs={{0,4},{1,17},{2,6},{3,19},{4,8},{5,21},{6,10},{7,23},{8,12},{9,25}... | collective-permute-start | bytes 1966088 | tf_op jit(solution)/shard_map/ppermute | solution.py:62
  166.9 23.7 %all-to-all-start.5 = ((f32[16,24,256]{2,1,0:T(8,128)}), f32[16,24,256]{2,1,0:T(8,128)S(1)}, u32[]{:S(2)}, u32[]{:S(2)}) async-start(f32[16,24,256]{2,1,0:T(8,128)} %broadcast_in_dim.15), calls=%async_computation.5 | async-start | bytes 786432 | tf_op jit(solution)/shard_map/all_to_all | solution.py:74

commit v5 on v4

--- a/solution.py
+++ b/solution.py
@@ -269,8 +269,7 @@
     near_parts = split(near[...])
     copies[3].wait()
 
-    def chunk(step, _):
-        k = lax.rem(step + 1, 4)
+    def chunk(k, _):
         for b in range(16):
             at = pl.ds(block_row(place, k, b), SHARE)
             u_part[b * SHARE : (b + 1) * SHARE, :] = duals[at, :]
@@ -280,8 +279,16 @@
         once = u + dot3(split(g - u), near_parts)
         twice = once + dot3(split(g - once), near_parts)
         v[k] = twice
+        pltpu.make_async_copy(v.at[k], v_hbm.at[k], outs.at[5 + k]).start()
         u_part[...] = rho * once
         g_part[...] = rho * twice
+
+        @pl.when(k == 0)
+        def _():
+            for b in range(16):
+                own[b * 80 : b * 80 + SHARE, :] = u_part[b * SHARE : (b + 1) * SHARE, :]
+                own[b * 80 + SHARE : b * 80 + 80, :] = g_part[b * SHARE : (b + 1) * SHARE, :]
+            pltpu.make_async_copy(own, a0, outs.at[3]).start()
 
         @pl.when(k > 0)
         def _():
@@ -302,18 +309,12 @@
         return 0
 
     lax.fori_loop(0, 4, chunk, 0)
-    for b in range(16):
-        own[b * 80 : b * 80 + SHARE, :] = u_part[b * SHARE : (b + 1) * SHARE, :]
-        own[b * 80 + SHARE : b * 80 + 80, :] = g_part[b * SHARE : (b + 1) * SHARE, :]
-    own_out = pltpu.make_async_copy(own, a0, outs.at[3])
-    own_out.start()
-    v_out = pltpu.make_async_copy(v, v_hbm, outs.at[5])
-    v_out.start()
     for n, out in enumerate((q1, q2, q3)):
         pltpu.make_async_copy(held.at[n], out, outs.at[n]).wait()
     prod_out.wait()
-    own_out.wait()
-    v_out.wait()
+    pltpu.make_async_copy(own, a0, outs.at[3]).wait()
+    for k in range(4):
+        pltpu.make_async_copy(v.at[k], v_hbm.at[k], outs.at[5 + k]).wait()
 
 
 def sum_kernel(own, r1, r2, r3, s0, q1, q2, q3, acc, part, coded):
@@ -325,6 +326,13 @@
     s0[...] = acc[0 : few * SHARE, :]
     for j, out in enumerate((q1, q2, q3)):
         encode_blocks(acc, (j + 1) * few, few, coded, out)
+
+
+def cut_kernel(r0, r1, r2, r3, out):
+    for j, r in enumerate((r0, r1, r2, r3)):
+        for i in range(4):
+            at = (j * 4 + i) * 80
+            out[at : at + 80, :] = r[i * 128 + 48 : i * 128 + 128, :]
 
 
 def owner_kernel(
@@ -464,7 +472,7 @@
             pltpu.VMEM((1024, R), BF16), (MONTHS, R), pltpu.VMEM((CAP, BLOCK, BLOCK), BF16),
             (ROWS, R), (CAP, BLOCK, R), (ROWS, R), (CHUNK, R), (CHUNK, R), (4, CHUNK, R),
             (2 * CHUNK, R), (tops[0], R), pltpu.VMEM((3, tops[0], R), jnp.int16),
-            pltpu.SemaphoreType.DMA((4,)), pltpu.SemaphoreType.DMA((6,)),
+            pltpu.SemaphoreType.DMA((4,)), pltpu.SemaphoreType.DMA((9,)),
         ],
         live_count, patient_block, code_block, month_index,
         near, rho, patient_factor, month_factor, tile_values, scaled_duals, limit=None,
@@ -489,9 +497,9 @@
         *s, consensus, mine, other, month_factor,
     )
     rows = jnp.concatenate(gather(rows, depth_move), 0)
-    rows = [r.reshape(4, 128, R) for r in gather(rows, second_move)]
-    two = jnp.concatenate([r[:, :48].reshape(192, R) for r in rows], 0)
-    both = jnp.concatenate([r[:, 48:].reshape(320, R) for r in rows], 0)
+    rows = gather(rows, second_move)
+    two = jnp.concatenate([r.reshape(4, 128, R)[:, :48].reshape(192, R) for r in rows], 0)
+    (both,) = call(cut_kernel, [codes(1280)], "vvvv" + "v", [], *rows)
     two = gather(two, first_move)
     both = gather(both, first_move)
     (sums,) = call(

time: 197 us -> 195 us (0.990)
  local copies, waits for them, and re-layouts: 7.44 us -> 4.51 us
    ppermute x23, starting transfers between devices: 33.4 us -> 40 us  [send(): return lax.ppermute(value, AXES, pairs)]
    all_to_all x3, starting transfers between devices: 19.7 us -> 14.9 us  [exchange(): return lax.all_to_all(value, axes, 0, 0, tiled=True)]
    slice x8 -> x4, local copies, waits for them, and re-layouts: 3.24 us -> 0.03 us  [compute(): r.reshape(4, 128, R)[:, :48].reshape(192, R)]
    pallas_call x8 -> x9, Pallas kernels: 37.2 us -> 36.2 us  [call(): pl.pallas_call(body, out_shape=[s if isinstance(s, jax.ShapeDtypeStruct)...]
  transfers between devices with their start and end apart: 26 -> 26, of which waited for: 15 -> 16; matrix products, arithmetic and copies ran while one was open for 3% -> 1% of each run, Pallas kernels for 11% -> 11%
where the time goes in v5:
time: 195 us; the launch traced here: 194 us
  starting transfers between devices  54.8 us (28%)
  blocking collectives  48 us (25%)
  waiting for transfers between devices  47.5 us (24%)
  Pallas kernels  36.2 us (19%)
  local copies, waits for them, and re-layouts  4.51 us (2%)
    all_to_all x3, blocking collectives, exchange(): return lax.all_to_all(value, axes, 0, 0, tiled=True)  48 us
    ppermute x23, waiting for transfers between devices, send(): return lax.ppermute(value, AXES, pairs)  43 us
    ppermute x23, starting transfers between devices, send(): return lax.ppermute(value, AXES, pairs)  40 us
    pallas_call x9, Pallas kernels, call(): pl.pallas_call(body, out_shape=[s if isinstance(s, jax.ShapeDtypeStruct)...  36.2 us
    all_to_all x3, starting transfers between devices, exchange(): return lax.all_to_all(value, axes, 0, 0, tiled=True)  14.9 us
    all_to_all x3, waiting for transfers between devices, exchange(): return lax.all_to_all(value, axes, 0, 0, tiled=True)  4.5 us
  transfers between devices with their start and end apart: 26, of which 16 were waited for; matrix products, arithmetic and copies ran while one was open for 1% of the time, Pallas kernels for 11%

profile of v5, /device:TPU:1, one launch (start us, length us, event | category | flops | bytes accessed | tf_op | source)
XLA Modules:
  0.0 193.5 jit_solution(3280223847565926894)
XLA Ops:
  0.6 7.5 %shard_map.112 = (f32[256,256]{1,0:T(8,128)}, f32[8,128]{1,0:T(8,128)}, f32[384,256]{1,0:T(8,128)}) custom-call(bf16[1024,256]{1,0:T(8,128)(2,1)} %patient_hbm.1, f32[120,256]{1,0:T(8,128)} %month.5), custom_call_target="tpu_custom_call" | custom-call | tf_op jit(solution)/shard_map/pallas_call | solution.py:443
  8.2 17.1 %all_to_all.30 = f32[16,24,256]{2,1,0:T(8,128)S(1)} all-to-all(f32[16,24,256]{2,1,0:T(8,128)} %bitcast.20), channel_id=1, replica_groups=mesh['z'=4,'y'=4,'x'=4,'h'=2,'c'=2] {'y','x'}, dimensions={0} | all-to-all | bytes 786432 | tf_op jit(solution)/shard_map/all_to_all | solution.py:74
  25.3 0.6 broadcast_in_dim.12
  25.9 5.6 %all-to-all-start.1 = ((f32[4,24,256]{2,1,0:T(8,128)}), f32[4,24,256]{2,1,0:T(8,128)S(1)}, u32[]{:S(2)}, u32[]{:S(2)}) async-start(f32[4,24,256]{2,1,0:T(8,128)} %broadcast_in_dim.12), calls=%async_computation.1 | async-start | bytes 196608 | tf_op jit(solution)/shard_map/all_to_all | solution.py:74
  32.2 9.9 %shard_map.113 = (f32[20,128,256]{2,1,0:T(8,128)}, f32[4,640,256]{2,1,0:T(8,128)}, f32[1280,256]{1,0:T(8,128)}, s16[1312,256]{1,0:T(8,128)(2,1)}, s16[1312,256]{1,0:T(8,128)(2,1)}, /*index=5*/s16[1312,256]{1,0:T(8,128)(2,1)}) custom-call(s32[1]{0:T(128)S(6)} %copy.15.live, s32[20]{0:T(128)} %patient_at.1, s32[20]{0:T(128)} %code_at.3, s32[20]{0:T(128)} %month_at.3, ...), custom_call_target="tpu_custom_call" | custom-call | tf_op jit(solution)/shard_map/pallas_call | solution.py:443
  42.1 0.1 collective-permute-start
  42.2 1.8 collective-permute-start.1
  44.0 0.8 collective-permute-start.2
  44.9 0.0 copy-start.1
  44.9 0.0 copy-start.8
  44.9 19.6 %all_to_all.31 = f32[16,24,256]{2,1,0:T(8,128)S(1)} all-to-all(f32[16,24,256]{2,1,0:T(8,128)S(1)} %broadcast_in_dim.13), channel_id=1, replica_groups=mesh['z'=4,'y'=4,'x'=4,'h'=2,'c'=2] {'y','x'}, dimensions={0} | all-to-all | bytes 786432 | tf_op jit(solution)/shard_map/all_to_all | solution.py:74
  64.5 3.7 %collective-permute-start.9 = (f32[384,256]{1,0:T(8,128)S(1)}, f32[384,256]{1,0:T(8,128)S(1)}, u32[]{:S(2)}, u32[]{:S(2)}) collective-permute-start(f32[384,256]{1,0:T(8,128)S(1)} %bitcast.14), channel_id=1, source_target_pairs={{0,1},{1,0},{2,3},{3,2},{4,5},{5,4},{6,7},{7,6},{8,9},{9,8},{10,11... | collective-permute-start | bytes 1179656 | tf_op jit(solution)/shard_map/ppermute | solution.py:62
  68.2 1.3 copy-done.2
  69.5 1.1 shard_map.114
  70.6 0.0 copy-start
  70.7 0.0 copy-start.10
  70.7 0.0 copy-start.11
  70.7 0.9 collective-permute-start.3
  71.6 3.0 %collective-permute-start.4 = (s16[336,256]{1,0:T(8,128)(2,1)S(1)}, s16[336,256]{1,0:T(8,128)(2,1)S(1)}, u32[]{:S(2)}, u32[]{:S(2)}) collective-permute-start(s16[336,256]{1,0:T(8,128)(2,1)S(1)} %get-tuple-element.32), channel_id=1, source_target_pairs={{0,32},{1,9},{2,34},{3,11},{4,36},{5,13},{6,38},{7,15},{8,40},{9,1... | collective-permute-start | bytes 516104 | tf_op jit(solution)/shard_map/ppermute | solution.py:62
  74.6 1.9 collective-permute-done.3.r1
  76.5 2.9 %collective-permute-done.4.r2 = s16[336,256]{1,0:T(8,128)(2,1)S(1)} collective-permute-done((s16[336,256]{1,0:T(8,128)(2,1)S(1)}, s16[336,256]{1,0:T(8,128)(2,1)S(1)}, u32[]{:S(2)}, u32[]{:S(2)}) %collective-permute-start.4) | collective-permute-done | bytes 172064 | tf_op jit(solution)/shard_map/ppermute | solution.py:62
  79.5 0.0 collective-permute-done.5.r3
  79.5 0.3 shard_map.115
  79.8 1.8 collective-permute-start.6
  81.6 2.1 %collective-permute-start.7 = (s16[96,256]{1,0:T(8,128)(2,1)S(1)}, s16[96,256]{1,0:T(8,128)(2,1)S(1)}, u32[]{:S(2)}, u32[]{:S(2)}) collective-permute-start(s16[96,256]{1,0:T(8,128)(2,1)S(1)} %get-tuple-element.36), channel_id=1, source_target_pairs={{0,128},{1,129},{2,130},{3,131},{4,132},{5,133},{6,134},{7,135},{8... | collective-permute-start | bytes 147464 | tf_op jit(solution)/shard_map/ppermute | solution.py:62
  83.7 1.2 collective-permute-start.8
  84.9 2.0 %collective-permute-done.7.s2 = s16[96,256]{1,0:T(8,128)(2,1)S(1)} collective-permute-done((s16[96,256]{1,0:T(8,128)(2,1)S(1)}, s16[96,256]{1,0:T(8,128)(2,1)S(1)}, u32[]{:S(2)}, u32[]{:S(2)}) %collective-permute-start.7) | collective-permute-done | bytes 49184 | tf_op jit(solution)/shard_map/ppermute | solution.py:62
  86.9 0.5 collective-permute-done.8.s3
  87.4 1.4 shard_map.116
  88.8 2.5 %collective-permute-start.10 = (s16[128,256]{1,0:T(8,128)(2,1)S(1)}, s16[128,256]{1,0:T(8,128)(2,1)S(1)}, u32[]{:S(2)}, u32[]{:S(2)}) collective-permute-start(s16[128,256]{1,0:T(8,128)(2,1)S(1)} %get-tuple-element.40), channel_id=1, source_target_pairs={{0,192},{1,193},{2,194},{3,195},{4,196},{5,197},{6,198},{7,199},{8... | collective-permute-start | bytes 196616 | tf_op jit(solution)/shard_map/ppermute | solution.py:62
  91.4 0.0 collective-permute-start.11
  91.4 0.3 collective-permute-start.12
  91.7 1.0 collective-permute-done.10
  92.7 2.7 %collective-permute-done.11 = s16[128,256]{1,0:T(8,128)(2,1)S(1)} collective-permute-done((s16[128,256]{1,0:T(8,128)(2,1)S(1)}, s16[128,256]{1,0:T(8,128)(2,1)S(1)}, u32[]{:S(2)}, u32[]{:S(2)}) %collective-permute-start.11) | collective-permute-done | bytes 65568 | tf_op jit(solution)/shard_map/ppermute | solution.py:62
  95.4 1.5 collective-permute-done.12
  97.0 1.6 collective-permute-start.13
  98.6 0.0 collective-permute-start.14
  98.6 0.7 collective-permute-start.15
  99.3 5.4 %collective-permute-done.13.r1 = s16[512,256]{1,0:T(8,128)(2,1)S(1)} collective-permute-done((s16[512,256]{1,0:T(8,128)(2,1)S(1)}, s16[512,256]{1,0:T(8,128)(2,1)S(1)}, u32[]{:S(2)}, u32[]{:S(2)}) %collective-permute-start.13) | collective-permute-done | bytes 262176 | tf_op jit(solution)/shard_map/ppermute | solution.py:62
  104.7 0.7 collective-permute-done.14.r2
  105.4 2.7 %collective-permute-done.15.r3 = s16[512,256]{1,0:T(8,128)(2,1)S(1)} collective-permute-done((s16[512,256]{1,0:T(8,128)(2,1)S(1)}, s16[512,256]{1,0:T(8,128)(2,1)S(1)}, u32[]{:S(2)}, u32[]{:S(2)}) %collective-permute-start.15) | collective-permute-done | bytes 262176 | tf_op jit(solution)/shard_map/ppermute | solution.py:62
  108.2 2.0 %collective-permute-start.19 = (s16[768,256]{1,0:T(8,128)(2,1)S(1)}, s16[768,256]{1,0:T(8,128)(2,1)S(1)}, u32[]{:S(2)}, u32[]{:S(2)}) collective-permute-start(s16[768,256]{1,0:T(8,128)(2,1)S(1)} %pad_add_fusion.refs_4_.w0), channel_id=1, source_target_pairs={{0,12},{1,49},{2,14},{3,51},{4,0},{5,53},{6,2},{7,55},{8,4},{9,57}... | collective-permute-start | bytes 1179656 | tf_op jit(solution)/shard_map/ppermute | solution.py:62
  110.2 0.7 collective-permute-start.21
  110.9 8.3 %collective-permute-done.19.refs_5_.w1 = s16[768,256]{1,0:T(8,128)(2,1)S(1)} collective-permute-done((s16[768,256]{1,0:T(8,128)(2,1)S(1)}, s16[768,256]{1,0:T(8,128)(2,1)S(1)}, u32[]{:S(2)}, u32[]{:S(2)}) %collective-permute-start.19) | collective-permute-done | bytes 393248 | tf_op jit(solution)/shard_map/ppermute | solution.py:62
  119.1 0.0 collective-permute-done.20.refs_6_.w2
  119.1 3.1 %collective-permute-done.21.refs_7_.w3 = s16[768,256]{1,0:T(8,128)(2,1)S(1)} collective-permute-done((s16[768,256]{1,0:T(8,128)(2,1)S(1)}, s16[768,256]{1,0:T(8,128)(2,1)S(1)}, u32[]{:S(2)}, u32[]{:S(2)}) %collective-permute-start.21) | collective-permute-done | bytes 393248 | tf_op jit(solution)/shard_map/ppermute | solution.py:62
  122.3 1.2 shard_map.119
  123.5 11.2 %all_to_all.32 = f32[16,24,256]{2,1,0:T(8,128)S(1)} all-to-all(f32[16,24,256]{2,1,0:T(8,128)S(1)} %bitcast.13), channel_id=1, replica_groups=mesh['z'=4,'y'=4,'x'=4,'h'=2,'c'=2] {'y','x'}, dimensions={0} | all-to-all | bytes 786432 | tf_op jit(solution)/shard_map/all_to_all | solution.py:74
  134.8 15.1 %collective-permute-start.22 = (f32[24,256]{1,0:T(8,128)S(1)}, f32[24,256]{1,0:T(8,128)S(1)}, u32[]{:S(2)}, u32[]{:S(2)}) collective-permute-start(f32[24,256]{1,0:T(8,128)S(1)} %reduce_sum.38), channel_id=1, source_target_pairs={{0,1},{1,0},{2,3},{3,2},{4,5},{5,4},{6,7},{7,6},{8,9},{9,8},{10,11... | collective-permute-start | bytes 73736 | tf_op jit(solution)/shard_map/ppermute | solution.py:62
  149.9 0.8 collective-permute-done.22
  150.8 0.7 broadcast_in_dim.14
  151.5 5.5 %all-to-all-start.4 = ((f32[8,24,256]{2,1,0:T(8,128)}), f32[8,24,256]{2,1,0:T(8,128)}, u32[]{:S(2)}, u32[]{:S(2)}) async-start(f32[8,24,256]{2,1,0:T(8,128)} %broadcast_in_dim.14), calls=%async_computation.4 | async-start | bytes 393216 | tf_op jit(solution)/shard_map/all_to_all | solution.py:74
  157.0 0.9 copy-done.5
  158.0 0.6 collective-permute-start.16
  158.6 0.7 collective-permute-start.17
  159.3 0.2 collective-permute-start.18
  159.5 4.5 %all-to-all-done.4 = f32[8,24,256]{2,1,0:T(8,128)} async-done(((f32[8,24,256]{2,1,0:T(8,128)}), f32[8,24,256]{2,1,0:T(8,128)}, u32[]{:S(2)}, u32[]{:S(2)}) %all-to-all-start.4) | async-done | bytes 196640 | tf_op jit(solution)/shard_map/all_to_all | solution.py:74
  164.0 0.9 reduce_sum.39
  164.9 0.8 broadcast_in_dim.15
  165.7 3.8 %all-to-all-start.5 = ((f32[16,24,256]{2,1,0:T(8,128)}), f32[16,24,256]{2,1,0:T(8,128)S(1)}, u32[]{:S(2)}, u32[]{:S(2)}) async-start(f32[16,24,256]{2,1,0:T(8,128)} %broadcast_in_dim.15), calls=%async_computation.5 | async-start | bytes 786432 | tf_op jit(solution)/shard_map/all_to_all | solution.py:74
  169.5 0.4 collective-permute-done.17.refs_2_
  170.0 8.8 %collective-permute-done.18.refs_3_ = s16[1280,256]{1,0:T(8,128)(2,1)} collective-permute-done((s16[1280,256]{1,0:T(8,128)(2,1)S(1)}, s16[1280,256]{1,0:T(8,128)(2,1)}, u32[]{:S(2)}, u32[]{:S(2)}) %collective-permute-start.18) | collective-permute-done | bytes 655392 | tf_op jit(solution)/shard_map/ppermute | solution.py:62
  178.8 9.1 %shard_map.118 = f32[2560,256]{1,0:T(8,128)} custom-call(s16[1280,256]{1,0:T(8,128)(2,1)S(1)} %shard_map.117.refs_0_, s16[1280,256]{1,0:T(8,128)(2,1)} %collective-permute-done.16.refs_1_, s16[1280,256]{1,0:T(8,128)(2,1)} %collective-permute-done.17.refs_2_, s16[1280,256]{1,0:T(8,128)(2,1)} %collective-permute-done.18.refs_3_, ...), custom_call_target="tpu_custom_call" | custom-call | tf_op jit(solution)/shard_map/pallas_call | solution.py:443
  187.9 5.6 %shard_map.120 = f32[120,256]{1,0:T(8,128)} custom-call(f32[384,256]{1,0:T(8,128)S(1)} %bitcast.12, f32[256,256]{1,0:T(8,128)S(1)} %copy-done.7, f32[120,256]{1,0:T(8,128)S(1)} %copy-done.1), custom_call_target="tpu_custom_call" | custom-call | tf_op jit(solution)/shard_map/pallas_call | solution.py:443
  (42 shorter events, 0.3 us)
Async XLA Ops:
  25.9 18.9 %all-to-all-start.1 = ((f32[4,24,256]{2,1,0:T(8,128)}), f32[4,24,256]{2,1,0:T(8,128)S(1)}, u32[]{:S(2)}, u32[]{:S(2)}) async-start(f32[4,24,256]{2,1,0:T(8,128)} %broadcast_in_dim.12), calls=%async_computation.1 | async-start | bytes 196608 | tf_op jit(solution)/shard_map/all_to_all | solution.py:74
  42.1 26.1 %collective-permute-start = (s16[1312,256]{1,0:T(8,128)(2,1)}, s16[1312,256]{1,0:T(8,128)(2,1)S(1)}, u32[]{:S(2)}, u32[]{:S(2)}) collective-permute-start(s16[1312,256]{1,0:T(8,128)(2,1)} %get-tuple-element.27), channel_id=1, source_target_pairs={{0,4},{1,17},{2,6},{3,19},{4,8},{5,21},{6,10},{7,23},{8,12},{9,25}... | collective-permute-start | bytes 2015240 | tf_op jit(solution)/shard_map/ppermute | solution.py:62
  42.2 26.0 %collective-permute-start.1 = (s16[1312,256]{1,0:T(8,128)(2,1)}, s16[1312,256]{1,0:T(8,128)(2,1)S(1)}, u32[]{:S(2)}, u32[]{:S(2)}) collective-permute-start(s16[1312,256]{1,0:T(8,128)(2,1)} %get-tuple-element.28), channel_id=1, source_target_pairs={{0,8},{1,33},{2,10},{3,35},{4,12},{5,37},{6,14},{7,39},{8,0},{9,41... | collective-permute-start | bytes 2015240 | tf_op jit(solution)/shard_map/ppermute | solution.py:62
  44.0 24.2 %collective-permute-start.2 = (s16[1312,256]{1,0:T(8,128)(2,1)}, s16[1312,256]{1,0:T(8,128)(2,1)S(1)}, u32[]{:S(2)}, u32[]{:S(2)}) collective-permute-start(s16[1312,256]{1,0:T(8,128)(2,1)} %get-tuple-element.29), channel_id=1, source_target_pairs={{0,12},{1,49},{2,14},{3,51},{4,0},{5,53},{6,2},{7,55},{8,4},{9,57}... | collective-permute-start | bytes 2015240 | tf_op jit(solution)/shard_map/ppermute | solution.py:62
  44.9 42.6 %copy-start.1 = (f32[120,256]{1,0:T(8,128)S(1)}, f32[120,256]{1,0:T(8,128)}, u32[]{:S(2)}) copy-start(f32[120,256]{1,0:T(8,128)} %month.5) | copy-start | bytes 368644
  44.9 42.6 %copy-start.8 = (f32[40,256]{1,0:T(8,128)S(1)}, f32[40,256]{1,0:T(8,128)}, u32[]{:S(2)}) copy-start(f32[40,256]{1,0:T(8,128)} %z0_ref.1) | copy-start | bytes 122884
  64.5 22.9 %collective-permute-start.9 = (f32[384,256]{1,0:T(8,128)S(1)}, f32[384,256]{1,0:T(8,128)S(1)}, u32[]{:S(2)}, u32[]{:S(2)}) collective-permute-start(f32[384,256]{1,0:T(8,128)S(1)} %bitcast.14), channel_id=1, source_target_pairs={{0,1},{1,0},{2,3},{3,2},{4,5},{5,4},{6,7},{7,6},{8,9},{9,8},{10,11... | collective-permute-start | bytes 1179656 | tf_op jit(solution)/shard_map/ppermute | solution.py:62
  68.2 1.3 copy-start.2
  70.6 51.6 %copy-start = (f32[20,128,256]{2,1,0:T(8,128)S(1)}, f32[20,128,256]{2,1,0:T(8,128)}, u32[]{:S(2)}) copy-start(f32[20,128,256]{2,1,0:T(8,128)} %get-tuple-element.42.prod) | copy-start | bytes 7864324
  70.7 51.6 %copy-start.10 = (s32[20]{0:T(128)S(1)}, s32[20]{0:T(128)}, u32[]{:S(2)}) copy-start(s32[20]{0:T(128)} %code_at.3) | copy-start | bytes 244
  70.7 51.6 %copy-start.11 = (s32[20]{0:T(128)S(1)}, s32[20]{0:T(128)}, u32[]{:S(2)}) copy-start(s32[20]{0:T(128)} %month_at.3) | copy-start | bytes 244
  70.7 5.8 %collective-permute-start.3 = (s16[336,256]{1,0:T(8,128)(2,1)S(1)}, s16[336,256]{1,0:T(8,128)(2,1)S(1)}, u32[]{:S(2)}, u32[]{:S(2)}) collective-permute-start(s16[336,256]{1,0:T(8,128)(2,1)S(1)} %get-tuple-element.31), channel_id=1, source_target_pairs={{0,16},{1,5},{2,18},{3,7},{4,20},{5,9},{6,22},{7,11},{8,24},{9,13}... | collective-permute-start | bytes 516104 | tf_op jit(solution)/shard_map/ppermute | solution.py:62
  71.6 7.9 %collective-permute-start.4 = (s16[336,256]{1,0:T(8,128)(2,1)S(1)}, s16[336,256]{1,0:T(8,128)(2,1)S(1)}, u32[]{:S(2)}, u32[]{:S(2)}) collective-permute-start(s16[336,256]{1,0:T(8,128)(2,1)S(1)} %get-tuple-element.32), channel_id=1, source_target_pairs={{0,32},{1,9},{2,34},{3,11},{4,36},{5,13},{6,38},{7,15},{8,40},{9,1... | collective-permute-start | bytes 516104 | tf_op jit(solution)/shard_map/ppermute | solution.py:62
  74.6 4.9 %collective-permute-start.5 = (s16[336,256]{1,0:T(8,128)(2,1)S(1)}, s16[336,256]{1,0:T(8,128)(2,1)S(1)}, u32[]{:S(2)}, u32[]{:S(2)}) collective-permute-start(s16[336,256]{1,0:T(8,128)(2,1)S(1)} %get-tuple-element.33), channel_id=1, source_target_pairs={{0,48},{1,13},{2,50},{3,15},{4,52},{5,1},{6,54},{7,3},{8,56},{9,5}... | collective-permute-start | bytes 516104 | tf_op jit(solution)/shard_map/ppermute | solution.py:62
  79.8 5.1 %collective-permute-start.6 = (s16[96,256]{1,0:T(8,128)(2,1)S(1)}, s16[96,256]{1,0:T(8,128)(2,1)S(1)}, u32[]{:S(2)}, u32[]{:S(2)}) collective-permute-start(s16[96,256]{1,0:T(8,128)(2,1)S(1)} %get-tuple-element.35), channel_id=1, source_target_pairs={{0,64},{1,65},{2,66},{3,67},{4,68},{5,69},{6,70},{7,71},{8,72},{9,... | collective-permute-start | bytes 147464 | tf_op jit(solution)/shard_map/ppermute | solution.py:62
  81.6 5.3 %collective-permute-start.7 = (s16[96,256]{1,0:T(8,128)(2,1)S(1)}, s16[96,256]{1,0:T(8,128)(2,1)S(1)}, u32[]{:S(2)}, u32[]{:S(2)}) collective-permute-start(s16[96,256]{1,0:T(8,128)(2,1)S(1)} %get-tuple-element.36), channel_id=1, source_target_pairs={{0,128},{1,129},{2,130},{3,131},{4,132},{5,133},{6,134},{7,135},{8... | collective-permute-start | bytes 147464 | tf_op jit(solution)/shard_map/ppermute | solution.py:62
  83.7 3.8 %collective-permute-start.8 = (s16[96,256]{1,0:T(8,128)(2,1)S(1)}, s16[96,256]{1,0:T(8,128)(2,1)S(1)}, u32[]{:S(2)}, u32[]{:S(2)}) collective-permute-start(s16[96,256]{1,0:T(8,128)(2,1)S(1)} %get-tuple-element.37), channel_id=1, source_target_pairs={{0,192},{1,193},{2,194},{3,195},{4,196},{5,197},{6,198},{7,199},{8... | collective-permute-start | bytes 147464 | tf_op jit(solution)/shard_map/ppermute | solution.py:62
  88.8 34.7 %copy-start.6 = (f32[256,256]{1,0:T(8,128)}, f32[256,256]{1,0:T(8,128)S(1)}, u32[]{:S(2)}) copy-start(f32[256,256]{1,0:T(8,128)S(1)} %get-tuple-element.44.gram) | copy-start | bytes 786436
  88.8 3.9 %collective-permute-start.10 = (s16[128,256]{1,0:T(8,128)(2,1)S(1)}, s16[128,256]{1,0:T(8,128)(2,1)S(1)}, u32[]{:S(2)}, u32[]{:S(2)}) collective-permute-start(s16[128,256]{1,0:T(8,128)(2,1)S(1)} %get-tuple-element.40), channel_id=1, source_target_pairs={{0,192},{1,193},{2,194},{3,195},{4,196},{5,197},{6,198},{7,199},{8... | collective-permute-start | bytes 196616 | tf_op jit(solution)/shard_map/ppermute | solution.py:62
  91.4 4.1 %collective-permute-start.11 = (s16[128,256]{1,0:T(8,128)(2,1)S(1)}, s16[128,256]{1,0:T(8,128)(2,1)S(1)}, u32[]{:S(2)}, u32[]{:S(2)}) collective-permute-start(s16[128,256]{1,0:T(8,128)(2,1)S(1)} %get-tuple-element.40), channel_id=1, source_target_pairs={{0,128},{1,129},{2,130},{3,131},{4,132},{5,133},{6,134},{7,135},{8... | collective-permute-start | bytes 196616 | tf_op jit(solution)/shard_map/ppermute | solution.py:62
  91.4 5.6 %collective-permute-start.12 = (s16[128,256]{1,0:T(8,128)(2,1)S(1)}, s16[128,256]{1,0:T(8,128)(2,1)S(1)}, u32[]{:S(2)}, u32[]{:S(2)}) collective-permute-start(s16[128,256]{1,0:T(8,128)(2,1)S(1)} %get-tuple-element.40), channel_id=1, source_target_pairs={{0,64},{1,65},{2,66},{3,67},{4,68},{5,69},{6,70},{7,71},{8,72},{9,... | collective-permute-start | bytes 196616 | tf_op jit(solution)/shard_map/ppermute | solution.py:62
  97.0 7.7 %collective-permute-start.13 = (s16[512,256]{1,0:T(8,128)(2,1)S(1)}, s16[512,256]{1,0:T(8,128)(2,1)S(1)}, u32[]{:S(2)}, u32[]{:S(2)}) collective-permute-start(s16[512,256]{1,0:T(8,128)(2,1)S(1)} %constant_dynamic-update-slice_fusion.r0), channel_id=1, source_target_pairs={{0,48},{1,13},{2,50},{3,15},{4,52},{5,1},{6,54},{7,3},{8,56},{9,5}... | collective-permute-start | bytes 786440 | tf_op jit(solution)/shard_map/ppermute | solution.py:62
  98.6 6.8 %collective-permute-start.14 = (s16[512,256]{1,0:T(8,128)(2,1)S(1)}, s16[512,256]{1,0:T(8,128)(2,1)S(1)}, u32[]{:S(2)}, u32[]{:S(2)}) collective-permute-start(s16[512,256]{1,0:T(8,128)(2,1)S(1)} %constant_dynamic-update-slice_fusion.r0), channel_id=1, source_target_pairs={{0,32},{1,9},{2,34},{3,11},{4,36},{5,13},{6,38},{7,15},{8,40},{9,1... | collective-permute-start | bytes 786440 | tf_op jit(solution)/shard_map/ppermute | solution.py:62
  98.6 9.5 %collective-permute-start.15 = (s16[512,256]{1,0:T(8,128)(2,1)S(1)}, s16[512,256]{1,0:T(8,128)(2,1)S(1)}, u32[]{:S(2)}, u32[]{:S(2)}) collective-permute-start(s16[512,256]{1,0:T(8,128)(2,1)S(1)} %constant_dynamic-update-slice_fusion.r0), channel_id=1, source_target_pairs={{0,16},{1,5},{2,18},{3,7},{4,20},{5,9},{6,22},{7,11},{8,24},{9,13}... | collective-permute-start | bytes 786440 | tf_op jit(solution)/shard_map/ppermute | solution.py:62
  108.1 14.1 %copy-start.4 = (s16[512,256]{1,0:T(8,128)(2,1)}, s16[512,256]{1,0:T(8,128)(2,1)S(1)}, u32[]{:S(2)}) copy-start(s16[512,256]{1,0:T(8,128)(2,1)S(1)} %collective-permute-done.15.r3) | copy-start | bytes 786436
  108.2 11.0 %collective-permute-start.19 = (s16[768,256]{1,0:T(8,128)(2,1)S(1)}, s16[768,256]{1,0:T(8,128)(2,1)S(1)}, u32[]{:S(2)}, u32[]{:S(2)}) collective-permute-start(s16[768,256]{1,0:T(8,128)(2,1)S(1)} %pad_add_fusion.refs_4_.w0), channel_id=1, source_target_pairs={{0,12},{1,49},{2,14},{3,51},{4,0},{5,53},{6,2},{7,55},{8,4},{9,57}... | collective-permute-start | bytes 1179656 | tf_op jit(solution)/shard_map/ppermute | solution.py:62
  110.2 8.9 %collective-permute-start.20 = (s16[768,256]{1,0:T(8,128)(2,1)S(1)}, s16[768,256]{1,0:T(8,128)(2,1)S(1)}, u32[]{:S(2)}, u32[]{:S(2)}) collective-permute-start(s16[768,256]{1,0:T(8,128)(2,1)S(1)} %pad_add_fusion.refs_4_.w0), channel_id=1, source_target_pairs={{0,8},{1,33},{2,10},{3,35},{4,12},{5,37},{6,14},{7,39},{8,0},{9,41... | collective-permute-start | bytes 1179656 | tf_op jit(solution)/shard_map/ppermute | solution.py:62
  110.2 12.1 %collective-permute-start.21 = (s16[768,256]{1,0:T(8,128)(2,1)S(1)}, s16[768,256]{1,0:T(8,128)(2,1)S(1)}, u32[]{:S(2)}, u32[]{:S(2)}) collective-permute-start(s16[768,256]{1,0:T(8,128)(2,1)S(1)} %pad_add_fusion.refs_4_.w0), channel_id=1, source_target_pairs={{0,4},{1,17},{2,6},{3,19},{4,8},{5,21},{6,10},{7,23},{8,12},{9,25}... | collective-permute-start | bytes 1179656 | tf_op jit(solution)/shard_map/ppermute | solution.py:62
  123.5 55.3 %copy-start.3 = (f32[256,256]{1,0:T(8,128)S(1)}, f32[256,256]{1,0:T(8,128)}, u32[]{:S(2)}) copy-start(f32[256,256]{1,0:T(8,128)} %get-tuple-element.24.near.refs_9_) | copy-start | bytes 786436
  123.5 55.3 %copy-start.9 = (f32[8,128]{1,0:T(8,128)S(1)}, f32[8,128]{1,0:T(8,128)}, u32[]{:S(2)}) copy-start(f32[8,128]{1,0:T(8,128)} %get-tuple-element.25.rho_ref.refs_10_) | copy-start | bytes 12292
  134.8 16.0 %collective-permute-start.22 = (f32[24,256]{1,0:T(8,128)S(1)}, f32[24,256]{1,0:T(8,128)S(1)}, u32[]{:S(2)}, u32[]{:S(2)}) collective-permute-start(f32[24,256]{1,0:T(8,128)S(1)} %reduce_sum.38), channel_id=1, source_target_pairs={{0,1},{1,0},{2,3},{3,2},{4,5},{5,4},{6,7},{7,6},{8,9},{9,8},{10,11... | collective-permute-start | bytes 73736 | tf_op jit(solution)/shard_map/ppermute | solution.py:62
  151.5 12.5 %all-to-all-start.4 = ((f32[8,24,256]{2,1,0:T(8,128)}), f32[8,24,256]{2,1,0:T(8,128)}, u32[]{:S(2)}, u32[]{:S(2)}) async-start(f32[8,24,256]{2,1,0:T(8,128)} %broadcast_in_dim.14), calls=%async_computation.4 | async-start | bytes 393216 | tf_op jit(solution)/shard_map/all_to_all | solution.py:74
  157.0 0.9 copy-start.5
  158.0 11.6 %collective-permute-start.16 = (s16[1280,256]{1,0:T(8,128)(2,1)S(1)}, s16[1280,256]{1,0:T(8,128)(2,1)}, u32[]{:S(2)}, u32[]{:S(2)}) collective-permute-start(s16[1280,256]{1,0:T(8,128)(2,1)S(1)} %shard_map.117.refs_0_), channel_id=1, source_target_pairs={{0,12},{1,49},{2,14},{3,51},{4,0},{5,53},{6,2},{7,55},{8,4},{9,57}... | collective-permute-start | bytes 1966088 | tf_op jit(solution)/shard_map/ppermute | solution.py:62
  158.6 11.4 %collective-permute-start.17 = (s16[1280,256]{1,0:T(8,128)(2,1)S(1)}, s16[1280,256]{1,0:T(8,128)(2,1)}, u32[]{:S(2)}, u32[]{:S(2)}) collective-permute-start(s16[1280,256]{1,0:T(8,128)(2,1)S(1)} %shard_map.117.refs_0_), channel_id=1, source_target_pairs={{0,8},{1,33},{2,10},{3,35},{4,12},{5,37},{6,14},{7,39},{8,0},{9,41... | collective-permute-start | bytes 1966088 | tf_op jit(solution)/shard_map/ppermute | solution.py:62
  159.3 19.5 %collective-permute-start.18 = (s16[1280,256]{1,0:T(8,128)(2,1)S(1)}, s16[1280,256]{1,0:T(8,128)(2,1)}, u32[]{:S(2)}, u32[]{:S(2)}) collective-permute-start(s16[1280,256]{1,0:T(8,128)(2,1)S(1)} %shard_map.117.refs_0_), channel_id=1, source_target_pairs={{0,4},{1,17},{2,6},{3,19},{4,8},{5,21},{6,10},{7,23},{8,12},{9,25}... | collective-permute-start | bytes 1966088 | tf_op jit(solution)/shard_map/ppermute | solution.py:62
  165.7 22.2 %all-to-all-start.5 = ((f32[16,24,256]{2,1,0:T(8,128)}), f32[16,24,256]{2,1,0:T(8,128)S(1)}, u32[]{:S(2)}, u32[]{:S(2)}) async-start(f32[16,24,256]{2,1,0:T(8,128)} %broadcast_in_dim.15), calls=%async_computation.5 | async-start | bytes 786432 | tf_op jit(solution)/shard_map/all_to_all | solution.py:74
  178.8 9.1 %copy-start.7 = (f32[256,256]{1,0:T(8,128)S(1)}, f32[256,256]{1,0:T(8,128)}, u32[]{:S(2)}) copy-start(f32[256,256]{1,0:T(8,128)} %copy-done.6) | copy-start | bytes 786436

commit v6 on v5

--- a/solution.py
+++ b/solution.py
@@ -16,6 +16,7 @@
 CHUNK = 640
 ROWS = 2560
 CAP = 20
+SLOTS = 120
 F32 = jnp.float32
 BF16 = jnp.bfloat16
 AXES = ("z", "y", "x", "h", "c")
@@ -74,16 +75,17 @@
     return lax.all_to_all(value, axes, 0, 0, tiled=True)
 
 
-def sum_to_all(value, count, axes):
-    return jnp.sum(exchange(jnp.broadcast_to(value, (count, *value.shape)), axes), axis=0)
-
-
-def sum_slices(value, axes):
-    return jnp.sum(exchange(value.reshape(16, -1, R), axes), axis=0)
-
-
-def spread_slices(value, axes):
-    return exchange(jnp.broadcast_to(value, (16, *value.shape)), axes).reshape(-1, R)
+def fan_kernel(got, out):
+    count = got.shape[0]
+    total_ = got[0]
+    for n in range(1, count):
+        total_ = total_ + got[n]
+    for n in range(out.shape[0]):
+        out[n] = total_
+
+
+def fan(got, copies):
+    return call(fan_kernel, [(copies, *got.shape[1:])], "v" + "v", [], got)[0]
 
 
 def split(a):
@@ -232,8 +234,8 @@
 
 def local_kernel(
     live, patient_at, code_at, month_at, near, rho_ref, patient_hbm, month_hbm, tiles_hbm, duals_hbm,
-    prod_hbm, v_hbm, a0, q1, q2, q3,
-    patient, month, tiles, duals, prod, grad, u_part, g_part, v, own, coded, held, sems, outs,
+    prod_hbm, v_hbm, g_hbm, q1, q2, q3,
+    patient, month, tiles, duals, prod, grad, u_part, g_part, v, g_own, coded, held, sems, outs,
 ):
     copies = [
         pltpu.make_async_copy(src, dst, sems.at[n])
@@ -264,42 +266,34 @@
         return 0
 
     lax.fori_loop(0, (live[0] + 3) // 4, visit, 0)
-    prod_out = pltpu.make_async_copy(prod, prod_hbm, outs.at[4])
+    prod_out = pltpu.make_async_copy(prod, prod_hbm.at[pl.ds(0, CAP)], outs.at[4])
     prod_out.start()
     near_parts = split(near[...])
     copies[3].wait()
 
-    def chunk(k, _):
+    for b in range(16):
+        g_own[b * SHARE : (b + 1) * SHARE, :] = grad[pl.ds(block_row(place, 0, b), SHARE), :]
+    g_out = pltpu.make_async_copy(g_own, g_hbm, outs.at[3])
+    g_out.start()
+
+    def chunk(step, _):
+        k = lax.rem(step + 1, 3) + 1
         for b in range(16):
             at = pl.ds(block_row(place, k, b), SHARE)
             u_part[b * SHARE : (b + 1) * SHARE, :] = duals[at, :]
             g_part[b * SHARE : (b + 1) * SHARE, :] = grad[at, :]
-        u = u_part[...]
-        g = g_part[...] * (1.0 / rho)
-        once = u + dot3(split(g - u), near_parts)
-        twice = once + dot3(split(g - once), near_parts)
-        v[k] = twice
-        pltpu.make_async_copy(v.at[k], v_hbm.at[k], outs.at[5 + k]).start()
+        once, twice = two_rounds(u_part[...], g_part[...], rho, near_parts)
+        v[k - 1] = twice
+        pltpu.make_async_copy(v.at[k - 1], v_hbm.at[k - 1], outs.at[4 + k]).start()
         u_part[...] = rho * once
         g_part[...] = rho * twice
-
-        @pl.when(k == 0)
-        def _():
-            for b in range(16):
-                own[b * 80 : b * 80 + SHARE, :] = u_part[b * SHARE : (b + 1) * SHARE, :]
-                own[b * 80 + SHARE : b * 80 + 80, :] = g_part[b * SHARE : (b + 1) * SHARE, :]
-            pltpu.make_async_copy(own, a0, outs.at[3]).start()
-
-        @pl.when(k > 0)
-        def _():
-            for b in range(16):
-                for q, part in enumerate((u_part, g_part)):
-                    whole, code = encode(part[b * SHARE : (b + 1) * SHARE, :])
-                    row = b * 80 + q * SHARE
-                    coded[row : row + SHARE, :] = whole
-                    coded[1280 + 2 * b + q : 1281 + 2 * b + q, :] = code
-            held[k - 1] = to_codes(coded[...])
-
+        for b in range(16):
+            for q, part in enumerate((u_part, g_part)):
+                whole, code = encode(part[b * SHARE : (b + 1) * SHARE, :])
+                row = b * 80 + q * SHARE
+                coded[row : row + SHARE, :] = whole
+                coded[1280 + 2 * b + q : 1281 + 2 * b + q, :] = code
+        held[k - 1] = to_codes(coded[...])
         for n, out in enumerate((q1, q2, q3)):
 
             @pl.when(k == n + 1)
@@ -308,13 +302,43 @@
 
         return 0
 
-    lax.fori_loop(0, 4, chunk, 0)
+    lax.fori_loop(0, 3, chunk, 0)
     for n, out in enumerate((q1, q2, q3)):
         pltpu.make_async_copy(held.at[n], out, outs.at[n]).wait()
     prod_out.wait()
-    pltpu.make_async_copy(own, a0, outs.at[3]).wait()
-    for k in range(4):
+    g_out.wait()
+    for k in range(3):
         pltpu.make_async_copy(v.at[k], v_hbm.at[k], outs.at[5 + k]).wait()
+
+
+def two_rounds(u, g, rho, near_parts):
+    g = g * (1.0 / rho)
+    once = u + dot3(split(g - u), near_parts)
+    return once, once + dot3(split(g - once), near_parts)
+
+
+def own_kernel(near, rho_ref, g_part, duals_hbm, a0, v0, u_part, sems):
+    place = placed()
+    copies = [
+        pltpu.make_async_copy(
+            duals_hbm.at[pl.ds(block_row(place, 0, b), SHARE), :],
+            u_part.at[pl.ds(b * SHARE, SHARE), :],
+            sems.at[b],
+        )
+        for b in range(16)
+    ]
+    for copy in copies:
+        copy.start()
+    rho = rho_ref[0:1, 0:1]
+    near_parts = split(near[...])
+    for copy in copies:
+        copy.wait()
+    once, twice = two_rounds(u_part[...], g_part[...], rho, near_parts)
+    v0[...] = twice
+    u_part[...] = rho * once
+    for b in range(16):
+        a0[b * 80 : b * 80 + SHARE, :] = u_part[b * SHARE : (b + 1) * SHARE, :]
+        a0[b * 80 + SHARE : b * 80 + 80, :] = rho * v0[b * SHARE : (b + 1) * SHARE, :]
 
 
 def sum_kernel(own, r1, r2, r3, s0, q1, q2, q3, acc, part, coded):
@@ -372,8 +396,16 @@
     code_ref[...] = gram_of(z2, lax.Precision.HIGHEST)
 
 
-def month_kernel(live, code_at, month_at, w0, w1, w2, w3, prod, code, out, natural, part):
+def month_kernel(
+    live, code_at, month_at, w0, w1, w2, w3, prod_hbm, code, out, natural, part, prod, sems
+):
     place = placed()
+
+    def fetch(k, _):
+        pltpu.make_async_copy(prod_hbm.at[k], prod.at[k], sems.at[k]).start()
+        return 0
+
+    lax.fori_loop(0, live[0], fetch, 0)
     for k, w in enumerate((w0, w1, w2, w3)):
         part[...] = from_codes(w[...])
         for b in range(16):
@@ -386,6 +418,7 @@
 
     def visit(k, _):
         at = pl.ds(pl.multiple_of(code_at[k] * BLOCK, BLOCK), BLOCK)
+        pltpu.make_async_copy(prod_hbm.at[k], prod.at[k], sems.at[k]).wait()
         column = jnp.sum(prod[k] * natural[at, :], axis=0, keepdims=True)
         m = month_at[k]
         out[pl.ds((m // 8) * 24 + m % 8, 1), :] += column
@@ -397,7 +430,7 @@
 def duals_kernel(*refs):
     place = placed()
     both, two = refs[0:4], refs[4:8]
-    v, near, _, out, part, z0_part, z1_part, z2_part = refs[8:]
+    v0, v, near, _, out, part, z0_part, z1_part, z2_part, v_part = refs[8:]
     near_parts = split(near[...])
 
     def chunk(k, _):
@@ -407,6 +440,7 @@
             def _(n=n):
                 part[0:1280, :] = from_codes(both[n][...])
                 part[1280:, :] = from_codes(two[n][...])
+                v_part[...] = v0[...] if n == 0 else v[n - 1]
 
         for b in range(16):
             rows = slice(b * SHARE, (b + 1) * SHARE)
@@ -418,7 +452,7 @@
         z0 = z0_part[...]
         z1 = z1_part[...]
         inner = z0 - dot3(split(z0), near_parts) + 2.0 * z1
-        z2_part[...] = v[k] + dot3(split(inner), near_parts) - z1 - z2_part[...]
+        z2_part[...] = v_part[...] + dot3(split(inner), near_parts) - z1 - z2_part[...]
         for b in range(16):
             out[pl.ds(block_row(place, k, b), SHARE), :] = z2_part[b * SHARE : (b + 1) * SHARE, :]
         return 0
@@ -458,32 +492,36 @@
         inverse_kernel, [(R, R), (8, 128), (384, R)], "vv" + "vvv", [(R, R), (R, R)],
         patient_factor, month_factor, limit=None,
     )
-    m = sum_slices(weights, PLANE)
+    m = exchange(weights.reshape(16, -1, R), PLANE)
 
     def codes(rows):
         return jax.ShapeDtypeStruct((rows, R), jnp.int16)
 
     tops = [coded_rows(n) for n in (32, 8, 2)]
-    prod, v, *s = call(
+    prod, v, g_own, *s = call(
         local_kernel,
-        [(CAP, BLOCK, R), (4, CHUNK, R), (2 * CHUNK, R)] + [codes(tops[0])] * 3,
+        [(SLOTS, BLOCK, R), (3, CHUNK, R), (CHUNK, R)] + [codes(tops[0])] * 3,
         "ssssvvhhhh" + "hhhhhh",
         [
             pltpu.VMEM((1024, R), BF16), (MONTHS, R), pltpu.VMEM((CAP, BLOCK, BLOCK), BF16),
-            (ROWS, R), (CAP, BLOCK, R), (ROWS, R), (CHUNK, R), (CHUNK, R), (4, CHUNK, R),
-            (2 * CHUNK, R), (tops[0], R), pltpu.VMEM((3, tops[0], R), jnp.int16),
-            pltpu.SemaphoreType.DMA((4,)), pltpu.SemaphoreType.DMA((9,)),
+            (ROWS, R), (CAP, BLOCK, R), (ROWS, R), (CHUNK, R), (CHUNK, R), (3, CHUNK, R),
+            (CHUNK, R), (tops[0], R), pltpu.VMEM((3, tops[0], R), jnp.int16),
+            pltpu.SemaphoreType.DMA((4,)), pltpu.SemaphoreType.DMA((8,)),
         ],
         live_count, patient_block, code_block, month_index,
         near, rho, patient_factor, month_factor, tile_values, scaled_duals, limit=None,
     )
-    s = scatter_sum(s, first_move)
-    m = sum_to_all(m, 4, "z")
-    mine = spread_slices(m, PLANE)
+    s = [send(s[k - 1], first_move(k)) for k in (1, 2, 3)]
+    a0, v0 = call(
+        own_kernel, [(2 * CHUNK, R), (CHUNK, R)], "vvvh" + "vv",
+        [(CHUNK, R), pltpu.SemaphoreType.DMA((16,))], near, rho, g_own, scaled_duals,
+    )
+    m = exchange(fan(m, 4), "z")
+    mine = exchange(fan(m, 16), PLANE).reshape(-1, R)
     other = send(mine, CORE_MOVE)
     s = call(
         sum_kernel, [(320, R)] + [codes(tops[1])] * 3, "vvvv" + "vvvv",
-        [(2 * CHUNK, R), (tops[0], R), (tops[1], R)], *s,
+        [(2 * CHUNK, R), (tops[0], R), (tops[1], R)], a0, *s,
     )
     s = scatter_sum(s, second_move)
     s = call(
@@ -503,16 +541,18 @@
     two = gather(two, first_move)
     both = gather(both, first_move)
     (sums,) = call(
-        month_kernel, [(384, R)], "sssvvvvvv" + "v", [(ROWS, R), (768, R)],
+        month_kernel, [(384, R)], "sssvvvvhv" + "v",
+        [(ROWS, R), (768, R), (CAP, BLOCK, R), pltpu.SemaphoreType.DMA((CAP,))],
         live_count, code_block, month_index, *two, prod, code_gram,
     )
-    t = sum_slices(sums, PLANE)
-    t = t + send(t, CORE_MOVE)
-    t = sum_to_all(t, 8, ("z", "h"))
-    t = spread_slices(t, PLANE)
+    t = exchange(sums.reshape(16, -1, R), PLANE)
+    t = fan(t, 1)
+    t = jnp.concatenate([t, send(t, CORE_MOVE)], 0)
+    t = exchange(fan(t, 8), ("z", "h"))
+    t = exchange(fan(t, 16), PLANE).reshape(-1, R)
     (duals,) = call(
-        duals_kernel, [(ROWS, R)], "v" * 12, [(2048, R)] + [(CHUNK, R)] * 3,
-        *both, *two, v, near, rho,
+        duals_kernel, [(ROWS, R)], "v" * 13, [(2048, R)] + [(CHUNK, R)] * 4,
+        *both, *two, v0, v, near, rho,
     )
     (new_months,) = call(
         tail_kernel, [(MONTHS, R)], "vvvv", [(R, R), (R, R), (BLOCK, R)], t, gram, month_factor

time: 195 us -> 199 us (1.021)
  Pallas kernels: 36.2 us -> 41.5 us
    ppermute x23, starting transfers between devices: 40 us -> 33.7 us  [send(): return lax.ppermute(value, AXES, pairs)]
    pallas_call x9 -> x15, Pallas kernels: 36.2 us -> 41.5 us  [call(): pl.pallas_call(body, out_shape=[s if isinstance(s, jax.ShapeDtypeStruct)...]
    all_to_all x3, starting transfers between devices: 14.9 us -> 19.3 us  [exchange(): return lax.all_to_all(value, axes, 0, 0, tiled=True)]
    unnamed x27 -> x35, local copies, waits for them, and re-layouts: 2.32 us -> 5.67 us
    ppermute x23, waiting for transfers between devices: 43 us -> 45.7 us  [send(): return lax.ppermute(value, AXES, pairs)]
    broadcast_in_dim x4 -> x0, local copies, waits for them, and re-layouts: 2.15 us -> none  [the longest x2 1.34 us: sum_to_all(): jnp.broadcast_to(value, (count, *value.shape))]
  transfers between devices with their start and end apart: 26 -> 26, of which waited for: 16 -> 17; matrix products, arithmetic and copies ran while one was open for 1% -> 0% of each run, Pallas kernels for 11% -> 12%
where the time goes in v6:
time: 199 us
  starting transfers between devices  53 us (27%)
  waiting for transfers between devices  49.2 us (25%)
  blocking collectives  47.6 us (24%)
  Pallas kernels  41.5 us (21%)
  local copies, waits for them, and re-layouts  5.7 us (3%)
    all_to_all x3, blocking collectives, exchange(): return lax.all_to_all(value, axes, 0, 0, tiled=True)  47.6 us
    ppermute x23, waiting for transfers between devices, send(): return lax.ppermute(value, AXES, pairs)  45.7 us
    pallas_call x15, Pallas kernels, call(): pl.pallas_call(body, out_shape=[s if isinstance(s, jax.ShapeDtypeStruct)...  41.5 us
    ppermute x23, starting transfers between devices, send(): return lax.ppermute(value, AXES, pairs)  33.7 us
    all_to_all x3, starting transfers between devices, exchange(): return lax.all_to_all(value, axes, 0, 0, tiled=True)  19.3 us
    unnamed x35, local copies, waits for them, and re-layouts  5.67 us
  transfers between devices with their start and end apart: 26, of which 17 were waited for; matrix products, arithmetic and copies ran while one was open for 0% of the time, Pallas kernels for 12%

profile of v6, /device:TPU:1, one launch (start us, length us, event | category | flops | bytes accessed | tf_op | source)
XLA Modules:
  0.0 198.5 jit_solution(3619532092757516888)
XLA Ops:
  0.6 7.5 %shard_map.112 = (f32[256,256]{1,0:T(8,128)}, f32[8,128]{1,0:T(8,128)}, f32[384,256]{1,0:T(8,128)}) custom-call(bf16[1024,256]{1,0:T(8,128)(2,1)} %patient_hbm.1, f32[120,256]{1,0:T(8,128)} %month.5), custom_call_target="tpu_custom_call" | custom-call | tf_op jit(solution)/shard_map/pallas_call | solution.py:477
  8.2 17.1 %all_to_all.30.got = f32[16,24,256]{2,1,0:T(8,128)S(1)} all-to-all(f32[16,24,256]{2,1,0:T(8,128)} %bitcast.20), channel_id=1, replica_groups=mesh['z'=4,'y'=4,'x'=4,'h'=2,'c'=2] {'y','x'}, dimensions={0} | all-to-all | bytes 786432 | tf_op jit(solution)/shard_map/all_to_all | solution.py:75
  25.3 0.7 shard_map.117
  25.9 5.6 %all-to-all-start.1 = ((f32[4,24,256]{2,1,0:T(8,128)}), f32[4,24,256]{2,1,0:T(8,128)S(1)}, u32[]{:S(2)}, u32[]{:S(2)}) async-start(f32[4,24,256]{2,1,0:T(8,128)} %shard_map.117), calls=%async_computation.1 | async-start | bytes 196608 | tf_op jit(solution)/shard_map/all_to_all | solution.py:75
  32.2 0.0 copy-start
  32.2 0.0 copy-start.13
  32.2 8.5 %shard_map.113 = (f32[120,128,256]{2,1,0:T(8,128)}, f32[3,640,256]{2,1,0:T(8,128)}, f32[640,256]{1,0:T(8,128)}, s16[1312,256]{1,0:T(8,128)(2,1)}, s16[1312,256]{1,0:T(8,128)(2,1)}, /*index=5*/s16[1312,256]{1,0:T(8,128)(2,1)}) custom-call(s32[1]{0:T(128)S(6)} %copy.15.live, s32[20]{0:T(128)} %patient_at.1, s32[20]{0:T(128)} %code_at.3, s32[20]{0:T(128)} %month_at.3, ...), custom_call_target="tpu_custom_call" | custom-call | tf_op jit(solution)/shard_map/pallas_call | solution.py:477
  40.8 0.1 collective-permute-start
  40.9 1.8 collective-permute-start.1
  42.7 0.8 collective-permute-start.2
  43.6 19.7 %all_to_all.31 = f32[16,24,256]{2,1,0:T(8,128)S(1)} all-to-all(f32[16,24,256]{2,1,0:T(8,128)S(1)} %shard_map.118), channel_id=1, replica_groups=mesh['z'=4,'y'=4,'x'=4,'h'=2,'c'=2] {'y','x'}, dimensions={0} | all-to-all | bytes 786432 | tf_op jit(solution)/shard_map/all_to_all | solution.py:75
  63.3 3.7 %collective-permute-start.9 = (f32[384,256]{1,0:T(8,128)S(1)}, f32[384,256]{1,0:T(8,128)S(1)}, u32[]{:S(2)}, u32[]{:S(2)}) collective-permute-start(f32[384,256]{1,0:T(8,128)S(1)} %bitcast.13), channel_id=1, source_target_pairs={{0,1},{1,0},{2,3},{3,2},{4,5},{5,4},{6,7},{7,6},{8,9},{9,8},{10,11... | collective-permute-start | bytes 1179656 | tf_op jit(solution)/shard_map/ppermute | solution.py:63
  66.9 1.1 copy-done.5
  68.0 2.2 %shard_map.114 = (f32[1280,256]{1,0:T(8,128)S(1)}, f32[640,256]{1,0:T(8,128)S(1)}) custom-call(f32[256,256]{1,0:T(8,128)S(1)} %copy-done.1, f32[8,128]{1,0:T(8,128)S(1)} %copy-done.13, f32[640,256]{1,0:T(8,128)S(1)} %copy-done.5, f32[2560,256]{1,0:T(8,128)S(1)} %copy-done), custom_call_target="tpu_custom_call" | custom-call | tf_op jit(solution)/shard_map/pallas_call | solution.py:477
  70.2 0.8 copy-done.3
  71.1 2.6 %shard_map.115 = (f32[320,256]{1,0:T(8,128)S(1)}, s16[336,256]{1,0:T(8,128)(2,1)S(1)}, s16[336,256]{1,0:T(8,128)(2,1)S(1)}, s16[336,256]{1,0:T(8,128)(2,1)S(1)}) custom-call(f32[1280,256]{1,0:T(8,128)S(1)} %get-tuple-element.29.own, s16[1312,256]{1,0:T(8,128)(2,1)} %collective-permute-done.r1, s16[1312,256]{1,0:T(8,128)(2,1)} %collective-permute-done.1.r2, ...), custom_call_target="tpu_custom_call" | custom-call | tf_op jit(solution)/shard_map/pallas_call | solution.py:477
  73.7 0.0 copy-start.14
  73.8 0.0 copy-start.15
  73.8 0.9 collective-permute-start.3
  74.6 3.0 %collective-permute-start.4 = (s16[336,256]{1,0:T(8,128)(2,1)S(1)}, s16[336,256]{1,0:T(8,128)(2,1)S(1)}, u32[]{:S(2)}, u32[]{:S(2)}) collective-permute-start(s16[336,256]{1,0:T(8,128)(2,1)S(1)} %get-tuple-element.35), channel_id=1, source_target_pairs={{0,32},{1,9},{2,34},{3,11},{4,36},{5,13},{6,38},{7,15},{8,40},{9,1... | collective-permute-start | bytes 516104 | tf_op jit(solution)/shard_map/ppermute | solution.py:63
  77.7 1.9 collective-permute-done.3.r1
  79.6 2.9 %collective-permute-done.4.r2 = s16[336,256]{1,0:T(8,128)(2,1)S(1)} collective-permute-done((s16[336,256]{1,0:T(8,128)(2,1)S(1)}, s16[336,256]{1,0:T(8,128)(2,1)S(1)}, u32[]{:S(2)}, u32[]{:S(2)}) %collective-permute-start.4) | collective-permute-done | bytes 172064 | tf_op jit(solution)/shard_map/ppermute | solution.py:63
  82.6 0.3 shard_map.116
  82.9 2.0 collective-permute-start.6
  84.8 2.1 %collective-permute-start.7 = (s16[96,256]{1,0:T(8,128)(2,1)S(1)}, s16[96,256]{1,0:T(8,128)(2,1)S(1)}, u32[]{:S(2)}, u32[]{:S(2)}) collective-permute-start(s16[96,256]{1,0:T(8,128)(2,1)S(1)} %get-tuple-element.39), channel_id=1, source_target_pairs={{0,128},{1,129},{2,130},{3,131},{4,132},{5,133},{6,134},{7,135},{8... | collective-permute-start | bytes 147464 | tf_op jit(solution)/shard_map/ppermute | solution.py:63
  86.9 1.2 collective-permute-start.8
  88.1 2.0 %collective-permute-done.7.s2 = s16[96,256]{1,0:T(8,128)(2,1)S(1)} collective-permute-done((s16[96,256]{1,0:T(8,128)(2,1)S(1)}, s16[96,256]{1,0:T(8,128)(2,1)S(1)}, u32[]{:S(2)}, u32[]{:S(2)}) %collective-permute-start.7) | collective-permute-done | bytes 49184 | tf_op jit(solution)/shard_map/ppermute | solution.py:63
  90.1 0.5 collective-permute-done.8.s3
  90.7 1.4 shard_map.119
  92.1 2.6 %collective-permute-start.10 = (s16[128,256]{1,0:T(8,128)(2,1)S(1)}, s16[128,256]{1,0:T(8,128)(2,1)S(1)}, u32[]{:S(2)}, u32[]{:S(2)}) collective-permute-start(s16[128,256]{1,0:T(8,128)(2,1)S(1)} %get-tuple-element.43), channel_id=1, source_target_pairs={{0,192},{1,193},{2,194},{3,195},{4,196},{5,197},{6,198},{7,199},{8... | collective-permute-start | bytes 196616 | tf_op jit(solution)/shard_map/ppermute | solution.py:63
  94.7 0.3 collective-permute-start.12
  95.0 1.0 collective-permute-done.10
  96.0 2.7 %collective-permute-done.11 = s16[128,256]{1,0:T(8,128)(2,1)S(1)} collective-permute-done((s16[128,256]{1,0:T(8,128)(2,1)S(1)}, s16[128,256]{1,0:T(8,128)(2,1)S(1)}, u32[]{:S(2)}, u32[]{:S(2)}) %collective-permute-start.11) | collective-permute-done | bytes 65568 | tf_op jit(solution)/shard_map/ppermute | solution.py:63
  98.7 1.6 collective-permute-done.12
  100.3 1.6 collective-permute-start.13
  101.9 0.7 collective-permute-start.15
  102.5 5.4 %collective-permute-done.13.r1 = s16[512,256]{1,0:T(8,128)(2,1)S(1)} collective-permute-done((s16[512,256]{1,0:T(8,128)(2,1)S(1)}, s16[512,256]{1,0:T(8,128)(2,1)S(1)}, u32[]{:S(2)}, u32[]{:S(2)}) %collective-permute-start.13) | collective-permute-done | bytes 262176 | tf_op jit(solution)/shard_map/ppermute | solution.py:63
  108.0 0.7 collective-permute-done.14.r2
  108.7 2.7 %collective-permute-done.15.r3 = s16[512,256]{1,0:T(8,128)(2,1)S(1)} collective-permute-done((s16[512,256]{1,0:T(8,128)(2,1)S(1)}, s16[512,256]{1,0:T(8,128)(2,1)S(1)}, u32[]{:S(2)}, u32[]{:S(2)}) %collective-permute-start.15) | collective-permute-done | bytes 262176 | tf_op jit(solution)/shard_map/ppermute | solution.py:63
  111.4 0.7 copy-done.8
  112.1 2.0 %collective-permute-start.19 = (s16[768,256]{1,0:T(8,128)(2,1)S(1)}, s16[768,256]{1,0:T(8,128)(2,1)S(1)}, u32[]{:S(2)}, u32[]{:S(2)}) collective-permute-start(s16[768,256]{1,0:T(8,128)(2,1)S(1)} %pad_add_fusion.refs_4_.w0), channel_id=1, source_target_pairs={{0,12},{1,49},{2,14},{3,51},{4,0},{5,53},{6,2},{7,55},{8,4},{9,57}... | collective-permute-start | bytes 1179656 | tf_op jit(solution)/shard_map/ppermute | solution.py:63
  114.2 0.7 collective-permute-start.21
  114.8 8.3 %collective-permute-done.19.refs_5_.w1 = s16[768,256]{1,0:T(8,128)(2,1)S(1)} collective-permute-done((s16[768,256]{1,0:T(8,128)(2,1)S(1)}, s16[768,256]{1,0:T(8,128)(2,1)S(1)}, u32[]{:S(2)}, u32[]{:S(2)}) %collective-permute-start.19) | collective-permute-done | bytes 393248 | tf_op jit(solution)/shard_map/ppermute | solution.py:63
  123.1 3.4 %collective-permute-done.21.refs_7_.w3 = s16[768,256]{1,0:T(8,128)(2,1)S(1)} collective-permute-done((s16[768,256]{1,0:T(8,128)(2,1)S(1)}, s16[768,256]{1,0:T(8,128)(2,1)S(1)}, u32[]{:S(2)}, u32[]{:S(2)}) %collective-permute-start.21) | collective-permute-done | bytes 393248 | tf_op jit(solution)/shard_map/ppermute | solution.py:63
  126.5 2.0 shard_map.122
  128.5 10.9 %all_to_all.32.got = f32[16,24,256]{2,1,0:T(8,128)S(1)} all-to-all(f32[16,24,256]{2,1,0:T(8,128)S(1)} %bitcast.15), channel_id=1, replica_groups=mesh['z'=4,'y'=4,'x'=4,'h'=2,'c'=2] {'y','x'}, dimensions={0} | all-to-all | bytes 786432 | tf_op jit(solution)/shard_map/all_to_all | solution.py:75
  139.4 8.6 %collective-permute-start.22 = (f32[1,24,256]{2,1,0:T(8,128)S(1)}, f32[1,24,256]{2,1,0:T(8,128)S(1)}, u32[]{:S(2)}, u32[]{:S(2)}) collective-permute-start(f32[1,24,256]{2,1,0:T(8,128)S(1)} %shard_map.123), channel_id=1, source_target_pairs={{0,1},{1,0},{2,3},{3,2},{4,5},{5,4},{6,7},{7,6},{8,9},{9,8},{10,11... | collective-permute-start | bytes 73736 | tf_op jit(solution)/shard_map/ppermute | solution.py:63
  148.0 0.8 collective-permute-done.22
  148.9 0.7 shard_map.124
  149.6 10.2 %all-to-all-start.4 = ((f32[8,24,256]{2,1,0:T(8,128)}), f32[8,24,256]{2,1,0:T(8,128)S(1)}, u32[]{:S(2)}, u32[]{:S(2)}) async-start(f32[8,24,256]{2,1,0:T(8,128)} %shard_map.124), calls=%async_computation.4 | async-start | bytes 393216 | tf_op jit(solution)/shard_map/all_to_all | solution.py:75
  159.8 0.9 copy-done.7
  160.7 0.9 copy-done.9
  161.7 0.6 collective-permute-start.16
  162.3 0.7 collective-permute-start.17
  163.1 0.2 collective-permute-start.18
  163.3 3.4 %all-to-all-done.4.got = f32[8,24,256]{2,1,0:T(8,128)S(1)} async-done(((f32[8,24,256]{2,1,0:T(8,128)}), f32[8,24,256]{2,1,0:T(8,128)S(1)}, u32[]{:S(2)}, u32[]{:S(2)}) %all-to-all-start.4) | async-done | bytes 196640 | tf_op jit(solution)/shard_map/all_to_all | solution.py:75
  166.7 0.8 shard_map.125
  167.5 3.6 %all-to-all-start.5 = ((f32[16,24,256]{2,1,0:T(8,128)}), f32[16,24,256]{2,1,0:T(8,128)S(1)}, u32[]{:S(2)}, u32[]{:S(2)}) async-start(f32[16,24,256]{2,1,0:T(8,128)} %shard_map.125), calls=%async_computation.5 | async-start | bytes 786432 | tf_op jit(solution)/shard_map/all_to_all | solution.py:75
  171.0 0.6 collective-permute-done.16.refs_1_
  171.6 2.1 %collective-permute-done.17.refs_2_ = s16[1280,256]{1,0:T(8,128)(2,1)} collective-permute-done((s16[1280,256]{1,0:T(8,128)(2,1)S(1)}, s16[1280,256]{1,0:T(8,128)(2,1)}, u32[]{:S(2)}, u32[]{:S(2)}) %collective-permute-start.17) | collective-permute-done | bytes 655392 | tf_op jit(solution)/shard_map/ppermute | solution.py:63
  173.7 9.1 %collective-permute-done.18.refs_3_ = s16[1280,256]{1,0:T(8,128)(2,1)} collective-permute-done((s16[1280,256]{1,0:T(8,128)(2,1)S(1)}, s16[1280,256]{1,0:T(8,128)(2,1)}, u32[]{:S(2)}, u32[]{:S(2)}) %collective-permute-start.18) | collective-permute-done | bytes 655392 | tf_op jit(solution)/shard_map/ppermute | solution.py:63
  182.8 1.1 copy-done.4
  183.9 9.0 %shard_map.121 = f32[2560,256]{1,0:T(8,128)} custom-call(s16[1280,256]{1,0:T(8,128)(2,1)S(1)} %shard_map.120.refs_0_, s16[1280,256]{1,0:T(8,128)(2,1)} %collective-permute-done.16.refs_1_, s16[1280,256]{1,0:T(8,128)(2,1)} %collective-permute-done.17.refs_2_, s16[1280,256]{1,0:T(8,128)(2,1)} %collective-permute-done.18.refs_3_, ...), custom_call_target="tpu_custom_call" | custom-call | tf_op jit(solution)/shard_map/pallas_call | solution.py:477
  192.9 5.6 %shard_map.126 = f32[120,256]{1,0:T(8,128)} custom-call(f32[384,256]{1,0:T(8,128)S(1)} %bitcast.12, f32[256,256]{1,0:T(8,128)S(1)} %copy-done.11, f32[120,256]{1,0:T(8,128)S(1)} %copy-done.2), custom_call_target="tpu_custom_call" | custom-call | tf_op jit(solution)/shard_map/pallas_call | solution.py:477
  (48 shorter events, 0.3 us)
Async XLA Ops:
  25.9 17.6 %all-to-all-start.1 = ((f32[4,24,256]{2,1,0:T(8,128)}), f32[4,24,256]{2,1,0:T(8,128)S(1)}, u32[]{:S(2)}, u32[]{:S(2)}) async-start(f32[4,24,256]{2,1,0:T(8,128)} %shard_map.117), calls=%async_computation.1 | async-start | bytes 196608 | tf_op jit(solution)/shard_map/all_to_all | solution.py:75
  32.2 34.7 %copy-start = (f32[2560,256]{1,0:T(8,128)S(1)}, f32[2560,256]{1,0:T(8,128)}, u32[]{:S(2)}) copy-start(f32[2560,256]{1,0:T(8,128)} %duals_hbm.3) | copy-start | bytes 7864324
  32.2 34.7 %copy-start.1 = (f32[256,256]{1,0:T(8,128)S(1)}, f32[256,256]{1,0:T(8,128)}, u32[]{:S(2)}) copy-start(f32[256,256]{1,0:T(8,128)} %get-tuple-element.26.near.refs_10_) | copy-start | bytes 786436
  32.2 34.7 %copy-start.13 = (f32[8,128]{1,0:T(8,128)S(1)}, f32[8,128]{1,0:T(8,128)}, u32[]{:S(2)}) copy-start(f32[8,128]{1,0:T(8,128)} %get-tuple-element.27.rho_ref.refs_11_) | copy-start | bytes 12292
  40.8 30.3 %collective-permute-start = (s16[1312,256]{1,0:T(8,128)(2,1)}, s16[1312,256]{1,0:T(8,128)(2,1)}, u32[]{:S(2)}, u32[]{:S(2)}) collective-permute-start(s16[1312,256]{1,0:T(8,128)(2,1)} %get-tuple-element.30), channel_id=1, source_target_pairs={{0,4},{1,17},{2,6},{3,19},{4,8},{5,21},{6,10},{7,23},{8,12},{9,25}... | collective-permute-start | bytes 2015240 | tf_op jit(solution)/shard_map/ppermute | solution.py:63
  40.9 30.2 %collective-permute-start.1 = (s16[1312,256]{1,0:T(8,128)(2,1)}, s16[1312,256]{1,0:T(8,128)(2,1)}, u32[]{:S(2)}, u32[]{:S(2)}) collective-permute-start(s16[1312,256]{1,0:T(8,128)(2,1)} %get-tuple-element.31), channel_id=1, source_target_pairs={{0,8},{1,33},{2,10},{3,35},{4,12},{5,37},{6,14},{7,39},{8,0},{9,41... | collective-permute-start | bytes 2015240 | tf_op jit(solution)/shard_map/ppermute | solution.py:63
  42.7 28.4 %collective-permute-start.2 = (s16[1312,256]{1,0:T(8,128)(2,1)}, s16[1312,256]{1,0:T(8,128)(2,1)}, u32[]{:S(2)}, u32[]{:S(2)}) collective-permute-start(s16[1312,256]{1,0:T(8,128)(2,1)} %get-tuple-element.32), channel_id=1, source_target_pairs={{0,12},{1,49},{2,14},{3,51},{4,0},{5,53},{6,2},{7,55},{8,4},{9,57}... | collective-permute-start | bytes 2015240 | tf_op jit(solution)/shard_map/ppermute | solution.py:63
  63.3 27.4 %collective-permute-start.9 = (f32[384,256]{1,0:T(8,128)S(1)}, f32[384,256]{1,0:T(8,128)S(1)}, u32[]{:S(2)}, u32[]{:S(2)}) collective-permute-start(f32[384,256]{1,0:T(8,128)S(1)} %bitcast.13), channel_id=1, source_target_pairs={{0,1},{1,0},{2,3},{3,2},{4,5},{5,4},{6,7},{7,6},{8,9},{9,8},{10,11... | collective-permute-start | bytes 1179656 | tf_op jit(solution)/shard_map/ppermute | solution.py:63
  66.9 1.1 copy-start.5
  70.2 0.9 copy-start.3
  71.1 19.6 %copy-start.2 = (f32[120,256]{1,0:T(8,128)S(1)}, f32[120,256]{1,0:T(8,128)}, u32[]{:S(2)}) copy-start(f32[120,256]{1,0:T(8,128)} %month.5) | copy-start | bytes 368644
  71.1 19.6 %copy-start.12 = (f32[40,256]{1,0:T(8,128)S(1)}, f32[40,256]{1,0:T(8,128)}, u32[]{:S(2)}) copy-start(f32[40,256]{1,0:T(8,128)} %z0_ref.1) | copy-start | bytes 122884
  73.7 52.8 %copy-start.14 = (s32[20]{0:T(128)S(1)}, s32[20]{0:T(128)}, u32[]{:S(2)}) copy-start(s32[20]{0:T(128)} %code_at.3) | copy-start | bytes 244
  73.8 52.8 %copy-start.15 = (s32[20]{0:T(128)S(1)}, s32[20]{0:T(128)}, u32[]{:S(2)}) copy-start(s32[20]{0:T(128)} %month_at.3) | copy-start | bytes 244
  73.8 5.8 %collective-permute-start.3 = (s16[336,256]{1,0:T(8,128)(2,1)S(1)}, s16[336,256]{1,0:T(8,128)(2,1)S(1)}, u32[]{:S(2)}, u32[]{:S(2)}) collective-permute-start(s16[336,256]{1,0:T(8,128)(2,1)S(1)} %get-tuple-element.34), channel_id=1, source_target_pairs={{0,16},{1,5},{2,18},{3,7},{4,20},{5,9},{6,22},{7,11},{8,24},{9,13}... | collective-permute-start | bytes 516104 | tf_op jit(solution)/shard_map/ppermute | solution.py:63
  74.6 7.9 %collective-permute-start.4 = (s16[336,256]{1,0:T(8,128)(2,1)S(1)}, s16[336,256]{1,0:T(8,128)(2,1)S(1)}, u32[]{:S(2)}, u32[]{:S(2)}) collective-permute-start(s16[336,256]{1,0:T(8,128)(2,1)S(1)} %get-tuple-element.35), channel_id=1, source_target_pairs={{0,32},{1,9},{2,34},{3,11},{4,36},{5,13},{6,38},{7,15},{8,40},{9,1... | collective-permute-start | bytes 516104 | tf_op jit(solution)/shard_map/ppermute | solution.py:63
  77.7 4.9 %collective-permute-start.5 = (s16[336,256]{1,0:T(8,128)(2,1)S(1)}, s16[336,256]{1,0:T(8,128)(2,1)S(1)}, u32[]{:S(2)}, u32[]{:S(2)}) collective-permute-start(s16[336,256]{1,0:T(8,128)(2,1)S(1)} %get-tuple-element.36), channel_id=1, source_target_pairs={{0,48},{1,13},{2,50},{3,15},{4,52},{5,1},{6,54},{7,3},{8,56},{9,5}... | collective-permute-start | bytes 516104 | tf_op jit(solution)/shard_map/ppermute | solution.py:63
  82.9 5.3 %collective-permute-start.6 = (s16[96,256]{1,0:T(8,128)(2,1)S(1)}, s16[96,256]{1,0:T(8,128)(2,1)S(1)}, u32[]{:S(2)}, u32[]{:S(2)}) collective-permute-start(s16[96,256]{1,0:T(8,128)(2,1)S(1)} %get-tuple-element.38), channel_id=1, source_target_pairs={{0,64},{1,65},{2,66},{3,67},{4,68},{5,69},{6,70},{7,71},{8,72},{9,... | collective-permute-start | bytes 147464 | tf_op jit(solution)/shard_map/ppermute | solution.py:63
  84.8 5.3 %collective-permute-start.7 = (s16[96,256]{1,0:T(8,128)(2,1)S(1)}, s16[96,256]{1,0:T(8,128)(2,1)S(1)}, u32[]{:S(2)}, u32[]{:S(2)}) collective-permute-start(s16[96,256]{1,0:T(8,128)(2,1)S(1)} %get-tuple-element.39), channel_id=1, source_target_pairs={{0,128},{1,129},{2,130},{3,131},{4,132},{5,133},{6,134},{7,135},{8... | collective-permute-start | bytes 147464 | tf_op jit(solution)/shard_map/ppermute | solution.py:63
  86.9 3.7 %collective-permute-start.8 = (s16[96,256]{1,0:T(8,128)(2,1)S(1)}, s16[96,256]{1,0:T(8,128)(2,1)S(1)}, u32[]{:S(2)}, u32[]{:S(2)}) collective-permute-start(s16[96,256]{1,0:T(8,128)(2,1)S(1)} %get-tuple-element.40), channel_id=1, source_target_pairs={{0,192},{1,193},{2,194},{3,195},{4,196},{5,197},{6,198},{7,199},{8... | collective-permute-start | bytes 147464 | tf_op jit(solution)/shard_map/ppermute | solution.py:63
  92.1 36.4 %copy-start.10 = (f32[256,256]{1,0:T(8,128)}, f32[256,256]{1,0:T(8,128)S(1)}, u32[]{:S(2)}) copy-start(f32[256,256]{1,0:T(8,128)S(1)} %get-tuple-element.48.gram) | copy-start | bytes 786436
  92.1 3.9 %collective-permute-start.10 = (s16[128,256]{1,0:T(8,128)(2,1)S(1)}, s16[128,256]{1,0:T(8,128)(2,1)S(1)}, u32[]{:S(2)}, u32[]{:S(2)}) collective-permute-start(s16[128,256]{1,0:T(8,128)(2,1)S(1)} %get-tuple-element.43), channel_id=1, source_target_pairs={{0,192},{1,193},{2,194},{3,195},{4,196},{5,197},{6,198},{7,199},{8... | collective-permute-start | bytes 196616 | tf_op jit(solution)/shard_map/ppermute | solution.py:63
  94.7 4.0 %collective-permute-start.11 = (s16[128,256]{1,0:T(8,128)(2,1)S(1)}, s16[128,256]{1,0:T(8,128)(2,1)S(1)}, u32[]{:S(2)}, u32[]{:S(2)}) collective-permute-start(s16[128,256]{1,0:T(8,128)(2,1)S(1)} %get-tuple-element.43), channel_id=1, source_target_pairs={{0,128},{1,129},{2,130},{3,131},{4,132},{5,133},{6,134},{7,135},{8... | collective-permute-start | bytes 196616 | tf_op jit(solution)/shard_map/ppermute | solution.py:63
  94.7 5.6 %collective-permute-start.12 = (s16[128,256]{1,0:T(8,128)(2,1)S(1)}, s16[128,256]{1,0:T(8,128)(2,1)S(1)}, u32[]{:S(2)}, u32[]{:S(2)}) collective-permute-start(s16[128,256]{1,0:T(8,128)(2,1)S(1)} %get-tuple-element.43), channel_id=1, source_target_pairs={{0,64},{1,65},{2,66},{3,67},{4,68},{5,69},{6,70},{7,71},{8,72},{9,... | collective-permute-start | bytes 196616 | tf_op jit(solution)/shard_map/ppermute | solution.py:63
  100.3 7.7 %collective-permute-start.13 = (s16[512,256]{1,0:T(8,128)(2,1)S(1)}, s16[512,256]{1,0:T(8,128)(2,1)S(1)}, u32[]{:S(2)}, u32[]{:S(2)}) collective-permute-start(s16[512,256]{1,0:T(8,128)(2,1)S(1)} %constant_dynamic-update-slice_fusion.r0), channel_id=1, source_target_pairs={{0,48},{1,13},{2,50},{3,15},{4,52},{5,1},{6,54},{7,3},{8,56},{9,5}... | collective-permute-start | bytes 786440 | tf_op jit(solution)/shard_map/ppermute | solution.py:63
  101.9 6.8 %collective-permute-start.14 = (s16[512,256]{1,0:T(8,128)(2,1)S(1)}, s16[512,256]{1,0:T(8,128)(2,1)S(1)}, u32[]{:S(2)}, u32[]{:S(2)}) collective-permute-start(s16[512,256]{1,0:T(8,128)(2,1)S(1)} %constant_dynamic-update-slice_fusion.r0), channel_id=1, source_target_pairs={{0,32},{1,9},{2,34},{3,11},{4,36},{5,13},{6,38},{7,15},{8,40},{9,1... | collective-permute-start | bytes 786440 | tf_op jit(solution)/shard_map/ppermute | solution.py:63
  101.9 9.5 %collective-permute-start.15 = (s16[512,256]{1,0:T(8,128)(2,1)S(1)}, s16[512,256]{1,0:T(8,128)(2,1)S(1)}, u32[]{:S(2)}, u32[]{:S(2)}) collective-permute-start(s16[512,256]{1,0:T(8,128)(2,1)S(1)} %constant_dynamic-update-slice_fusion.r0), channel_id=1, source_target_pairs={{0,16},{1,5},{2,18},{3,7},{4,20},{5,9},{6,22},{7,11},{8,24},{9,13}... | collective-permute-start | bytes 786440 | tf_op jit(solution)/shard_map/ppermute | solution.py:63
  108.7 3.4 %copy-start.6 = (s16[512,256]{1,0:T(8,128)(2,1)}, s16[512,256]{1,0:T(8,128)(2,1)S(1)}, u32[]{:S(2)}) copy-start(s16[512,256]{1,0:T(8,128)(2,1)S(1)} %collective-permute-done.14.r2) | copy-start | bytes 786436
  111.4 0.7 copy-start.8
  112.1 11.0 %collective-permute-start.19 = (s16[768,256]{1,0:T(8,128)(2,1)S(1)}, s16[768,256]{1,0:T(8,128)(2,1)S(1)}, u32[]{:S(2)}, u32[]{:S(2)}) collective-permute-start(s16[768,256]{1,0:T(8,128)(2,1)S(1)} %pad_add_fusion.refs_4_.w0), channel_id=1, source_target_pairs={{0,12},{1,49},{2,14},{3,51},{4,0},{5,53},{6,2},{7,55},{8,4},{9,57}... | collective-permute-start | bytes 1179656 | tf_op jit(solution)/shard_map/ppermute | solution.py:63
  114.2 8.9 %collective-permute-start.20 = (s16[768,256]{1,0:T(8,128)(2,1)S(1)}, s16[768,256]{1,0:T(8,128)(2,1)S(1)}, u32[]{:S(2)}, u32[]{:S(2)}) collective-permute-start(s16[768,256]{1,0:T(8,128)(2,1)S(1)} %pad_add_fusion.refs_4_.w0), channel_id=1, source_target_pairs={{0,8},{1,33},{2,10},{3,35},{4,12},{5,37},{6,14},{7,39},{8,0},{9,41... | collective-permute-start | bytes 1179656 | tf_op jit(solution)/shard_map/ppermute | solution.py:63
  114.2 12.3 %collective-permute-start.21 = (s16[768,256]{1,0:T(8,128)(2,1)S(1)}, s16[768,256]{1,0:T(8,128)(2,1)S(1)}, u32[]{:S(2)}, u32[]{:S(2)}) collective-permute-start(s16[768,256]{1,0:T(8,128)(2,1)S(1)} %pad_add_fusion.refs_4_.w0), channel_id=1, source_target_pairs={{0,4},{1,17},{2,6},{3,19},{4,8},{5,21},{6,10},{7,23},{8,12},{9,25}... | collective-permute-start | bytes 1179656 | tf_op jit(solution)/shard_map/ppermute | solution.py:63
  139.4 9.5 %collective-permute-start.22 = (f32[1,24,256]{2,1,0:T(8,128)S(1)}, f32[1,24,256]{2,1,0:T(8,128)S(1)}, u32[]{:S(2)}, u32[]{:S(2)}) collective-permute-start(f32[1,24,256]{2,1,0:T(8,128)S(1)} %shard_map.123), channel_id=1, source_target_pairs={{0,1},{1,0},{2,3},{3,2},{4,5},{5,4},{6,7},{7,6},{8,9},{9,8},{10,11... | collective-permute-start | bytes 73736 | tf_op jit(solution)/shard_map/ppermute | solution.py:63
  149.6 17.1 %all-to-all-start.4 = ((f32[8,24,256]{2,1,0:T(8,128)}), f32[8,24,256]{2,1,0:T(8,128)S(1)}, u32[]{:S(2)}, u32[]{:S(2)}) async-start(f32[8,24,256]{2,1,0:T(8,128)} %shard_map.124), calls=%async_computation.4 | async-start | bytes 393216 | tf_op jit(solution)/shard_map/all_to_all | solution.py:75
  159.8 0.9 copy-start.7
  160.7 0.9 copy-start.9
  161.7 9.9 %collective-permute-start.16 = (s16[1280,256]{1,0:T(8,128)(2,1)S(1)}, s16[1280,256]{1,0:T(8,128)(2,1)}, u32[]{:S(2)}, u32[]{:S(2)}) collective-permute-start(s16[1280,256]{1,0:T(8,128)(2,1)S(1)} %shard_map.120.refs_0_), channel_id=1, source_target_pairs={{0,12},{1,49},{2,14},{3,51},{4,0},{5,53},{6,2},{7,55},{8,4},{9,57}... | collective-permute-start | bytes 1966088 | tf_op jit(solution)/shard_map/ppermute | solution.py:63
  162.3 11.4 %collective-permute-start.17 = (s16[1280,256]{1,0:T(8,128)(2,1)S(1)}, s16[1280,256]{1,0:T(8,128)(2,1)}, u32[]{:S(2)}, u32[]{:S(2)}) collective-permute-start(s16[1280,256]{1,0:T(8,128)(2,1)S(1)} %shard_map.120.refs_0_), channel_id=1, source_target_pairs={{0,8},{1,33},{2,10},{3,35},{4,12},{5,37},{6,14},{7,39},{8,0},{9,41... | collective-permute-start | bytes 1966088 | tf_op jit(solution)/shard_map/ppermute | solution.py:63
  163.1 19.7 %collective-permute-start.18 = (s16[1280,256]{1,0:T(8,128)(2,1)S(1)}, s16[1280,256]{1,0:T(8,128)(2,1)}, u32[]{:S(2)}, u32[]{:S(2)}) collective-permute-start(s16[1280,256]{1,0:T(8,128)(2,1)S(1)} %shard_map.120.refs_0_), channel_id=1, source_target_pairs={{0,4},{1,17},{2,6},{3,19},{4,8},{5,21},{6,10},{7,23},{8,12},{9,25}... | collective-permute-start | bytes 1966088 | tf_op jit(solution)/shard_map/ppermute | solution.py:63
  167.5 25.4 %all-to-all-start.5 = ((f32[16,24,256]{2,1,0:T(8,128)}), f32[16,24,256]{2,1,0:T(8,128)S(1)}, u32[]{:S(2)}, u32[]{:S(2)}) async-start(f32[16,24,256]{2,1,0:T(8,128)} %shard_map.125), calls=%async_computation.5 | async-start | bytes 786432 | tf_op jit(solution)/shard_map/all_to_all | solution.py:75
  182.8 1.1 copy-start.4
  183.9 9.0 %copy-start.11 = (f32[256,256]{1,0:T(8,128)S(1)}, f32[256,256]{1,0:T(8,128)}, u32[]{:S(2)}) copy-start(f32[256,256]{1,0:T(8,128)} %copy-done.10) | copy-start | bytes 786436

commit v7 on v6

--- a/solution.py
+++ b/solution.py
@@ -17,6 +17,7 @@
 ROWS = 2560
 CAP = 20
 SLOTS = 120
+ROOM_ROWS = 15360
 F32 = jnp.float32
 BF16 = jnp.bfloat16
 AXES = ("z", "y", "x", "h", "c")
@@ -234,7 +235,7 @@
 
 def local_kernel(
     live, patient_at, code_at, month_at, near, rho_ref, patient_hbm, month_hbm, tiles_hbm, duals_hbm,
-    prod_hbm, v_hbm, g_hbm, q1, q2, q3,
+    prod_hbm, v1, v2, v3, g_hbm, q1, q2, q3,
     patient, month, tiles, duals, prod, grad, u_part, g_part, v, g_own, coded, held, sems, outs,
 ):
     copies = [
@@ -284,7 +285,6 @@
             g_part[b * SHARE : (b + 1) * SHARE, :] = grad[at, :]
         once, twice = two_rounds(u_part[...], g_part[...], rho, near_parts)
         v[k - 1] = twice
-        pltpu.make_async_copy(v.at[k - 1], v_hbm.at[k - 1], outs.at[4 + k]).start()
         u_part[...] = rho * once
         g_part[...] = rho * twice
         for b in range(16):
@@ -294,11 +294,12 @@
                 coded[row : row + SHARE, :] = whole
                 coded[1280 + 2 * b + q : 1281 + 2 * b + q, :] = code
         held[k - 1] = to_codes(coded[...])
-        for n, out in enumerate((q1, q2, q3)):
+        for n, (out, v_out) in enumerate(((q1, v1), (q2, v2), (q3, v3))):
 
             @pl.when(k == n + 1)
-            def _(n=n, out=out):
+            def _(n=n, out=out, v_out=v_out):
                 pltpu.make_async_copy(held.at[n], out, outs.at[n]).start()
+                pltpu.make_async_copy(v.at[n], v_out, outs.at[5 + n]).start()
 
         return 0
 
@@ -307,8 +308,8 @@
         pltpu.make_async_copy(held.at[n], out, outs.at[n]).wait()
     prod_out.wait()
     g_out.wait()
-    for k in range(3):
-        pltpu.make_async_copy(v.at[k], v_hbm.at[k], outs.at[5 + k]).wait()
+    for k, v_out in enumerate((v1, v2, v3)):
+        pltpu.make_async_copy(v.at[k], v_out, outs.at[5 + k]).wait()
 
 
 def two_rounds(u, g, rho, near_parts):
@@ -317,7 +318,7 @@
     return once, once + dot3(split(g - once), near_parts)
 
 
-def own_kernel(near, rho_ref, g_part, duals_hbm, a0, v0, u_part, sems):
+def own_kernel(near, rho_ref, g_part, duals_hbm, a0_hbm, v0, u_part, a0, sems):
     place = placed()
     copies = [
         pltpu.make_async_copy(
@@ -339,6 +340,22 @@
     for b in range(16):
         a0[b * 80 : b * 80 + SHARE, :] = u_part[b * SHARE : (b + 1) * SHARE, :]
         a0[b * 80 + SHARE : b * 80 + 80, :] = rho * v0[b * SHARE : (b + 1) * SHARE, :]
+    out = pltpu.make_async_copy(a0, a0_hbm.at[pl.ds(0, 2 * CHUNK), :], sems.at[16])
+    out.start()
+    out.wait()
+
+
+def first_sum_kernel(own_hbm, r1, r2, r3, s0, q1, q2, q3, acc, part, coded, own, sem):
+    copy = pltpu.make_async_copy(own_hbm.at[pl.ds(0, 2 * CHUNK), :], own, sem)
+    copy.start()
+    acc[...] = jnp.zeros_like(acc)
+    for r in (r1, r2, r3):
+        add_blocks(acc, 32, part, r)
+    copy.wait()
+    acc[...] += own[...]
+    s0[...] = acc[0:320, :]
+    for j, out in enumerate((q1, q2, q3)):
+        encode_blocks(acc, (j + 1) * 8, 8, coded, out)
 
 
 def sum_kernel(own, r1, r2, r3, s0, q1, q2, q3, acc, part, coded):
@@ -427,37 +444,49 @@
     lax.fori_loop(0, live[0], visit, 0)
 
 
-def duals_kernel(*refs):
+def duals_kernel(first, near, rho_ref, *refs):
+    both, two, v = refs[0:2], refs[2:4], refs[4:6]
+    out, part, z0_part, z1_part, value, sems = refs[-6:]
     place = placed()
-    both, two = refs[0:4], refs[4:8]
-    v0, v, near, _, out, part, z0_part, z1_part, z2_part, v_part = refs[8:]
     near_parts = split(near[...])
 
     def chunk(k, _):
-        for n in range(4):
+        for n in range(2):
 
             @pl.when(k == n)
             def _(n=n):
                 part[0:1280, :] = from_codes(both[n][...])
                 part[1280:, :] = from_codes(two[n][...])
-                v_part[...] = v0[...] if n == 0 else v[n - 1]
+                value[n] = v[n][...]
 
         for b in range(16):
             rows = slice(b * SHARE, (b + 1) * SHARE)
             at = b * 80
             to = 1280 + b * 48
+            z1 = decode(part[at + 40 : at + 80, :], part[to + 42 : to + 43, :])
             z0_part[rows, :] = decode(part[at : at + 40, :], part[to + 41 : to + 42, :])
-            z1_part[rows, :] = decode(part[at + 40 : at + 80, :], part[to + 42 : to + 43, :])
-            z2_part[rows, :] = decode(part[to : to + 40, :], part[to + 40 : to + 41, :])
+            z1_part[rows, :] = 2.0 * z1
+            z2 = decode(part[to : to + 40, :], part[to + 40 : to + 41, :])
+            value[k, rows, :] = value[k, rows, :] - z1 - z2
         z0 = z0_part[...]
-        z1 = z1_part[...]
-        inner = z0 - dot3(split(z0), near_parts) + 2.0 * z1
-        z2_part[...] = v_part[...] + dot3(split(inner), near_parts) - z1 - z2_part[...]
+        inner = z0 - dot3(split(z0), near_parts) + z1_part[...]
+        value[k] = value[k] + dot3(split(inner), near_parts)
         for b in range(16):
-            out[pl.ds(block_row(place, k, b), SHARE), :] = z2_part[b * SHARE : (b + 1) * SHARE, :]
+            pltpu.make_async_copy(
+                value.at[k, pl.ds(b * SHARE, SHARE), :],
+                out.at[pl.ds(block_row(place, first + k, b), SHARE), :],
+                sems.at[k * 16 + b],
+            ).start()
         return 0
 
-    lax.fori_loop(0, 4, chunk, 0)
+    lax.fori_loop(0, 2, chunk, 0)
+    for k in range(2):
+        for b in range(16):
+            pltpu.make_async_copy(
+                value.at[k, pl.ds(b * SHARE, SHARE), :],
+                out.at[pl.ds(block_row(place, first + k, b), SHARE), :],
+                sems.at[k * 16 + b],
+            ).wait()
 
 
 def tail_kernel(sums, gram, month, out, mat, near, grad):
@@ -471,11 +500,12 @@
     out[...] = solved / (mean + 1e-06)
 
 
-def call(body, outs, spaces, scratch, *args, limit=48 << 20):
+def call(body, outs, spaces, scratch, *args, limit=48 << 20, aliases=None):
     n = len(args)
     space = {"s": pltpu.SMEM, "h": pltpu.HBM, "v": pltpu.VMEM}
     return pl.pallas_call(
         body,
+        input_output_aliases=aliases or {},
         out_shape=[s if isinstance(s, jax.ShapeDtypeStruct) else jax.ShapeDtypeStruct(s, F32) for s in outs],
         in_specs=[pl.BlockSpec(memory_space=space[c]) for c in spaces[:n]],
         out_specs=[pl.BlockSpec(memory_space=space[c]) for c in spaces[n:]],
@@ -498,10 +528,10 @@
         return jax.ShapeDtypeStruct((rows, R), jnp.int16)
 
     tops = [coded_rows(n) for n in (32, 8, 2)]
-    prod, v, g_own, *s = call(
+    prod, v1, v2, v3, g_own, *s = call(
         local_kernel,
-        [(SLOTS, BLOCK, R), (3, CHUNK, R), (CHUNK, R)] + [codes(tops[0])] * 3,
-        "ssssvvhhhh" + "hhhhhh",
+        [(SLOTS, BLOCK, R)] + [(CHUNK, R)] * 4 + [codes(tops[0])] * 3,
+        "ssssvvhhhh" + "hhhhhhhh",
         [
             pltpu.VMEM((1024, R), BF16), (MONTHS, R), pltpu.VMEM((CAP, BLOCK, BLOCK), BF16),
             (ROWS, R), (CAP, BLOCK, R), (ROWS, R), (CHUNK, R), (CHUNK, R), (3, CHUNK, R),
@@ -513,15 +543,17 @@
     )
     s = [send(s[k - 1], first_move(k)) for k in (1, 2, 3)]
     a0, v0 = call(
-        own_kernel, [(2 * CHUNK, R), (CHUNK, R)], "vvvh" + "vv",
-        [(CHUNK, R), pltpu.SemaphoreType.DMA((16,))], near, rho, g_own, scaled_duals,
+        own_kernel, [(ROOM_ROWS, R), (CHUNK, R)], "vvvh" + "hv",
+        [(CHUNK, R), (2 * CHUNK, R), pltpu.SemaphoreType.DMA((17,))],
+        near, rho, g_own, scaled_duals, limit=None,
     )
     m = exchange(fan(m, 4), "z")
     mine = exchange(fan(m, 16), PLANE).reshape(-1, R)
     other = send(mine, CORE_MOVE)
     s = call(
-        sum_kernel, [(320, R)] + [codes(tops[1])] * 3, "vvvv" + "vvvv",
-        [(2 * CHUNK, R), (tops[0], R), (tops[1], R)], a0, *s,
+        first_sum_kernel, [(320, R)] + [codes(tops[1])] * 3, "hvvv" + "vvvv",
+        [(2 * CHUNK, R), (tops[0], R), (tops[1], R), (2 * CHUNK, R), pltpu.SemaphoreType.DMA],
+        a0, *s,
     )
     s = scatter_sum(s, second_move)
     s = call(
@@ -546,13 +578,16 @@
         live_count, code_block, month_index, *two, prod, code_gram,
     )
     t = exchange(sums.reshape(16, -1, R), PLANE)
-    t = fan(t, 1)
-    t = jnp.concatenate([t, send(t, CORE_MOVE)], 0)
-    t = exchange(fan(t, 8), ("z", "h"))
+    t = exchange(fan(t, 16), ("z", "h", "c"))
     t = exchange(fan(t, 16), PLANE).reshape(-1, R)
+    scratch = [(2048, R), (CHUNK, R), (CHUNK, R), (2, CHUNK, R), pltpu.SemaphoreType.DMA((32,))]
     (duals,) = call(
-        duals_kernel, [(ROWS, R)], "v" * 13, [(2048, R)] + [(CHUNK, R)] * 4,
-        *both, *two, v0, v, near, rho,
+        functools.partial(duals_kernel, 0), [(ROWS, R)], "v" * 8 + "h", scratch,
+        near, rho, *both[:2], *two[:2], v0, v1,
+    )
+    (duals,) = call(
+        functools.partial(duals_kernel, 2), [(ROWS, R)], "v" * 8 + "h" + "h", scratch,
+        near, rho, *both[2:], *two[2:], v2, v3, duals, aliases={8: 0},
     )
     (new_months,) = call(
         tail_kernel, [(MONTHS, R)], "vvvv", [(R, R), (R, R), (BLOCK, R)], t, gram, month_factor

time: 199 us -> 199 us (level)
  waiting for transfers between devices: 49.2 us -> 40.5 us
  starting transfers between devices: 53 us -> 57.7 us
  Pallas kernels: 41.5 us -> 45.1 us
    ppermute x23 -> x22, waiting for transfers between devices: 45.7 us -> 29.7 us  [send(): return lax.ppermute(value, AXES, pairs)]
    all_to_all x3, starting transfers between devices: 19.3 us -> 30.7 us  [exchange(): return lax.all_to_all(value, axes, 0, 0, tiled=True)]
    all_to_all x3, waiting for transfers between devices: 3.45 us -> 10.8 us  [exchange(): return lax.all_to_all(value, axes, 0, 0, tiled=True)]
    ppermute x23 -> x22, starting transfers between devices: 33.7 us -> 26.9 us  [send(): return lax.ppermute(value, AXES, pairs)]
    pallas_call x15, Pallas kernels: 41.5 us -> 45.1 us  [call(): pl.pallas_call(body, input_output_aliases=aliases or {}, out_shape=[s if...]
  transfers between devices with their start and end apart: 26 -> 25, of which waited for: 17 -> 13; matrix products, arithmetic and copies ran while one was open for 0% -> 0% of each run, Pallas kernels for 12% -> 14%
where the time goes in v7:
time: 199 us; the launch traced here: 198 us
  starting transfers between devices  57.7 us (29%)
  blocking collectives  48.4 us (24%)
  Pallas kernels  45.1 us (23%)
  waiting for transfers between devices  40.5 us (20%)
  local copies, waits for them, and re-layouts  4.88 us (2%)
    all_to_all x3, blocking collectives, exchange(): return lax.all_to_all(value, axes, 0, 0, tiled=True)  48.4 us
    pallas_call x15, Pallas kernels, call(): pl.pallas_call(body, input_output_aliases=aliases or {}, out_shape=[s if...  45.1 us
    all_to_all x3, starting transfers between devices, exchange(): return lax.all_to_all(value, axes, 0, 0, tiled=True)  30.7 us
    ppermute x22, waiting for transfers between devices, send(): return lax.ppermute(value, AXES, pairs)  29.7 us
    ppermute x22, starting transfers between devices, send(): return lax.ppermute(value, AXES, pairs)  26.9 us
    all_to_all x3, waiting for transfers between devices, exchange(): return lax.all_to_all(value, axes, 0, 0, tiled=True)  10.8 us
    unnamed x35, local copies, waits for them, and re-layouts  4.84 us
  transfers between devices with their start and end apart: 25, of which 13 were waited for; matrix products, arithmetic and copies ran while one was open for 0% of the time, Pallas kernels for 14%

profile of v7, /device:TPU:1, one launch (start us, length us, event | category | flops | bytes accessed | tf_op | source)
XLA Modules:
  0.0 198.1 jit_solution(8942545287557082924)
XLA Ops:
  0.6 7.5 %shard_map.112 = (f32[256,256]{1,0:T(8,128)}, f32[8,128]{1,0:T(8,128)}, f32[384,256]{1,0:T(8,128)}) custom-call(bf16[1024,256]{1,0:T(8,128)(2,1)} %patient_hbm.1, f32[120,256]{1,0:T(8,128)} %month.5), custom_call_target="tpu_custom_call" | custom-call | tf_op jit(solution)/shard_map/pallas_call | solution.py:506
  8.2 17.1 %all_to_all.30.got = f32[16,24,256]{2,1,0:T(8,128)S(1)} all-to-all(f32[16,24,256]{2,1,0:T(8,128)} %bitcast.20), channel_id=1, replica_groups=mesh['z'=4,'y'=4,'x'=4,'h'=2,'c'=2] {'y','x'}, dimensions={0} | all-to-all | bytes 786432 | tf_op jit(solution)/shard_map/all_to_all | solution.py:76
  25.3 0.7 shard_map.117
  25.9 5.6 %all-to-all-start.1 = ((f32[4,24,256]{2,1,0:T(8,128)}), f32[4,24,256]{2,1,0:T(8,128)S(1)}, u32[]{:S(2)}, u32[]{:S(2)}) async-start(f32[4,24,256]{2,1,0:T(8,128)} %shard_map.117), calls=%async_computation.1 | async-start | bytes 196608 | tf_op jit(solution)/shard_map/all_to_all | solution.py:76
  32.2 8.5 %shard_map.113 = (f32[120,128,256]{2,1,0:T(8,128)}, f32[640,256]{1,0:T(8,128)}, f32[640,256]{1,0:T(8,128)}, f32[640,256]{1,0:T(8,128)}, f32[640,256]{1,0:T(8,128...) custom-call(s32[1]{0:T(128)S(6)} %copy.17.live, s32[20]{0:T(128)} %patient_at.1, ...), custom_call_target="tpu_custom_call" | custom-call | tf_op jit(solution)/shard_map/pallas_call | solution.py:506
  40.7 0.1 collective-permute-start
  40.8 1.8 collective-permute-start.1
  42.6 0.8 collective-permute-start.2
  43.4 0.0 all-to-all-done.1.got
  43.5 19.6 %all_to_all.31 = f32[16,24,256]{2,1,0:T(8,128)S(1)} all-to-all(f32[16,24,256]{2,1,0:T(8,128)S(1)} %shard_map.118), channel_id=1, replica_groups=mesh['z'=4,'y'=4,'x'=4,'h'=2,'c'=2] {'y','x'}, dimensions={0} | all-to-all | bytes 786432 | tf_op jit(solution)/shard_map/all_to_all | solution.py:76
  63.0 3.8 %collective-permute-start.9 = (f32[384,256]{1,0:T(8,128)S(1)}, f32[384,256]{1,0:T(8,128)S(1)}, u32[]{:S(2)}, u32[]{:S(2)}) collective-permute-start(f32[384,256]{1,0:T(8,128)S(1)} %bitcast.13), channel_id=1, source_target_pairs={{0,1},{1,0},{2,3},{3,2},{4,5},{5,4},{6,7},{7,6},{8,9},{9,8},{10,11... | collective-permute-start | bytes 1179656 | tf_op jit(solution)/shard_map/ppermute | solution.py:64
  66.8 5.5 %shard_map.114 = (f32[15360,256]{1,0:T(8,128)}, f32[640,256]{1,0:T(8,128)}) custom-call(f32[256,256]{1,0:T(8,128)} %get-tuple-element.28.near, f32[8,128]{1,0:T(8,128)} %get-tuple-element.29.rho_ref, f32[640,256]{1,0:T(8,128)} %get-tuple-element.30.g_part, f32[2560,256]{1,0:T(8,128)} %duals_hbm.3), custom_call_target="tpu_custom_call" | custom-call | tf_op jit(solution)/shard_map/pallas_call | solution.py:506
  72.3 0.0 collective-permute-done.r1
  72.3 0.0 collective-permute-done.1.r2
  72.3 0.0 copy-start.1
  72.3 0.0 copy-start.13
  72.3 1.7 shard_map.115
  74.1 0.0 copy-start.14
  74.1 0.0 copy-start.15
  74.1 0.9 collective-permute-start.3
  75.0 3.0 %collective-permute-start.4 = (s16[336,256]{1,0:T(8,128)(2,1)S(1)}, s16[336,256]{1,0:T(8,128)(2,1)S(1)}, u32[]{:S(2)}, u32[]{:S(2)}) collective-permute-start(s16[336,256]{1,0:T(8,128)(2,1)S(1)} %get-tuple-element.37), channel_id=1, source_target_pairs={{0,32},{1,9},{2,34},{3,11},{4,36},{5,13},{6,38},{7,15},{8,40},{9,1... | collective-permute-start | bytes 516104 | tf_op jit(solution)/shard_map/ppermute | solution.py:64
  78.0 0.0 collective-permute-start.5
  78.0 1.9 collective-permute-done.3.r1
  79.9 2.9 %collective-permute-done.4.r2 = s16[336,256]{1,0:T(8,128)(2,1)S(1)} collective-permute-done((s16[336,256]{1,0:T(8,128)(2,1)S(1)}, s16[336,256]{1,0:T(8,128)(2,1)S(1)}, u32[]{:S(2)}, u32[]{:S(2)}) %collective-permute-start.4) | collective-permute-done | bytes 172064 | tf_op jit(solution)/shard_map/ppermute | solution.py:64
  82.9 0.3 shard_map.116
  83.2 2.0 collective-permute-start.6
  85.1 2.1 %collective-permute-start.7 = (s16[96,256]{1,0:T(8,128)(2,1)S(1)}, s16[96,256]{1,0:T(8,128)(2,1)S(1)}, u32[]{:S(2)}, u32[]{:S(2)}) collective-permute-start(s16[96,256]{1,0:T(8,128)(2,1)S(1)} %get-tuple-element.41), channel_id=1, source_target_pairs={{0,128},{1,129},{2,130},{3,131},{4,132},{5,133},{6,134},{7,135},{8... | collective-permute-start | bytes 147464 | tf_op jit(solution)/shard_map/ppermute | solution.py:64
  87.2 1.2 collective-permute-start.8
  88.4 2.0 %collective-permute-done.7.s2 = s16[96,256]{1,0:T(8,128)(2,1)S(1)} collective-permute-done((s16[96,256]{1,0:T(8,128)(2,1)S(1)}, s16[96,256]{1,0:T(8,128)(2,1)S(1)}, u32[]{:S(2)}, u32[]{:S(2)}) %collective-permute-start.7) | collective-permute-done | bytes 49184 | tf_op jit(solution)/shard_map/ppermute | solution.py:64
  90.4 0.5 collective-permute-done.8.s3
  91.0 1.4 shard_map.119
  92.4 2.6 %collective-permute-start.10 = (s16[128,256]{1,0:T(8,128)(2,1)S(1)}, s16[128,256]{1,0:T(8,128)(2,1)S(1)}, u32[]{:S(2)}, u32[]{:S(2)}) collective-permute-start(s16[128,256]{1,0:T(8,128)(2,1)S(1)} %get-tuple-element.45), channel_id=1, source_target_pairs={{0,192},{1,193},{2,194},{3,195},{4,196},{5,197},{6,198},{7,199},{8... | collective-permute-start | bytes 196616 | tf_op jit(solution)/shard_map/ppermute | solution.py:64
  95.0 0.3 collective-permute-start.12
  95.3 1.0 collective-permute-done.10
  96.3 2.7 %collective-permute-done.11 = s16[128,256]{1,0:T(8,128)(2,1)S(1)} collective-permute-done((s16[128,256]{1,0:T(8,128)(2,1)S(1)}, s16[128,256]{1,0:T(8,128)(2,1)S(1)}, u32[]{:S(2)}, u32[]{:S(2)}) %collective-permute-start.11) | collective-permute-done | bytes 65568 | tf_op jit(solution)/shard_map/ppermute | solution.py:64
  99.0 1.6 collective-permute-done.12
  100.6 1.6 collective-permute-start.13
  102.2 0.7 collective-permute-start.15
  102.9 5.4 %collective-permute-done.13.r1 = s16[512,256]{1,0:T(8,128)(2,1)S(1)} collective-permute-done((s16[512,256]{1,0:T(8,128)(2,1)S(1)}, s16[512,256]{1,0:T(8,128)(2,1)S(1)}, u32[]{:S(2)}, u32[]{:S(2)}) %collective-permute-start.13) | collective-permute-done | bytes 262176 | tf_op jit(solution)/shard_map/ppermute | solution.py:64
  108.3 0.7 collective-permute-done.14.r2
  109.0 2.7 %collective-permute-done.15.r3 = s16[512,256]{1,0:T(8,128)(2,1)S(1)} collective-permute-done((s16[512,256]{1,0:T(8,128)(2,1)S(1)}, s16[512,256]{1,0:T(8,128)(2,1)S(1)}, u32[]{:S(2)}, u32[]{:S(2)}) %collective-permute-start.15) | collective-permute-done | bytes 262176 | tf_op jit(solution)/shard_map/ppermute | solution.py:64
  111.7 0.7 copy-done.8
  112.5 1.8 collective-permute-start.18
  114.3 0.8 collective-permute-start.19
  115.1 1.9 collective-permute-start.21
  116.9 3.9 %collective-permute-done.18.refs_2_.w2 = s16[768,256]{1,0:T(8,128)(2,1)S(1)} collective-permute-done((s16[768,256]{1,0:T(8,128)(2,1)S(1)}, s16[768,256]{1,0:T(8,128)(2,1)S(1)}, u32[]{:S(2)}, u32[]{:S(2)}) %collective-permute-start.18) | collective-permute-done | bytes 393248 | tf_op jit(solution)/shard_map/ppermute | solution.py:64
  120.8 4.4 %collective-permute-done.19.refs_3_.w3 = s16[768,256]{1,0:T(8,128)(2,1)S(1)} collective-permute-done((s16[768,256]{1,0:T(8,128)(2,1)S(1)}, s16[768,256]{1,0:T(8,128)(2,1)S(1)}, u32[]{:S(2)}, u32[]{:S(2)}) %collective-permute-start.19) | collective-permute-done | bytes 393248 | tf_op jit(solution)/shard_map/ppermute | solution.py:64
  125.2 2.0 %shard_map.123 = f32[384,256]{1,0:T(8,128)S(1)} custom-call(s32[1]{0:T(128)S(6)} %copy.17.live, s32[20]{0:T(128)S(1)} %copy-done.14, s32[20]{0:T(128)S(1)} %copy-done.15, s16[768,256]{1,0:T(8,128)(2,1)S(1)} %pad_add_fusion.refs_2_.w0, s16[768,256]{1,0:T(8,128)(2,1)S(1)} %collective-permute-done.21.refs_3_.w1, ...), custom_call_target="tpu_custom_call" | custom-call | tf_op jit(solution)/shard_map/pallas_call | solution.py:506
  127.2 11.7 %all_to_all.32.got = f32[16,24,256]{2,1,0:T(8,128)S(1)} all-to-all(f32[16,24,256]{2,1,0:T(8,128)S(1)} %bitcast.15), channel_id=1, replica_groups=mesh['z'=4,'y'=4,'x'=4,'h'=2,'c'=2] {'y','x'}, dimensions={0} | all-to-all | bytes 786432 | tf_op jit(solution)/shard_map/all_to_all | solution.py:76
  138.9 0.8 shard_map.124
  139.7 21.4 %all-to-all-start.4 = ((f32[16,24,256]{2,1,0:T(8,128)}), f32[16,24,256]{2,1,0:T(8,128)S(1)}, u32[]{:S(2)}, u32[]{:S(2)}) async-start(f32[16,24,256]{2,1,0:T(8,128)} %shard_map.124), calls=%async_computation.4 | async-start | bytes 786432 | tf_op jit(solution)/shard_map/all_to_all | solution.py:76
  161.0 0.9 copy-done.7
  162.0 0.9 copy-done.9
  163.0 0.7 collective-permute-start.20
  163.6 0.7 collective-permute-start.16
  164.4 0.2 collective-permute-start.17
  164.5 10.8 %all-to-all-done.4.got = f32[16,24,256]{2,1,0:T(8,128)S(1)} async-done(((f32[16,24,256]{2,1,0:T(8,128)}), f32[16,24,256]{2,1,0:T(8,128)S(1)}, u32[]{:S(2)}, u32[]{:S(2)}) %all-to-all-start.4) | async-done | bytes 393248 | tf_op jit(solution)/shard_map/all_to_all | solution.py:76
  175.4 0.8 shard_map.125
  176.2 3.8 %all-to-all-start.5 = ((f32[16,24,256]{2,1,0:T(8,128)}), f32[16,24,256]{2,1,0:T(8,128)S(1)}, u32[]{:S(2)}, u32[]{:S(2)}) async-start(f32[16,24,256]{2,1,0:T(8,128)} %shard_map.125), calls=%async_computation.5 | async-start | bytes 786432 | tf_op jit(solution)/shard_map/all_to_all | solution.py:76
  180.0 1.1 copy-done.4
  181.1 1.1 copy-done.5
  182.2 5.0 %shard_map.121.refs_6_ = f32[2560,256]{1,0:T(8,128)} custom-call(f32[256,256]{1,0:T(8,128)S(1)} %copy-done, f32[8,128]{1,0:T(8,128)S(1)} %copy-done.12, s16[1280,256]{1,0:T(8,128)(2,1)S(1)} %shard_map.120.refs_0_, s16[1280,256]{1,0:T(8,128)(2,1)} %collective-permute-done.20.refs_1_, s16[768,256]{1,0:T(8,128)(2,1)S(1)} %pad_add_fusion.refs_2_.w0, ...), custom_call_target="tpu_custom_call" | custom-call | tf_op jit(solution)/shard_map/pallas_call | solution.py:506
  187.2 5.2 %shard_map.122 = f32[2560,256]{1,0:T(8,128)} custom-call(f32[256,256]{1,0:T(8,128)S(1)} %copy-done, f32[8,128]{1,0:T(8,128)S(1)} %copy-done.12, s16[1280,256]{1,0:T(8,128)(2,1)} %collective-permute-done.16.refs_0_, s16[1280,256]{1,0:T(8,128)(2,1)} %collective-permute-done.17.refs_1_, ...), custom_call_target="tpu_custom_call", output_to_operand_aliasing={{}: (8, {})} | custom-call | tf_op jit(solution)/shard_map/pallas_call | solution.py:506
  192.4 5.7 %shard_map.126 = f32[120,256]{1,0:T(8,128)} custom-call(f32[384,256]{1,0:T(8,128)S(1)} %bitcast.12, f32[256,256]{1,0:T(8,128)S(1)} %copy-done.11, f32[120,256]{1,0:T(8,128)S(1)} %copy-done.1), custom_call_target="tpu_custom_call" | custom-call | tf_op jit(solution)/shard_map/pallas_call | solution.py:506
  (45 shorter events, 0.2 us)
Async XLA Ops:
  25.9 17.5 %all-to-all-start.1 = ((f32[4,24,256]{2,1,0:T(8,128)}), f32[4,24,256]{2,1,0:T(8,128)S(1)}, u32[]{:S(2)}, u32[]{:S(2)}) async-start(f32[4,24,256]{2,1,0:T(8,128)} %shard_map.117), calls=%async_computation.1 | async-start | bytes 196608 | tf_op jit(solution)/shard_map/all_to_all | solution.py:76
  40.7 31.6 %collective-permute-start = (s16[1312,256]{1,0:T(8,128)(2,1)}, s16[1312,256]{1,0:T(8,128)(2,1)S(1)}, u32[]{:S(2)}, u32[]{:S(2)}) collective-permute-start(s16[1312,256]{1,0:T(8,128)(2,1)} %get-tuple-element.32), channel_id=1, source_target_pairs={{0,4},{1,17},{2,6},{3,19},{4,8},{5,21},{6,10},{7,23},{8,12},{9,25}... | collective-permute-start | bytes 2015240 | tf_op jit(solution)/shard_map/ppermute | solution.py:64
  40.8 31.5 %collective-permute-start.1 = (s16[1312,256]{1,0:T(8,128)(2,1)}, s16[1312,256]{1,0:T(8,128)(2,1)S(1)}, u32[]{:S(2)}, u32[]{:S(2)}) collective-permute-start(s16[1312,256]{1,0:T(8,128)(2,1)} %get-tuple-element.33), channel_id=1, source_target_pairs={{0,8},{1,33},{2,10},{3,35},{4,12},{5,37},{6,14},{7,39},{8,0},{9,41... | collective-permute-start | bytes 2015240 | tf_op jit(solution)/shard_map/ppermute | solution.py:64
  42.6 29.7 %collective-permute-start.2 = (s16[1312,256]{1,0:T(8,128)(2,1)}, s16[1312,256]{1,0:T(8,128)(2,1)S(1)}, u32[]{:S(2)}, u32[]{:S(2)}) collective-permute-start(s16[1312,256]{1,0:T(8,128)(2,1)} %get-tuple-element.34), channel_id=1, source_target_pairs={{0,12},{1,49},{2,14},{3,51},{4,0},{5,53},{6,2},{7,55},{8,4},{9,57}... | collective-permute-start | bytes 2015240 | tf_op jit(solution)/shard_map/ppermute | solution.py:64
  63.0 27.9 %collective-permute-start.9 = (f32[384,256]{1,0:T(8,128)S(1)}, f32[384,256]{1,0:T(8,128)S(1)}, u32[]{:S(2)}, u32[]{:S(2)}) collective-permute-start(f32[384,256]{1,0:T(8,128)S(1)} %bitcast.13), channel_id=1, source_target_pairs={{0,1},{1,0},{2,3},{3,2},{4,5},{5,4},{6,7},{7,6},{8,9},{9,8},{10,11... | collective-permute-start | bytes 1179656 | tf_op jit(solution)/shard_map/ppermute | solution.py:64
  72.3 18.6 %copy-start.1 = (f32[120,256]{1,0:T(8,128)S(1)}, f32[120,256]{1,0:T(8,128)}, u32[]{:S(2)}) copy-start(f32[120,256]{1,0:T(8,128)} %month.5) | copy-start | bytes 368644
  72.3 18.6 %copy-start.13 = (f32[40,256]{1,0:T(8,128)S(1)}, f32[40,256]{1,0:T(8,128)}, u32[]{:S(2)}) copy-start(f32[40,256]{1,0:T(8,128)} %z0_ref.1) | copy-start | bytes 122884
  74.1 51.1 %copy-start.14 = (s32[20]{0:T(128)S(1)}, s32[20]{0:T(128)}, u32[]{:S(2)}) copy-start(s32[20]{0:T(128)} %code_at.3) | copy-start | bytes 244
  74.1 51.1 %copy-start.15 = (s32[20]{0:T(128)S(1)}, s32[20]{0:T(128)}, u32[]{:S(2)}) copy-start(s32[20]{0:T(128)} %month_at.3) | copy-start | bytes 244
  74.1 5.8 %collective-permute-start.3 = (s16[336,256]{1,0:T(8,128)(2,1)S(1)}, s16[336,256]{1,0:T(8,128)(2,1)S(1)}, u32[]{:S(2)}, u32[]{:S(2)}) collective-permute-start(s16[336,256]{1,0:T(8,128)(2,1)S(1)} %get-tuple-element.36), channel_id=1, source_target_pairs={{0,16},{1,5},{2,18},{3,7},{4,20},{5,9},{6,22},{7,11},{8,24},{9,13}... | collective-permute-start | bytes 516104 | tf_op jit(solution)/shard_map/ppermute | solution.py:64
  75.0 7.9 %collective-permute-start.4 = (s16[336,256]{1,0:T(8,128)(2,1)S(1)}, s16[336,256]{1,0:T(8,128)(2,1)S(1)}, u32[]{:S(2)}, u32[]{:S(2)}) collective-permute-start(s16[336,256]{1,0:T(8,128)(2,1)S(1)} %get-tuple-element.37), channel_id=1, source_target_pairs={{0,32},{1,9},{2,34},{3,11},{4,36},{5,13},{6,38},{7,15},{8,40},{9,1... | collective-permute-start | bytes 516104 | tf_op jit(solution)/shard_map/ppermute | solution.py:64
  78.0 4.9 %collective-permute-start.5 = (s16[336,256]{1,0:T(8,128)(2,1)S(1)}, s16[336,256]{1,0:T(8,128)(2,1)S(1)}, u32[]{:S(2)}, u32[]{:S(2)}) collective-permute-start(s16[336,256]{1,0:T(8,128)(2,1)S(1)} %get-tuple-element.38), channel_id=1, source_target_pairs={{0,48},{1,13},{2,50},{3,15},{4,52},{5,1},{6,54},{7,3},{8,56},{9,5}... | collective-permute-start | bytes 516104 | tf_op jit(solution)/shard_map/ppermute | solution.py:64
  83.2 5.3 %collective-permute-start.6 = (s16[96,256]{1,0:T(8,128)(2,1)S(1)}, s16[96,256]{1,0:T(8,128)(2,1)S(1)}, u32[]{:S(2)}, u32[]{:S(2)}) collective-permute-start(s16[96,256]{1,0:T(8,128)(2,1)S(1)} %get-tuple-element.40), channel_id=1, source_target_pairs={{0,64},{1,65},{2,66},{3,67},{4,68},{5,69},{6,70},{7,71},{8,72},{9,... | collective-permute-start | bytes 147464 | tf_op jit(solution)/shard_map/ppermute | solution.py:64
  85.1 5.3 %collective-permute-start.7 = (s16[96,256]{1,0:T(8,128)(2,1)S(1)}, s16[96,256]{1,0:T(8,128)(2,1)S(1)}, u32[]{:S(2)}, u32[]{:S(2)}) collective-permute-start(s16[96,256]{1,0:T(8,128)(2,1)S(1)} %get-tuple-element.41), channel_id=1, source_target_pairs={{0,128},{1,129},{2,130},{3,131},{4,132},{5,133},{6,134},{7,135},{8... | collective-permute-start | bytes 147464 | tf_op jit(solution)/shard_map/ppermute | solution.py:64
  87.2 3.7 %collective-permute-start.8 = (s16[96,256]{1,0:T(8,128)(2,1)S(1)}, s16[96,256]{1,0:T(8,128)(2,1)S(1)}, u32[]{:S(2)}, u32[]{:S(2)}) collective-permute-start(s16[96,256]{1,0:T(8,128)(2,1)S(1)} %get-tuple-element.42), channel_id=1, source_target_pairs={{0,192},{1,193},{2,194},{3,195},{4,196},{5,197},{6,198},{7,199},{8... | collective-permute-start | bytes 147464 | tf_op jit(solution)/shard_map/ppermute | solution.py:64
  92.4 34.8 %copy-start.10 = (f32[256,256]{1,0:T(8,128)}, f32[256,256]{1,0:T(8,128)S(1)}, u32[]{:S(2)}) copy-start(f32[256,256]{1,0:T(8,128)S(1)} %get-tuple-element.52.gram) | copy-start | bytes 786436
  92.4 4.0 %collective-permute-start.10 = (s16[128,256]{1,0:T(8,128)(2,1)S(1)}, s16[128,256]{1,0:T(8,128)(2,1)S(1)}, u32[]{:S(2)}, u32[]{:S(2)}) collective-permute-start(s16[128,256]{1,0:T(8,128)(2,1)S(1)} %get-tuple-element.45), channel_id=1, source_target_pairs={{0,192},{1,193},{2,194},{3,195},{4,196},{5,197},{6,198},{7,199},{8... | collective-permute-start | bytes 196616 | tf_op jit(solution)/shard_map/ppermute | solution.py:64
  95.0 4.0 %collective-permute-start.11 = (s16[128,256]{1,0:T(8,128)(2,1)S(1)}, s16[128,256]{1,0:T(8,128)(2,1)S(1)}, u32[]{:S(2)}, u32[]{:S(2)}) collective-permute-start(s16[128,256]{1,0:T(8,128)(2,1)S(1)} %get-tuple-element.45), channel_id=1, source_target_pairs={{0,128},{1,129},{2,130},{3,131},{4,132},{5,133},{6,134},{7,135},{8... | collective-permute-start | bytes 196616 | tf_op jit(solution)/shard_map/ppermute | solution.py:64
  95.0 5.6 %collective-permute-start.12 = (s16[128,256]{1,0:T(8,128)(2,1)S(1)}, s16[128,256]{1,0:T(8,128)(2,1)S(1)}, u32[]{:S(2)}, u32[]{:S(2)}) collective-permute-start(s16[128,256]{1,0:T(8,128)(2,1)S(1)} %get-tuple-element.45), channel_id=1, source_target_pairs={{0,64},{1,65},{2,66},{3,67},{4,68},{5,69},{6,70},{7,71},{8,72},{9,... | collective-permute-start | bytes 196616 | tf_op jit(solution)/shard_map/ppermute | solution.py:64
  100.6 7.7 %collective-permute-start.13 = (s16[512,256]{1,0:T(8,128)(2,1)S(1)}, s16[512,256]{1,0:T(8,128)(2,1)S(1)}, u32[]{:S(2)}, u32[]{:S(2)}) collective-permute-start(s16[512,256]{1,0:T(8,128)(2,1)S(1)} %constant_dynamic-update-slice_fusion.r0), channel_id=1, source_target_pairs={{0,48},{1,13},{2,50},{3,15},{4,52},{5,1},{6,54},{7,3},{8,56},{9,5}... | collective-permute-start | bytes 786440 | tf_op jit(solution)/shard_map/ppermute | solution.py:64
  102.2 6.8 %collective-permute-start.14 = (s16[512,256]{1,0:T(8,128)(2,1)S(1)}, s16[512,256]{1,0:T(8,128)(2,1)S(1)}, u32[]{:S(2)}, u32[]{:S(2)}) collective-permute-start(s16[512,256]{1,0:T(8,128)(2,1)S(1)} %constant_dynamic-update-slice_fusion.r0), channel_id=1, source_target_pairs={{0,32},{1,9},{2,34},{3,11},{4,36},{5,13},{6,38},{7,15},{8,40},{9,1... | collective-permute-start | bytes 786440 | tf_op jit(solution)/shard_map/ppermute | solution.py:64
  102.2 9.5 %collective-permute-start.15 = (s16[512,256]{1,0:T(8,128)(2,1)S(1)}, s16[512,256]{1,0:T(8,128)(2,1)S(1)}, u32[]{:S(2)}, u32[]{:S(2)}) collective-permute-start(s16[512,256]{1,0:T(8,128)(2,1)S(1)} %constant_dynamic-update-slice_fusion.r0), channel_id=1, source_target_pairs={{0,16},{1,5},{2,18},{3,7},{4,20},{5,9},{6,22},{7,11},{8,24},{9,13}... | collective-permute-start | bytes 786440 | tf_op jit(solution)/shard_map/ppermute | solution.py:64
  109.0 3.4 %copy-start.6 = (s16[512,256]{1,0:T(8,128)(2,1)}, s16[512,256]{1,0:T(8,128)(2,1)S(1)}, u32[]{:S(2)}) copy-start(s16[512,256]{1,0:T(8,128)(2,1)S(1)} %collective-permute-done.14.r2) | copy-start | bytes 786436
  111.7 0.7 copy-start.8
  112.5 8.3 %collective-permute-start.18 = (s16[768,256]{1,0:T(8,128)(2,1)S(1)}, s16[768,256]{1,0:T(8,128)(2,1)S(1)}, u32[]{:S(2)}, u32[]{:S(2)}) collective-permute-start(s16[768,256]{1,0:T(8,128)(2,1)S(1)} %pad_add_fusion.refs_2_.w0), channel_id=1, source_target_pairs={{0,8},{1,33},{2,10},{3,35},{4,12},{5,37},{6,14},{7,39},{8,0},{9,41... | collective-permute-start | bytes 1179656 | tf_op jit(solution)/shard_map/ppermute | solution.py:64
  114.3 10.9 %collective-permute-start.19 = (s16[768,256]{1,0:T(8,128)(2,1)S(1)}, s16[768,256]{1,0:T(8,128)(2,1)S(1)}, u32[]{:S(2)}, u32[]{:S(2)}) collective-permute-start(s16[768,256]{1,0:T(8,128)(2,1)S(1)} %pad_add_fusion.refs_2_.w0), channel_id=1, source_target_pairs={{0,4},{1,17},{2,6},{3,19},{4,8},{5,21},{6,10},{7,23},{8,12},{9,25}... | collective-permute-start | bytes 1179656 | tf_op jit(solution)/shard_map/ppermute | solution.py:64
  115.1 10.1 %collective-permute-start.21 = (s16[768,256]{1,0:T(8,128)(2,1)S(1)}, s16[768,256]{1,0:T(8,128)(2,1)S(1)}, u32[]{:S(2)}, u32[]{:S(2)}) collective-permute-start(s16[768,256]{1,0:T(8,128)(2,1)S(1)} %pad_add_fusion.refs_2_.w0), channel_id=1, source_target_pairs={{0,12},{1,49},{2,14},{3,51},{4,0},{5,53},{6,2},{7,55},{8,4},{9,57}... | collective-permute-start | bytes 1179656 | tf_op jit(solution)/shard_map/ppermute | solution.py:64
  138.9 41.1 %copy-start = (f32[256,256]{1,0:T(8,128)S(1)}, f32[256,256]{1,0:T(8,128)}, u32[]{:S(2)}) copy-start(f32[256,256]{1,0:T(8,128)} %get-tuple-element.28.near) | copy-start | bytes 786436
  138.9 41.1 %copy-start.12 = (f32[8,128]{1,0:T(8,128)S(1)}, f32[8,128]{1,0:T(8,128)}, u32[]{:S(2)}) copy-start(f32[8,128]{1,0:T(8,128)} %get-tuple-element.29.rho_ref) | copy-start | bytes 12292
  139.7 35.7 %all-to-all-start.4 = ((f32[16,24,256]{2,1,0:T(8,128)}), f32[16,24,256]{2,1,0:T(8,128)S(1)}, u32[]{:S(2)}, u32[]{:S(2)}) async-start(f32[16,24,256]{2,1,0:T(8,128)} %shard_map.124), calls=%async_computation.4 | async-start | bytes 786432 | tf_op jit(solution)/shard_map/all_to_all | solution.py:76
  161.0 0.9 copy-start.7
  162.0 0.9 copy-start.9
  163.0 17.0 %collective-permute-start.20 = (s16[1280,256]{1,0:T(8,128)(2,1)S(1)}, s16[1280,256]{1,0:T(8,128)(2,1)}, u32[]{:S(2)}, u32[]{:S(2)}) collective-permute-start(s16[1280,256]{1,0:T(8,128)(2,1)S(1)} %shard_map.120.refs_0_), channel_id=1, source_target_pairs={{0,12},{1,49},{2,14},{3,51},{4,0},{5,53},{6,2},{7,55},{8,4},{9,57}... | collective-permute-start | bytes 1966088 | tf_op jit(solution)/shard_map/ppermute | solution.py:64
  163.6 23.6 %collective-permute-start.16 = (s16[1280,256]{1,0:T(8,128)(2,1)S(1)}, s16[1280,256]{1,0:T(8,128)(2,1)}, u32[]{:S(2)}, u32[]{:S(2)}) collective-permute-start(s16[1280,256]{1,0:T(8,128)(2,1)S(1)} %shard_map.120.refs_0_), channel_id=1, source_target_pairs={{0,8},{1,33},{2,10},{3,35},{4,12},{5,37},{6,14},{7,39},{8,0},{9,41... | collective-permute-start | bytes 1966088 | tf_op jit(solution)/shard_map/ppermute | solution.py:64
  164.4 22.9 %collective-permute-start.17 = (s16[1280,256]{1,0:T(8,128)(2,1)S(1)}, s16[1280,256]{1,0:T(8,128)(2,1)}, u32[]{:S(2)}, u32[]{:S(2)}) collective-permute-start(s16[1280,256]{1,0:T(8,128)(2,1)S(1)} %shard_map.120.refs_0_), channel_id=1, source_target_pairs={{0,4},{1,17},{2,6},{3,19},{4,8},{5,21},{6,10},{7,23},{8,12},{9,25}... | collective-permute-start | bytes 1966088 | tf_op jit(solution)/shard_map/ppermute | solution.py:64
  176.2 16.3 %all-to-all-start.5 = ((f32[16,24,256]{2,1,0:T(8,128)}), f32[16,24,256]{2,1,0:T(8,128)S(1)}, u32[]{:S(2)}, u32[]{:S(2)}) async-start(f32[16,24,256]{2,1,0:T(8,128)} %shard_map.125), calls=%async_computation.5 | async-start | bytes 786432 | tf_op jit(solution)/shard_map/all_to_all | solution.py:76
  180.0 1.1 copy-start.4
  181.1 1.1 copy-start.5
  182.1 5.1 %copy-start.2 = (f32[640,256]{1,0:T(8,128)S(1)}, f32[640,256]{1,0:T(8,128)}, u32[]{:S(2)}) copy-start(f32[640,256]{1,0:T(8,128)} %get-tuple-element.46.refs_4_) | copy-start | bytes 1966084
  182.2 5.1 %copy-start.3 = (f32[640,256]{1,0:T(8,128)S(1)}, f32[640,256]{1,0:T(8,128)}, u32[]{:S(2)}) copy-start(f32[640,256]{1,0:T(8,128)} %get-tuple-element.47.refs_5_) | copy-start | bytes 1966084
  187.2 5.2 %copy-start.11 = (f32[256,256]{1,0:T(8,128)S(1)}, f32[256,256]{1,0:T(8,128)}, u32[]{:S(2)}) copy-start(f32[256,256]{1,0:T(8,128)} %copy-done.10) | copy-start | bytes 786436

commit v8 on v7

--- a/solution.py
+++ b/solution.py
@@ -235,7 +235,7 @@
 
 def local_kernel(
     live, patient_at, code_at, month_at, near, rho_ref, patient_hbm, month_hbm, tiles_hbm, duals_hbm,
-    prod_hbm, v1, v2, v3, g_hbm, q1, q2, q3,
+    store, g_hbm, q1, q2, q3,
     patient, month, tiles, duals, prod, grad, u_part, g_part, v, g_own, coded, held, sems, outs,
 ):
     copies = [
@@ -267,7 +267,7 @@
         return 0
 
     lax.fori_loop(0, (live[0] + 3) // 4, visit, 0)
-    prod_out = pltpu.make_async_copy(prod, prod_hbm.at[pl.ds(0, CAP)], outs.at[4])
+    prod_out = pltpu.make_async_copy(prod, store.at[pl.ds(0, CAP)], outs.at[4])
     prod_out.start()
     near_parts = split(near[...])
     copies[3].wait()
@@ -284,7 +284,7 @@
             u_part[b * SHARE : (b + 1) * SHARE, :] = duals[at, :]
             g_part[b * SHARE : (b + 1) * SHARE, :] = grad[at, :]
         once, twice = two_rounds(u_part[...], g_part[...], rho, near_parts)
-        v[k - 1] = twice
+        v[k - 1] = twice.reshape(5, BLOCK, R)
         u_part[...] = rho * once
         g_part[...] = rho * twice
         for b in range(16):
@@ -294,12 +294,13 @@
                 coded[row : row + SHARE, :] = whole
                 coded[1280 + 2 * b + q : 1281 + 2 * b + q, :] = code
         held[k - 1] = to_codes(coded[...])
-        for n, (out, v_out) in enumerate(((q1, v1), (q2, v2), (q3, v3))):
+        for n, out in enumerate((q1, q2, q3)):
 
             @pl.when(k == n + 1)
-            def _(n=n, out=out, v_out=v_out):
+            def _(n=n, out=out):
                 pltpu.make_async_copy(held.at[n], out, outs.at[n]).start()
-                pltpu.make_async_copy(v.at[n], v_out, outs.at[5 + n]).start()
+                at = pl.ds(CAP + 5 * n, 5)
+                pltpu.make_async_copy(v.at[n], store.at[at], outs.at[5 + n]).start()
 
         return 0
 
@@ -308,8 +309,8 @@
         pltpu.make_async_copy(held.at[n], out, outs.at[n]).wait()
     prod_out.wait()
     g_out.wait()
-    for k, v_out in enumerate((v1, v2, v3)):
-        pltpu.make_async_copy(v.at[k], v_out, outs.at[5 + k]).wait()
+    for n in range(3):
+        pltpu.make_async_copy(v.at[n], store.at[pl.ds(CAP + 5 * n, 5)], outs.at[5 + n]).wait()
 
 
 def two_rounds(u, g, rho, near_parts):
@@ -318,7 +319,7 @@
     return once, once + dot3(split(g - once), near_parts)
 
 
-def own_kernel(near, rho_ref, g_part, duals_hbm, a0_hbm, v0, u_part, a0, sems):
+def own_kernel(near, rho_ref, g_part, duals_hbm, room, v0, u_part, a0, sems):
     place = placed()
     copies = [
         pltpu.make_async_copy(
@@ -340,9 +341,12 @@
     for b in range(16):
         a0[b * 80 : b * 80 + SHARE, :] = u_part[b * SHARE : (b + 1) * SHARE, :]
         a0[b * 80 + SHARE : b * 80 + 80, :] = rho * v0[b * SHARE : (b + 1) * SHARE, :]
-    out = pltpu.make_async_copy(a0, a0_hbm.at[pl.ds(0, 2 * CHUNK), :], sems.at[16])
+    out = pltpu.make_async_copy(a0, room.at[pl.ds(0, 2 * CHUNK), :], sems.at[16])
     out.start()
+    v_out = pltpu.make_async_copy(v0, room.at[pl.ds(2 * CHUNK, CHUNK), :], sems.at[17])
+    v_out.start()
     out.wait()
+    v_out.wait()
 
 
 def first_sum_kernel(own_hbm, r1, r2, r3, s0, q1, q2, q3, acc, part, coded, own, sem):
@@ -445,9 +449,18 @@
 
 
 def duals_kernel(first, near, rho_ref, *refs):
-    both, two, v = refs[0:2], refs[2:4], refs[4:6]
-    out, part, z0_part, z1_part, value, sems = refs[-6:]
+    both, two, store, room = refs[0:2], refs[2:4], refs[4], refs[5]
+    out, part, z0_part, z1_part, value, own, less, done, sems = refs[-9:]
     place = placed()
+    fetches = []
+    for n in range(2):
+        at = CAP + 5 * (first + n - 1)
+        source = store.at[pl.ds(at, 5)]
+        target = value.at[pl.ds(n * 5, 5)]
+        if first + n == 0:
+            source, target = room.at[pl.ds(2 * CHUNK, CHUNK), :], own
+        fetches.append(pltpu.make_async_copy(source, target, sems.at[32 + n]))
+        fetches[n].start()
     near_parts = split(near[...])
 
     def chunk(k, _):
@@ -457,7 +470,6 @@
             def _(n=n):
                 part[0:1280, :] = from_codes(both[n][...])
                 part[1280:, :] = from_codes(two[n][...])
-                value[n] = v[n][...]
 
         for b in range(16):
             rows = slice(b * SHARE, (b + 1) * SHARE)
@@ -467,13 +479,21 @@
             z0_part[rows, :] = decode(part[at : at + 40, :], part[to + 41 : to + 42, :])
             z1_part[rows, :] = 2.0 * z1
             z2 = decode(part[to : to + 40, :], part[to + 40 : to + 41, :])
-            value[k, rows, :] = value[k, rows, :] - z1 - z2
+            less[rows, :] = z1 + z2
         z0 = z0_part[...]
         inner = z0 - dot3(split(z0), near_parts) + z1_part[...]
-        value[k] = value[k] + dot3(split(inner), near_parts)
+        less[...] = dot3(split(inner), near_parts) - less[...]
+        for n in range(2):
+
+            @pl.when(k == n)
+            def _(n=n):
+                fetches[n].wait()
+                base = own[...] if first + n == 0 else value[n * 5 : n * 5 + 5].reshape(CHUNK, R)
+                done[n] = base + less[...]
+
         for b in range(16):
             pltpu.make_async_copy(
-                value.at[k, pl.ds(b * SHARE, SHARE), :],
+                done.at[k, pl.ds(b * SHARE, SHARE), :],
                 out.at[pl.ds(block_row(place, first + k, b), SHARE), :],
                 sems.at[k * 16 + b],
             ).start()
@@ -483,7 +503,7 @@
     for k in range(2):
         for b in range(16):
             pltpu.make_async_copy(
-                value.at[k, pl.ds(b * SHARE, SHARE), :],
+                done.at[k, pl.ds(b * SHARE, SHARE), :],
                 out.at[pl.ds(block_row(place, first + k, b), SHARE), :],
                 sems.at[k * 16 + b],
             ).wait()
@@ -528,13 +548,13 @@
         return jax.ShapeDtypeStruct((rows, R), jnp.int16)
 
     tops = [coded_rows(n) for n in (32, 8, 2)]
-    prod, v1, v2, v3, g_own, *s = call(
+    store, g_own, *s = call(
         local_kernel,
-        [(SLOTS, BLOCK, R)] + [(CHUNK, R)] * 4 + [codes(tops[0])] * 3,
-        "ssssvvhhhh" + "hhhhhhhh",
+        [(SLOTS, BLOCK, R), (CHUNK, R)] + [codes(tops[0])] * 3,
+        "ssssvvhhhh" + "hhhhh",
         [
             pltpu.VMEM((1024, R), BF16), (MONTHS, R), pltpu.VMEM((CAP, BLOCK, BLOCK), BF16),
-            (ROWS, R), (CAP, BLOCK, R), (ROWS, R), (CHUNK, R), (CHUNK, R), (3, CHUNK, R),
+            (ROWS, R), (CAP, BLOCK, R), (ROWS, R), (CHUNK, R), (CHUNK, R), (3, 5, BLOCK, R),
             (CHUNK, R), (tops[0], R), pltpu.VMEM((3, tops[0], R), jnp.int16),
             pltpu.SemaphoreType.DMA((4,)), pltpu.SemaphoreType.DMA((8,)),
         ],
@@ -542,9 +562,9 @@
         near, rho, patient_factor, month_factor, tile_values, scaled_duals, limit=None,
     )
     s = [send(s[k - 1], first_move(k)) for k in (1, 2, 3)]
-    a0, v0 = call(
-        own_kernel, [(ROOM_ROWS, R), (CHUNK, R)], "vvvh" + "hv",
-        [(CHUNK, R), (2 * CHUNK, R), pltpu.SemaphoreType.DMA((17,))],
+    (room,) = call(
+        own_kernel, [(ROOM_ROWS, R)], "vvvh" + "h",
+        [(CHUNK, R), (CHUNK, R), (2 * CHUNK, R), pltpu.SemaphoreType.DMA((18,))],
         near, rho, g_own, scaled_duals, limit=None,
     )
     m = exchange(fan(m, 4), "z")
@@ -553,7 +573,7 @@
     s = call(
         first_sum_kernel, [(320, R)] + [codes(tops[1])] * 3, "hvvv" + "vvvv",
         [(2 * CHUNK, R), (tops[0], R), (tops[1], R), (2 * CHUNK, R), pltpu.SemaphoreType.DMA],
-        a0, *s,
+        room, *s,
     )
     s = scatter_sum(s, second_move)
     s = call(
@@ -575,19 +595,24 @@
     (sums,) = call(
         month_kernel, [(384, R)], "sssvvvvhv" + "v",
         [(ROWS, R), (768, R), (CAP, BLOCK, R), pltpu.SemaphoreType.DMA((CAP,))],
-        live_count, code_block, month_index, *two, prod, code_gram,
+        live_count, code_block, month_index, *two, store, code_gram,
     )
     t = exchange(sums.reshape(16, -1, R), PLANE)
-    t = exchange(fan(t, 16), ("z", "h", "c"))
+    t = fan(t, 1)
+    t = jnp.concatenate([t, send(t, CORE_MOVE)], 0)
+    t = exchange(fan(t, 8), ("z", "h"))
     t = exchange(fan(t, 16), PLANE).reshape(-1, R)
-    scratch = [(2048, R), (CHUNK, R), (CHUNK, R), (2, CHUNK, R), pltpu.SemaphoreType.DMA((32,))]
+    scratch = [
+        (2048, R), (CHUNK, R), (CHUNK, R), (10, BLOCK, R), (CHUNK, R), (CHUNK, R), (2, CHUNK, R),
+        pltpu.SemaphoreType.DMA((34,)),
+    ]
     (duals,) = call(
-        functools.partial(duals_kernel, 0), [(ROWS, R)], "v" * 8 + "h", scratch,
-        near, rho, *both[:2], *two[:2], v0, v1,
+        functools.partial(duals_kernel, 0), [(ROWS, R)], "vvvvvvhh" + "h", scratch,
+        near, rho, *both[:2], *two[:2], store, room,
     )
     (duals,) = call(
-        functools.partial(duals_kernel, 2), [(ROWS, R)], "v" * 8 + "h" + "h", scratch,
-        near, rho, *both[2:], *two[2:], v2, v3, duals, aliases={8: 0},
+        functools.partial(duals_kernel, 2), [(ROWS, R)], "vvvvvvhhh" + "h", scratch,
+        near, rho, *both[2:], *two[2:], store, room, duals, aliases={8: 0},
     )
     (new_months,) = call(
         tail_kernel, [(MONTHS, R)], "vvvv", [(R, R), (R, R), (BLOCK, R)], t, gram, month_factor

time: 199 us -> 190 us (0.955)
  starting transfers between devices: 57.7 us -> 49.9 us
  local copies, waits for them, and re-layouts: 4.88 us -> 2.64 us
    all_to_all x3, starting transfers between devices: 30.7 us -> 15 us  [exchange(): return lax.all_to_all(value, axes, 0, 0, tiled=True)]
    ppermute x22 -> x23, starting transfers between devices: 26.9 us -> 34.9 us  [send(): return lax.ppermute(value, AXES, pairs)]
    all_to_all x3, waiting for transfers between devices: 10.8 us -> 2.88 us  [exchange(): return lax.all_to_all(value, axes, 0, 0, tiled=True)]
    ppermute x22 -> x23, waiting for transfers between devices: 29.7 us -> 37.4 us  [send(): return lax.ppermute(value, AXES, pairs)]
    unnamed x35 -> x27, local copies, waits for them, and re-layouts: 4.84 us -> 2.6 us
    pallas_call x15 -> x16, Pallas kernels: 45.1 us -> 44.3 us  [call(): pl.pallas_call(body, input_output_aliases=aliases or {}, out_shape=[s if...]
  transfers between devices with their start and end apart: 25 -> 26, of which waited for: 13 -> 13; matrix products, arithmetic and copies ran while one was open for 0% -> 0% of each run, Pallas kernels for 14% -> 14%
where the time goes in v8:
time: 190 us; the launch traced here: 188 us
  starting transfers between devices  49.9 us (26%)
  blocking collectives  49.5 us (26%)
  Pallas kernels  44.3 us (23%)
  waiting for transfers between devices  40.3 us (21%)
  local copies, waits for them, and re-layouts  2.64 us (1%)
    all_to_all x3, blocking collectives, exchange(): return lax.all_to_all(value, axes, 0, 0, tiled=True)  49.5 us
    pallas_call x16, Pallas kernels, call(): pl.pallas_call(body, input_output_aliases=aliases or {}, out_shape=[s if...  44.3 us
    ppermute x23, waiting for transfers between devices, send(): return lax.ppermute(value, AXES, pairs)  37.4 us
    ppermute x23, starting transfers between devices, send(): return lax.ppermute(value, AXES, pairs)  34.9 us
    all_to_all x3, starting transfers between devices, exchange(): return lax.all_to_all(value, axes, 0, 0, tiled=True)  15 us
  transfers between devices with their start and end apart: 26, of which 13 were waited for; matrix products, arithmetic and copies ran while one was open for 0% of the time, Pallas kernels for 14%

profile of v8, /device:TPU:1, one launch (start us, length us, event | category | flops | bytes accessed | tf_op | source)
XLA Modules:
  0.0 188.2 jit_solution(13284518888595046652)
XLA Ops:
  0.6 7.5 %shard_map.112 = (f32[256,256]{1,0:T(8,128)}, f32[8,128]{1,0:T(8,128)}, f32[384,256]{1,0:T(8,128)}) custom-call(bf16[1024,256]{1,0:T(8,128)(2,1)} %patient_hbm.1, f32[120,256]{1,0:T(8,128)} %month.5), custom_call_target="tpu_custom_call" | custom-call | tf_op jit(solution)/shard_map/pallas_call | solution.py:526
  8.2 17.1 %all_to_all.30.got = f32[16,24,256]{2,1,0:T(8,128)S(1)} all-to-all(f32[16,24,256]{2,1,0:T(8,128)} %bitcast.20), channel_id=1, replica_groups=mesh['z'=4,'y'=4,'x'=4,'h'=2,'c'=2] {'y','x'}, dimensions={0} | all-to-all | bytes 786432 | tf_op jit(solution)/shard_map/all_to_all | solution.py:76
  25.3 0.7 shard_map.117
  25.9 5.6 %all-to-all-start.1 = ((f32[4,24,256]{2,1,0:T(8,128)}), f32[4,24,256]{2,1,0:T(8,128)S(1)}, u32[]{:S(2)}, u32[]{:S(2)}) async-start(f32[4,24,256]{2,1,0:T(8,128)} %shard_map.117), calls=%async_computation.1 | async-start | bytes 196608 | tf_op jit(solution)/shard_map/all_to_all | solution.py:76
  32.2 8.4 %shard_map.113 = (f32[120,128,256]{2,1,0:T(8,128)}, f32[640,256]{1,0:T(8,128)}, s16[1312,256]{1,0:T(8,128)(2,1)}, s16[1312,256]{1,0:T(8,128)(2,1)}, s16[1312,256]{1,0:T(8,128)(2,1)}) custom-call(s32[1]{0:T(128)S(6)} %copy.17.live, s32[20]{0:T(128)} %patient_at.1, s32[20]{0:T(128)} %code_at.3, s32[20]{0:T(128)} %month_at.3, ...), custom_call_target="tpu_custom_call" | custom-call | tf_op jit(solution)/shard_map/pallas_call | solution.py:526
  40.6 0.1 collective-permute-start
  40.7 1.8 collective-permute-start.1
  42.6 0.8 collective-permute-start.2
  43.4 0.0 all-to-all-done.1.got
  43.4 19.6 %all_to_all.31 = f32[16,24,256]{2,1,0:T(8,128)S(1)} all-to-all(f32[16,24,256]{2,1,0:T(8,128)S(1)} %shard_map.118), channel_id=1, replica_groups=mesh['z'=4,'y'=4,'x'=4,'h'=2,'c'=2] {'y','x'}, dimensions={0} | all-to-all | bytes 786432 | tf_op jit(solution)/shard_map/all_to_all | solution.py:76
  63.0 3.8 %collective-permute-start.9 = (f32[384,256]{1,0:T(8,128)S(1)}, f32[384,256]{1,0:T(8,128)S(1)}, u32[]{:S(2)}, u32[]{:S(2)}) collective-permute-start(f32[384,256]{1,0:T(8,128)S(1)} %bitcast.13), channel_id=1, source_target_pairs={{0,1},{1,0},{2,3},{3,2},{4,5},{5,4},{6,7},{7,6},{8,9},{9,8},{10,11... | collective-permute-start | bytes 1179656 | tf_op jit(solution)/shard_map/ppermute | solution.py:64
  66.8 4.8 %shard_map.114.own_hbm.refs_5_ = f32[15360,256]{1,0:T(8,128)} custom-call(f32[256,256]{1,0:T(8,128)} %get-tuple-element.23.near, f32[8,128]{1,0:T(8,128)} %get-tuple-element.24.rho_ref, f32[640,256]{1,0:T(8,128)} %get-tuple-element.25.g_part, f32[2560,256]{1,0:T(8,128)} %duals_hbm.3), custom_call_target="tpu_custom_call" | custom-call | tf_op jit(solution)/shard_map/pallas_call | solution.py:526
  71.6 0.0 copy-start.1
  71.6 0.0 copy-start.9
  71.6 0.0 collective-permute-done.1.r2
  71.7 0.0 collective-permute-done.2.r3
  71.7 1.7 shard_map.115
  73.4 0.0 copy-start.10
  73.4 0.0 copy-start.11
  73.4 0.9 collective-permute-start.3
  74.3 3.0 %collective-permute-start.4 = (s16[336,256]{1,0:T(8,128)(2,1)S(1)}, s16[336,256]{1,0:T(8,128)(2,1)S(1)}, u32[]{:S(2)}, u32[]{:S(2)}) collective-permute-start(s16[336,256]{1,0:T(8,128)(2,1)S(1)} %get-tuple-element.31), channel_id=1, source_target_pairs={{0,32},{1,9},{2,34},{3,11},{4,36},{5,13},{6,38},{7,15},{8,40},{9,1... | collective-permute-start | bytes 516104 | tf_op jit(solution)/shard_map/ppermute | solution.py:64
  77.3 1.9 %collective-permute-done.3.r1 = s16[336,256]{1,0:T(8,128)(2,1)S(1)} collective-permute-done((s16[336,256]{1,0:T(8,128)(2,1)S(1)}, s16[336,256]{1,0:T(8,128)(2,1)S(1)}, u32[]{:S(2)}, u32[]{:S(2)}) %collective-permute-start.3) | collective-permute-done | bytes 172064 | tf_op jit(solution)/shard_map/ppermute | solution.py:64
  79.3 2.9 %collective-permute-done.4.r2 = s16[336,256]{1,0:T(8,128)(2,1)S(1)} collective-permute-done((s16[336,256]{1,0:T(8,128)(2,1)S(1)}, s16[336,256]{1,0:T(8,128)(2,1)S(1)}, u32[]{:S(2)}, u32[]{:S(2)}) %collective-permute-start.4) | collective-permute-done | bytes 172064 | tf_op jit(solution)/shard_map/ppermute | solution.py:64
  82.2 0.3 shard_map.116
  82.5 2.0 %collective-permute-start.6 = (s16[96,256]{1,0:T(8,128)(2,1)S(1)}, s16[96,256]{1,0:T(8,128)(2,1)S(1)}, u32[]{:S(2)}, u32[]{:S(2)}) collective-permute-start(s16[96,256]{1,0:T(8,128)(2,1)S(1)} %get-tuple-element.34), channel_id=1, source_target_pairs={{0,64},{1,65},{2,66},{3,67},{4,68},{5,69},{6,70},{7,71},{8,72},{9,... | collective-permute-start | bytes 147464 | tf_op jit(solution)/shard_map/ppermute | solution.py:64
  84.5 2.1 %collective-permute-start.7 = (s16[96,256]{1,0:T(8,128)(2,1)S(1)}, s16[96,256]{1,0:T(8,128)(2,1)S(1)}, u32[]{:S(2)}, u32[]{:S(2)}) collective-permute-start(s16[96,256]{1,0:T(8,128)(2,1)S(1)} %get-tuple-element.35), channel_id=1, source_target_pairs={{0,128},{1,129},{2,130},{3,131},{4,132},{5,133},{6,134},{7,135},{8... | collective-permute-start | bytes 147464 | tf_op jit(solution)/shard_map/ppermute | solution.py:64
  86.6 1.2 collective-permute-start.8
  87.8 2.0 %collective-permute-done.7.s2 = s16[96,256]{1,0:T(8,128)(2,1)S(1)} collective-permute-done((s16[96,256]{1,0:T(8,128)(2,1)S(1)}, s16[96,256]{1,0:T(8,128)(2,1)S(1)}, u32[]{:S(2)}, u32[]{:S(2)}) %collective-permute-start.7) | collective-permute-done | bytes 49184 | tf_op jit(solution)/shard_map/ppermute | solution.py:64
  89.8 0.5 collective-permute-done.8.s3
  90.3 1.4 shard_map.119
  91.7 1.3 collective-permute-start.12
  93.1 1.5 collective-permute-start.11
  94.6 0.6 collective-permute-start.10
  95.2 4.3 %collective-permute-done.10 = s16[128,256]{1,0:T(8,128)(2,1)S(1)} collective-permute-done((s16[128,256]{1,0:T(8,128)(2,1)S(1)}, s16[128,256]{1,0:T(8,128)(2,1)S(1)}, u32[]{:S(2)}, u32[]{:S(2)}) %collective-permute-start.10) | collective-permute-done | bytes 65568 | tf_op jit(solution)/shard_map/ppermute | solution.py:64
  99.6 0.1 collective-permute-start.15
  99.7 1.4 collective-permute-start.14
  101.1 1.5 collective-permute-start.13
  102.6 6.5 %collective-permute-done.15.r3 = s16[512,256]{1,0:T(8,128)(2,1)S(1)} collective-permute-done((s16[512,256]{1,0:T(8,128)(2,1)S(1)}, s16[512,256]{1,0:T(8,128)(2,1)S(1)}, u32[]{:S(2)}, u32[]{:S(2)}) %collective-permute-start.15) | collective-permute-done | bytes 262176 | tf_op jit(solution)/shard_map/ppermute | solution.py:64
  109.1 0.7 collective-permute-done.13.r1
  109.9 0.6 copy-done.4
  110.5 0.2 collective-permute-start.21
  110.7 1.3 collective-permute-start.19
  112.0 0.0 collective-permute-start.18
  112.0 5.4 %collective-permute-done.21.refs_3_.w1 = s16[768,256]{1,0:T(8,128)(2,1)S(1)} collective-permute-done((s16[768,256]{1,0:T(8,128)(2,1)S(1)}, s16[768,256]{1,0:T(8,128)(2,1)S(1)}, u32[]{:S(2)}, u32[]{:S(2)}) %collective-permute-start.21) | collective-permute-done | bytes 393248 | tf_op jit(solution)/shard_map/ppermute | solution.py:64
  117.4 5.6 %collective-permute-done.19.refs_3_.w3 = s16[768,256]{1,0:T(8,128)(2,1)S(1)} collective-permute-done((s16[768,256]{1,0:T(8,128)(2,1)S(1)}, s16[768,256]{1,0:T(8,128)(2,1)S(1)}, u32[]{:S(2)}, u32[]{:S(2)}) %collective-permute-start.19) | collective-permute-done | bytes 393248 | tf_op jit(solution)/shard_map/ppermute | solution.py:64
  123.0 2.0 %shard_map.123 = f32[384,256]{1,0:T(8,128)S(1)} custom-call(s32[1]{0:T(128)S(6)} %copy.17.live, s32[20]{0:T(128)S(1)} %copy-done.10, s32[20]{0:T(128)S(1)} %copy-done.11, s16[768,256]{1,0:T(8,128)(2,1)S(1)} %pad_add_fusion.refs_2_.w0, s16[768,256]{1,0:T(8,128)(2,1)S(1)} %collective-permute-done.21.refs_3_.w1, ...), custom_call_target="tpu_custom_call" | custom-call | tf_op jit(solution)/shard_map/pallas_call | solution.py:526
  125.0 12.8 %all_to_all.32.got = f32[16,24,256]{2,1,0:T(8,128)S(1)} all-to-all(f32[16,24,256]{2,1,0:T(8,128)S(1)} %bitcast.15), channel_id=1, replica_groups=mesh['z'=4,'y'=4,'x'=4,'h'=2,'c'=2] {'y','x'}, dimensions={0} | all-to-all | bytes 786432 | tf_op jit(solution)/shard_map/all_to_all | solution.py:76
  137.9 9.1 %collective-permute-start.22 = (f32[1,24,256]{2,1,0:T(8,128)S(1)}, f32[1,24,256]{2,1,0:T(8,128)S(1)}, u32[]{:S(2)}, u32[]{:S(2)}) collective-permute-start(f32[1,24,256]{2,1,0:T(8,128)S(1)} %shard_map.124), channel_id=1, source_target_pairs={{0,1},{1,0},{2,3},{3,2},{4,5},{5,4},{6,7},{7,6},{8,9},{9,8},{10,11... | collective-permute-start | bytes 73736 | tf_op jit(solution)/shard_map/ppermute | solution.py:64
  146.9 0.8 collective-permute-done.22
  147.8 0.7 shard_map.125
  148.5 5.8 %all-to-all-start.4 = ((f32[8,24,256]{2,1,0:T(8,128)}), f32[8,24,256]{2,1,0:T(8,128)S(1)}, u32[]{:S(2)}, u32[]{:S(2)}) async-start(f32[8,24,256]{2,1,0:T(8,128)} %shard_map.125), calls=%async_computation.4 | async-start | bytes 393216 | tf_op jit(solution)/shard_map/all_to_all | solution.py:76
  154.3 0.9 copy-done.3
  155.2 0.9 copy-done.5
  156.2 0.7 collective-permute-start.20
  156.9 0.9 collective-permute-start.17
  157.8 0.6 collective-permute-start.16
  158.3 2.9 %all-to-all-done.4.got = f32[8,24,256]{2,1,0:T(8,128)S(1)} async-done(((f32[8,24,256]{2,1,0:T(8,128)}), f32[8,24,256]{2,1,0:T(8,128)S(1)}, u32[]{:S(2)}, u32[]{:S(2)}) %all-to-all-start.4) | async-done | bytes 196640 | tf_op jit(solution)/shard_map/all_to_all | solution.py:76
  161.2 0.8 shard_map.126
  162.0 3.6 %all-to-all-start.5 = ((f32[16,24,256]{2,1,0:T(8,128)}), f32[16,24,256]{2,1,0:T(8,128)S(1)}, u32[]{:S(2)}, u32[]{:S(2)}) async-start(f32[16,24,256]{2,1,0:T(8,128)} %shard_map.126), calls=%async_computation.5 | async-start | bytes 786432 | tf_op jit(solution)/shard_map/all_to_all | solution.py:76
  165.6 0.6 collective-permute-done.20.refs_1_
  166.1 5.0 %shard_map.121.refs_6_ = f32[2560,256]{1,0:T(8,128)} custom-call(f32[256,256]{1,0:T(8,128)S(1)} %copy-done, f32[8,128]{1,0:T(8,128)S(1)} %copy-done.8, s16[1280,256]{1,0:T(8,128)(2,1)S(1)} %shard_map.120.refs_0_, s16[1280,256]{1,0:T(8,128)(2,1)} %collective-permute-done.20.refs_1_, s16[768,256]{1,0:T(8,128)(2,1)S(1)} %pad_add_fusion.refs_2_.w0, ...), custom_call_target="tpu_custom_call" | custom-call | tf_op jit(solution)/shard_map/pallas_call | solution.py:526
  171.2 6.1 %collective-permute-done.17.refs_1_ = s16[1280,256]{1,0:T(8,128)(2,1)} collective-permute-done((s16[1280,256]{1,0:T(8,128)(2,1)S(1)}, s16[1280,256]{1,0:T(8,128)(2,1)}, u32[]{:S(2)}, u32[]{:S(2)}) %collective-permute-start.17) | collective-permute-done | bytes 655392 | tf_op jit(solution)/shard_map/ppermute | solution.py:64
  177.3 5.2 %shard_map.122 = f32[2560,256]{1,0:T(8,128)} custom-call(f32[256,256]{1,0:T(8,128)S(1)} %copy-done, f32[8,128]{1,0:T(8,128)S(1)} %copy-done.8, s16[1280,256]{1,0:T(8,128)(2,1)} %collective-permute-done.16.refs_0_, s16[1280,256]{1,0:T(8,128)(2,1)} %collective-permute-done.17.refs_1_, ...), custom_call_target="tpu_custom_call", output_to_operand_aliasing={{}: (8, {})} | custom-call | tf_op jit(solution)/shard_map/pallas_call | solution.py:526
  182.5 5.7 %shard_map.127 = f32[120,256]{1,0:T(8,128)} custom-call(f32[384,256]{1,0:T(8,128)S(1)} %bitcast.12, f32[256,256]{1,0:T(8,128)S(1)} %copy-done.7, f32[120,256]{1,0:T(8,128)S(1)} %copy-done.1), custom_call_target="tpu_custom_call" | custom-call | tf_op jit(solution)/shard_map/pallas_call | solution.py:526
  (41 shorter events, 0.3 us)
Async XLA Ops:
  25.9 17.4 %all-to-all-start.1 = ((f32[4,24,256]{2,1,0:T(8,128)}), f32[4,24,256]{2,1,0:T(8,128)S(1)}, u32[]{:S(2)}, u32[]{:S(2)}) async-start(f32[4,24,256]{2,1,0:T(8,128)} %shard_map.117), calls=%async_computation.1 | async-start | bytes 196608 | tf_op jit(solution)/shard_map/all_to_all | solution.py:76
  40.6 31.0 %collective-permute-start = (s16[1312,256]{1,0:T(8,128)(2,1)}, s16[1312,256]{1,0:T(8,128)(2,1)S(1)}, u32[]{:S(2)}, u32[]{:S(2)}) collective-permute-start(s16[1312,256]{1,0:T(8,128)(2,1)} %get-tuple-element.26), channel_id=1, source_target_pairs={{0,4},{1,17},{2,6},{3,19},{4,8},{5,21},{6,10},{7,23},{8,12},{9,25}... | collective-permute-start | bytes 2015240 | tf_op jit(solution)/shard_map/ppermute | solution.py:64
  40.7 30.9 %collective-permute-start.1 = (s16[1312,256]{1,0:T(8,128)(2,1)}, s16[1312,256]{1,0:T(8,128)(2,1)S(1)}, u32[]{:S(2)}, u32[]{:S(2)}) collective-permute-start(s16[1312,256]{1,0:T(8,128)(2,1)} %get-tuple-element.27), channel_id=1, source_target_pairs={{0,8},{1,33},{2,10},{3,35},{4,12},{5,37},{6,14},{7,39},{8,0},{9,41... | collective-permute-start | bytes 2015240 | tf_op jit(solution)/shard_map/ppermute | solution.py:64
  42.6 29.1 %collective-permute-start.2 = (s16[1312,256]{1,0:T(8,128)(2,1)}, s16[1312,256]{1,0:T(8,128)(2,1)S(1)}, u32[]{:S(2)}, u32[]{:S(2)}) collective-permute-start(s16[1312,256]{1,0:T(8,128)(2,1)} %get-tuple-element.28), channel_id=1, source_target_pairs={{0,12},{1,49},{2,14},{3,51},{4,0},{5,53},{6,2},{7,55},{8,4},{9,57}... | collective-permute-start | bytes 2015240 | tf_op jit(solution)/shard_map/ppermute | solution.py:64
  63.0 27.3 %collective-permute-start.9 = (f32[384,256]{1,0:T(8,128)S(1)}, f32[384,256]{1,0:T(8,128)S(1)}, u32[]{:S(2)}, u32[]{:S(2)}) collective-permute-start(f32[384,256]{1,0:T(8,128)S(1)} %bitcast.13), channel_id=1, source_target_pairs={{0,1},{1,0},{2,3},{3,2},{4,5},{5,4},{6,7},{7,6},{8,9},{9,8},{10,11... | collective-permute-start | bytes 1179656 | tf_op jit(solution)/shard_map/ppermute | solution.py:64
  71.6 18.7 %copy-start.1 = (f32[120,256]{1,0:T(8,128)S(1)}, f32[120,256]{1,0:T(8,128)}, u32[]{:S(2)}) copy-start(f32[120,256]{1,0:T(8,128)} %month.5) | copy-start | bytes 368644
  71.6 18.7 %copy-start.9 = (f32[40,256]{1,0:T(8,128)S(1)}, f32[40,256]{1,0:T(8,128)}, u32[]{:S(2)}) copy-start(f32[40,256]{1,0:T(8,128)} %z0_ref.1) | copy-start | bytes 122884
  73.4 49.6 %copy-start.10 = (s32[20]{0:T(128)S(1)}, s32[20]{0:T(128)}, u32[]{:S(2)}) copy-start(s32[20]{0:T(128)} %code_at.3) | copy-start | bytes 244
  73.4 49.6 %copy-start.11 = (s32[20]{0:T(128)S(1)}, s32[20]{0:T(128)}, u32[]{:S(2)}) copy-start(s32[20]{0:T(128)} %month_at.3) | copy-start | bytes 244
  73.4 5.8 %collective-permute-start.3 = (s16[336,256]{1,0:T(8,128)(2,1)S(1)}, s16[336,256]{1,0:T(8,128)(2,1)S(1)}, u32[]{:S(2)}, u32[]{:S(2)}) collective-permute-start(s16[336,256]{1,0:T(8,128)(2,1)S(1)} %get-tuple-element.30), channel_id=1, source_target_pairs={{0,16},{1,5},{2,18},{3,7},{4,20},{5,9},{6,22},{7,11},{8,24},{9,13}... | collective-permute-start | bytes 516104 | tf_op jit(solution)/shard_map/ppermute | solution.py:64
  74.3 7.9 %collective-permute-start.4 = (s16[336,256]{1,0:T(8,128)(2,1)S(1)}, s16[336,256]{1,0:T(8,128)(2,1)S(1)}, u32[]{:S(2)}, u32[]{:S(2)}) collective-permute-start(s16[336,256]{1,0:T(8,128)(2,1)S(1)} %get-tuple-element.31), channel_id=1, source_target_pairs={{0,32},{1,9},{2,34},{3,11},{4,36},{5,13},{6,38},{7,15},{8,40},{9,1... | collective-permute-start | bytes 516104 | tf_op jit(solution)/shard_map/ppermute | solution.py:64
  77.3 4.9 %collective-permute-start.5 = (s16[336,256]{1,0:T(8,128)(2,1)S(1)}, s16[336,256]{1,0:T(8,128)(2,1)S(1)}, u32[]{:S(2)}, u32[]{:S(2)}) collective-permute-start(s16[336,256]{1,0:T(8,128)(2,1)S(1)} %get-tuple-element.32), channel_id=1, source_target_pairs={{0,48},{1,13},{2,50},{3,15},{4,52},{5,1},{6,54},{7,3},{8,56},{9,5}... | collective-permute-start | bytes 516104 | tf_op jit(solution)/shard_map/ppermute | solution.py:64
  82.5 5.3 %collective-permute-start.6 = (s16[96,256]{1,0:T(8,128)(2,1)S(1)}, s16[96,256]{1,0:T(8,128)(2,1)S(1)}, u32[]{:S(2)}, u32[]{:S(2)}) collective-permute-start(s16[96,256]{1,0:T(8,128)(2,1)S(1)} %get-tuple-element.34), channel_id=1, source_target_pairs={{0,64},{1,65},{2,66},{3,67},{4,68},{5,69},{6,70},{7,71},{8,72},{9,... | collective-permute-start | bytes 147464 | tf_op jit(solution)/shard_map/ppermute | solution.py:64
  84.5 5.3 %collective-permute-start.7 = (s16[96,256]{1,0:T(8,128)(2,1)S(1)}, s16[96,256]{1,0:T(8,128)(2,1)S(1)}, u32[]{:S(2)}, u32[]{:S(2)}) collective-permute-start(s16[96,256]{1,0:T(8,128)(2,1)S(1)} %get-tuple-element.35), channel_id=1, source_target_pairs={{0,128},{1,129},{2,130},{3,131},{4,132},{5,133},{6,134},{7,135},{8... | collective-permute-start | bytes 147464 | tf_op jit(solution)/shard_map/ppermute | solution.py:64
  86.6 3.7 %collective-permute-start.8 = (s16[96,256]{1,0:T(8,128)(2,1)S(1)}, s16[96,256]{1,0:T(8,128)(2,1)S(1)}, u32[]{:S(2)}, u32[]{:S(2)}) collective-permute-start(s16[96,256]{1,0:T(8,128)(2,1)S(1)} %get-tuple-element.36), channel_id=1, source_target_pairs={{0,192},{1,193},{2,194},{3,195},{4,196},{5,197},{6,198},{7,199},{8... | collective-permute-start | bytes 147464 | tf_op jit(solution)/shard_map/ppermute | solution.py:64
  91.7 33.3 %copy-start.6 = (f32[256,256]{1,0:T(8,128)}, f32[256,256]{1,0:T(8,128)S(1)}, u32[]{:S(2)}) copy-start(f32[256,256]{1,0:T(8,128)S(1)} %get-tuple-element.42.gram) | copy-start | bytes 786436
  91.7 7.8 %collective-permute-start.12 = (s16[128,256]{1,0:T(8,128)(2,1)S(1)}, s16[128,256]{1,0:T(8,128)(2,1)S(1)}, u32[]{:S(2)}, u32[]{:S(2)}) collective-permute-start(s16[128,256]{1,0:T(8,128)(2,1)S(1)} %get-tuple-element.39), channel_id=1, source_target_pairs={{0,64},{1,65},{2,66},{3,67},{4,68},{5,69},{6,70},{7,71},{8,72},{9,... | collective-permute-start | bytes 196616 | tf_op jit(solution)/shard_map/ppermute | solution.py:64
  93.1 6.5 %collective-permute-start.11 = (s16[128,256]{1,0:T(8,128)(2,1)S(1)}, s16[128,256]{1,0:T(8,128)(2,1)S(1)}, u32[]{:S(2)}, u32[]{:S(2)}) collective-permute-start(s16[128,256]{1,0:T(8,128)(2,1)S(1)} %get-tuple-element.39), channel_id=1, source_target_pairs={{0,128},{1,129},{2,130},{3,131},{4,132},{5,133},{6,134},{7,135},{8... | collective-permute-start | bytes 196616 | tf_op jit(solution)/shard_map/ppermute | solution.py:64
  94.6 4.9 %collective-permute-start.10 = (s16[128,256]{1,0:T(8,128)(2,1)S(1)}, s16[128,256]{1,0:T(8,128)(2,1)S(1)}, u32[]{:S(2)}, u32[]{:S(2)}) collective-permute-start(s16[128,256]{1,0:T(8,128)(2,1)S(1)} %get-tuple-element.39), channel_id=1, source_target_pairs={{0,192},{1,193},{2,194},{3,195},{4,196},{5,197},{6,198},{7,199},{8... | collective-permute-start | bytes 196616 | tf_op jit(solution)/shard_map/ppermute | solution.py:64
  99.6 9.5 %collective-permute-start.15 = (s16[512,256]{1,0:T(8,128)(2,1)S(1)}, s16[512,256]{1,0:T(8,128)(2,1)S(1)}, u32[]{:S(2)}, u32[]{:S(2)}) collective-permute-start(s16[512,256]{1,0:T(8,128)(2,1)S(1)} %constant_dynamic-update-slice_fusion.r0), channel_id=1, source_target_pairs={{0,16},{1,5},{2,18},{3,7},{4,20},{5,9},{6,22},{7,11},{8,24},{9,13}... | collective-permute-start | bytes 786440 | tf_op jit(solution)/shard_map/ppermute | solution.py:64
  99.7 9.4 %collective-permute-start.14 = (s16[512,256]{1,0:T(8,128)(2,1)S(1)}, s16[512,256]{1,0:T(8,128)(2,1)S(1)}, u32[]{:S(2)}, u32[]{:S(2)}) collective-permute-start(s16[512,256]{1,0:T(8,128)(2,1)S(1)} %constant_dynamic-update-slice_fusion.r0), channel_id=1, source_target_pairs={{0,32},{1,9},{2,34},{3,11},{4,36},{5,13},{6,38},{7,15},{8,40},{9,1... | collective-permute-start | bytes 786440 | tf_op jit(solution)/shard_map/ppermute | solution.py:64
  101.1 8.7 %collective-permute-start.13 = (s16[512,256]{1,0:T(8,128)(2,1)S(1)}, s16[512,256]{1,0:T(8,128)(2,1)S(1)}, u32[]{:S(2)}, u32[]{:S(2)}) collective-permute-start(s16[512,256]{1,0:T(8,128)(2,1)S(1)} %constant_dynamic-update-slice_fusion.r0), channel_id=1, source_target_pairs={{0,48},{1,13},{2,50},{3,15},{4,52},{5,1},{6,54},{7,3},{8,56},{9,5}... | collective-permute-start | bytes 786440 | tf_op jit(solution)/shard_map/ppermute | solution.py:64
  109.1 0.8 copy-start.2
  109.8 0.7 copy-start.4
  110.5 6.9 %collective-permute-start.21 = (s16[768,256]{1,0:T(8,128)(2,1)S(1)}, s16[768,256]{1,0:T(8,128)(2,1)S(1)}, u32[]{:S(2)}, u32[]{:S(2)}) collective-permute-start(s16[768,256]{1,0:T(8,128)(2,1)S(1)} %pad_add_fusion.refs_2_.w0), channel_id=1, source_target_pairs={{0,12},{1,49},{2,14},{3,51},{4,0},{5,53},{6,2},{7,55},{8,4},{9,57}... | collective-permute-start | bytes 1179656 | tf_op jit(solution)/shard_map/ppermute | solution.py:64
  110.7 12.3 %collective-permute-start.19 = (s16[768,256]{1,0:T(8,128)(2,1)S(1)}, s16[768,256]{1,0:T(8,128)(2,1)S(1)}, u32[]{:S(2)}, u32[]{:S(2)}) collective-permute-start(s16[768,256]{1,0:T(8,128)(2,1)S(1)} %pad_add_fusion.refs_2_.w0), channel_id=1, source_target_pairs={{0,4},{1,17},{2,6},{3,19},{4,8},{5,21},{6,10},{7,23},{8,12},{9,25}... | collective-permute-start | bytes 1179656 | tf_op jit(solution)/shard_map/ppermute | solution.py:64
  112.0 11.0 %collective-permute-start.18 = (s16[768,256]{1,0:T(8,128)(2,1)S(1)}, s16[768,256]{1,0:T(8,128)(2,1)S(1)}, u32[]{:S(2)}, u32[]{:S(2)}) collective-permute-start(s16[768,256]{1,0:T(8,128)(2,1)S(1)} %pad_add_fusion.refs_2_.w0), channel_id=1, source_target_pairs={{0,8},{1,33},{2,10},{3,35},{4,12},{5,37},{6,14},{7,39},{8,0},{9,41... | collective-permute-start | bytes 1179656 | tf_op jit(solution)/shard_map/ppermute | solution.py:64
  125.0 41.1 %copy-start = (f32[256,256]{1,0:T(8,128)S(1)}, f32[256,256]{1,0:T(8,128)}, u32[]{:S(2)}) copy-start(f32[256,256]{1,0:T(8,128)} %get-tuple-element.23.near) | copy-start | bytes 786436
  125.0 41.1 %copy-start.8 = (f32[8,128]{1,0:T(8,128)S(1)}, f32[8,128]{1,0:T(8,128)}, u32[]{:S(2)}) copy-start(f32[8,128]{1,0:T(8,128)} %get-tuple-element.24.rho_ref) | copy-start | bytes 12292
  137.9 9.9 %collective-permute-start.22 = (f32[1,24,256]{2,1,0:T(8,128)S(1)}, f32[1,24,256]{2,1,0:T(8,128)S(1)}, u32[]{:S(2)}, u32[]{:S(2)}) collective-permute-start(f32[1,24,256]{2,1,0:T(8,128)S(1)} %shard_map.124), channel_id=1, source_target_pairs={{0,1},{1,0},{2,3},{3,2},{4,5},{5,4},{6,7},{7,6},{8,9},{9,8},{10,11... | collective-permute-start | bytes 73736 | tf_op jit(solution)/shard_map/ppermute | solution.py:64
  148.5 12.7 %all-to-all-start.4 = ((f32[8,24,256]{2,1,0:T(8,128)}), f32[8,24,256]{2,1,0:T(8,128)S(1)}, u32[]{:S(2)}, u32[]{:S(2)}) async-start(f32[8,24,256]{2,1,0:T(8,128)} %shard_map.125), calls=%async_computation.4 | async-start | bytes 393216 | tf_op jit(solution)/shard_map/all_to_all | solution.py:76
  154.3 0.9 copy-start.3
  155.2 0.9 copy-start.5
  156.2 9.9 %collective-permute-start.20 = (s16[1280,256]{1,0:T(8,128)(2,1)S(1)}, s16[1280,256]{1,0:T(8,128)(2,1)}, u32[]{:S(2)}, u32[]{:S(2)}) collective-permute-start(s16[1280,256]{1,0:T(8,128)(2,1)S(1)} %shard_map.120.refs_0_), channel_id=1, source_target_pairs={{0,12},{1,49},{2,14},{3,51},{4,0},{5,53},{6,2},{7,55},{8,4},{9,57}... | collective-permute-start | bytes 1966088 | tf_op jit(solution)/shard_map/ppermute | solution.py:64
  156.9 20.4 %collective-permute-start.17 = (s16[1280,256]{1,0:T(8,128)(2,1)S(1)}, s16[1280,256]{1,0:T(8,128)(2,1)}, u32[]{:S(2)}, u32[]{:S(2)}) collective-permute-start(s16[1280,256]{1,0:T(8,128)(2,1)S(1)} %shard_map.120.refs_0_), channel_id=1, source_target_pairs={{0,4},{1,17},{2,6},{3,19},{4,8},{5,21},{6,10},{7,23},{8,12},{9,25}... | collective-permute-start | bytes 1966088 | tf_op jit(solution)/shard_map/ppermute | solution.py:64
  157.8 19.5 %collective-permute-start.16 = (s16[1280,256]{1,0:T(8,128)(2,1)S(1)}, s16[1280,256]{1,0:T(8,128)(2,1)}, u32[]{:S(2)}, u32[]{:S(2)}) collective-permute-start(s16[1280,256]{1,0:T(8,128)(2,1)S(1)} %shard_map.120.refs_0_), channel_id=1, source_target_pairs={{0,8},{1,33},{2,10},{3,35},{4,12},{5,37},{6,14},{7,39},{8,0},{9,41... | collective-permute-start | bytes 1966088 | tf_op jit(solution)/shard_map/ppermute | solution.py:64
  162.0 20.5 %all-to-all-start.5 = ((f32[16,24,256]{2,1,0:T(8,128)}), f32[16,24,256]{2,1,0:T(8,128)S(1)}, u32[]{:S(2)}, u32[]{:S(2)}) async-start(f32[16,24,256]{2,1,0:T(8,128)} %shard_map.126), calls=%async_computation.5 | async-start | bytes 786432 | tf_op jit(solution)/shard_map/all_to_all | solution.py:76
  171.1 11.4 %copy-start.7 = (f32[256,256]{1,0:T(8,128)S(1)}, f32[256,256]{1,0:T(8,128)}, u32[]{:S(2)}) copy-start(f32[256,256]{1,0:T(8,128)} %copy-done.6) | copy-start | bytes 786436

commit v9 on v8

--- a/solution.py
+++ b/solution.py
@@ -349,17 +349,27 @@
     v_out.wait()
 
 
-def first_sum_kernel(own_hbm, r1, r2, r3, s0, q1, q2, q3, acc, part, coded, own, sem):
+def first_sum_kernel(own_hbm, r1, r2, r3, s0, q1, q2, q3, p1, p2, p3, c1, c2, c3, own, sem):
     copy = pltpu.make_async_copy(own_hbm.at[pl.ds(0, 2 * CHUNK), :], own, sem)
     copy.start()
-    acc[...] = jnp.zeros_like(acc)
-    for r in (r1, r2, r3):
-        add_blocks(acc, 32, part, r)
+    parts = (p1, p2, p3)
+    for p, r in zip(parts, (r1, r2, r3)):
+        p[...] = from_codes(r[...])
     copy.wait()
-    acc[...] += own[...]
-    s0[...] = acc[0:320, :]
-    for j, out in enumerate((q1, q2, q3)):
-        encode_blocks(acc, (j + 1) * 8, 8, coded, out)
+    for coded in (c1, c2, c3):
+        coded[320:, :] = jnp.zeros((coded.shape[0] - 320, R), F32)
+    for b in range(32):
+        rows = slice(b * SHARE, (b + 1) * SHARE)
+        d1, d2, d3 = [decode(p[rows, :], p[1280 + b : 1281 + b, :]) for p in parts]
+        value = (own[rows, :] + d1) + (d2 + d3)
+        j, at = b // 8, b % 8
+        if j == 0:
+            s0[rows, :] = value
+        else:
+            coded = (c1, c2, c3)[j - 1]
+            coded[at * SHARE : (at + 1) * SHARE, :], coded[320 + at : 321 + at, :] = encode(value)
+    for coded, out in zip((c1, c2, c3), (q1, q2, q3)):
+        out[...] = to_codes(coded[...])
 
 
 def sum_kernel(own, r1, r2, r3, s0, q1, q2, q3, acc, part, coded):
@@ -572,7 +582,7 @@
     other = send(mine, CORE_MOVE)
     s = call(
         first_sum_kernel, [(320, R)] + [codes(tops[1])] * 3, "hvvv" + "vvvv",
-        [(2 * CHUNK, R), (tops[0], R), (tops[1], R), (2 * CHUNK, R), pltpu.SemaphoreType.DMA],
+        [(tops[0], R)] * 3 + [(tops[1], R)] * 3 + [(2 * CHUNK, R), pltpu.SemaphoreType.DMA],
         room, *s,
     )
     s = scatter_sum(s, second_move)

time: 190 us -> 190 us (level)
  no operation moved by 1% of the time
where the time goes in v9:
time: 190 us; the launch traced here: 188 us
  starting transfers between devices  49.9 us (26%)
  blocking collectives  49.3 us (26%)
  Pallas kernels  44.6 us (23%)
  waiting for transfers between devices  40.2 us (21%)
  local copies, waits for them, and re-layouts  2.64 us (1%)
    all_to_all x3, blocking collectives, exchange(): return lax.all_to_all(value, axes, 0, 0, tiled=True)  49.3 us
    pallas_call x16, Pallas kernels, call(): pl.pallas_call(body, input_output_aliases=aliases or {}, out_shape=[s if...  44.6 us
    ppermute x23, waiting for transfers between devices, send(): return lax.ppermute(value, AXES, pairs)  37.3 us
    ppermute x23, starting transfers between devices, send(): return lax.ppermute(value, AXES, pairs)  34.7 us
    all_to_all x3, starting transfers between devices, exchange(): return lax.all_to_all(value, axes, 0, 0, tiled=True)  15.2 us
  transfers between devices with their start and end apart: 26, of which 13 were waited for; matrix products, arithmetic and copies ran while one was open for 0% of the time, Pallas kernels for 14%

profile of v9, /device:TPU:1, one launch (start us, length us, event | category | flops | bytes accessed | tf_op | source)
XLA Modules:
  0.0 188.3 jit_solution(1566533327164029337)
XLA Ops:
  0.6 7.5 %shard_map.112 = (f32[256,256]{1,0:T(8,128)}, f32[8,128]{1,0:T(8,128)}, f32[384,256]{1,0:T(8,128)}) custom-call(bf16[1024,256]{1,0:T(8,128)(2,1)} %patient_hbm.1, f32[120,256]{1,0:T(8,128)} %month.5), custom_call_target="tpu_custom_call" | custom-call | tf_op jit(solution)/shard_map/pallas_call | solution.py:536
  8.2 17.1 %all_to_all.30.got = f32[16,24,256]{2,1,0:T(8,128)S(1)} all-to-all(f32[16,24,256]{2,1,0:T(8,128)} %bitcast.20), channel_id=1, replica_groups=mesh['z'=4,'y'=4,'x'=4,'h'=2,'c'=2] {'y','x'}, dimensions={0} | all-to-all | bytes 786432 | tf_op jit(solution)/shard_map/all_to_all | solution.py:76
  25.3 0.7 shard_map.117
  25.9 5.6 %all-to-all-start.1 = ((f32[4,24,256]{2,1,0:T(8,128)}), f32[4,24,256]{2,1,0:T(8,128)S(1)}, u32[]{:S(2)}, u32[]{:S(2)}) async-start(f32[4,24,256]{2,1,0:T(8,128)} %shard_map.117), calls=%async_computation.1 | async-start | bytes 196608 | tf_op jit(solution)/shard_map/all_to_all | solution.py:76
  32.2 8.4 %shard_map.113 = (f32[120,128,256]{2,1,0:T(8,128)}, f32[640,256]{1,0:T(8,128)}, s16[1312,256]{1,0:T(8,128)(2,1)}, s16[1312,256]{1,0:T(8,128)(2,1)}, s16[1312,256]{1,0:T(8,128)(2,1)}) custom-call(s32[1]{0:T(128)S(6)} %copy.17.live, s32[20]{0:T(128)} %patient_at.1, s32[20]{0:T(128)} %code_at.3, s32[20]{0:T(128)} %month_at.3, ...), custom_call_target="tpu_custom_call" | custom-call | tf_op jit(solution)/shard_map/pallas_call | solution.py:536
  40.6 0.1 collective-permute-start
  40.7 1.8 collective-permute-start.1
  42.6 0.8 collective-permute-start.2
  43.4 0.0 all-to-all-done.1.got
  43.4 19.6 %all_to_all.31 = f32[16,24,256]{2,1,0:T(8,128)S(1)} all-to-all(f32[16,24,256]{2,1,0:T(8,128)S(1)} %shard_map.118), channel_id=1, replica_groups=mesh['z'=4,'y'=4,'x'=4,'h'=2,'c'=2] {'y','x'}, dimensions={0} | all-to-all | bytes 786432 | tf_op jit(solution)/shard_map/all_to_all | solution.py:76
  63.0 3.8 %collective-permute-start.9 = (f32[384,256]{1,0:T(8,128)S(1)}, f32[384,256]{1,0:T(8,128)S(1)}, u32[]{:S(2)}, u32[]{:S(2)}) collective-permute-start(f32[384,256]{1,0:T(8,128)S(1)} %bitcast.13), channel_id=1, source_target_pairs={{0,1},{1,0},{2,3},{3,2},{4,5},{5,4},{6,7},{7,6},{8,9},{9,8},{10,11... | collective-permute-start | bytes 1179656 | tf_op jit(solution)/shard_map/ppermute | solution.py:64
  66.8 4.8 %shard_map.114.own_hbm.refs_5_ = f32[15360,256]{1,0:T(8,128)} custom-call(f32[256,256]{1,0:T(8,128)} %get-tuple-element.23.near, f32[8,128]{1,0:T(8,128)} %get-tuple-element.24.rho_ref, f32[640,256]{1,0:T(8,128)} %get-tuple-element.25.g_part, f32[2560,256]{1,0:T(8,128)} %duals_hbm.3), custom_call_target="tpu_custom_call" | custom-call | tf_op jit(solution)/shard_map/pallas_call | solution.py:536
  71.6 0.0 copy-start.1
  71.6 0.0 copy-start.9
  71.6 0.0 collective-permute-done.1.r2
  71.7 0.0 collective-permute-done.2.r3
  71.7 2.0 %shard_map.115 = (f32[320,256]{1,0:T(8,128)S(1)}, s16[336,256]{1,0:T(8,128)(2,1)S(1)}, s16[336,256]{1,0:T(8,128)(2,1)S(1)}, s16[336,256]{1,0:T(8,128)(2,1)S(1)}) custom-call(f32[15360,256]{1,0:T(8,128)} %shard_map.114.own_hbm.refs_5_, s16[1312,256]{1,0:T(8,128)(2,1)S(1)} %collective-permute-done.r1, s16[1312,256]{1,0:T(8,128)(2,1)S(1)} %collective-permute-done.1.r2, ...), custom_call_target="tpu_custom_call" | custom-call | tf_op jit(solution)/shard_map/pallas_call | solution.py:536
  73.7 0.0 copy-start.10
  73.7 0.0 copy-start.11
  73.7 0.9 collective-permute-start.3
  74.6 3.0 %collective-permute-start.4 = (s16[336,256]{1,0:T(8,128)(2,1)S(1)}, s16[336,256]{1,0:T(8,128)(2,1)S(1)}, u32[]{:S(2)}, u32[]{:S(2)}) collective-permute-start(s16[336,256]{1,0:T(8,128)(2,1)S(1)} %get-tuple-element.31), channel_id=1, source_target_pairs={{0,32},{1,9},{2,34},{3,11},{4,36},{5,13},{6,38},{7,15},{8,40},{9,1... | collective-permute-start | bytes 516104 | tf_op jit(solution)/shard_map/ppermute | solution.py:64
  77.6 1.9 %collective-permute-done.3.r1 = s16[336,256]{1,0:T(8,128)(2,1)S(1)} collective-permute-done((s16[336,256]{1,0:T(8,128)(2,1)S(1)}, s16[336,256]{1,0:T(8,128)(2,1)S(1)}, u32[]{:S(2)}, u32[]{:S(2)}) %collective-permute-start.3) | collective-permute-done | bytes 172064 | tf_op jit(solution)/shard_map/ppermute | solution.py:64
  79.5 2.9 %collective-permute-done.4.r2 = s16[336,256]{1,0:T(8,128)(2,1)S(1)} collective-permute-done((s16[336,256]{1,0:T(8,128)(2,1)S(1)}, s16[336,256]{1,0:T(8,128)(2,1)S(1)}, u32[]{:S(2)}, u32[]{:S(2)}) %collective-permute-start.4) | collective-permute-done | bytes 172064 | tf_op jit(solution)/shard_map/ppermute | solution.py:64
  82.5 0.3 shard_map.116
  82.8 1.8 collective-permute-start.6
  84.6 2.1 %collective-permute-start.7 = (s16[96,256]{1,0:T(8,128)(2,1)S(1)}, s16[96,256]{1,0:T(8,128)(2,1)S(1)}, u32[]{:S(2)}, u32[]{:S(2)}) collective-permute-start(s16[96,256]{1,0:T(8,128)(2,1)S(1)} %get-tuple-element.35), channel_id=1, source_target_pairs={{0,128},{1,129},{2,130},{3,131},{4,132},{5,133},{6,134},{7,135},{8... | collective-permute-start | bytes 147464 | tf_op jit(solution)/shard_map/ppermute | solution.py:64
  86.6 1.2 collective-permute-start.8
  87.9 2.0 %collective-permute-done.7.s2 = s16[96,256]{1,0:T(8,128)(2,1)S(1)} collective-permute-done((s16[96,256]{1,0:T(8,128)(2,1)S(1)}, s16[96,256]{1,0:T(8,128)(2,1)S(1)}, u32[]{:S(2)}, u32[]{:S(2)}) %collective-permute-start.7) | collective-permute-done | bytes 49184 | tf_op jit(solution)/shard_map/ppermute | solution.py:64
  89.9 0.5 collective-permute-done.8.s3
  90.4 1.4 shard_map.119
  91.8 1.3 collective-permute-start.12
  93.2 1.5 collective-permute-start.11
  94.7 0.6 collective-permute-start.10
  95.3 4.3 %collective-permute-done.10 = s16[128,256]{1,0:T(8,128)(2,1)S(1)} collective-permute-done((s16[128,256]{1,0:T(8,128)(2,1)S(1)}, s16[128,256]{1,0:T(8,128)(2,1)S(1)}, u32[]{:S(2)}, u32[]{:S(2)}) %collective-permute-start.10) | collective-permute-done | bytes 65568 | tf_op jit(solution)/shard_map/ppermute | solution.py:64
  99.7 0.1 collective-permute-start.15
  99.7 1.4 collective-permute-start.14
  101.2 1.5 collective-permute-start.13
  102.7 6.5 %collective-permute-done.15.r3 = s16[512,256]{1,0:T(8,128)(2,1)S(1)} collective-permute-done((s16[512,256]{1,0:T(8,128)(2,1)S(1)}, s16[512,256]{1,0:T(8,128)(2,1)S(1)}, u32[]{:S(2)}, u32[]{:S(2)}) %collective-permute-start.15) | collective-permute-done | bytes 262176 | tf_op jit(solution)/shard_map/ppermute | solution.py:64
  109.2 0.7 collective-permute-done.13.r1
  110.0 0.6 copy-done.4
  110.6 0.3 collective-permute-start.21
  110.9 1.2 collective-permute-start.19
  112.1 0.0 collective-permute-start.18
  112.1 5.4 %collective-permute-done.21.refs_3_.w1 = s16[768,256]{1,0:T(8,128)(2,1)S(1)} collective-permute-done((s16[768,256]{1,0:T(8,128)(2,1)S(1)}, s16[768,256]{1,0:T(8,128)(2,1)S(1)}, u32[]{:S(2)}, u32[]{:S(2)}) %collective-permute-start.21) | collective-permute-done | bytes 393248 | tf_op jit(solution)/shard_map/ppermute | solution.py:64
  117.5 5.7 %collective-permute-done.19.refs_3_.w3 = s16[768,256]{1,0:T(8,128)(2,1)S(1)} collective-permute-done((s16[768,256]{1,0:T(8,128)(2,1)S(1)}, s16[768,256]{1,0:T(8,128)(2,1)S(1)}, u32[]{:S(2)}, u32[]{:S(2)}) %collective-permute-start.19) | collective-permute-done | bytes 393248 | tf_op jit(solution)/shard_map/ppermute | solution.py:64
  123.2 2.0 %shard_map.123 = f32[384,256]{1,0:T(8,128)S(1)} custom-call(s32[1]{0:T(128)S(6)} %copy.17.live, s32[20]{0:T(128)S(1)} %copy-done.10, s32[20]{0:T(128)S(1)} %copy-done.11, s16[768,256]{1,0:T(8,128)(2,1)S(1)} %pad_add_fusion.refs_2_.w0, s16[768,256]{1,0:T(8,128)(2,1)S(1)} %collective-permute-done.21.refs_3_.w1, ...), custom_call_target="tpu_custom_call" | custom-call | tf_op jit(solution)/shard_map/pallas_call | solution.py:536
  125.3 12.7 %all_to_all.32.got = f32[16,24,256]{2,1,0:T(8,128)S(1)} all-to-all(f32[16,24,256]{2,1,0:T(8,128)S(1)} %bitcast.15), channel_id=1, replica_groups=mesh['z'=4,'y'=4,'x'=4,'h'=2,'c'=2] {'y','x'}, dimensions={0} | all-to-all | bytes 786432 | tf_op jit(solution)/shard_map/all_to_all | solution.py:76
  137.9 9.1 %collective-permute-start.22 = (f32[1,24,256]{2,1,0:T(8,128)S(1)}, f32[1,24,256]{2,1,0:T(8,128)S(1)}, u32[]{:S(2)}, u32[]{:S(2)}) collective-permute-start(f32[1,24,256]{2,1,0:T(8,128)S(1)} %shard_map.124), channel_id=1, source_target_pairs={{0,1},{1,0},{2,3},{3,2},{4,5},{5,4},{6,7},{7,6},{8,9},{9,8},{10,11... | collective-permute-start | bytes 73736 | tf_op jit(solution)/shard_map/ppermute | solution.py:64
  147.0 0.8 collective-permute-done.22
  147.9 0.7 shard_map.125
  148.6 5.8 %all-to-all-start.4 = ((f32[8,24,256]{2,1,0:T(8,128)}), f32[8,24,256]{2,1,0:T(8,128)S(1)}, u32[]{:S(2)}, u32[]{:S(2)}) async-start(f32[8,24,256]{2,1,0:T(8,128)} %shard_map.125), calls=%async_computation.4 | async-start | bytes 393216 | tf_op jit(solution)/shard_map/all_to_all | solution.py:76
  154.4 0.9 copy-done.3
  155.3 0.9 copy-done.5
  156.3 0.7 collective-permute-start.20
  157.0 0.9 collective-permute-start.17
  157.9 0.6 collective-permute-start.16
  158.4 2.9 %all-to-all-done.4.got = f32[8,24,256]{2,1,0:T(8,128)S(1)} async-done(((f32[8,24,256]{2,1,0:T(8,128)}), f32[8,24,256]{2,1,0:T(8,128)S(1)}, u32[]{:S(2)}, u32[]{:S(2)}) %all-to-all-start.4) | async-done | bytes 196640 | tf_op jit(solution)/shard_map/all_to_all | solution.py:76
  161.3 0.8 shard_map.126
  162.1 3.8 %all-to-all-start.5 = ((f32[16,24,256]{2,1,0:T(8,128)}), f32[16,24,256]{2,1,0:T(8,128)S(1)}, u32[]{:S(2)}, u32[]{:S(2)}) async-start(f32[16,24,256]{2,1,0:T(8,128)} %shard_map.126), calls=%async_computation.5 | async-start | bytes 786432 | tf_op jit(solution)/shard_map/all_to_all | solution.py:76
  165.9 0.4 collective-permute-done.20.refs_1_
  166.2 5.0 %shard_map.121.refs_6_ = f32[2560,256]{1,0:T(8,128)} custom-call(f32[256,256]{1,0:T(8,128)S(1)} %copy-done, f32[8,128]{1,0:T(8,128)S(1)} %copy-done.8, s16[1280,256]{1,0:T(8,128)(2,1)S(1)} %shard_map.120.refs_0_, s16[1280,256]{1,0:T(8,128)(2,1)} %collective-permute-done.20.refs_1_, s16[768,256]{1,0:T(8,128)(2,1)S(1)} %pad_add_fusion.refs_2_.w0, ...), custom_call_target="tpu_custom_call" | custom-call | tf_op jit(solution)/shard_map/pallas_call | solution.py:536
  171.2 6.1 %collective-permute-done.17.refs_1_ = s16[1280,256]{1,0:T(8,128)(2,1)} collective-permute-done((s16[1280,256]{1,0:T(8,128)(2,1)S(1)}, s16[1280,256]{1,0:T(8,128)(2,1)}, u32[]{:S(2)}, u32[]{:S(2)}) %collective-permute-start.17) | collective-permute-done | bytes 655392 | tf_op jit(solution)/shard_map/ppermute | solution.py:64
  177.4 5.2 %shard_map.122 = f32[2560,256]{1,0:T(8,128)} custom-call(f32[256,256]{1,0:T(8,128)S(1)} %copy-done, f32[8,128]{1,0:T(8,128)S(1)} %copy-done.8, s16[1280,256]{1,0:T(8,128)(2,1)} %collective-permute-done.16.refs_0_, s16[1280,256]{1,0:T(8,128)(2,1)} %collective-permute-done.17.refs_1_, ...), custom_call_target="tpu_custom_call", output_to_operand_aliasing={{}: (8, {})} | custom-call | tf_op jit(solution)/shard_map/pallas_call | solution.py:536
  182.6 5.7 %shard_map.127 = f32[120,256]{1,0:T(8,128)} custom-call(f32[384,256]{1,0:T(8,128)S(1)} %bitcast.12, f32[256,256]{1,0:T(8,128)S(1)} %copy-done.7, f32[120,256]{1,0:T(8,128)S(1)} %copy-done.1), custom_call_target="tpu_custom_call" | custom-call | tf_op jit(solution)/shard_map/pallas_call | solution.py:536
  (41 shorter events, 0.3 us)
Async XLA Ops:
  25.9 17.4 %all-to-all-start.1 = ((f32[4,24,256]{2,1,0:T(8,128)}), f32[4,24,256]{2,1,0:T(8,128)S(1)}, u32[]{:S(2)}, u32[]{:S(2)}) async-start(f32[4,24,256]{2,1,0:T(8,128)} %shard_map.117), calls=%async_computation.1 | async-start | bytes 196608 | tf_op jit(solution)/shard_map/all_to_all | solution.py:76
  40.6 31.0 %collective-permute-start = (s16[1312,256]{1,0:T(8,128)(2,1)}, s16[1312,256]{1,0:T(8,128)(2,1)S(1)}, u32[]{:S(2)}, u32[]{:S(2)}) collective-permute-start(s16[1312,256]{1,0:T(8,128)(2,1)} %get-tuple-element.26), channel_id=1, source_target_pairs={{0,4},{1,17},{2,6},{3,19},{4,8},{5,21},{6,10},{7,23},{8,12},{9,25}... | collective-permute-start | bytes 2015240 | tf_op jit(solution)/shard_map/ppermute | solution.py:64
  40.7 30.9 %collective-permute-start.1 = (s16[1312,256]{1,0:T(8,128)(2,1)}, s16[1312,256]{1,0:T(8,128)(2,1)S(1)}, u32[]{:S(2)}, u32[]{:S(2)}) collective-permute-start(s16[1312,256]{1,0:T(8,128)(2,1)} %get-tuple-element.27), channel_id=1, source_target_pairs={{0,8},{1,33},{2,10},{3,35},{4,12},{5,37},{6,14},{7,39},{8,0},{9,41... | collective-permute-start | bytes 2015240 | tf_op jit(solution)/shard_map/ppermute | solution.py:64
  42.6 29.1 %collective-permute-start.2 = (s16[1312,256]{1,0:T(8,128)(2,1)}, s16[1312,256]{1,0:T(8,128)(2,1)S(1)}, u32[]{:S(2)}, u32[]{:S(2)}) collective-permute-start(s16[1312,256]{1,0:T(8,128)(2,1)} %get-tuple-element.28), channel_id=1, source_target_pairs={{0,12},{1,49},{2,14},{3,51},{4,0},{5,53},{6,2},{7,55},{8,4},{9,57}... | collective-permute-start | bytes 2015240 | tf_op jit(solution)/shard_map/ppermute | solution.py:64
  63.0 27.4 %collective-permute-start.9 = (f32[384,256]{1,0:T(8,128)S(1)}, f32[384,256]{1,0:T(8,128)S(1)}, u32[]{:S(2)}, u32[]{:S(2)}) collective-permute-start(f32[384,256]{1,0:T(8,128)S(1)} %bitcast.13), channel_id=1, source_target_pairs={{0,1},{1,0},{2,3},{3,2},{4,5},{5,4},{6,7},{7,6},{8,9},{9,8},{10,11... | collective-permute-start | bytes 1179656 | tf_op jit(solution)/shard_map/ppermute | solution.py:64
  71.6 18.8 %copy-start.1 = (f32[120,256]{1,0:T(8,128)S(1)}, f32[120,256]{1,0:T(8,128)}, u32[]{:S(2)}) copy-start(f32[120,256]{1,0:T(8,128)} %month.5) | copy-start | bytes 368644
  71.6 18.8 %copy-start.9 = (f32[40,256]{1,0:T(8,128)S(1)}, f32[40,256]{1,0:T(8,128)}, u32[]{:S(2)}) copy-start(f32[40,256]{1,0:T(8,128)} %z0_ref.1) | copy-start | bytes 122884
  73.7 49.6 %copy-start.10 = (s32[20]{0:T(128)S(1)}, s32[20]{0:T(128)}, u32[]{:S(2)}) copy-start(s32[20]{0:T(128)} %code_at.3) | copy-start | bytes 244
  73.7 49.6 %copy-start.11 = (s32[20]{0:T(128)S(1)}, s32[20]{0:T(128)}, u32[]{:S(2)}) copy-start(s32[20]{0:T(128)} %month_at.3) | copy-start | bytes 244
  73.7 5.8 %collective-permute-start.3 = (s16[336,256]{1,0:T(8,128)(2,1)S(1)}, s16[336,256]{1,0:T(8,128)(2,1)S(1)}, u32[]{:S(2)}, u32[]{:S(2)}) collective-permute-start(s16[336,256]{1,0:T(8,128)(2,1)S(1)} %get-tuple-element.30), channel_id=1, source_target_pairs={{0,16},{1,5},{2,18},{3,7},{4,20},{5,9},{6,22},{7,11},{8,24},{9,13}... | collective-permute-start | bytes 516104 | tf_op jit(solution)/shard_map/ppermute | solution.py:64
  74.6 7.9 %collective-permute-start.4 = (s16[336,256]{1,0:T(8,128)(2,1)S(1)}, s16[336,256]{1,0:T(8,128)(2,1)S(1)}, u32[]{:S(2)}, u32[]{:S(2)}) collective-permute-start(s16[336,256]{1,0:T(8,128)(2,1)S(1)} %get-tuple-element.31), channel_id=1, source_target_pairs={{0,32},{1,9},{2,34},{3,11},{4,36},{5,13},{6,38},{7,15},{8,40},{9,1... | collective-permute-start | bytes 516104 | tf_op jit(solution)/shard_map/ppermute | solution.py:64
  77.6 4.9 %collective-permute-start.5 = (s16[336,256]{1,0:T(8,128)(2,1)S(1)}, s16[336,256]{1,0:T(8,128)(2,1)S(1)}, u32[]{:S(2)}, u32[]{:S(2)}) collective-permute-start(s16[336,256]{1,0:T(8,128)(2,1)S(1)} %get-tuple-element.32), channel_id=1, source_target_pairs={{0,48},{1,13},{2,50},{3,15},{4,52},{5,1},{6,54},{7,3},{8,56},{9,5}... | collective-permute-start | bytes 516104 | tf_op jit(solution)/shard_map/ppermute | solution.py:64
  82.8 5.1 %collective-permute-start.6 = (s16[96,256]{1,0:T(8,128)(2,1)S(1)}, s16[96,256]{1,0:T(8,128)(2,1)S(1)}, u32[]{:S(2)}, u32[]{:S(2)}) collective-permute-start(s16[96,256]{1,0:T(8,128)(2,1)S(1)} %get-tuple-element.34), channel_id=1, source_target_pairs={{0,64},{1,65},{2,66},{3,67},{4,68},{5,69},{6,70},{7,71},{8,72},{9,... | collective-permute-start | bytes 147464 | tf_op jit(solution)/shard_map/ppermute | solution.py:64
  84.6 5.3 %collective-permute-start.7 = (s16[96,256]{1,0:T(8,128)(2,1)S(1)}, s16[96,256]{1,0:T(8,128)(2,1)S(1)}, u32[]{:S(2)}, u32[]{:S(2)}) collective-permute-start(s16[96,256]{1,0:T(8,128)(2,1)S(1)} %get-tuple-element.35), channel_id=1, source_target_pairs={{0,128},{1,129},{2,130},{3,131},{4,132},{5,133},{6,134},{7,135},{8... | collective-permute-start | bytes 147464 | tf_op jit(solution)/shard_map/ppermute | solution.py:64
  86.6 3.7 %collective-permute-start.8 = (s16[96,256]{1,0:T(8,128)(2,1)S(1)}, s16[96,256]{1,0:T(8,128)(2,1)S(1)}, u32[]{:S(2)}, u32[]{:S(2)}) collective-permute-start(s16[96,256]{1,0:T(8,128)(2,1)S(1)} %get-tuple-element.36), channel_id=1, source_target_pairs={{0,192},{1,193},{2,194},{3,195},{4,196},{5,197},{6,198},{7,199},{8... | collective-permute-start | bytes 147464 | tf_op jit(solution)/shard_map/ppermute | solution.py:64
  91.8 33.4 %copy-start.6 = (f32[256,256]{1,0:T(8,128)}, f32[256,256]{1,0:T(8,128)S(1)}, u32[]{:S(2)}) copy-start(f32[256,256]{1,0:T(8,128)S(1)} %get-tuple-element.42.gram) | copy-start | bytes 786436
  91.8 7.8 %collective-permute-start.12 = (s16[128,256]{1,0:T(8,128)(2,1)S(1)}, s16[128,256]{1,0:T(8,128)(2,1)S(1)}, u32[]{:S(2)}, u32[]{:S(2)}) collective-permute-start(s16[128,256]{1,0:T(8,128)(2,1)S(1)} %get-tuple-element.39), channel_id=1, source_target_pairs={{0,64},{1,65},{2,66},{3,67},{4,68},{5,69},{6,70},{7,71},{8,72},{9,... | collective-permute-start | bytes 196616 | tf_op jit(solution)/shard_map/ppermute | solution.py:64
  93.2 6.5 %collective-permute-start.11 = (s16[128,256]{1,0:T(8,128)(2,1)S(1)}, s16[128,256]{1,0:T(8,128)(2,1)S(1)}, u32[]{:S(2)}, u32[]{:S(2)}) collective-permute-start(s16[128,256]{1,0:T(8,128)(2,1)S(1)} %get-tuple-element.39), channel_id=1, source_target_pairs={{0,128},{1,129},{2,130},{3,131},{4,132},{5,133},{6,134},{7,135},{8... | collective-permute-start | bytes 196616 | tf_op jit(solution)/shard_map/ppermute | solution.py:64
  94.7 4.9 %collective-permute-start.10 = (s16[128,256]{1,0:T(8,128)(2,1)S(1)}, s16[128,256]{1,0:T(8,128)(2,1)S(1)}, u32[]{:S(2)}, u32[]{:S(2)}) collective-permute-start(s16[128,256]{1,0:T(8,128)(2,1)S(1)} %get-tuple-element.39), channel_id=1, source_target_pairs={{0,192},{1,193},{2,194},{3,195},{4,196},{5,197},{6,198},{7,199},{8... | collective-permute-start | bytes 196616 | tf_op jit(solution)/shard_map/ppermute | solution.py:64
  99.7 9.5 %collective-permute-start.15 = (s16[512,256]{1,0:T(8,128)(2,1)S(1)}, s16[512,256]{1,0:T(8,128)(2,1)S(1)}, u32[]{:S(2)}, u32[]{:S(2)}) collective-permute-start(s16[512,256]{1,0:T(8,128)(2,1)S(1)} %constant_dynamic-update-slice_fusion.r0), channel_id=1, source_target_pairs={{0,16},{1,5},{2,18},{3,7},{4,20},{5,9},{6,22},{7,11},{8,24},{9,13}... | collective-permute-start | bytes 786440 | tf_op jit(solution)/shard_map/ppermute | solution.py:64
  99.7 9.4 %collective-permute-start.14 = (s16[512,256]{1,0:T(8,128)(2,1)S(1)}, s16[512,256]{1,0:T(8,128)(2,1)S(1)}, u32[]{:S(2)}, u32[]{:S(2)}) collective-permute-start(s16[512,256]{1,0:T(8,128)(2,1)S(1)} %constant_dynamic-update-slice_fusion.r0), channel_id=1, source_target_pairs={{0,32},{1,9},{2,34},{3,11},{4,36},{5,13},{6,38},{7,15},{8,40},{9,1... | collective-permute-start | bytes 786440 | tf_op jit(solution)/shard_map/ppermute | solution.py:64
  101.2 8.7 %collective-permute-start.13 = (s16[512,256]{1,0:T(8,128)(2,1)S(1)}, s16[512,256]{1,0:T(8,128)(2,1)S(1)}, u32[]{:S(2)}, u32[]{:S(2)}) collective-permute-start(s16[512,256]{1,0:T(8,128)(2,1)S(1)} %constant_dynamic-update-slice_fusion.r0), channel_id=1, source_target_pairs={{0,48},{1,13},{2,50},{3,15},{4,52},{5,1},{6,54},{7,3},{8,56},{9,5}... | collective-permute-start | bytes 786440 | tf_op jit(solution)/shard_map/ppermute | solution.py:64
  109.2 0.8 copy-start.2
  109.9 0.7 copy-start.4
  110.6 6.9 %collective-permute-start.21 = (s16[768,256]{1,0:T(8,128)(2,1)S(1)}, s16[768,256]{1,0:T(8,128)(2,1)S(1)}, u32[]{:S(2)}, u32[]{:S(2)}) collective-permute-start(s16[768,256]{1,0:T(8,128)(2,1)S(1)} %pad_add_fusion.refs_2_.w0), channel_id=1, source_target_pairs={{0,12},{1,49},{2,14},{3,51},{4,0},{5,53},{6,2},{7,55},{8,4},{9,57}... | collective-permute-start | bytes 1179656 | tf_op jit(solution)/shard_map/ppermute | solution.py:64
  110.9 12.3 %collective-permute-start.19 = (s16[768,256]{1,0:T(8,128)(2,1)S(1)}, s16[768,256]{1,0:T(8,128)(2,1)S(1)}, u32[]{:S(2)}, u32[]{:S(2)}) collective-permute-start(s16[768,256]{1,0:T(8,128)(2,1)S(1)} %pad_add_fusion.refs_2_.w0), channel_id=1, source_target_pairs={{0,4},{1,17},{2,6},{3,19},{4,8},{5,21},{6,10},{7,23},{8,12},{9,25}... | collective-permute-start | bytes 1179656 | tf_op jit(solution)/shard_map/ppermute | solution.py:64
  112.1 11.2 %collective-permute-start.18 = (s16[768,256]{1,0:T(8,128)(2,1)S(1)}, s16[768,256]{1,0:T(8,128)(2,1)S(1)}, u32[]{:S(2)}, u32[]{:S(2)}) collective-permute-start(s16[768,256]{1,0:T(8,128)(2,1)S(1)} %pad_add_fusion.refs_2_.w0), channel_id=1, source_target_pairs={{0,8},{1,33},{2,10},{3,35},{4,12},{5,37},{6,14},{7,39},{8,0},{9,41... | collective-permute-start | bytes 1179656 | tf_op jit(solution)/shard_map/ppermute | solution.py:64
  125.2 41.0 %copy-start = (f32[256,256]{1,0:T(8,128)S(1)}, f32[256,256]{1,0:T(8,128)}, u32[]{:S(2)}) copy-start(f32[256,256]{1,0:T(8,128)} %get-tuple-element.23.near) | copy-start | bytes 786436
  125.2 41.0 %copy-start.8 = (f32[8,128]{1,0:T(8,128)S(1)}, f32[8,128]{1,0:T(8,128)}, u32[]{:S(2)}) copy-start(f32[8,128]{1,0:T(8,128)} %get-tuple-element.24.rho_ref) | copy-start | bytes 12292
  137.9 9.9 %collective-permute-start.22 = (f32[1,24,256]{2,1,0:T(8,128)S(1)}, f32[1,24,256]{2,1,0:T(8,128)S(1)}, u32[]{:S(2)}, u32[]{:S(2)}) collective-permute-start(f32[1,24,256]{2,1,0:T(8,128)S(1)} %shard_map.124), channel_id=1, source_target_pairs={{0,1},{1,0},{2,3},{3,2},{4,5},{5,4},{6,7},{7,6},{8,9},{9,8},{10,11... | collective-permute-start | bytes 73736 | tf_op jit(solution)/shard_map/ppermute | solution.py:64
  148.6 12.7 %all-to-all-start.4 = ((f32[8,24,256]{2,1,0:T(8,128)}), f32[8,24,256]{2,1,0:T(8,128)S(1)}, u32[]{:S(2)}, u32[]{:S(2)}) async-start(f32[8,24,256]{2,1,0:T(8,128)} %shard_map.125), calls=%async_computation.4 | async-start | bytes 393216 | tf_op jit(solution)/shard_map/all_to_all | solution.py:76
  154.4 0.9 copy-start.3
  155.3 0.9 copy-start.5
  156.3 9.9 %collective-permute-start.20 = (s16[1280,256]{1,0:T(8,128)(2,1)S(1)}, s16[1280,256]{1,0:T(8,128)(2,1)}, u32[]{:S(2)}, u32[]{:S(2)}) collective-permute-start(s16[1280,256]{1,0:T(8,128)(2,1)S(1)} %shard_map.120.refs_0_), channel_id=1, source_target_pairs={{0,12},{1,49},{2,14},{3,51},{4,0},{5,53},{6,2},{7,55},{8,4},{9,57}... | collective-permute-start | bytes 1966088 | tf_op jit(solution)/shard_map/ppermute | solution.py:64
  157.0 20.4 %collective-permute-start.17 = (s16[1280,256]{1,0:T(8,128)(2,1)S(1)}, s16[1280,256]{1,0:T(8,128)(2,1)}, u32[]{:S(2)}, u32[]{:S(2)}) collective-permute-start(s16[1280,256]{1,0:T(8,128)(2,1)S(1)} %shard_map.120.refs_0_), channel_id=1, source_target_pairs={{0,4},{1,17},{2,6},{3,19},{4,8},{5,21},{6,10},{7,23},{8,12},{9,25}... | collective-permute-start | bytes 1966088 | tf_op jit(solution)/shard_map/ppermute | solution.py:64
  157.9 19.5 %collective-permute-start.16 = (s16[1280,256]{1,0:T(8,128)(2,1)S(1)}, s16[1280,256]{1,0:T(8,128)(2,1)}, u32[]{:S(2)}, u32[]{:S(2)}) collective-permute-start(s16[1280,256]{1,0:T(8,128)(2,1)S(1)} %shard_map.120.refs_0_), channel_id=1, source_target_pairs={{0,8},{1,33},{2,10},{3,35},{4,12},{5,37},{6,14},{7,39},{8,0},{9,41... | collective-permute-start | bytes 1966088 | tf_op jit(solution)/shard_map/ppermute | solution.py:64
  162.1 20.5 %all-to-all-start.5 = ((f32[16,24,256]{2,1,0:T(8,128)}), f32[16,24,256]{2,1,0:T(8,128)S(1)}, u32[]{:S(2)}, u32[]{:S(2)}) async-start(f32[16,24,256]{2,1,0:T(8,128)} %shard_map.126), calls=%async_computation.5 | async-start | bytes 786432 | tf_op jit(solution)/shard_map/all_to_all | solution.py:76
  171.2 11.4 %copy-start.7 = (f32[256,256]{1,0:T(8,128)S(1)}, f32[256,256]{1,0:T(8,128)}, u32[]{:S(2)}) copy-start(f32[256,256]{1,0:T(8,128)} %copy-done.6) | copy-start | bytes 786436
